TPU v7x, 32 devices: a whole 2x2x4 slice. The times are simulated.
32 devices in a mesh: date: 8 (over y, x, core), range: 4 (over z).
Axes of the slice: x: 2, y: 2, z: 4, core: 2. Of those that a mesh axis runs over, the one named last changes fastest.
Arguments:
- epoch_tiles_quadrature: bfloat16 [16, 2, 256, 1024], P('date', None, None, 'range'), may hold values from -6 to 6
- along_track_whole_displacement: int32 [16], replicated, may hold values from -8 to 8
- along_track_subpixel_weights: int32 [16], replicated, may hold values from 0 to 15
- slant_whole_displacement: int32 [16], replicated, may hold values from -12 to 12
- slant_subpixel_weights: int32 [16], replicated, may hold values from 0 to 15
- sweeps_each_epoch: int32 [16], replicated, may hold values from 1 to 4
- baseline_companion_gap: int32 [16, 2], replicated, may hold values from 2 to 3, as said below
- master_epoch_image: int32 [1], replicated, may hold values from 0 to 15
Outputs:
- interferograms: float32 [16, 6, 16, 256], P('date', None, None, 'range')
- coherence: float32 [16, 3, 16, 256], P('date', None, None, 'range')
Inputs may be any that keep to these rules, and one draw needn't show every extreme that they name: `baseline_companion_gap`: the later gap is 3 for odd dates and 2 or 3 for even dates; the earlier gap is 3 for even dates and 2 or 3 for odd dates.
All inputs are finite; a program needn't handle non-finite values.
Results may differ from a plain program's by a relative error of at most 0.0061.
Values may be sent and summed in bfloat16 or wider, within the bound.
No kernel may reach another device: no remote copies, remote signals or barrier semaphores. Data moves between devices by JAX's collectives and lax.ppermute only.
A program may use at most 64 MiB of HBM per device.

v0:
```python
import jax
import jax.numpy as jnp
from jax import lax
from jax.sharding import PartitionSpec as P

MAX_SWEEPS = 4
TAPS = 8
FRACTIONS = 16
MARGIN = 16
LOOK_AZ = 16
LOOK_RG = 4


def with_halo(block, sides, width):
    for axis, dim in sides:
        count = lax.axis_size(axis)
        forward = [(i, i + 1) for i in range(count - 1)]
        backward = [(target, source) for source, target in forward]
        low = lax.ppermute(
            lax.slice_in_dim(block, block.shape[dim] - width, None, axis=dim), axis, forward
        )
        high = lax.ppermute(lax.slice_in_dim(block, 0, width, axis=dim), axis, backward)
        block = jnp.concatenate([low, block, high], axis=dim)
    return block


def from_root(array, axis, root):
    mine = lax.axis_index(axis) == root
    return lax.psum(jnp.where(mine, array, jnp.zeros_like(array)), axis)


def shifted_2(block, axis, distance):
    devices = range(lax.axis_size(axis))
    route = [(i - distance, i) for i in devices if i - distance in devices]
    return lax.ppermute(block, axis, route)


def kernel_weights():
    fraction = jnp.arange(FRACTIONS, dtype=jnp.float32)[:, None] / FRACTIONS
    spacing = jnp.arange(TAPS, dtype=jnp.float32)[None, :] - (TAPS // 2 - 1) - fraction
    window = jnp.cos(jnp.pi * spacing / (TAPS + 1)) ** 2
    weights = jnp.sinc(spacing) * window
    return (weights / jnp.sum(weights, axis=1, keepdims=True)).astype(jnp.bfloat16)


def tap_matrix(weights, tap_offsets):
    result = jnp.zeros(tap_offsets.shape, jnp.float32)
    for tap in range(TAPS):
        result = result + jnp.where(tap_offsets == tap, weights[tap].astype(jnp.float32), 0.0)
    return result.astype(jnp.bfloat16)


def window_pool(values):
    return values.reshape(
        values.shape[0] // LOOK_AZ, LOOK_AZ, values.shape[1] // LOOK_RG, LOOK_RG
    ).sum(axis=(1, 3))


def looks(first, second):
    left = first.astype(jnp.float32)
    right = second.astype(jnp.float32)
    real_part = window_pool(left[0] * right[0] + left[1] * right[1])
    imag_part = window_pool(left[1] * right[0] - left[0] * right[1])
    power_left = window_pool(left[0] * left[0] + left[1] * left[1])
    power_right = window_pool(right[0] * right[0] + right[1] * right[1])
    scale = 1.0 / jnp.sqrt(jnp.float32(LOOK_AZ * LOOK_RG))
    coherent = jnp.sqrt(real_part * real_part + imag_part * imag_part) / jnp.sqrt(
        power_left * power_right + 1e-06
    )
    return (jnp.stack([real_part * scale, imag_part * scale]), coherent)


def pair_date(present_epoch_number, baseline_companion_gap, total_dates, kind):
    safe_index = jnp.minimum(present_epoch_number, total_dates - 1)
    distance = baseline_companion_gap[safe_index, kind]
    if kind == 0:
        forward = safe_index + distance
        return jnp.where(forward < total_dates, forward, safe_index - distance)
    backward = safe_index - distance
    return jnp.where(backward >= 0, backward, safe_index + distance)


def body(
    epoch_tiles_quadrature,
    along_track_whole_displacement,
    along_track_subpixel_weights,
    slant_whole_displacement,
    slant_subpixel_weights,
    sweeps_each_epoch,
    baseline_companion_gap,
    master_epoch_image,
):
    sinc_weight_table = kernel_weights()
    along_track_height = epoch_tiles_quadrature.shape[2]
    column_count = epoch_tiles_quadrature.shape[3]
    local_dates = epoch_tiles_quadrature.shape[0]
    total_dates = local_dates * lax.axis_size("date")
    device_index = lax.axis_index("date")
    first_date = device_index * local_dates
    wide = with_halo(epoch_tiles_quadrature, (("range", 3),), MARGIN)
    wide_rows = jnp.arange(column_count + 2 * MARGIN, dtype=jnp.int32)[:, None]
    out_columns = jnp.arange(column_count, dtype=jnp.int32)[None, :]
    line_rows = jnp.arange(along_track_height, dtype=jnp.int32)[:, None]
    line_columns = jnp.arange(along_track_height, dtype=jnp.int32)[None, :]

    def resample_one(source_block, present_epoch_number):
        column_offsets = (
            wide_rows
            - out_columns
            - MARGIN
            - slant_whole_displacement[present_epoch_number]
            + (TAPS // 2 - 1)
        )
        column_taps = tap_matrix(
            sinc_weight_table[slant_subpixel_weights[present_epoch_number]], column_offsets
        )
        ranged = jnp.einsum(
            "pli,ic->plc", source_block, column_taps, preferred_element_type=jnp.float32
        ).astype(jnp.bfloat16)
        line_offsets = (
            line_columns
            - line_rows
            - along_track_whole_displacement[present_epoch_number]
            + (TAPS // 2 - 1)
        )
        line_taps = tap_matrix(
            sinc_weight_table[along_track_subpixel_weights[present_epoch_number]], line_offsets
        )
        shifted = jnp.einsum("ml,plc->pmc", line_taps, ranged, preferred_element_type=jnp.float32)
        usable_scanline_flags = (
            jnp.arange(along_track_height, dtype=jnp.int32)
            < sweeps_each_epoch[present_epoch_number] * (along_track_height // MAX_SWEEPS)
        ).astype(jnp.float32)
        return (shifted * usable_scanline_flags[None, :, None]).astype(jnp.bfloat16)

    resampled_own = jnp.stack(
        [resample_one(wide[slot], first_date + slot) for slot in range(local_dates)]
    )
    owner = master_epoch_image[0] // local_dates
    local_slot = master_epoch_image[0] % local_dates
    mine = lax.dynamic_index_in_dim(resampled_own, local_slot, 0, keepdims=False)
    ref_block = from_root(mine, "date", owner)
    from_next = shifted_2(resampled_own, "date", -1)
    ahead = shifted_2(resampled_own[0], "date", -2)
    candidates = [
        (resampled_own[0], first_date),
        (resampled_own[1], first_date + 1),
        (from_next[0], first_date + 2),
        (from_next[1], first_date + 3),
        (ahead, first_date + 4),
    ]
    from_prev = shifted_2(resampled_own, "date", 1)
    behind = shifted_2(resampled_own[1], "date", 2)
    candidates = candidates + [
        (from_prev[1], first_date - 1),
        (from_prev[0], first_date - 2),
        (behind, first_date - 3),
    ]
    candidate_stack = jnp.stack(
        [block for block, block_date in candidates] + [jnp.zeros_like(resampled_own[0])]
    )
    empty_slot = len(candidates)
    ifg_list = []
    coh_list = []
    for slot in range(local_dates):
        present_epoch_number = first_date + slot
        ref_ifg, ref_coh = looks(resampled_own[slot], ref_block)
        ifg_parts = [ref_ifg]
        coh_parts = [ref_coh]
        for kind in range(2):
            partner = pair_date(present_epoch_number, baseline_companion_gap, total_dates, kind)
            position = jnp.int32(empty_slot)
            for number, (candidate, candidate_date) in enumerate(candidates):
                position = jnp.where(partner == candidate_date, jnp.int32(number), position)
            partner_block = lax.dynamic_index_in_dim(candidate_stack, position, 0, keepdims=False)
            pair_ifg, pair_coh = looks(resampled_own[slot], partner_block)
            ifg_parts.append(pair_ifg)
            coh_parts.append(pair_coh)
        ifg_list.append(jnp.concatenate(ifg_parts, axis=0))
        coh_list.append(jnp.stack(coh_parts))
    return (jnp.stack(ifg_list), jnp.stack(coh_list))


def solution(mesh):
    in_specs = (P("date", None, None, "range"), P(), P(), P(), P(), P(), P(), P())
    out_specs = (P("date", None, None, "range"), P("date", None, None, "range"))
    return jax.shard_map(body, mesh=mesh, in_specs=in_specs, out_specs=out_specs, check_vma=False)
```

profile of v0, /device:TPU:8, one launch (start us, length us, event | category | flops | bytes accessed | tf_op | source)
XLA Modules:
  0.0 200.2 jit_solution(604179163001344328)
XLA Ops:
  8.5 3.5 %collective-permute-start = (bf16[2,2,256,16]{2,3,1,0:T(8,128)(2,1)S(1)}, bf16[2,2,256,16]{2,3,1,0:T(8,128)(2,1)S(1)}, u32[]{:S(2)}, u32[]{:S(2)}) collective-permute-start(bf16[2,2,256,16]{2,3,1,0:T(8,128)(2,1)S(1)} %get-tuple-element.30), channel_id=1, source_target_pairs={{0,1},{1,2},{2,3},{4,5},{5,6},{6,7},{8,9},{9,10},{10,11},{12,13},{... | collective-permute-start | bytes 98312 | tf_op jit(solution)/shard_map/ppermute | solution.py:19
  12.0 2.4 %collective-permute-start.1 = (bf16[2,2,256,16]{2,3,1,0:T(8,128)(2,1)S(1)}, bf16[2,2,256,16]{2,3,1,0:T(8,128)(2,1)S(1)}, u32[]{:S(2)}, u32[]{:S(2)}) collective-permute-start(bf16[2,2,256,16]{2,3,1,0:T(8,128)(2,1)S(1)} %get-tuple-element.31), channel_id=1, source_target_pairs={{1,0},{2,1},{3,2},{5,4},{6,5},{7,6},{9,8},{10,9},{11,10},{13,12},{... | collective-permute-start | bytes 98312 | tf_op jit(solution)/shard_map/ppermute | solution.py:22
  57.9 2.9 %constant_dynamic-update-slice_fusion.2 = (bf16[9,2,256,256]{2,3,1,0:T(8,128)(2,1)}, bf16[2,256,256]{2,1,0:T(8,128)(2,1)S(1)}) fusion(f32[256]{0:T(256)S(1)} %compare_convert_fusion.1, f32[]{:T(128)S(6)} %convert.47, f32[]{:T(128)S(6)} %convert.46, f32[]{:T(128)S(6)} %convert.45, f32[]{:T(128)S(6)} %convert.44, f32[]{:T(128)S(6)} %convert.43, ...), kind=kOutput, calls=%fused_computation.175 | convolution fusion | flops 146833408 | bytes 820296 | tf_op jit(solution)/shard_map/ml,plc->pmc/dot_general | solution.py:129
  60.8 2.9 %constant_dynamic-update-slice_fusion.1 = (bf16[9,2,256,256]{2,3,1,0:T(8,128)(2,1)}, bf16[2,256,256]{2,1,0:T(8,128)(2,1)}) fusion(bf16[9,2,256,256]{2,3,1,0:T(8,128)(2,1)} %get-tuple-element.100, f32[256]{0:T(256)S(1)} %compare_convert_fusion, f32[]{:T(128)S(6)} %convert.63, f32[]{:T(128)S(6)} %convert.62, f32[]{:T(128)S(6)} %convert.61, f32[]{:T(128)S(6)} %convert.60, ...), kind=kOutput, calls=%fused_computation.174 | convolution fusion | flops 146833408 | bytes 821312 | tf_op jit(solution)/shard_map/ml,plc->pmc/dot_general | solution.py:129
  63.7 1.8 pad_maximum_fusion
  66.8 3.8 %collective-permute-start.4 = (bf16[2,2,256,256]{2,3,1,0:T(8,128)(2,1)}, bf16[2,2,256,256]{2,3,1,0:T(8,128)(2,1)}, u32[]{:S(2)}, u32[]{:S(2)}) collective-permute-start(bf16[2,2,256,256]{2,3,1,0:T(8,128)(2,1)} %pad_maximum_fusion), channel_id=1, source_target_pairs={{0,4},{4,8},{8,12},{12,16},{16,20},{20,24},{24,28},{1,5},{5,9},{9,... | collective-permute-start | bytes 1572872 | tf_op jit(solution)/shard_map/ppermute | solution.py:35
  73.0 5.3 %collective-permute-start.5 = (bf16[2,256,256]{1,2,0:T(8,128)(2,1)}, bf16[2,256,256]{1,2,0:T(8,128)(2,1)}, u32[]{:S(2)}, u32[]{:S(2)}) collective-permute-start(bf16[2,256,256]{1,2,0:T(8,128)(2,1)} %bitcast.51), channel_id=1, source_target_pairs={{0,8},{4,12},{8,16},{12,20},{16,24},{20,28},{1,9},{5,13},{9,17},{1... | collective-permute-start | bytes 786440 | tf_op jit(solution)/shard_map/ppermute | solution.py:35
  78.3 1.8 fusion.20
  80.1 54.5 %all-reduce.2.cloned.1.call-done = bf16[2,256,256]{1,2,0:T(8,128)(2,1)} async-done(((bf16[2,256,256]{1,2,0:T(8,128)(2,1)}), bf16[2,256,256]{1,2,0:T(8,128)(2,1)}) %all-reduce.2.cloned.1.call-update) | async-done | bytes 262160 | tf_op jit(solution)/shard_map/psum | solution.py:29
  136.6 1.7 add.597
  138.2 2.8 %sub.243 = f32[16,16,64,4]{1,0,3,2:T(8,128)} reshape(f32[1,256,256]{1,2,0:T(8,128)} %get-tuple-element.18) | data formatting | bytes 524288 | tf_op jit(solution)/shard_map/sub | solution.py:63
  141.3 1.8 reduce_sum.208
  143.1 1.7 add.609
  145.0 1.7 add.621
  147.0 1.9 constant_dynamic-update-slice_fusion
  148.8 1.7 bitcast_dynamic-update-slice_fusion.1
  150.5 1.7 slice_dynamic-update-slice_fusion.1
  152.2 1.7 slice_dynamic-update-slice_fusion
  153.9 1.7 bitcast_dynamic-update-slice_fusion
  156.4 2.4 %dynamic-slice_convert_fusion.2 = (f32[1,2,256,256]{2,3,1,0:T(8,128)}, f32[1,2,256,256]{2,3,1,0:T(8,128)S(1)}, f32[1,2,256,256]{2,3,1,0:T(8,128)S(1)}, f32[1,2,256,256]{2,3,1,0:T(8,128)}) fusion(bf16[9,2,256,256]{2,3,1,0:T(8,128)(2,1)} %broadcast_dynamic-update-slice_fusion, s32[]{:T(128)S(6)} %select_n.370, s32[]{:T(128)S(6)} %select_n.389, ...), kind=kLoop, calls=%fused_computation.65 | loop fusion | flops 524288 | bytes 3145744 | tf_op jit(solution)/shard_map/convert_element_type | solution.py:61
  160.6 1.7 add.601
  163.1 1.7 sub.246
  172.0 2.0 multiply_subtract_fusion.3
  184.2 1.7 add.592
  (131 shorter events, 43.9 us)
Async XLA Ops:
  7.2 127.4 %all-reduce.2.cloned.1.call-start = ((), (), s32[]{:S(2)}) async-start(), calls=%async_computation | async-start | bytes 524288 | tf_op jit(solution)/shard_map/psum | solution.py:29
  8.5 49.3 %collective-permute-start = (bf16[2,2,256,16]{2,3,1,0:T(8,128)(2,1)S(1)}, bf16[2,2,256,16]{2,3,1,0:T(8,128)(2,1)S(1)}, u32[]{:S(2)}, u32[]{:S(2)}) collective-permute-start(bf16[2,2,256,16]{2,3,1,0:T(8,128)(2,1)S(1)} %get-tuple-element.30), channel_id=1, source_target_pairs={{0,1},{1,2},{2,3},{4,5},{5,6},{6,7},{8,9},{9,10},{10,11},{12,13},{... | collective-permute-start | bytes 98312 | tf_op jit(solution)/shard_map/ppermute | solution.py:19
  12.0 45.9 %collective-permute-start.1 = (bf16[2,2,256,16]{2,3,1,0:T(8,128)(2,1)S(1)}, bf16[2,2,256,16]{2,3,1,0:T(8,128)(2,1)S(1)}, u32[]{:S(2)}, u32[]{:S(2)}) collective-permute-start(bf16[2,2,256,16]{2,3,1,0:T(8,128)(2,1)S(1)} %get-tuple-element.31), channel_id=1, source_target_pairs={{1,0},{2,1},{3,2},{5,4},{6,5},{7,6},{9,8},{10,9},{11,10},{13,12},{... | collective-permute-start | bytes 98312 | tf_op jit(solution)/shard_map/ppermute | solution.py:22
  65.5 81.4 %collective-permute-start.2 = (bf16[2,2,256,256]{2,3,1,0:T(8,128)(2,1)}, bf16[2,2,256,256]{2,3,1,0:T(8,128)(2,1)}, u32[]{:S(2)}, u32[]{:S(2)}) collective-permute-start(bf16[2,2,256,256]{2,3,1,0:T(8,128)(2,1)} %pad_maximum_fusion), channel_id=1, source_target_pairs={{4,0},{8,4},{12,8},{16,12},{20,16},{24,20},{28,24},{5,1},{9,5},{13... | collective-permute-start | bytes 1572872 | tf_op jit(solution)/shard_map/ppermute | solution.py:35
  66.8 83.7 %collective-permute-start.4 = (bf16[2,2,256,256]{2,3,1,0:T(8,128)(2,1)}, bf16[2,2,256,256]{2,3,1,0:T(8,128)(2,1)}, u32[]{:S(2)}, u32[]{:S(2)}) collective-permute-start(bf16[2,2,256,256]{2,3,1,0:T(8,128)(2,1)} %pad_maximum_fusion), channel_id=1, source_target_pairs={{0,4},{4,8},{8,12},{12,16},{16,20},{20,24},{24,28},{1,5},{5,9},{9,... | collective-permute-start | bytes 1572872 | tf_op jit(solution)/shard_map/ppermute | solution.py:35
  71.7 64.9 %copy-start = (f32[2,256,256]{1,2,0:T(8,128)}, f32[2,256,256]{1,2,0:T(8,128)S(1)}, u32[]{:S(2)}) copy-start(f32[2,256,256]{1,2,0:T(8,128)S(1)} %bitcast_convert_fusion) | copy-start | bytes 1572868
  71.7 77.2 %collective-permute-start.3 = (bf16[2,256,256]{1,2,0:T(8,128)(2,1)S(1)}, bf16[2,256,256]{1,2,0:T(8,128)(2,1)}, u32[]{:S(2)}, u32[]{:S(2)}) collective-permute-start(bf16[2,256,256]{1,2,0:T(8,128)(2,1)S(1)} %bitcast.278), channel_id=1, source_target_pairs={{8,0},{12,4},{16,8},{20,12},{24,16},{28,20},{9,1},{13,5},{17,9},{2... | collective-permute-start | bytes 786440 | tf_op jit(solution)/shard_map/ppermute | solution.py:35
  73.0 80.9 %collective-permute-start.5 = (bf16[2,256,256]{1,2,0:T(8,128)(2,1)}, bf16[2,256,256]{1,2,0:T(8,128)(2,1)}, u32[]{:S(2)}, u32[]{:S(2)}) collective-permute-start(bf16[2,256,256]{1,2,0:T(8,128)(2,1)} %bitcast.51), channel_id=1, source_target_pairs={{0,8},{4,12},{8,16},{12,20},{16,24},{20,28},{1,9},{5,13},{9,17},{1... | collective-permute-start | bytes 786440 | tf_op jit(solution)/shard_map/ppermute | solution.py:35
  153.9 5.6 %copy-start.1 = (f32[2,256,256]{1,2,0:T(8,128)S(1)}, f32[2,256,256]{1,2,0:T(8,128)}, u32[]{:S(2)}) copy-start(f32[2,256,256]{1,2,0:T(8,128)} %copy-done) | copy-start | bytes 1572868
  182.0 1.5 copy-start.2
  188.5 1.0 copy-start.3
  189.4 1.0 copy-start.4
  189.4 1.0 copy-start.5
  189.4 1.0 copy-start.6
  189.4 1.0 copy-start.7
  189.4 1.0 copy-start.8
  189.4 1.0 copy-start.9
  189.5 1.0 copy-start.10
  189.5 1.0 copy-start.11
  189.5 1.0 copy-start.12
  189.5 1.0 copy-start.13
  189.5 1.0 copy-start.14
Sparse Core Ops, SparseCore 0:
  80.2 54.3 all-reduce.1
where the time goes:
time: 202 us; the launch traced here: 200 us
  waiting for transfers between devices  54.5 us (27%)
  between operations  49.7 us (25%)
  local copies, waits for them, and re-layouts  44.7 us (22%)
  other arithmetic  27.8 us (14%)
  starting transfers between devices  17.6 us (9%)
  matrix products  5.83 us (3%)
    psum x1, waiting for transfers between devices, from_root(): return lax.psum(jnp.where(mine, array, jnp.zeros_like(array)), axis)  54.5 us
    reduce_sum x19, other arithmetic, window_pool(): return values.reshape(values.shape[0] // LOOK_AZ, LOOK_AZ, values.shape[1...  12.4 us
    ppermute x4, starting transfers between devices, shifted_2(): return lax.ppermute(block, axis, route)  11.7 us
    unnamed x46, local copies, waits for them, and re-layouts  10.1 us
    sub x6, local copies, waits for them, and re-layouts, looks(): imag_part = window_pool(left[1] * right[0] - left[0] * right[1])  9.11 us
    add x6, local copies, waits for them, and re-layouts, looks(): real_part = window_pool(left[0] * right[0] + left[1] * right[1])  8.95 us
    dot_general x2, matrix products, resample_one(): jnp.einsum('ml,plc->pmc', line_taps, ranged, preferred_element_type=jnp.f...  5.83 us
    sub x4, other arithmetic, looks(): imag_part = window_pool(left[1] * right[0] - left[0] * right[1])  4.9 us
  transfers between devices with their start and end apart: 7, of which 1 were waited for; matrix products, arithmetic and copies ran while one was open for 15% of the time, Pallas kernels for 0%

commit v1 on v0

v1 whole, which is shorter than its diff:
```python
import functools

import jax
import jax.numpy as jnp
from jax import lax
from jax.experimental import pallas as pl
from jax.experimental.pallas import tpu as pltpu
from jax.sharding import PartitionSpec as P

MAX_SWEEPS = 4
TAPS = 8
FRACTIONS = 16
MARGIN = 16
LOOK_AZ = 16
LOOK_RG = 4
QUANTITIES = 8
KINDS = 3
CHANNELS = 9

SMEM = pl.BlockSpec(memory_space=pltpu.SMEM)
VMEM = pl.BlockSpec(memory_space=pltpu.VMEM)


def kernel_weights():
    fraction = jnp.arange(FRACTIONS, dtype=jnp.float32)[:, None] / FRACTIONS
    spacing = jnp.arange(TAPS, dtype=jnp.float32)[None, :] - (TAPS // 2 - 1) - fraction
    window = jnp.cos(jnp.pi * spacing / (TAPS + 1)) ** 2
    weights = jnp.sinc(spacing) * window
    return (weights / jnp.sum(weights, axis=1, keepdims=True)).astype(jnp.bfloat16)


def shifted(block, axis, distance):
    count = lax.axis_size(axis)
    return lax.ppermute(
        block, axis, [(i, i + distance) for i in range(count) if 0 <= i + distance < count]
    )


def banded(offsets, table_ref, row):
    result = jnp.zeros(offsets.shape, jnp.float32)
    for tap in range(TAPS):
        result = jnp.where(offsets == tap, table_ref[row, tap], result)
    return result


def taps_kernel(
    table_ref, az_whole, az_part, rg_whole, rg_part, sweeps, own_ref, edge_ref, line_ref
):
    dates, columns, _ = own_ref.shape
    lines = line_ref.shape[1]
    images, edge_rows, _ = edge_ref.shape
    first = lax.axis_index("date") * dates
    half = edge_rows // 2

    def grid(rows, cols):
        return (
            lax.broadcasted_iota(jnp.int32, (rows, cols), 0),
            lax.broadcasted_iota(jnp.int32, (rows, cols), 1),
        )

    for slot in range(dates):
        date = first + slot
        shift = TAPS // 2 - 1 - rg_whole[date]
        row, col = grid(columns, columns)
        own_ref[slot] = banded(row - col + shift, table_ref, rg_part[date]).astype(jnp.bfloat16)
        row, col = grid(edge_rows, columns)
        inner = row % MARGIN
        source = jnp.where(row < half, inner - MARGIN, columns + inner)
        edge = banded(source - col + shift, table_ref, rg_part[date])
        owner = (row % half) // MARGIN
        for image in range(images // dates):
            number = slot * (images // dates) + image
            edge_ref[number] = jnp.where(owner == number, edge, 0.0).astype(jnp.bfloat16)
        row, col = grid(lines, lines)
        band = banded(col - row - az_whole[date] + TAPS // 2 - 1, table_ref, az_part[date])
        usable = row < sweeps[date] * (lines // MAX_SWEEPS)
        line_ref[slot] = jnp.where(usable, band, 0.0).astype(jnp.bfloat16)


def resample_kernel(split, x_ref, low_ref, high_ref, own_ref, edge_ref, line_ref, out_ref):
    dates, parts = x_ref.shape[:2]
    line_groups, column_groups, tile_lines, tile_columns = split
    edges = jnp.concatenate([low_ref[...], high_ref[...]], axis=1)
    for slot in range(dates):
        for part in range(parts):
            ranged = jnp.dot(x_ref[slot, part], own_ref[slot], preferred_element_type=jnp.float32)
            ranged += jnp.dot(
                edges, edge_ref[slot * parts + part], preferred_element_type=jnp.float32
            )
            moved = jnp.dot(
                line_ref[slot], ranged.astype(jnp.bfloat16), preferred_element_type=jnp.float32
            ).astype(jnp.bfloat16)
            for i in range(line_groups):
                for j in range(column_groups):
                    out_ref[i * column_groups + j, slot, part] = moved[
                        i * tile_lines : (i + 1) * tile_lines,
                        j * tile_columns : (j + 1) * tile_columns,
                    ]


def partners(date, gap_ref, master_ref, total):
    ahead = date + gap_ref[date, 0]
    later = jnp.where(ahead < total, ahead, date - gap_ref[date, 0])
    back = date - gap_ref[date, 1]
    earlier = jnp.where(back >= 0, back, date + gap_ref[date, 1])
    return (master_ref[0], later, earlier)


def looks_kernel(gap_ref, master_ref, r_ref, out_ref, sums, pooled, powers):
    total, _, tile_lines, tile_columns = r_ref.shape
    owners, per_owner, lanes = out_ref.shape
    dates = per_owner // CHANNELS
    line_looks = tile_lines // LOOK_AZ
    unroll = total if total <= 16 else 1

    def collect(date, carry):
        left0 = r_ref[date, 0].astype(jnp.float32)
        left1 = r_ref[date, 1].astype(jnp.float32)
        values = []
        for partner in partners(date, gap_ref, master_ref, total):
            right0 = r_ref[partner, 0].astype(jnp.float32)
            right1 = r_ref[partner, 1].astype(jnp.float32)
            values += [left0 * right0 + left1 * right1, left1 * right0 - left0 * right1]
        values.append(left0 * left0 + left1 * left1)
        for number, value in enumerate(values):
            for look in range(line_looks):
                rows = value[look * LOOK_AZ : (look + 1) * LOOK_AZ]
                sums[
                    pl.ds(date * QUANTITIES + number, 1),
                    look * tile_columns : (look + 1) * tile_columns,
                ] = jnp.sum(rows, axis=0, keepdims=True)
        sums[pl.ds(date * QUANTITIES + len(values), 1), :] = jnp.zeros(
            (1, line_looks * tile_columns), jnp.float32
        )
        return carry

    lax.fori_loop(0, total, collect, 0, unroll=unroll)
    shape = (line_looks * tile_columns, lanes)
    row = lax.broadcasted_iota(jnp.int32, shape, 0)
    col = lax.broadcasted_iota(jnp.int32, shape, 1)
    pool = (row // LOOK_RG == col).astype(jnp.float32)
    pooled[...] = jnp.dot(
        sums[...], pool, preferred_element_type=jnp.float32, precision=lax.Precision.HIGHEST
    )

    def gather(date, carry):
        for kind, partner in enumerate(partners(date, gap_ref, master_ref, total)):
            powers[kind, pl.ds(date, 1), :] = pooled[
                pl.ds(partner * QUANTITIES + 2 * KINDS, 1), :
            ]
        return carry

    lax.fori_loop(0, total, gather, 0, unroll=unroll)
    scale = 1.0 / (LOOK_AZ * LOOK_RG) ** 0.5

    for slot in range(dates):

        def every(number):
            return pooled[pl.ds(slot * QUANTITIES + number, owners, stride=dates * QUANTITIES), :]

        power_left = every(2 * KINDS)
        for kind in range(KINDS):
            real, imag = every(2 * kind), every(2 * kind + 1)
            power_right = powers[kind, pl.ds(slot, owners, stride=dates), :]
            out_ref[:, slot * CHANNELS + 2 * kind, :] = real * scale
            out_ref[:, slot * CHANNELS + 2 * kind + 1, :] = imag * scale
            out_ref[:, slot * CHANNELS + 2 * KINDS + kind, :] = jnp.sqrt(
                real * real + imag * imag
            ) / jnp.sqrt(power_left * power_right + 1e-06)


def place_kernel(x_ref, ifg_ref, coh_ref):
    sources, rows, lanes = x_ref.shape
    dates, _, lines, columns = ifg_ref.shape
    looks = lanes // columns
    for slot in range(dates):
        for channel in range(CHANNELS):
            values = x_ref[:, slot * CHANNELS + channel, :]
            for look in range(looks):
                part = values[:, look * columns : (look + 1) * columns]
                where = pl.ds(look, sources, stride=looks)
                if channel < 2 * KINDS:
                    ifg_ref[slot, channel, where, :] = part
                else:
                    coh_ref[slot, channel - 2 * KINDS, where, :] = part


def body(
    epoch_tiles_quadrature,
    along_track_whole_displacement,
    along_track_subpixel_weights,
    slant_whole_displacement,
    slant_subpixel_weights,
    sweeps_each_epoch,
    baseline_companion_gap,
    master_epoch_image,
):
    block = epoch_tiles_quadrature
    dates, parts, lines, columns = block.shape
    owners = lax.axis_size("date")
    total = owners * dates
    images = dates * parts
    line_groups = min(owners, lines // LOOK_AZ)
    column_groups = owners // line_groups
    tile_lines, tile_columns = lines // line_groups, columns // column_groups
    line_looks, column_looks = tile_lines // LOOK_AZ, tile_columns // LOOK_RG
    lanes = line_looks * column_looks

    def edge(piece):
        return jnp.transpose(piece, (2, 0, 1, 3)).reshape(lines, images * MARGIN)

    low = shifted(edge(block[..., columns - MARGIN :]), "range", 1)
    high = shifted(edge(block[..., :MARGIN]), "range", -1)

    table = kernel_weights().astype(jnp.float32)
    own_taps, edge_taps, line_taps = pl.pallas_call(
        taps_kernel,
        out_shape=(
            jax.ShapeDtypeStruct((dates, columns, columns), jnp.bfloat16),
            jax.ShapeDtypeStruct((images, 2 * images * MARGIN, columns), jnp.bfloat16),
            jax.ShapeDtypeStruct((dates, lines, lines), jnp.bfloat16),
        ),
        in_specs=[SMEM] * 6,
        out_specs=(VMEM,) * 3,
        cost_estimate=pl.CostEstimate(flops=4000000, bytes_accessed=800000, transcendentals=0),
        name="taps",
    )(
        table,
        along_track_whole_displacement,
        along_track_subpixel_weights,
        slant_whole_displacement,
        slant_subpixel_weights,
        sweeps_each_epoch,
    )
    tiles = pl.pallas_call(
        functools.partial(
            resample_kernel, (line_groups, column_groups, tile_lines, tile_columns)
        ),
        out_shape=jax.ShapeDtypeStruct(
            (owners, dates, parts, tile_lines, tile_columns), jnp.bfloat16
        ),
        in_specs=[VMEM] * 6,
        out_specs=VMEM,
        name="resample",
    )(block, low, high, own_taps, edge_taps, line_taps)

    tiles = lax.all_to_all(tiles, "date", 0, 0)
    stack = tiles.reshape(total, parts, tile_lines, tile_columns)
    results = pl.pallas_call(
        looks_kernel,
        out_shape=jax.ShapeDtypeStruct((owners, dates * CHANNELS, lanes), jnp.float32),
        in_specs=[SMEM, SMEM, VMEM],
        out_specs=VMEM,
        scratch_shapes=[
            pltpu.VMEM((total * QUANTITIES, line_looks * tile_columns), jnp.float32),
            pltpu.VMEM((total * QUANTITIES, lanes), jnp.float32),
            pltpu.VMEM((KINDS, total, lanes), jnp.float32),
        ],
        name="looks",
    )(baseline_companion_gap, master_epoch_image, stack)
    results = lax.all_to_all(results, "date", 0, 0)

    rows, cols = lines // LOOK_AZ, columns // LOOK_RG
    if column_groups == 1:
        return pl.pallas_call(
            place_kernel,
            out_shape=(
                jax.ShapeDtypeStruct((dates, 2 * KINDS, rows, cols), jnp.float32),
                jax.ShapeDtypeStruct((dates, KINDS, rows, cols), jnp.float32),
            ),
            in_specs=[VMEM],
            out_specs=(VMEM, VMEM),
            name="place",
        )(results)
    whole = results.reshape(
        line_groups, column_groups, dates, CHANNELS, line_looks, column_looks
    )
    whole = jnp.transpose(whole, (2, 3, 0, 4, 1, 5)).reshape(dates, CHANNELS, rows, cols)
    return (whole[:, : 2 * KINDS], whole[:, 2 * KINDS :])


def solution(mesh):
    in_specs = (P("date", None, None, "range"), P(), P(), P(), P(), P(), P(), P())
    out_specs = (P("date", None, None, "range"), P("date", None, None, "range"))
    return jax.shard_map(body, mesh=mesh, in_specs=in_specs, out_specs=out_specs, check_vma=False)
```

time: 202 us -> 46.5 us (0.23)
  the two profiles are of different devices: /device:TPU:8 before, /device:TPU:0 now
where the time goes in v1:
time: 46.5 us; the launch traced here: 46 us
  Pallas kernels  10.8 us (23%)
  starting transfers between devices  10.1 us (22%)
  waiting for transfers between devices  9.92 us (21%)
  blocking collectives  9.16 us (20%)
  local copies, waits for them, and re-layouts  3.73 us (8%)
  between operations  1.34 us (3%)
  other arithmetic  0.98 us (2%)
    all_to_all x1, blocking collectives, body(): results = lax.all_to_all(results, 'date', 0, 0)  9.16 us
    all_to_all x1, waiting for transfers between devices, body(): tiles = lax.all_to_all(tiles, 'date', 0, 0)  8.41 us
    ppermute x2, starting transfers between devices, shifted(): lax.ppermute(block, axis, [(i, i + distance) for i in range(count) if 0 <...  6.22 us
    all_to_all x1, starting transfers between devices, body(): tiles = lax.all_to_all(tiles, 'date', 0, 0)  3.85 us
    pallas_call x1, Pallas kernels, body(): pl.pallas_call(functools.partial(resample_kernel, (line_groups, column_gr...  3.58 us
    pallas_call x1, Pallas kernels, body(): pl.pallas_call(looks_kernel, out_shape=jax.ShapeDtypeStruct((owners, date...  3.21 us
    pallas_call x1, Pallas kernels, body(): pl.pallas_call(taps_kernel, out_shape=(jax.ShapeDtypeStruct((dates, colum...  2.35 us
    unnamed x11, local copies, waits for them, and re-layouts  2.31 us
  transfers between devices with their start and end apart: 3, of which 2 were waited for; matrix products, arithmetic and copies ran while one was open for 4% of the time, Pallas kernels for 5%

profile of v1, /device:TPU:0, one launch (start us, length us, event | category | flops | bytes accessed | tf_op | source)
XLA Modules:
  0.0 46.0 jit_solution(4336047334071879742)
XLA Ops:
  0.6 1.2 %fusion.28 = (bf16[2,2,256,16]{3,2,1,0:T(8,128)(2,1)S(1)}, bf16[2,2,256,16]{3,2,1,0:T(8,128)(2,1)S(1)}) fusion(bf16[2,2,256,256]{3,2,1,0:T(8,128)(2,1)} %x_ref.1), kind=kLoop, calls=%fused_computation.39 | loop fusion | bytes 131072 | tf_op jit(solution)/shard_map/slice | solution.py:213
  1.8 0.1 copy.18
  1.9 0.1 copy.14
  2.0 4.9 %collective-permute-start = (bf16[256,64]{1,0:T(8,128)(2,1)S(1)}, bf16[256,64]{1,0:T(8,128)(2,1)S(1)}, u32[]{:S(2)}, u32[]{:S(2)}) collective-permute-start(bf16[256,64]{1,0:T(8,128)(2,1)S(1)} %copy.14), channel_id=1, source_target_pairs={{0,1},{1,2},{2,3},{4,5},{5,6},{6,7},{8,9},{9,10},{10,11},{12,13},{... | collective-permute-start | bytes 98312 | tf_op jit(solution)/shard_map/ppermute | solution.py:34
  7.0 0.1 copy.19
  7.1 0.1 copy.16
  7.2 1.3 %collective-permute-start.1 = (bf16[256,64]{1,0:T(8,128)(2,1)S(1)}, bf16[256,64]{1,0:T(8,128)(2,1)S(1)}, u32[]{:S(2)}, u32[]{:S(2)}) collective-permute-start(bf16[256,64]{1,0:T(8,128)(2,1)S(1)} %copy.16), channel_id=1, source_target_pairs={{1,0},{2,1},{3,2},{5,4},{6,5},{7,6},{9,8},{10,9},{11,10},{13,12},{... | collective-permute-start | bytes 98312 | tf_op jit(solution)/shard_map/ppermute | solution.py:34
  8.5 0.2 fusion.27
  8.8 0.7 %fusion.26.table_ref = f32[16,8]{1,0:T(8,128)} fusion(f32[16]{0:T(128)S(1)} %fusion.27, f32[16]{0:T(128)S(1)} %iota_multiply_fusion, f32[8]{0:T(128)S(1)} %iota_add_fusion), kind=kLoop, calls=%fused_computation.35 | loop fusion | flops 5120 | bytes 672 | tf_op jit(solution)/shard_map/convert_element_type | solution.py:215
  9.5 2.3 %taps.1 = (bf16[2,256,256]{2,1,0:T(8,128)(2,1)}, bf16[4,128,256]{2,1,0:T(8,128)(2,1)}, bf16[2,256,256]{2,1,0:T(8,128)(2,1)}) custom-call(f32[16,8]{1,0:T(8,128)} %fusion.26.table_ref, s32[16]{0:T(128)} %az_whole.1, s32[16]{0:T(128)} %az_part.1, s32[16]{0:T(128)} %rg_whole.1, s32[16]{0:T(128)} %rg_part.1, s32[16]{0:T(128)} %sweeps.1), custom_call_target="tpu_custom_call" | custom-call | flops 4000000 | bytes 800000 | tf_op jit(solution)/shard_map/taps/pallas_call | solution.py:216
  11.9 0.0 collective-permute-done.low_ref
  11.9 0.0 copy-start.1
  11.9 1.5 %collective-permute-done.1.high_ref = bf16[256,64]{1,0:T(8,128)(2,1)S(1)} collective-permute-done((bf16[256,64]{1,0:T(8,128)(2,1)S(1)}, bf16[256,64]{1,0:T(8,128)(2,1)S(1)}, u32[]{:S(2)}, u32[]{:S(2)}) %collective-permute-start.1) | collective-permute-done | bytes 32800 | tf_op jit(solution)/shard_map/ppermute | solution.py:34
  13.4 0.0 copy-done.1
  13.4 0.6 %copy-done.2 = bf16[256,64]{1,0:T(8,128)(2,1)} copy-done((bf16[256,64]{1,0:T(8,128)(2,1)}, bf16[256,64]{1,0:T(8,128)(2,1)S(1)}, u32[]{:S(2)}) %copy-start.2) | copy-done | bytes 32792
  14.0 3.6 %resample.1 = bf16[8,2,2,32,256]{4,3,2,1,0:T(8,128)(2,1)} custom-call(bf16[2,2,256,256]{3,2,1,0:T(8,128)(2,1)} %x_ref.1, bf16[256,64]{1,0:T(8,128)(2,1)} %copy-done.1, bf16[256,64]{1,0:T(8,128)(2,1)} %copy-done.2, bf16[2,256,256]{2,1,0:T(8,128)(2,1)} %get-tuple-element.5.own_ref, bf16[4,128,256]{2,1,0:T(8,128)(2,1)} %get-tuple-element.6.edge_ref, ...), custom_call_target="tpu_custom_call" | custom-call | tf_op jit(solution)/shard_map/resample/pallas_call | solution.py:235
  17.6 3.9 %all-to-all-start = ((bf16[8,2,2,32,256]{4,3,2,1,0:T(8,128)(2,1)}), bf16[8,2,2,32,256]{4,3,2,1,0:T(8,128)(2,1)S(1)}, u32[]{:S(2)}, u32[]{:S(2)}) async-start(bf16[8,2,2,32,256]{4,3,2,1,0:T(8,128)(2,1)} %resample.1), calls=%async_computation | async-start | bytes 1048576 | tf_op jit(solution)/shard_map/all_to_all | solution.py:247
  21.4 0.0 copy-done.3
  21.4 0.7 %copy.17.gap_ref = s32[16,2]{1,0:T(8,128)} copy(s32[16,2]{0,1:T(2,128)S(1)} %copy-done.3) | data formatting | bytes 256 | tf_op args[6]
  22.8 8.4 %all-to-all-done = bf16[8,2,2,32,256]{4,3,2,1,0:T(8,128)(2,1)S(1)} async-done(((bf16[8,2,2,32,256]{4,3,2,1,0:T(8,128)(2,1)}), bf16[8,2,2,32,256]{4,3,2,1,0:T(8,128)(2,1)S(1)}, u32[]{:S(2)}, u32[]{:S(2)}) %all-to-all-start) | async-done | bytes 524320 | tf_op jit(solution)/shard_map/all_to_all | solution.py:247
  31.2 0.8 %copy-done = bf16[8,2,2,32,256]{4,3,2,1,0:T(8,128)(2,1)} copy-done((bf16[8,2,2,32,256]{4,3,2,1,0:T(8,128)(2,1)}, bf16[8,2,2,32,256]{4,3,2,1,0:T(8,128)(2,1)S(1)}, u32[]{:S(2)}) %copy-start) | copy-done | bytes 524312
  32.0 3.2 %looks.1 = f32[8,18,128]{2,1,0:T(8,128)} custom-call(s32[16,2]{1,0:T(8,128)} %copy.17.gap_ref, s32[1]{0:T(128)S(6)} %copy.20.master_ref, bf16[16,2,32,256]{3,2,1,0:T(8,128)(2,1)} %bitcast.7), custom_call_target="tpu_custom_call" | custom-call | tf_op jit(solution)/shard_map/looks/pallas_call | solution.py:249
  35.2 9.2 %all_to_all.10.x_ref = f32[8,18,128]{2,1,0:T(8,128)} all-to-all(f32[8,18,128]{2,1,0:T(8,128)} %looks.1), channel_id=1, replica_groups=mesh['date'=8,'range'=4] {'date'}, dimensions={0} | all-to-all | bytes 147456 | tf_op jit(solution)/shard_map/all_to_all | solution.py:261
  44.3 1.7 %place.1 = (f32[2,6,16,64]{3,2,1,0:T(8,128)}, f32[2,3,16,64]{3,2,1,0:T(8,128)}) custom-call(f32[8,18,128]{2,1,0:T(8,128)} %all_to_all.10.x_ref), custom_call_target="tpu_custom_call" | custom-call | tf_op jit(solution)/shard_map/place/pallas_call | solution.py:265
  (5 shorter events, 0.0 us)
Async XLA Ops:
  2.0 9.8 %collective-permute-start = (bf16[256,64]{1,0:T(8,128)(2,1)S(1)}, bf16[256,64]{1,0:T(8,128)(2,1)S(1)}, u32[]{:S(2)}, u32[]{:S(2)}) collective-permute-start(bf16[256,64]{1,0:T(8,128)(2,1)S(1)} %copy.14), channel_id=1, source_target_pairs={{0,1},{1,2},{2,3},{4,5},{5,6},{6,7},{8,9},{9,10},{10,11},{12,13},{... | collective-permute-start | bytes 98312 | tf_op jit(solution)/shard_map/ppermute | solution.py:34
  7.2 6.2 %collective-permute-start.1 = (bf16[256,64]{1,0:T(8,128)(2,1)S(1)}, bf16[256,64]{1,0:T(8,128)(2,1)S(1)}, u32[]{:S(2)}, u32[]{:S(2)}) collective-permute-start(bf16[256,64]{1,0:T(8,128)(2,1)S(1)} %copy.16), channel_id=1, source_target_pairs={{1,0},{2,1},{3,2},{5,4},{6,5},{7,6},{9,8},{10,9},{11,10},{13,12},{... | collective-permute-start | bytes 98312 | tf_op jit(solution)/shard_map/ppermute | solution.py:34
  11.9 1.5 %copy-start.1 = (bf16[256,64]{1,0:T(8,128)(2,1)}, bf16[256,64]{1,0:T(8,128)(2,1)S(1)}, u32[]{:S(2)}) copy-start(bf16[256,64]{1,0:T(8,128)(2,1)S(1)} %collective-permute-done.low_ref) | copy-start | bytes 98308
  13.4 0.6 %copy-start.2 = (bf16[256,64]{1,0:T(8,128)(2,1)}, bf16[256,64]{1,0:T(8,128)(2,1)S(1)}, u32[]{:S(2)}) copy-start(bf16[256,64]{1,0:T(8,128)(2,1)S(1)} %collective-permute-done.1.high_ref) | copy-start | bytes 98308
  17.6 3.9 %copy-start.3 = (s32[16,2]{0,1:T(2,128)S(1)}, s32[16,2]{0,1:T(2,128)}, u32[]{:S(2)}) copy-start(s32[16,2]{0,1:T(2,128)} %param.14) | copy-start | bytes 388
  17.6 13.6 %all-to-all-start = ((bf16[8,2,2,32,256]{4,3,2,1,0:T(8,128)(2,1)}), bf16[8,2,2,32,256]{4,3,2,1,0:T(8,128)(2,1)S(1)}, u32[]{:S(2)}, u32[]{:S(2)}) async-start(bf16[8,2,2,32,256]{4,3,2,1,0:T(8,128)(2,1)} %resample.1), calls=%async_computation | async-start | bytes 1048576 | tf_op jit(solution)/shard_map/all_to_all | solution.py:247
  31.2 0.8 %copy-start = (bf16[8,2,2,32,256]{4,3,2,1,0:T(8,128)(2,1)}, bf16[8,2,2,32,256]{4,3,2,1,0:T(8,128)(2,1)S(1)}, u32[]{:S(2)}) copy-start(bf16[8,2,2,32,256]{4,3,2,1,0:T(8,128)(2,1)S(1)} %all-to-all-done) | copy-start | bytes 1572868

commit v2 on v1

v2 whole, which is shorter than its diff:
```python
import functools

import jax
import jax.numpy as jnp
from jax import lax
from jax.experimental import pallas as pl
from jax.experimental.pallas import tpu as pltpu
from jax.sharding import PartitionSpec as P

MAX_SWEEPS = 4
TAPS = 8
FRACTIONS = 16
MARGIN = 16
LOOK_AZ = 16
LOOK_RG = 4
QUANTITIES = 8
KINDS = 3
CHANNELS = 9
LANES = 128
GRANT = 24 * 2**20

SMEM = pl.BlockSpec(memory_space=pltpu.SMEM)
VMEM = pl.BlockSpec(memory_space=pltpu.VMEM)


def shifted(block, axis, distance):
    count = lax.axis_size(axis)
    return lax.ppermute(
        block, axis, [(i, i + distance) for i in range(count) if 0 <= i + distance < count]
    )


def near(array):
    return pltpu.with_memory_space_constraint(array, pltpu.VMEM)


def iotas(rows, cols):
    return (
        lax.broadcasted_iota(jnp.int32, (rows, cols), 0),
        lax.broadcasted_iota(jnp.int32, (rows, cols), 1),
    )


def edges_kernel(x_ref, last_ref, first_ref):
    dates, parts, _, columns = x_ref.shape
    for slot in range(dates):
        for part in range(parts):
            spot = slice((slot * parts + part) * MARGIN, (slot * parts + part + 1) * MARGIN)
            last_ref[:, spot] = x_ref[slot, part, :, columns - MARGIN :]
            first_ref[:, spot] = x_ref[slot, part, :, :MARGIN]


def weight_rows(fractions):
    row, lane = iotas(8, LANES)
    spot = jnp.zeros((8, LANES), jnp.float32)
    for number, fraction in enumerate(fractions):
        spot = jnp.where(row == number, fraction.astype(jnp.float32), spot)
    spacing = (lane - 1 - (TAPS // 2 - 1)).astype(jnp.float32) - spot / FRACTIONS
    angle = jnp.pi * spacing
    sinc = jnp.where(spacing == 0.0, 1.0, jnp.sin(angle) / jnp.where(spacing == 0.0, 1.0, angle))
    weights = sinc * jnp.cos(angle / (TAPS + 1)) ** 2
    weights = jnp.where((lane >= 1) & (lane <= TAPS), weights, 0.0)
    weights = weights / jnp.sum(weights, axis=1, keepdims=True)
    return weights.astype(jnp.bfloat16).astype(jnp.float32)


def banded(offsets, weights):
    rows, cols = offsets.shape
    lanes = jnp.broadcast_to(weights, (rows, LANES))
    spots = jnp.clip(offsets + 1, 0, TAPS + 1)
    return jnp.concatenate(
        [
            jnp.take_along_axis(lanes, spots[:, start : start + LANES], axis=1)
            for start in range(0, cols, LANES)
        ],
        axis=1,
    )


def taps_kernel(az_whole, az_part, rg_whole, rg_part, sweeps, own_ref, low_ref, high_ref, line_ref):
    dates, columns, _ = own_ref.shape
    lines = line_ref.shape[1]
    edge_rows = low_ref.shape[0]
    parts = edge_rows // MARGIN // dates
    first = lax.axis_index("date") * dates
    centre = TAPS // 2 - 1
    present = [first + slot for slot in range(dates)]
    table = weight_rows([rg_part[d] for d in present] + [az_part[d] for d in present])
    for slot, date in enumerate(present):
        shift = centre - rg_whole[date]
        weights = table[slot : slot + 1]
        row, col = iotas(columns, columns)
        own_ref[slot] = banded(row - col + shift, weights).astype(jnp.bfloat16)
        row, col = iotas(edge_rows, LANES)
        low = banded(row % MARGIN - MARGIN - col + shift, weights)
        high = banded(row % MARGIN + LANES - col + shift, weights)
        for part in range(parts):
            image = slot * parts + part
            held = row // MARGIN == image
            spot = slice(image * LANES, (image + 1) * LANES)
            low_ref[:, spot] = jnp.where(held, low, 0.0).astype(jnp.bfloat16)
            high_ref[:, spot] = jnp.where(held, high, 0.0).astype(jnp.bfloat16)
        row, col = iotas(lines, lines)
        weights = table[dates + slot : dates + slot + 1]
        band = banded(col - row + (centre - az_whole[date]), weights)
        usable = row < sweeps[date] * (lines // MAX_SWEEPS)
        line_ref[slot] = jnp.where(usable, band, 0.0).astype(jnp.bfloat16)


def resample_kernel(
    split, x_ref, last_ref, first_ref, own_ref, low_ref, high_ref, line_ref, out_ref
):
    dates, parts, _, columns = x_ref.shape
    line_groups, column_groups, tile_lines, tile_columns = split
    low = jnp.dot(last_ref[...], low_ref[...], preferred_element_type=jnp.float32)
    high = jnp.dot(first_ref[...], high_ref[...], preferred_element_type=jnp.float32)
    for slot in range(dates):
        for part in range(parts):
            spot = slice((slot * parts + part) * LANES, (slot * parts + part + 1) * LANES)
            ranged = jnp.dot(x_ref[slot, part], own_ref[slot], preferred_element_type=jnp.float32)
            pieces = [ranged[:, start : start + LANES] for start in range(0, columns, LANES)]
            pieces[0] += low[:, spot]
            pieces[-1] += high[:, spot]
            ranged = jnp.concatenate(pieces, axis=1)
            moved = jnp.dot(
                line_ref[slot], ranged.astype(jnp.bfloat16), preferred_element_type=jnp.float32
            ).astype(jnp.bfloat16)
            for i in range(line_groups):
                for j in range(column_groups):
                    out_ref[i * column_groups + j, slot, part] = moved[
                        i * tile_lines : (i + 1) * tile_lines,
                        j * tile_columns : (j + 1) * tile_columns,
                    ]


def partners(date, gap_ref, master_ref, total):
    ahead = date + gap_ref[0, date]
    later = jnp.where(ahead < total, ahead, date - gap_ref[0, date])
    back = date - gap_ref[1, date]
    earlier = jnp.where(back >= 0, back, date + gap_ref[1, date])
    return (master_ref[0], later, earlier)


def row_sums(values):
    row = lax.broadcasted_iota(jnp.int32, values[0].shape, 0)
    order = (3, 2, 1, 0, 7, 6, 5, 4)
    values = [values[number] for number in order]
    upper = row < 4
    values = [
        jnp.where(upper, a, b) + pltpu.roll(jnp.where(upper, b, a), 4, 0)
        for a, b in zip(values[:4], values[4:])
    ]
    for step, kept in ((2, row % 4 >= 2), (1, row % 2 == 1)):
        values = [
            jnp.where(kept, a + pltpu.roll(a, step, 0), b + pltpu.roll(b, 8 - step, 0))
            for a, b in zip(values[:step], values[step:])
        ]
    return values[0]


def looks_kernel(gap_ref, master_ref, r_ref, out_ref, sums, pooled, powers):
    total, _, tile_lines, tile_columns = r_ref.shape
    owners, per_owner, lanes = out_ref.shape
    dates = per_owner // CHANNELS
    line_looks = tile_lines // LOOK_AZ
    unroll = total if total <= 16 else 1

    def collect(date, carry):
        left0 = r_ref[date, 0].astype(jnp.float32)
        left1 = r_ref[date, 1].astype(jnp.float32)
        values = []
        for partner in partners(date, gap_ref, master_ref, total):
            right0 = r_ref[partner, 0].astype(jnp.float32)
            right1 = r_ref[partner, 1].astype(jnp.float32)
            values += [left0 * right0 + left1 * right1, left1 * right0 - left0 * right1]
        values.append(left0 * left0 + left1 * left1)
        values.append(jnp.zeros_like(left0))
        rows = pl.ds(pl.multiple_of(date * QUANTITIES, QUANTITIES), QUANTITIES)
        for look in range(line_looks):
            start = look * LOOK_AZ
            sums[rows, look * tile_columns : (look + 1) * tile_columns] = row_sums(
                [value[start : start + 8] + value[start + 8 : start + 16] for value in values]
            )
        return carry

    lax.fori_loop(0, total, collect, 0, unroll=unroll)
    shape = (line_looks * tile_columns, lanes)
    row = lax.broadcasted_iota(jnp.int32, shape, 0)
    col = lax.broadcasted_iota(jnp.int32, shape, 1)
    pool = jnp.where(row // LOOK_RG == col, 1.0, 0.0).astype(jnp.bfloat16)
    whole = sums[...]
    coarse = whole.astype(jnp.bfloat16)
    fine = (whole - coarse.astype(jnp.float32)).astype(jnp.bfloat16)
    pooled[...] = jnp.dot(coarse, pool, preferred_element_type=jnp.float32) + jnp.dot(
        fine, pool, preferred_element_type=jnp.float32
    )

    def gather(date, carry):
        for kind, partner in enumerate(partners(date, gap_ref, master_ref, total)):
            powers[kind, pl.ds(date, 1), :] = pooled[
                pl.ds(partner * QUANTITIES + 2 * KINDS, 1), :
            ]
        return carry

    lax.fori_loop(0, total, gather, 0, unroll=unroll)
    scale = 1.0 / (LOOK_AZ * LOOK_RG) ** 0.5

    for slot in range(dates):

        def every(number):
            return pooled[pl.ds(slot * QUANTITIES + number, owners, stride=dates * QUANTITIES), :]

        power_left = every(2 * KINDS)
        for kind in range(KINDS):
            real, imag = every(2 * kind), every(2 * kind + 1)
            power_right = powers[kind, pl.ds(slot, owners, stride=dates), :]
            out_ref[:, slot * CHANNELS + 2 * kind, :] = real * scale
            out_ref[:, slot * CHANNELS + 2 * kind + 1, :] = imag * scale
            out_ref[:, slot * CHANNELS + 2 * KINDS + kind, :] = jnp.sqrt(
                real * real + imag * imag
            ) / jnp.sqrt(power_left * power_right + 1e-06)


def place_kernel(x_ref, ifg_ref, coh_ref):
    sources, rows, lanes = x_ref.shape
    dates, _, lines, columns = ifg_ref.shape
    looks = lanes // columns
    for slot in range(dates):
        for channel in range(CHANNELS):
            values = x_ref[:, slot * CHANNELS + channel, :]
            for look in range(looks):
                part = values[:, look * columns : (look + 1) * columns]
                where = pl.ds(look, sources, stride=looks)
                if channel < 2 * KINDS:
                    ifg_ref[slot, channel, where, :] = part
                else:
                    coh_ref[slot, channel - 2 * KINDS, where, :] = part


def body(
    epoch_tiles_quadrature,
    along_track_whole_displacement,
    along_track_subpixel_weights,
    slant_whole_displacement,
    slant_subpixel_weights,
    sweeps_each_epoch,
    baseline_companion_gap,
    master_epoch_image,
):
    block = epoch_tiles_quadrature
    dates, parts, lines, columns = block.shape
    owners = lax.axis_size("date")
    total = owners * dates
    images = dates * parts
    line_groups = min(owners, lines // LOOK_AZ)
    column_groups = owners // line_groups
    tile_lines, tile_columns = lines // line_groups, columns // column_groups
    line_looks, column_looks = tile_lines // LOOK_AZ, tile_columns // LOOK_RG
    lanes = line_looks * column_looks

    block = near(block)
    last, first = pl.pallas_call(
        edges_kernel,
        out_shape=(pltpu.VMEM((lines, images * MARGIN), jnp.bfloat16),) * 2,
        in_specs=[VMEM],
        out_specs=(VMEM, VMEM),
        name="edges",
        compiler_params=pltpu.CompilerParams(vmem_limit_bytes=GRANT),
    )(block)
    last = shifted(last, "range", 1)
    first = shifted(first, "range", -1)

    taps = pl.pallas_call(
        taps_kernel,
        out_shape=(
            pltpu.VMEM((dates, columns, columns), jnp.bfloat16),
            pltpu.VMEM((images * MARGIN, images * LANES), jnp.bfloat16),
            pltpu.VMEM((images * MARGIN, images * LANES), jnp.bfloat16),
            pltpu.VMEM((dates, lines, lines), jnp.bfloat16),
        ),
        in_specs=[SMEM] * 5,
        out_specs=(VMEM,) * 4,
        cost_estimate=pl.CostEstimate(flops=4000000, bytes_accessed=800000, transcendentals=0),
        name="taps",
        compiler_params=pltpu.CompilerParams(vmem_limit_bytes=GRANT),
    )(
        along_track_whole_displacement,
        along_track_subpixel_weights,
        slant_whole_displacement,
        slant_subpixel_weights,
        sweeps_each_epoch,
    )
    tiles = pl.pallas_call(
        functools.partial(
            resample_kernel, (line_groups, column_groups, tile_lines, tile_columns)
        ),
        out_shape=pltpu.VMEM((owners, dates, parts, tile_lines, tile_columns), jnp.bfloat16),
        in_specs=[VMEM] * 7,
        out_specs=VMEM,
        name="resample",
        compiler_params=pltpu.CompilerParams(vmem_limit_bytes=GRANT),
    )(block, near(last), near(first), *[near(tap) for tap in taps])

    tiles = lax.all_to_all(tiles, "date", 0, 0)
    stack = tiles.reshape(total, parts, tile_lines, tile_columns)
    results = pl.pallas_call(
        looks_kernel,
        out_shape=pltpu.VMEM((owners, dates * CHANNELS, lanes), jnp.float32),
        in_specs=[SMEM, SMEM, VMEM],
        out_specs=VMEM,
        scratch_shapes=[
            pltpu.VMEM((total * QUANTITIES, line_looks * tile_columns), jnp.float32),
            pltpu.VMEM((total * QUANTITIES, lanes), jnp.float32),
            pltpu.VMEM((KINDS, total, lanes), jnp.float32),
        ],
        name="looks",
        compiler_params=pltpu.CompilerParams(vmem_limit_bytes=GRANT),
    )(baseline_companion_gap.T, master_epoch_image, near(stack))
    results = lax.all_to_all(results, "date", 0, 0)

    rows, cols = lines // LOOK_AZ, columns // LOOK_RG
    if column_groups == 1:
        return pl.pallas_call(
            place_kernel,
            out_shape=(
                jax.ShapeDtypeStruct((dates, 2 * KINDS, rows, cols), jnp.float32),
                jax.ShapeDtypeStruct((dates, KINDS, rows, cols), jnp.float32),
            ),
            in_specs=[VMEM],
            out_specs=(VMEM, VMEM),
            name="place",
            compiler_params=pltpu.CompilerParams(vmem_limit_bytes=GRANT),
        )(near(results))
    whole = results.reshape(
        line_groups, column_groups, dates, CHANNELS, line_looks, column_looks
    )
    whole = jnp.transpose(whole, (2, 3, 0, 4, 1, 5)).reshape(dates, CHANNELS, rows, cols)
    return (whole[:, : 2 * KINDS], whole[:, 2 * KINDS :])


def solution(mesh):
    in_specs = (P("date", None, None, "range"), P(), P(), P(), P(), P(), P(), P())
    out_specs = (P("date", None, None, "range"), P("date", None, None, "range"))
    return jax.shard_map(body, mesh=mesh, in_specs=in_specs, out_specs=out_specs, check_vma=False)
```

time: 46.5 us -> 39.3 us (0.85)
  Pallas kernels: 10.8 us -> 5.82 us
  waiting for transfers between devices: 9.92 us -> 12.3 us
  local copies, waits for them, and re-layouts: 3.73 us -> 1.75 us
  blocking collectives: 9.16 us -> 7.58 us
  other arithmetic: 0.98 us -> 0 us
    pallas_call x1, Pallas kernels: 3.58 us -> 1.52 us  [body(): pl.pallas_call(functools.partial(resample_kernel, (line_groups, column_gr...]
    pallas_call x2 -> x3, Pallas kernels: 5.56 us -> 3.54 us  [the longest x1 1.67 us: body(): pl.pallas_call(looks_kernel, out_shape=pltpu.VMEM((owners, dates * CHANNE...]
    ppermute x2, waiting for transfers between devices: 1.51 us -> 3.23 us  [shifted(): lax.ppermute(block, axis, [(i, i + distance) for i in range(count) if 0 <...]
    all_to_all x1, blocking collectives: 9.16 us -> 7.58 us  [body(): results = lax.all_to_all(results, 'date', 0, 0)]
    slice x1 -> x0, local copies, waits for them, and re-layouts: 1.17 us -> none  [body(): high = shifted(edge(block[..., :MARGIN]), 'range', -1)]
    pallas_call x1, Pallas kernels: 1.65 us -> 0.76 us  [body(): pl.pallas_call(place_kernel, out_shape=(jax.ShapeDtypeStruct((dates, 2 *...]
    convert_element_type x1 -> x0, other arithmetic: 0.74 us -> none  [body(): table = kernel_weights().astype(jnp.float32)]
    all_to_all x1, waiting for transfers between devices: 8.41 us -> 9.09 us  [body(): tiles = lax.all_to_all(tiles, 'date', 0, 0)]
  transfers between devices with their start and end apart: 3 -> 3, of which waited for: 2 -> 2; matrix products, arithmetic and copies ran while one was open for 4% -> 0% of each run, Pallas kernels for 5% -> 4%
where the time goes in v2:
time: 39.3 us; the launch traced here: 38.9 us
  waiting for transfers between devices  12.3 us (31%)
  starting transfers between devices  10.1 us (26%)
  blocking collectives  7.58 us (19%)
  Pallas kernels  5.82 us (15%)
  local copies, waits for them, and re-layouts  1.75 us (4%)
  between operations  1.4 us (4%)
    all_to_all x1, waiting for transfers between devices, body(): tiles = lax.all_to_all(tiles, 'date', 0, 0)  9.09 us
    all_to_all x1, blocking collectives, body(): results = lax.all_to_all(results, 'date', 0, 0)  7.58 us
    ppermute x2, starting transfers between devices, shifted(): lax.ppermute(block, axis, [(i, i + distance) for i in range(count) if 0 <...  6.35 us
    all_to_all x1, starting transfers between devices, body(): tiles = lax.all_to_all(tiles, 'date', 0, 0)  3.72 us
    ppermute x2, waiting for transfers between devices, shifted(): lax.ppermute(block, axis, [(i, i + distance) for i in range(count) if 0 <...  3.23 us
    unnamed x16, local copies, waits for them, and re-layouts  1.75 us
    pallas_call x1, Pallas kernels, body(): pl.pallas_call(looks_kernel, out_shape=pltpu.VMEM((owners, dates * CHANNE...  1.67 us
    pallas_call x1, Pallas kernels, body(): pl.pallas_call(taps_kernel, out_shape=(pltpu.VMEM((dates, columns, column...  1.58 us
  transfers between devices with their start and end apart: 3, of which 2 were waited for; matrix products, arithmetic and copies ran while one was open for 0% of the time, Pallas kernels for 4%

profile of v2, /device:TPU:0, one launch (start us, length us, event | category | flops | bytes accessed | tf_op | source)
XLA Modules:
  0.0 38.9 jit_solution(10179515902362512664)
XLA Ops:
  0.6 0.0 copy-start
  0.6 1.0 %copy-done = bf16[2,2,256,256]{3,2,1,0:T(8,128)(2,1)S(1)} copy-done((bf16[2,2,256,256]{3,2,1,0:T(8,128)(2,1)S(1)}, bf16[2,2,256,256]{3,2,1,0:T(8,128)(2,1)}, u32[]{:S(2)}) %copy-start) | copy-done | bytes 524312
  1.7 0.3 edges.1
  2.0 0.0 copy-start.6
  2.0 0.0 copy-start.7
  2.0 0.0 copy-start.3
  2.0 0.0 copy-start.4
  2.0 0.0 copy-start.5
  2.0 5.1 %collective-permute-start = (bf16[256,64]{1,0:T(8,128)(2,1)S(1)}, bf16[256,64]{1,0:T(8,128)(2,1)S(1)}, u32[]{:S(2)}, u32[]{:S(2)}) collective-permute-start(bf16[256,64]{1,0:T(8,128)(2,1)S(1)} %get-tuple-element.8), channel_id=1, source_target_pairs={{0,1},{1,2},{2,3},{4,5},{5,6},{6,7},{8,9},{9,10},{10,11},{12,13},{... | collective-permute-start | bytes 98312 | tf_op jit(solution)/shard_map/ppermute | solution.py:28
  7.1 1.3 %collective-permute-start.1 = (bf16[256,64]{1,0:T(8,128)(2,1)S(1)}, bf16[256,64]{1,0:T(8,128)(2,1)S(1)}, u32[]{:S(2)}, u32[]{:S(2)}) collective-permute-start(bf16[256,64]{1,0:T(8,128)(2,1)S(1)} %get-tuple-element.9), channel_id=1, source_target_pairs={{1,0},{2,1},{3,2},{5,4},{6,5},{7,6},{9,8},{10,9},{11,10},{13,12},{... | collective-permute-start | bytes 98312 | tf_op jit(solution)/shard_map/ppermute | solution.py:28
  8.4 0.0 copy-done.6
  8.4 0.0 copy-done.7
  8.4 0.0 copy-done.3
  8.4 0.0 copy-done.4
  8.5 1.6 %taps.1 = (bf16[2,256,256]{2,1,0:T(8,128)(2,1)S(1)}, bf16[64,512]{1,0:T(8,128)(2,1)S(1)}, bf16[64,512]{1,0:T(8,128)(2,1)S(1)}, bf16[2,256,256]{2,1,0:T(8,128)(2,1)S(1)}) custom-call(s32[16]{0:T(128)S(1)} %copy-done.3, s32[16]{0:T(128)S(1)} %copy-done.4, s32[16]{0:T(128)S(1)} %copy-done.5, s32[16]{0:T(128)S(1)} %copy-done.6, s32[16]{0:T(128)S(1)} %copy-done.7), custom_call_target="tpu_custom_call" | custom-call | flops 4000000 | bytes 800000 | tf_op jit(solution)/shard_map/taps/pallas_call | solution.py:273
  10.0 0.0 collective-permute-done.last_ref
  10.0 3.2 %collective-permute-done.1.first_ref = bf16[256,64]{1,0:T(8,128)(2,1)S(1)} collective-permute-done((bf16[256,64]{1,0:T(8,128)(2,1)S(1)}, bf16[256,64]{1,0:T(8,128)(2,1)S(1)}, u32[]{:S(2)}, u32[]{:S(2)}) %collective-permute-start.1) | collective-permute-done | bytes 32800 | tf_op jit(solution)/shard_map/ppermute | solution.py:28
  13.3 1.5 %resample.1 = bf16[8,2,2,32,256]{4,3,2,1,0:T(8,128)(2,1)} custom-call(bf16[2,2,256,256]{3,2,1,0:T(8,128)(2,1)S(1)} %copy-done.1, bf16[256,64]{1,0:T(8,128)(2,1)S(1)} %collective-permute-done.last_ref, bf16[256,64]{1,0:T(8,128)(2,1)S(1)} %collective-permute-done.1.first_ref, bf16[2,256,256]{2,1,0:T(8,128)(2,1)S(1)} %get-tuple-element.10.own_ref, ...), custom_call_target="tpu_custom_call" | custom-call | tf_op jit(solution)/shard_map/resample/pallas_call | solution.py:293
  14.8 3.7 %all-to-all-start = ((bf16[8,2,2,32,256]{4,3,2,1,0:T(8,128)(2,1)}), bf16[8,2,2,32,256]{4,3,2,1,0:T(8,128)(2,1)S(1)}, u32[]{:S(2)}, u32[]{:S(2)}) async-start(bf16[8,2,2,32,256]{4,3,2,1,0:T(8,128)(2,1)} %resample.1), calls=%async_computation | async-start | bytes 1048576 | tf_op jit(solution)/shard_map/all_to_all | solution.py:304
  19.2 9.1 %all-to-all-done = bf16[8,2,2,32,256]{4,3,2,1,0:T(8,128)(2,1)S(1)} async-done(((bf16[8,2,2,32,256]{4,3,2,1,0:T(8,128)(2,1)}), bf16[8,2,2,32,256]{4,3,2,1,0:T(8,128)(2,1)S(1)}, u32[]{:S(2)}, u32[]{:S(2)}) %all-to-all-start) | async-done | bytes 524320 | tf_op jit(solution)/shard_map/all_to_all | solution.py:304
  28.3 0.7 %copy-done.2 = s32[16,2]{0,1:T(2,128)S(1)} copy-done((s32[16,2]{0,1:T(2,128)S(1)}, s32[16,2]{0,1:T(2,128)}, u32[]{:S(2)}) %copy-start.2) | copy-done | bytes 152
  28.9 1.7 %looks.1 = f32[8,18,128]{2,1,0:T(8,128)S(1)} custom-call(s32[2,16]{1,0:T(2,128)S(1)} %bitcast.3, s32[1]{0:T(128)S(6)} %copy.10.master_ref, bf16[16,2,32,256]{3,2,1,0:T(8,128)(2,1)S(1)} %bitcast.2), custom_call_target="tpu_custom_call" | custom-call | tf_op jit(solution)/shard_map/looks/pallas_call | solution.py:306
  30.6 7.6 %all_to_all.10.x_ref = f32[8,18,128]{2,1,0:T(8,128)S(1)} all-to-all(f32[8,18,128]{2,1,0:T(8,128)S(1)} %looks.1), channel_id=1, replica_groups=mesh['date'=8,'range'=4] {'date'}, dimensions={0} | all-to-all | bytes 147456 | tf_op jit(solution)/shard_map/all_to_all | solution.py:319
  38.2 0.8 %place.1 = (f32[2,6,16,64]{3,2,1,0:T(8,128)}, f32[2,3,16,64]{3,2,1,0:T(8,128)}) custom-call(f32[8,18,128]{2,1,0:T(8,128)S(1)} %all_to_all.10.x_ref), custom_call_target="tpu_custom_call" | custom-call | tf_op jit(solution)/shard_map/place/pallas_call | solution.py:323
  (4 shorter events, 0.0 us)
Async XLA Ops:
  0.6 1.0 %copy-start = (bf16[2,2,256,256]{3,2,1,0:T(8,128)(2,1)S(1)}, bf16[2,2,256,256]{3,2,1,0:T(8,128)(2,1)}, u32[]{:S(2)}) copy-start(bf16[2,2,256,256]{3,2,1,0:T(8,128)(2,1)} %x_ref.3) | copy-start | bytes 1572868
  1.7 11.6 %copy-start.1 = (bf16[2,2,256,256]{3,2,1,0:T(8,128)(2,1)S(1)}, bf16[2,2,256,256]{3,2,1,0:T(8,128)(2,1)}, u32[]{:S(2)}) copy-start(bf16[2,2,256,256]{3,2,1,0:T(8,128)(2,1)} %x_ref.3) | copy-start | bytes 1572868
  2.0 6.4 %copy-start.6 = (s32[16]{0:T(128)S(1)}, s32[16]{0:T(128)}, u32[]{:S(2)}) copy-start(s32[16]{0:T(128)} %rg_part.1) | copy-start | bytes 196
  2.0 6.4 %copy-start.7 = (s32[16]{0:T(128)S(1)}, s32[16]{0:T(128)}, u32[]{:S(2)}) copy-start(s32[16]{0:T(128)} %sweeps.1) | copy-start | bytes 196
  2.0 6.4 %copy-start.3 = (s32[16]{0:T(128)S(1)}, s32[16]{0:T(128)}, u32[]{:S(2)}) copy-start(s32[16]{0:T(128)} %az_whole.1) | copy-start | bytes 196
  2.0 6.4 %copy-start.4 = (s32[16]{0:T(128)S(1)}, s32[16]{0:T(128)}, u32[]{:S(2)}) copy-start(s32[16]{0:T(128)} %az_part.1) | copy-start | bytes 196
  2.0 6.4 %copy-start.5 = (s32[16]{0:T(128)S(1)}, s32[16]{0:T(128)}, u32[]{:S(2)}) copy-start(s32[16]{0:T(128)} %rg_whole.1) | copy-start | bytes 196
  2.0 8.0 %collective-permute-start = (bf16[256,64]{1,0:T(8,128)(2,1)S(1)}, bf16[256,64]{1,0:T(8,128)(2,1)S(1)}, u32[]{:S(2)}, u32[]{:S(2)}) collective-permute-start(bf16[256,64]{1,0:T(8,128)(2,1)S(1)} %get-tuple-element.8), channel_id=1, source_target_pairs={{0,1},{1,2},{2,3},{4,5},{5,6},{6,7},{8,9},{9,10},{10,11},{12,13},{... | collective-permute-start | bytes 98312 | tf_op jit(solution)/shard_map/ppermute | solution.py:28
  7.1 6.2 %collective-permute-start.1 = (bf16[256,64]{1,0:T(8,128)(2,1)S(1)}, bf16[256,64]{1,0:T(8,128)(2,1)S(1)}, u32[]{:S(2)}, u32[]{:S(2)}) collective-permute-start(bf16[256,64]{1,0:T(8,128)(2,1)S(1)} %get-tuple-element.9), channel_id=1, source_target_pairs={{1,0},{2,1},{3,2},{5,4},{6,5},{7,6},{9,8},{10,9},{11,10},{13,12},{... | collective-permute-start | bytes 98312 | tf_op jit(solution)/shard_map/ppermute | solution.py:28
  14.8 13.5 %all-to-all-start = ((bf16[8,2,2,32,256]{4,3,2,1,0:T(8,128)(2,1)}), bf16[8,2,2,32,256]{4,3,2,1,0:T(8,128)(2,1)S(1)}, u32[]{:S(2)}, u32[]{:S(2)}) async-start(bf16[8,2,2,32,256]{4,3,2,1,0:T(8,128)(2,1)} %resample.1), calls=%async_computation | async-start | bytes 1048576 | tf_op jit(solution)/shard_map/all_to_all | solution.py:304
  28.2 0.7 %copy-start.2 = (s32[16,2]{0,1:T(2,128)S(1)}, s32[16,2]{0,1:T(2,128)}, u32[]{:S(2)}) copy-start(s32[16,2]{0,1:T(2,128)} %param.14) | copy-start | bytes 388

commit v3 on v2

--- a/solution.py
+++ b/solution.py
@@ -23,11 +23,8 @@
 VMEM = pl.BlockSpec(memory_space=pltpu.VMEM)
 
 
-def shifted(block, axis, distance):
-    count = lax.axis_size(axis)
-    return lax.ppermute(
-        block, axis, [(i, i + distance) for i in range(count) if 0 <= i + distance < count]
-    )
+def exchanged(array, axis, pairs):
+    return lax.ppermute(array, axis, [route for a, b in pairs for route in ((a, b), (b, a))])
 
 
 def near(array):
@@ -41,13 +38,23 @@
     )
 
 
-def edges_kernel(x_ref, last_ref, first_ref):
+def edges_kernel(x_ref, near_ref, even_ref, odd_ref, sems):
     dates, parts, _, columns = x_ref.shape
-    for slot in range(dates):
-        for part in range(parts):
-            spot = slice((slot * parts + part) * MARGIN, (slot * parts + part + 1) * MARGIN)
-            last_ref[:, spot] = x_ref[slot, part, :, columns - MARGIN :]
-            first_ref[:, spot] = x_ref[slot, part, :, :MARGIN]
+    forward = lax.axis_index("range") % 2 == 0
+    images = [(slot, part) for slot in range(dates) for part in range(parts)]
+    copies = [
+        pltpu.make_async_copy(x_ref.at[image], near_ref.at[image], sems.at[number])
+        for number, image in enumerate(images)
+    ]
+    for copy in copies:
+        copy.start()
+    for number, (slot, part) in enumerate(images):
+        copies[number].wait()
+        spot = slice(number * MARGIN, (number + 1) * MARGIN)
+        last = near_ref[slot, part, :, columns - MARGIN :]
+        first = near_ref[slot, part, :, :MARGIN]
+        even_ref[:, spot] = jnp.where(forward, last, first)
+        odd_ref[:, spot] = jnp.where(forward, first, last)
 
 
 def weight_rows(fractions):
@@ -64,6 +71,16 @@
     return weights.astype(jnp.bfloat16).astype(jnp.float32)
 
 
+def by_pairs(owners):
+    return owners in (2, 4, 8)
+
+
+def tile_order(position):
+    if by_pairs(lax.axis_size("date")):
+        return position ^ lax.axis_index("date")
+    return position
+
+
 def banded(offsets, weights):
     rows, cols = offsets.shape
     lanes = jnp.broadcast_to(weights, (rows, LANES))
@@ -77,8 +94,23 @@
     )
 
 
-def taps_kernel(az_whole, az_part, rg_whole, rg_part, sweeps, own_ref, low_ref, high_ref, line_ref):
+def taps_kernel(
+    tile_lines,
+    az_whole,
+    az_part,
+    rg_whole,
+    rg_part,
+    sweeps,
+    gap_ref,
+    master_ref,
+    own_ref,
+    low_ref,
+    high_ref,
+    line_ref,
+    partner_ref,
+):
     dates, columns, _ = own_ref.shape
+    total = partner_ref.shape[1]
     lines = line_ref.shape[1]
     edge_rows = low_ref.shape[0]
     parts = edge_rows // MARGIN // dates
@@ -101,19 +133,31 @@
             low_ref[:, spot] = jnp.where(held, low, 0.0).astype(jnp.bfloat16)
             high_ref[:, spot] = jnp.where(held, high, 0.0).astype(jnp.bfloat16)
         row, col = iotas(lines, lines)
+        row = tile_order(row // tile_lines) * tile_lines + row % tile_lines
         weights = table[dates + slot : dates + slot + 1]
         band = banded(col - row + (centre - az_whole[date]), weights)
         usable = row < sweeps[date] * (lines // MAX_SWEEPS)
         line_ref[slot] = jnp.where(usable, band, 0.0).astype(jnp.bfloat16)
 
-
-def resample_kernel(
-    split, x_ref, last_ref, first_ref, own_ref, low_ref, high_ref, line_ref, out_ref
-):
+    def find(date, carry):
+        for kind, partner in enumerate(partners(date, gap_ref, master_ref, total)):
+            partner_ref[kind, date] = partner
+        return carry
+
+    lax.fori_loop(0, total, find, 0)
+
+
+def resample_kernel(split, x_ref, even_ref, odd_ref, own_ref, low_ref, high_ref, line_ref, *outs):
     dates, parts, _, columns = x_ref.shape
     line_groups, column_groups, tile_lines, tile_columns = split
-    low = jnp.dot(last_ref[...], low_ref[...], preferred_element_type=jnp.float32)
-    high = jnp.dot(first_ref[...], high_ref[...], preferred_element_type=jnp.float32)
+    forward = lax.axis_index("range") % 2 == 0
+    even, odd = even_ref[...], odd_ref[...]
+    low = jnp.dot(
+        jnp.where(forward, odd, even), low_ref[...], preferred_element_type=jnp.float32
+    )
+    high = jnp.dot(
+        jnp.where(forward, even, odd), high_ref[...], preferred_element_type=jnp.float32
+    )
     for slot in range(dates):
         for part in range(parts):
             spot = slice((slot * parts + part) * LANES, (slot * parts + part + 1) * LANES)
@@ -127,10 +171,14 @@
             ).astype(jnp.bfloat16)
             for i in range(line_groups):
                 for j in range(column_groups):
-                    out_ref[i * column_groups + j, slot, part] = moved[
+                    tile = moved[
                         i * tile_lines : (i + 1) * tile_lines,
                         j * tile_columns : (j + 1) * tile_columns,
                     ]
+                    if len(outs) == 1:
+                        outs[0][i * column_groups + j, slot, part] = tile
+                    else:
+                        outs[i][slot, part] = tile
 
 
 def partners(date, gap_ref, master_ref, total):
@@ -158,20 +206,30 @@
     return values[0]
 
 
-def looks_kernel(gap_ref, master_ref, r_ref, out_ref, sums, pooled, powers):
-    total, _, tile_lines, tile_columns = r_ref.shape
+def looks_kernel(partner_ref, *refs):
+    tiles, (out_ref, stack, sums, pooled, powers) = refs[:-5], refs[-5:]
+    total, _, tile_lines, tile_columns = stack.shape
     owners, per_owner, lanes = out_ref.shape
     dates = per_owner // CHANNELS
     line_looks = tile_lines // LOOK_AZ
     unroll = total if total <= 16 else 1
+    if len(tiles) > 1:
+        for position, tile_ref in enumerate(tiles):
+            stack[pl.ds(tile_order(position) * dates, dates)] = tile_ref[...].astype(jnp.float32)
+    else:
+
+        def widen(owner, carry):
+            stack[pl.ds(owner * dates, dates)] = tiles[0][owner].astype(jnp.float32)
+            return carry
+
+        lax.fori_loop(0, owners, widen, 0)
 
     def collect(date, carry):
-        left0 = r_ref[date, 0].astype(jnp.float32)
-        left1 = r_ref[date, 1].astype(jnp.float32)
+        left0, left1 = stack[date, 0], stack[date, 1]
         values = []
-        for partner in partners(date, gap_ref, master_ref, total):
-            right0 = r_ref[partner, 0].astype(jnp.float32)
-            right1 = r_ref[partner, 1].astype(jnp.float32)
+        for kind in range(KINDS):
+            partner = partner_ref[kind, date]
+            right0, right1 = stack[partner, 0], stack[partner, 1]
             values += [left0 * right0 + left1 * right1, left1 * right0 - left0 * right1]
         values.append(left0 * left0 + left1 * left1)
         values.append(jnp.zeros_like(left0))
@@ -196,10 +254,9 @@
     )
 
     def gather(date, carry):
-        for kind, partner in enumerate(partners(date, gap_ref, master_ref, total)):
-            powers[kind, pl.ds(date, 1), :] = pooled[
-                pl.ds(partner * QUANTITIES + 2 * KINDS, 1), :
-            ]
+        for kind in range(KINDS):
+            power = partner_ref[kind, date] * QUANTITIES + 2 * KINDS
+            powers[kind, pl.ds(date, 1), :] = pooled[pl.ds(power, 1), :]
         return carry
 
     lax.fori_loop(0, total, gather, 0, unroll=unroll)
@@ -258,28 +315,34 @@
     line_looks, column_looks = tile_lines // LOOK_AZ, tile_columns // LOOK_RG
     lanes = line_looks * column_looks
 
-    block = near(block)
-    last, first = pl.pallas_call(
+    block, even, odd = pl.pallas_call(
         edges_kernel,
-        out_shape=(pltpu.VMEM((lines, images * MARGIN), jnp.bfloat16),) * 2,
-        in_specs=[VMEM],
-        out_specs=(VMEM, VMEM),
+        out_shape=(
+            pltpu.VMEM(block.shape, block.dtype),
+            pltpu.VMEM((lines, images * MARGIN), jnp.bfloat16),
+            pltpu.VMEM((lines, images * MARGIN), jnp.bfloat16),
+        ),
+        in_specs=[pl.BlockSpec(memory_space=pltpu.HBM)],
+        out_specs=(VMEM,) * 3,
+        scratch_shapes=[pltpu.SemaphoreType.DMA((images,))],
         name="edges",
         compiler_params=pltpu.CompilerParams(vmem_limit_bytes=GRANT),
     )(block)
-    last = shifted(last, "range", 1)
-    first = shifted(first, "range", -1)
-
-    taps = pl.pallas_call(
-        taps_kernel,
+    width = lax.axis_size("range")
+    odd = exchanged(odd, "range", [(j, j + 1) for j in range(1, width - 1, 2)])
+    even = exchanged(even, "range", [(j, j + 1) for j in range(0, width - 1, 2)])
+
+    *taps, table = pl.pallas_call(
+        functools.partial(taps_kernel, tile_lines),
         out_shape=(
             pltpu.VMEM((dates, columns, columns), jnp.bfloat16),
             pltpu.VMEM((images * MARGIN, images * LANES), jnp.bfloat16),
             pltpu.VMEM((images * MARGIN, images * LANES), jnp.bfloat16),
             pltpu.VMEM((dates, lines, lines), jnp.bfloat16),
+            pltpu.SMEM((KINDS, total), jnp.int32),
         ),
-        in_specs=[SMEM] * 5,
-        out_specs=(VMEM,) * 4,
+        in_specs=[SMEM] * 7,
+        out_specs=(VMEM,) * 4 + (SMEM,),
         cost_estimate=pl.CostEstimate(flops=4000000, bytes_accessed=800000, transcendentals=0),
         name="taps",
         compiler_params=pltpu.CompilerParams(vmem_limit_bytes=GRANT),
@@ -289,33 +352,49 @@
         slant_whole_displacement,
         slant_subpixel_weights,
         sweeps_each_epoch,
-    )
+        baseline_companion_gap.T,
+        master_epoch_image,
+    )
+    tile = (dates, parts, tile_lines, tile_columns)
+    if by_pairs(owners):
+        out_shape = (pltpu.VMEM(tile, jnp.bfloat16),) * owners
+    else:
+        out_shape = (pltpu.VMEM((owners,) + tile, jnp.bfloat16),)
     tiles = pl.pallas_call(
         functools.partial(
             resample_kernel, (line_groups, column_groups, tile_lines, tile_columns)
         ),
-        out_shape=pltpu.VMEM((owners, dates, parts, tile_lines, tile_columns), jnp.bfloat16),
+        out_shape=out_shape,
         in_specs=[VMEM] * 7,
-        out_specs=VMEM,
+        out_specs=(VMEM,) * len(out_shape),
         name="resample",
         compiler_params=pltpu.CompilerParams(vmem_limit_bytes=GRANT),
-    )(block, near(last), near(first), *[near(tap) for tap in taps])
-
-    tiles = lax.all_to_all(tiles, "date", 0, 0)
-    stack = tiles.reshape(total, parts, tile_lines, tile_columns)
+    )(near(block), near(even), near(odd), *[near(tap) for tap in taps])
+
+    if by_pairs(owners):
+        tiles = [tiles[0]] + [
+            exchanged(tiles[s], "date", [(i, i ^ s) for i in range(owners) if i < i ^ s])
+            for s in range(1, owners)
+        ]
+    else:
+        tiles = [lax.all_to_all(tiles[0], "date", 0, 0)]
     results = pl.pallas_call(
         looks_kernel,
         out_shape=pltpu.VMEM((owners, dates * CHANNELS, lanes), jnp.float32),
-        in_specs=[SMEM, SMEM, VMEM],
+        in_specs=[SMEM] + [VMEM] * len(tiles),
         out_specs=VMEM,
         scratch_shapes=[
+            pltpu.VMEM((total, parts, tile_lines, tile_columns), jnp.float32),
             pltpu.VMEM((total * QUANTITIES, line_looks * tile_columns), jnp.float32),
             pltpu.VMEM((total * QUANTITIES, lanes), jnp.float32),
             pltpu.VMEM((KINDS, total, lanes), jnp.float32),
         ],
         name="looks",
         compiler_params=pltpu.CompilerParams(vmem_limit_bytes=GRANT),
-    )(baseline_companion_gap.T, master_epoch_image, near(stack))
+    )(
+        pltpu.with_memory_space_constraint(table, pltpu.SMEM),
+        *[near(tile) for tile in tiles],
+    )
     results = lax.all_to_all(results, "date", 0, 0)
 
     rows, cols = lines // LOOK_AZ, columns // LOOK_RG

time: 39.3 us -> 33.5 us (0.85)
  the two profiles are of different devices: /device:TPU:0 before, /device:TPU:8 now
where the time goes in v3:
time: 33.5 us; the launch traced here: 33.3 us
  starting transfers between devices  11.4 us (34%)
  blocking collectives  8.03 us (24%)
  Pallas kernels  5.99 us (18%)
  waiting for transfers between devices  4.71 us (14%)
  local copies, waits for them, and re-layouts  1.69 us (5%)
  between operations  1.44 us (4%)
    ppermute x9, starting transfers between devices, exchanged(): lax.ppermute(array, axis, [route for a, b in pairs for route in ((a, b),...  11.4 us
    all_to_all x1, blocking collectives, body(): results = lax.all_to_all(results, 'date', 0, 0)  8.03 us
    ppermute x9, waiting for transfers between devices, exchanged(): lax.ppermute(array, axis, [route for a, b in pairs for route in ((a, b),...  4.71 us
    pallas_call x1, Pallas kernels, body(): pl.pallas_call(functools.partial(taps_kernel, tile_lines), out_shape=(plt...  1.77 us
    unnamed x14, local copies, waits for them, and re-layouts  1.69 us
    pallas_call x1, Pallas kernels, body(): pl.pallas_call(edges_kernel, out_shape=(pltpu.VMEM(block.shape, block.dty...  1.67 us
    pallas_call x1, Pallas kernels, body(): pl.pallas_call(looks_kernel, out_shape=pltpu.VMEM((owners, dates * CHANNE...  1.07 us
    pallas_call x1, Pallas kernels, body(): pl.pallas_call(place_kernel, out_shape=(jax.ShapeDtypeStruct((dates, 2 *...  0.76 us
  transfers between devices with their start and end apart: 9, of which 3 were waited for; matrix products, arithmetic and copies ran while one was open for 0% of the time, Pallas kernels for 5%

profile of v3, /device:TPU:8, one launch (start us, length us, event | category | flops | bytes accessed | tf_op | source)
XLA Modules:
  0.0 33.3 jit_solution(7324967899735775317)
XLA Ops:
  0.6 1.0 %copy-done = bf16[2,2,256,256]{3,2,1,0:T(8,128)(2,1)S(1)} copy-done((bf16[2,2,256,256]{3,2,1,0:T(8,128)(2,1)S(1)}, bf16[2,2,256,256]{3,2,1,0:T(8,128)(2,1)}, u32[]{:S(2)}) %copy-start) | copy-done | bytes 524312
  1.7 1.7 %edges.1 = (bf16[2,2,256,256]{3,2,1,0:T(8,128)(2,1)S(1)}, bf16[256,64]{1,0:T(8,128)(2,1)S(1)}, bf16[256,64]{1,0:T(8,128)(2,1)S(1)}) custom-call(bf16[2,2,256,256]{3,2,1,0:T(8,128)(2,1)S(1)} %copy-done), custom_call_target="tpu_custom_call" | custom-call | tf_op jit(solution)/shard_map/edges/pallas_call | solution.py:318
  3.3 0.0 copy-start.3
  3.4 0.0 copy-start.5
  3.4 0.0 copy-start.6
  3.4 0.1 collective-permute-start
  3.5 5.0 %collective-permute-start.1 = (bf16[256,64]{1,0:T(8,128)(2,1)S(1)}, bf16[256,64]{1,0:T(8,128)(2,1)S(1)}, u32[]{:S(2)}, u32[]{:S(2)}) collective-permute-start(bf16[256,64]{1,0:T(8,128)(2,1)S(1)} %get-tuple-element.21), channel_id=1, source_target_pairs={{1,2},{2,1},{5,6},{6,5},{9,10},{10,9},{13,14},{14,13},{17,18},{18,... | collective-permute-start | bytes 98312 | tf_op jit(solution)/shard_map/ppermute | solution.py:27
  9.2 0.0 copy-start.1
  9.2 0.6 %copy-done.1 = s32[16,2]{0,1:T(2,128)S(1)} copy-done((s32[16,2]{0,1:T(2,128)S(1)}, s32[16,2]{0,1:T(2,128)}, u32[]{:S(2)}) %copy-start.1) | copy-done | bytes 152
  9.8 1.8 %taps.1 = (bf16[2,256,256]{2,1,0:T(8,128)(2,1)S(1)}, bf16[64,512]{1,0:T(8,128)(2,1)S(1)}, bf16[64,512]{1,0:T(8,128)(2,1)S(1)}, bf16[2,256,256]{2,1,0:T(8,128)(2,1)S(1)}, s32[3,16]{1,0:T(4,128)S(4)}) custom-call(s32[16]{0:T(128)S(1)} %copy-done.2, s32[16]{0:T(128)S(1)} %copy-done.3, s32[16]{0:T(128)S(1)} %copy-done.4, s32[16]{0:T(128)S(1)} %copy-done.5, ...), custom_call_target="tpu_custom_call" | custom-call | flops 4000000 | bytes 800000 | tf_op jit(solution)/shard_map/taps/pallas_call | solution.py:335
  11.6 0.7 %resample.1 = (bf16[2,2,32,256]{3,2,1,0:T(8,128)(2,1)S(1)}, bf16[2,2,32,256]{3,2,1,0:T(8,128)(2,1)S(1)}, bf16[2,2,32,256]{3,2,1,0:T(8,128)(2,1)S(1)}, bf16[2,2,3...) custom-call(bf16[2,2,256,256]{3,2,1,0:T(8,128)(2,1)S(1)} %get-tuple-, ...), custom_call_target="tpu_custom_call" | custom-call | tf_op jit(solution)/shard_map/resample/pallas_call | solution.py:363
  12.4 0.1 collective-permute-start.2
  12.5 1.6 %collective-permute-start.3 = (bf16[2,2,32,256]{3,2,1,0:T(8,128)(2,1)S(1)}, bf16[2,2,32,256]{3,2,1,0:T(8,128)(2,1)S(1)}, u32[]{:S(2)}, u32[]{:S(2)}) collective-permute-start(bf16[2,2,32,256]{3,2,1,0:T(8,128)(2,1)S(1)} %get-tuple-element.28), channel_id=1, source_target_pairs={{0,8},{8,0},{4,12},{12,4},{16,24},{24,16},{20,28},{28,20},{1,9},{9... | collective-permute-start | bytes 196616 | tf_op jit(solution)/shard_map/ppermute | solution.py:27
  14.0 0.3 collective-permute-start.4
  14.3 1.5 %collective-permute-start.5 = (bf16[2,2,32,256]{3,2,1,0:T(8,128)(2,1)S(1)}, bf16[2,2,32,256]{3,2,1,0:T(8,128)(2,1)S(1)}, u32[]{:S(2)}, u32[]{:S(2)}) collective-permute-start(bf16[2,2,32,256]{3,2,1,0:T(8,128)(2,1)S(1)} %get-tuple-element.30), channel_id=1, source_target_pairs={{0,16},{16,0},{4,20},{20,4},{8,24},{24,8},{12,28},{28,12},{1,17},{... | collective-permute-start | bytes 196616 | tf_op jit(solution)/shard_map/ppermute | solution.py:27
  15.8 0.2 collective-permute-start.6
  16.0 2.4 %collective-permute-start.7 = (bf16[2,2,32,256]{3,2,1,0:T(8,128)(2,1)S(1)}, bf16[2,2,32,256]{3,2,1,0:T(8,128)(2,1)S(1)}, u32[]{:S(2)}, u32[]{:S(2)}) collective-permute-start(bf16[2,2,32,256]{3,2,1,0:T(8,128)(2,1)S(1)} %get-tuple-element.32), channel_id=1, source_target_pairs={{0,24},{24,0},{4,28},{28,4},{8,16},{16,8},{12,20},{20,12},{1,25},{... | collective-permute-start | bytes 196616 | tf_op jit(solution)/shard_map/ppermute | solution.py:27
  18.5 0.2 collective-permute-start.8
  18.7 1.3 %collective-permute-done.6.refs_5_ = bf16[2,2,32,256]{3,2,1,0:T(8,128)(2,1)S(1)} collective-permute-done((bf16[2,2,32,256]{3,2,1,0:T(8,128)(2,1)S(1)}, bf16[2,2,32,256]{3,2,1,0:T(8,128)(2,1)S(1)}, u32[]{:S(2)}, u32[]{:S(2)}) %collective-permute-start.6) | collective-permute-done | bytes 65568 | tf_op jit(solution)/shard_map/ppermute | solution.py:27
  20.0 1.5 %collective-permute-done.7.refs_6_ = bf16[2,2,32,256]{3,2,1,0:T(8,128)(2,1)S(1)} collective-permute-done((bf16[2,2,32,256]{3,2,1,0:T(8,128)(2,1)S(1)}, bf16[2,2,32,256]{3,2,1,0:T(8,128)(2,1)S(1)}, u32[]{:S(2)}, u32[]{:S(2)}) %collective-permute-start.7) | collective-permute-done | bytes 65568 | tf_op jit(solution)/shard_map/ppermute | solution.py:27
  21.5 1.9 %collective-permute-done.8.refs_7_ = bf16[2,2,32,256]{3,2,1,0:T(8,128)(2,1)S(1)} collective-permute-done((bf16[2,2,32,256]{3,2,1,0:T(8,128)(2,1)S(1)}, bf16[2,2,32,256]{3,2,1,0:T(8,128)(2,1)S(1)}, u32[]{:S(2)}, u32[]{:S(2)}) %collective-permute-start.8) | collective-permute-done | bytes 65568 | tf_op jit(solution)/shard_map/ppermute | solution.py:27
  23.4 1.1 %looks.1 = f32[8,18,128]{2,1,0:T(8,128)S(1)} custom-call(s32[3,16]{1,0:T(4,128)S(4)} %get-tuple-element.18.partner_ref, bf16[2,2,32,256]{3,2,1,0:T(8,128)(2,1)S(1)} %get-tuple-element.26.refs_0_, bf16[2,2,32,256]{3,2,1,0:T(8,128)(2,1)S(1)} %collective-permute-done.2.refs_1_, bf16[2,2,32,256]{3,2,1,0:T(8,128)(2,1)S(1)} %collective-permute-done.3.refs_2_, ...), custom_call_target="tpu_custom_call" | custom-call | tf_op jit(solution)/shard_map/looks/pallas_call | solution.py:381
  24.5 8.0 %all_to_all.5.x_ref = f32[8,18,128]{2,1,0:T(8,128)S(1)} all-to-all(f32[8,18,128]{2,1,0:T(8,128)S(1)} %looks.1), channel_id=1, replica_groups=mesh['date'=8,'range'=4] {'date'}, dimensions={0} | all-to-all | bytes 147456 | tf_op jit(solution)/shard_map/all_to_all | solution.py:398
  32.5 0.8 %place.1 = (f32[2,6,16,64]{3,2,1,0:T(8,128)}, f32[2,3,16,64]{3,2,1,0:T(8,128)}) custom-call(f32[8,18,128]{2,1,0:T(8,128)S(1)} %all_to_all.5.x_ref), custom_call_target="tpu_custom_call" | custom-call | tf_op jit(solution)/shard_map/place/pallas_call | solution.py:402
  (14 shorter events, 0.0 us)
Async XLA Ops:
  0.6 1.0 %copy-start = (bf16[2,2,256,256]{3,2,1,0:T(8,128)(2,1)S(1)}, bf16[2,2,256,256]{3,2,1,0:T(8,128)(2,1)}, u32[]{:S(2)}) copy-start(bf16[2,2,256,256]{3,2,1,0:T(8,128)(2,1)} %x_ref.1) | copy-start | bytes 1572868
  3.3 5.8 %copy-start.3 = (s32[16]{0:T(128)S(1)}, s32[16]{0:T(128)}, u32[]{:S(2)}) copy-start(s32[16]{0:T(128)} %az_part.1) | copy-start | bytes 196
  3.4 5.8 %copy-start.4 = (s32[16]{0:T(128)S(1)}, s32[16]{0:T(128)}, u32[]{:S(2)}) copy-start(s32[16]{0:T(128)} %rg_whole.1) | copy-start | bytes 196
  3.4 5.8 %copy-start.5 = (s32[16]{0:T(128)S(1)}, s32[16]{0:T(128)}, u32[]{:S(2)}) copy-start(s32[16]{0:T(128)} %rg_part.1) | copy-start | bytes 196
  3.4 5.8 %copy-start.6 = (s32[16]{0:T(128)S(1)}, s32[16]{0:T(128)}, u32[]{:S(2)}) copy-start(s32[16]{0:T(128)} %sweeps.1) | copy-start | bytes 196
  3.4 8.2 %collective-permute-start = (bf16[256,64]{1,0:T(8,128)(2,1)S(1)}, bf16[256,64]{1,0:T(8,128)(2,1)S(1)}, u32[]{:S(2)}, u32[]{:S(2)}) collective-permute-start(bf16[256,64]{1,0:T(8,128)(2,1)S(1)} %get-tuple-element.20), channel_id=1, source_target_pairs={{0,1},{1,0},{2,3},{3,2},{4,5},{5,4},{6,7},{7,6},{8,9},{9,8},{10,11... | collective-permute-start | bytes 98312 | tf_op jit(solution)/shard_map/ppermute | solution.py:27
  3.5 8.2 %collective-permute-start.1 = (bf16[256,64]{1,0:T(8,128)(2,1)S(1)}, bf16[256,64]{1,0:T(8,128)(2,1)S(1)}, u32[]{:S(2)}, u32[]{:S(2)}) collective-permute-start(bf16[256,64]{1,0:T(8,128)(2,1)S(1)} %get-tuple-element.21), channel_id=1, source_target_pairs={{1,2},{2,1},{5,6},{6,5},{9,10},{10,9},{13,14},{14,13},{17,18},{18,... | collective-permute-start | bytes 98312 | tf_op jit(solution)/shard_map/ppermute | solution.py:27
  9.2 0.7 %copy-start.1 = (s32[16,2]{0,1:T(2,128)S(1)}, s32[16,2]{0,1:T(2,128)}, u32[]{:S(2)}) copy-start(s32[16,2]{0,1:T(2,128)} %param.14) | copy-start | bytes 388
  9.2 0.7 %copy-start.2 = (s32[16]{0:T(128)S(1)}, s32[16]{0:T(128)}, u32[]{:S(2)}) copy-start(s32[16]{0:T(128)} %az_whole.1) | copy-start | bytes 196
  12.4 3.6 %collective-permute-start.2 = (bf16[2,2,32,256]{3,2,1,0:T(8,128)(2,1)S(1)}, bf16[2,2,32,256]{3,2,1,0:T(8,128)(2,1)S(1)}, u32[]{:S(2)}, u32[]{:S(2)}) collective-permute-start(bf16[2,2,32,256]{3,2,1,0:T(8,128)(2,1)S(1)} %get-tuple-element.27), channel_id=1, source_target_pairs={{0,4},{4,0},{8,12},{12,8},{16,20},{20,16},{24,28},{28,24},{1,5},{5... | collective-permute-start | bytes 196616 | tf_op jit(solution)/shard_map/ppermute | solution.py:27
  12.5 6.0 %collective-permute-start.3 = (bf16[2,2,32,256]{3,2,1,0:T(8,128)(2,1)S(1)}, bf16[2,2,32,256]{3,2,1,0:T(8,128)(2,1)S(1)}, u32[]{:S(2)}, u32[]{:S(2)}) collective-permute-start(bf16[2,2,32,256]{3,2,1,0:T(8,128)(2,1)S(1)} %get-tuple-element.28), channel_id=1, source_target_pairs={{0,8},{8,0},{4,12},{12,4},{16,24},{24,16},{20,28},{28,20},{1,9},{9... | collective-permute-start | bytes 196616 | tf_op jit(solution)/shard_map/ppermute | solution.py:27
  14.0 4.7 %collective-permute-start.4 = (bf16[2,2,32,256]{3,2,1,0:T(8,128)(2,1)S(1)}, bf16[2,2,32,256]{3,2,1,0:T(8,128)(2,1)S(1)}, u32[]{:S(2)}, u32[]{:S(2)}) collective-permute-start(bf16[2,2,32,256]{3,2,1,0:T(8,128)(2,1)S(1)} %get-tuple-element.29), channel_id=1, source_target_pairs={{0,12},{12,0},{4,8},{8,4},{16,28},{28,16},{20,24},{24,20},{1,13},{... | collective-permute-start | bytes 196616 | tf_op jit(solution)/shard_map/ppermute | solution.py:27
  14.3 4.4 %collective-permute-start.5 = (bf16[2,2,32,256]{3,2,1,0:T(8,128)(2,1)S(1)}, bf16[2,2,32,256]{3,2,1,0:T(8,128)(2,1)S(1)}, u32[]{:S(2)}, u32[]{:S(2)}) collective-permute-start(bf16[2,2,32,256]{3,2,1,0:T(8,128)(2,1)S(1)} %get-tuple-element.30), channel_id=1, source_target_pairs={{0,16},{16,0},{4,20},{20,4},{8,24},{24,8},{12,28},{28,12},{1,17},{... | collective-permute-start | bytes 196616 | tf_op jit(solution)/shard_map/ppermute | solution.py:27
  15.8 4.2 %collective-permute-start.6 = (bf16[2,2,32,256]{3,2,1,0:T(8,128)(2,1)S(1)}, bf16[2,2,32,256]{3,2,1,0:T(8,128)(2,1)S(1)}, u32[]{:S(2)}, u32[]{:S(2)}) collective-permute-start(bf16[2,2,32,256]{3,2,1,0:T(8,128)(2,1)S(1)} %get-tuple-element.31), channel_id=1, source_target_pairs={{0,20},{20,0},{4,16},{16,4},{8,28},{28,8},{12,24},{24,12},{1,21},{... | collective-permute-start | bytes 196616 | tf_op jit(solution)/shard_map/ppermute | solution.py:27
  16.0 5.4 %collective-permute-start.7 = (bf16[2,2,32,256]{3,2,1,0:T(8,128)(2,1)S(1)}, bf16[2,2,32,256]{3,2,1,0:T(8,128)(2,1)S(1)}, u32[]{:S(2)}, u32[]{:S(2)}) collective-permute-start(bf16[2,2,32,256]{3,2,1,0:T(8,128)(2,1)S(1)} %get-tuple-element.32), channel_id=1, source_target_pairs={{0,24},{24,0},{4,28},{28,4},{8,16},{16,8},{12,20},{20,12},{1,25},{... | collective-permute-start | bytes 196616 | tf_op jit(solution)/shard_map/ppermute | solution.py:27
  18.5 4.9 %collective-permute-start.8 = (bf16[2,2,32,256]{3,2,1,0:T(8,128)(2,1)S(1)}, bf16[2,2,32,256]{3,2,1,0:T(8,128)(2,1)S(1)}, u32[]{:S(2)}, u32[]{:S(2)}) collective-permute-start(bf16[2,2,32,256]{3,2,1,0:T(8,128)(2,1)S(1)} %get-tuple-element.33), channel_id=1, source_target_pairs={{0,28},{28,0},{4,24},{24,4},{8,20},{20,8},{12,16},{16,12},{1,29},{... | collective-permute-start | bytes 196616 | tf_op jit(solution)/shard_map/ppermute | solution.py:27

commit v4 on v3

--- a/solution.py
+++ b/solution.py
@@ -36,25 +36,6 @@
         lax.broadcasted_iota(jnp.int32, (rows, cols), 0),
         lax.broadcasted_iota(jnp.int32, (rows, cols), 1),
     )
-
-
-def edges_kernel(x_ref, near_ref, even_ref, odd_ref, sems):
-    dates, parts, _, columns = x_ref.shape
-    forward = lax.axis_index("range") % 2 == 0
-    images = [(slot, part) for slot in range(dates) for part in range(parts)]
-    copies = [
-        pltpu.make_async_copy(x_ref.at[image], near_ref.at[image], sems.at[number])
-        for number, image in enumerate(images)
-    ]
-    for copy in copies:
-        copy.start()
-    for number, (slot, part) in enumerate(images):
-        copies[number].wait()
-        spot = slice(number * MARGIN, (number + 1) * MARGIN)
-        last = near_ref[slot, part, :, columns - MARGIN :]
-        first = near_ref[slot, part, :, :MARGIN]
-        even_ref[:, spot] = jnp.where(forward, last, first)
-        odd_ref[:, spot] = jnp.where(forward, first, last)
 
 
 def weight_rows(fractions):
@@ -94,33 +75,90 @@
     )
 
 
-def taps_kernel(
+def start_kernel(
     tile_lines,
+    x_ref,
+    az_whole_ref,
+    az_part_ref,
+    rg_whole_ref,
+    rg_part_ref,
+    sweeps_ref,
+    gap_ref,
+    near_ref,
+    even_ref,
+    odd_ref,
+    line_ref,
+    weights_ref,
+    shift_ref,
+    partner_ref,
     az_whole,
     az_part,
     rg_whole,
     rg_part,
     sweeps,
-    gap_ref,
-    master_ref,
-    own_ref,
-    low_ref,
-    high_ref,
-    line_ref,
-    partner_ref,
+    gap,
+    sems,
 ):
+    dates, parts, lines, columns = x_ref.shape
+    total = partner_ref.shape[1]
+    images = [(slot, part) for slot in range(dates) for part in range(parts)]
+    small = [
+        (az_whole_ref, az_whole),
+        (az_part_ref, az_part),
+        (rg_whole_ref, rg_whole),
+        (rg_part_ref, rg_part),
+        (sweeps_ref, sweeps),
+        (gap_ref, gap),
+    ]
+    copies = [
+        pltpu.make_async_copy(source, target, sems.at[number])
+        for number, (source, target) in enumerate(
+            small + [(x_ref.at[image], near_ref.at[image]) for image in images]
+        )
+    ]
+    for copy in copies:
+        copy.start()
+    for copy in copies[: len(small)]:
+        copy.wait()
+
+    present = [lax.axis_index("date") * dates + slot for slot in range(dates)]
+    centre = TAPS // 2 - 1
+    weights = weight_rows([rg_part[d] for d in present] + [az_part[d] for d in present])
+    weights_ref[...] = weights
+    for slot, date in enumerate(present):
+        shift_ref[slot] = centre - rg_whole[date]
+        row, col = iotas(lines, lines)
+        row = tile_order(row // tile_lines) * tile_lines + row % tile_lines
+        band = banded(col - row + (centre - az_whole[date]), weights[dates + slot : dates + slot + 1])
+        usable = row < sweeps[date] * (lines // MAX_SWEEPS)
+        line_ref[slot] = jnp.where(usable, band, 0.0).astype(jnp.bfloat16)
+
+    def find(date, carry):
+        for kind, partner in enumerate(partners(date, gap, total)):
+            partner_ref[kind, date] = partner
+        return carry
+
+    lax.fori_loop(0, total, find, 0)
+
+    forward = lax.axis_index("range") % 2 == 0
+    for number, (slot, part) in enumerate(images):
+        copies[len(small) + number].wait()
+        spot = slice(number * MARGIN, (number + 1) * MARGIN)
+        last = near_ref[slot, part, :, columns - MARGIN :]
+        first = near_ref[slot, part, :, :MARGIN]
+        even_ref[:, spot] = jnp.where(forward, last, first)
+        odd_ref[:, spot] = jnp.where(forward, first, last)
+
+
+def taps_kernel(shift_ref, master_ref, weights_ref, own_ref, low_ref, high_ref, root_ref):
+    for number in range(root_ref.shape[0]):
+        root_ref[number] = master_ref[0]
     dates, columns, _ = own_ref.shape
-    total = partner_ref.shape[1]
-    lines = line_ref.shape[1]
     edge_rows = low_ref.shape[0]
     parts = edge_rows // MARGIN // dates
-    first = lax.axis_index("date") * dates
-    centre = TAPS // 2 - 1
-    present = [first + slot for slot in range(dates)]
-    table = weight_rows([rg_part[d] for d in present] + [az_part[d] for d in present])
-    for slot, date in enumerate(present):
-        shift = centre - rg_whole[date]
-        weights = table[slot : slot + 1]
+    for slot in range(dates):
+        shift = shift_ref[slot]
+        weights = weights_ref[slot : slot + 1, :]
         row, col = iotas(columns, columns)
         own_ref[slot] = banded(row - col + shift, weights).astype(jnp.bfloat16)
         row, col = iotas(edge_rows, LANES)
@@ -132,19 +170,6 @@
             spot = slice(image * LANES, (image + 1) * LANES)
             low_ref[:, spot] = jnp.where(held, low, 0.0).astype(jnp.bfloat16)
             high_ref[:, spot] = jnp.where(held, high, 0.0).astype(jnp.bfloat16)
-        row, col = iotas(lines, lines)
-        row = tile_order(row // tile_lines) * tile_lines + row % tile_lines
-        weights = table[dates + slot : dates + slot + 1]
-        band = banded(col - row + (centre - az_whole[date]), weights)
-        usable = row < sweeps[date] * (lines // MAX_SWEEPS)
-        line_ref[slot] = jnp.where(usable, band, 0.0).astype(jnp.bfloat16)
-
-    def find(date, carry):
-        for kind, partner in enumerate(partners(date, gap_ref, master_ref, total)):
-            partner_ref[kind, date] = partner
-        return carry
-
-    lax.fori_loop(0, total, find, 0)
 
 
 def resample_kernel(split, x_ref, even_ref, odd_ref, own_ref, low_ref, high_ref, line_ref, *outs):
@@ -181,12 +206,12 @@
                         outs[i][slot, part] = tile
 
 
-def partners(date, gap_ref, master_ref, total):
+def partners(date, gap_ref, total):
     ahead = date + gap_ref[0, date]
     later = jnp.where(ahead < total, ahead, date - gap_ref[0, date])
     back = date - gap_ref[1, date]
     earlier = jnp.where(back >= 0, back, date + gap_ref[1, date])
-    return (master_ref[0], later, earlier)
+    return (later, earlier)
 
 
 def row_sums(values):
@@ -206,7 +231,7 @@
     return values[0]
 
 
-def looks_kernel(partner_ref, *refs):
+def looks_kernel(root_ref, partner_ref, *refs):
     tiles, (out_ref, stack, sums, pooled, powers) = refs[:-5], refs[-5:]
     total, _, tile_lines, tile_columns = stack.shape
     owners, per_owner, lanes = out_ref.shape
@@ -224,11 +249,14 @@
 
         lax.fori_loop(0, owners, widen, 0)
 
+    def partner_of(kind, date):
+        return partner_ref[kind - 1, date] if kind else root_ref[0]
+
     def collect(date, carry):
         left0, left1 = stack[date, 0], stack[date, 1]
         values = []
         for kind in range(KINDS):
-            partner = partner_ref[kind, date]
+            partner = partner_of(kind, date)
             right0, right1 = stack[partner, 0], stack[partner, 1]
             values += [left0 * right0 + left1 * right1, left1 * right0 - left0 * right1]
         values.append(left0 * left0 + left1 * left1)
@@ -255,7 +283,7 @@
 
     def gather(date, carry):
         for kind in range(KINDS):
-            power = partner_ref[kind, date] * QUANTITIES + 2 * KINDS
+            power = partner_of(kind, date) * QUANTITIES + 2 * KINDS
             powers[kind, pl.ds(date, 1), :] = pooled[pl.ds(power, 1), :]
         return carry
 
@@ -315,46 +343,51 @@
     line_looks, column_looks = tile_lines // LOOK_AZ, tile_columns // LOOK_RG
     lanes = line_looks * column_looks
 
-    block, even, odd = pl.pallas_call(
-        edges_kernel,
-        out_shape=(
-            pltpu.VMEM(block.shape, block.dtype),
-            pltpu.VMEM((lines, images * MARGIN), jnp.bfloat16),
-            pltpu.VMEM((lines, images * MARGIN), jnp.bfloat16),
-        ),
-        in_specs=[pl.BlockSpec(memory_space=pltpu.HBM)],
-        out_specs=(VMEM,) * 3,
-        scratch_shapes=[pltpu.SemaphoreType.DMA((images,))],
-        name="edges",
-        compiler_params=pltpu.CompilerParams(vmem_limit_bytes=GRANT),
-    )(block)
-    width = lax.axis_size("range")
-    odd = exchanged(odd, "range", [(j, j + 1) for j in range(1, width - 1, 2)])
-    even = exchanged(even, "range", [(j, j + 1) for j in range(0, width - 1, 2)])
-
-    *taps, table = pl.pallas_call(
-        functools.partial(taps_kernel, tile_lines),
-        out_shape=(
-            pltpu.VMEM((dates, columns, columns), jnp.bfloat16),
-            pltpu.VMEM((images * MARGIN, images * LANES), jnp.bfloat16),
-            pltpu.VMEM((images * MARGIN, images * LANES), jnp.bfloat16),
-            pltpu.VMEM((dates, lines, lines), jnp.bfloat16),
-            pltpu.SMEM((KINDS, total), jnp.int32),
-        ),
-        in_specs=[SMEM] * 7,
-        out_specs=(VMEM,) * 4 + (SMEM,),
-        cost_estimate=pl.CostEstimate(flops=4000000, bytes_accessed=800000, transcendentals=0),
-        name="taps",
-        compiler_params=pltpu.CompilerParams(vmem_limit_bytes=GRANT),
-    )(
+    arguments = (
+        block,
         along_track_whole_displacement,
         along_track_subpixel_weights,
         slant_whole_displacement,
         slant_subpixel_weights,
         sweeps_each_epoch,
         baseline_companion_gap.T,
-        master_epoch_image,
-    )
+    )
+    block, even, odd, line_taps, weights, shift, table = pl.pallas_call(
+        functools.partial(start_kernel, tile_lines),
+        out_shape=(
+            pltpu.VMEM(block.shape, block.dtype),
+            pltpu.VMEM((lines, images * MARGIN), jnp.bfloat16),
+            pltpu.VMEM((lines, images * MARGIN), jnp.bfloat16),
+            pltpu.VMEM((dates, lines, lines), jnp.bfloat16),
+            pltpu.VMEM((8, LANES), jnp.float32),
+            pltpu.SMEM((dates,), jnp.int32),
+            pltpu.SMEM((KINDS - 1, total), jnp.int32),
+        ),
+        in_specs=[pl.BlockSpec(memory_space=pltpu.HBM)] * len(arguments),
+        out_specs=(VMEM,) * 5 + (SMEM,) * 2,
+        scratch_shapes=[pltpu.SMEM(array.shape, array.dtype) for array in arguments[1:]]
+        + [pltpu.SemaphoreType.DMA((len(arguments) - 1 + images,))],
+        name="start",
+        compiler_params=pltpu.CompilerParams(vmem_limit_bytes=GRANT),
+    )(*[pltpu.with_memory_space_constraint(array, pltpu.HBM) for array in arguments])
+    width = lax.axis_size("range")
+    odd = exchanged(odd, "range", [(j, j + 1) for j in range(1, width - 1, 2)])
+    even = exchanged(even, "range", [(j, j + 1) for j in range(0, width - 1, 2)])
+
+    own_taps, low_taps, high_taps, root = pl.pallas_call(
+        taps_kernel,
+        out_shape=(
+            pltpu.VMEM((dates, columns, columns), jnp.bfloat16),
+            pltpu.VMEM((images * MARGIN, images * LANES), jnp.bfloat16),
+            pltpu.VMEM((images * MARGIN, images * LANES), jnp.bfloat16),
+            pltpu.SMEM((8,), jnp.int32),
+        ),
+        in_specs=[SMEM, SMEM, VMEM],
+        out_specs=(VMEM,) * 3 + (SMEM,),
+        cost_estimate=pl.CostEstimate(flops=4000000, bytes_accessed=800000, transcendentals=0),
+        name="taps",
+        compiler_params=pltpu.CompilerParams(vmem_limit_bytes=GRANT),
+    )(pltpu.with_memory_space_constraint(shift, pltpu.SMEM), master_epoch_image, near(weights))
     tile = (dates, parts, tile_lines, tile_columns)
     if by_pairs(owners):
         out_shape = (pltpu.VMEM(tile, jnp.bfloat16),) * owners
@@ -369,7 +402,7 @@
         out_specs=(VMEM,) * len(out_shape),
         name="resample",
         compiler_params=pltpu.CompilerParams(vmem_limit_bytes=GRANT),
-    )(near(block), near(even), near(odd), *[near(tap) for tap in taps])
+    )(*[near(array) for array in (block, even, odd, own_taps, low_taps, high_taps, line_taps)])
 
     if by_pairs(owners):
         tiles = [tiles[0]] + [
@@ -381,7 +414,7 @@
     results = pl.pallas_call(
         looks_kernel,
         out_shape=pltpu.VMEM((owners, dates * CHANNELS, lanes), jnp.float32),
-        in_specs=[SMEM] + [VMEM] * len(tiles),
+        in_specs=[SMEM] * 2 + [VMEM] * len(tiles),
         out_specs=VMEM,
         scratch_shapes=[
             pltpu.VMEM((total, parts, tile_lines, tile_columns), jnp.float32),
@@ -392,6 +425,7 @@
         name="looks",
         compiler_params=pltpu.CompilerParams(vmem_limit_bytes=GRANT),
     )(
+        pltpu.with_memory_space_constraint(root, pltpu.SMEM),
         pltpu.with_memory_space_constraint(table, pltpu.SMEM),
         *[near(tile) for tile in tiles],
     )

time: 33.5 us -> 32.8 us (0.979); the launches traced: 33.3 us -> 32.2 us
  local copies, waits for them, and re-layouts: 1.69 us -> 0 us
  waiting for transfers between devices: 4.71 us -> 5.8 us
  Pallas kernels: 5.99 us -> 5.61 us
    unnamed x14 -> x0, local copies, waits for them, and re-layouts: 1.69 us -> none
    ppermute x9, waiting for transfers between devices: 4.71 us -> 5.8 us  [exchanged(): lax.ppermute(array, axis, [route for a, b in pairs for route in ((a, b),...]
    pallas_call x2, Pallas kernels: 3.43 us -> 3.06 us  [the longest x1 2.58 us: body(): pl.pallas_call(functools.partial(start_kernel, tile_lines), out_shape=(pl...]
  transfers between devices with their start and end apart: 9 -> 9, of which waited for: 3 -> 4; matrix products, arithmetic and copies ran while one was open for 0% -> 0% of each run, Pallas kernels for 5% -> 1%
where the time goes in v4:
time: 32.8 us; the launch traced here: 32.2 us
  starting transfers between devices  11.4 us (35%)
  blocking collectives  8.04 us (25%)
  waiting for transfers between devices  5.8 us (18%)
  Pallas kernels  5.61 us (17%)
  between operations  1.33 us (4%)
    ppermute x9, starting transfers between devices, exchanged(): lax.ppermute(array, axis, [route for a, b in pairs for route in ((a, b),...  11.4 us
    all_to_all x1, blocking collectives, body(): results = lax.all_to_all(results, 'date', 0, 0)  8.04 us
    ppermute x9, waiting for transfers between devices, exchanged(): lax.ppermute(array, axis, [route for a, b in pairs for route in ((a, b),...  5.8 us
    pallas_call x1, Pallas kernels, body(): pl.pallas_call(functools.partial(start_kernel, tile_lines), out_shape=(pl...  2.58 us
    pallas_call x1, Pallas kernels, body(): pl.pallas_call(looks_kernel, out_shape=pltpu.VMEM((owners, dates * CHANNE...  1.07 us
    pallas_call x1, Pallas kernels, body(): pl.pallas_call(place_kernel, out_shape=(jax.ShapeDtypeStruct((dates, 2 *...  0.76 us
    pallas_call x1, Pallas kernels, body(): pl.pallas_call(functools.partial(resample_kernel, (line_groups, column_gr...  0.72 us
  transfers between devices with their start and end apart: 9, of which 4 were waited for; matrix products, arithmetic and copies ran while one was open for 0% of the time, Pallas kernels for 1%

profile of v4, /device:TPU:8, one launch (start us, length us, event | category | flops | bytes accessed | tf_op | source)
XLA Modules:
  0.0 32.2 jit_solution(14363908986692329728)
XLA Ops:
  0.6 2.6 %start.1 = (bf16[2,2,256,256]{3,2,1,0:T(8,128)(2,1)S(1)}, bf16[256,64]{1,0:T(8,128)(2,1)S(1)}, bf16[256,64]{1,0:T(8,128)(2,1)S(1)}, bf16[2,256,256]{2,1,0:T(8,12...) custom-call(bf16[2,2,256,256]{3,2,1,0:T(8,128)(2,1)} %x_ref.1, s32[16]{0:T(128)} %az_whole_ref.1, ...), custom_call_target="tpu_custom_call" | custom-call | tf_op jit(solution)/shard_map/start/pallas_call | solution.py:355
  3.2 0.1 collective-permute-start
  3.3 5.0 %collective-permute-start.1 = (bf16[256,64]{1,0:T(8,128)(2,1)S(1)}, bf16[256,64]{1,0:T(8,128)(2,1)S(1)}, u32[]{:S(2)}, u32[]{:S(2)}) collective-permute-start(bf16[256,64]{1,0:T(8,128)(2,1)S(1)} %get-tuple-element.27), channel_id=1, source_target_pairs={{1,2},{2,1},{5,6},{6,5},{9,10},{10,9},{13,14},{14,13},{17,18},{18,... | collective-permute-start | bytes 98312 | tf_op jit(solution)/shard_map/ppermute | solution.py:27
  9.0 0.5 %taps.1 = (bf16[2,256,256]{2,1,0:T(8,128)(2,1)S(1)}, bf16[64,512]{1,0:T(8,128)(2,1)S(1)}, bf16[64,512]{1,0:T(8,128)(2,1)S(1)}, s32[8]{0:T(128)S(4)}) custom-call(s32[2]{0:T(128)S(4)} %get-tuple-element.21.shift_ref, s32[1]{0:T(128)S(6)} %copy.10.master_ref, f32[8,128]{1,0:T(8,128)S(1)} %get-tuple-element.22.weights_ref), custom_call_target="tpu_custom_call" | custom-call | flops 4000000 | bytes 800000 | tf_op jit(solution)/shard_map/taps/pallas_call | solution.py:377
  9.5 0.0 collective-permute-done.even_ref
  9.5 1.1 %collective-permute-done.1.odd_ref = bf16[256,64]{1,0:T(8,128)(2,1)S(1)} collective-permute-done((bf16[256,64]{1,0:T(8,128)(2,1)S(1)}, bf16[256,64]{1,0:T(8,128)(2,1)S(1)}, u32[]{:S(2)}, u32[]{:S(2)}) %collective-permute-start.1) | collective-permute-done | bytes 32800 | tf_op jit(solution)/shard_map/ppermute | solution.py:27
  10.6 0.7 %resample.1 = (bf16[2,2,32,256]{3,2,1,0:T(8,128)(2,1)S(1)}, bf16[2,2,32,256]{3,2,1,0:T(8,128)(2,1)S(1)}, bf16[2,2,32,256]{3,2,1,0:T(8,128)(2,1)S(1)}, bf16[2,2,3...) custom-call(bf16[2,2,256,256]{3,2,1,0:T(8,128)(2,1)S(1)} %get-tuple-, ...), custom_call_target="tpu_custom_call" | custom-call | tf_op jit(solution)/shard_map/resample/pallas_call | solution.py:396
  11.3 0.1 collective-permute-start.2
  11.4 1.6 %collective-permute-start.3 = (bf16[2,2,32,256]{3,2,1,0:T(8,128)(2,1)S(1)}, bf16[2,2,32,256]{3,2,1,0:T(8,128)(2,1)S(1)}, u32[]{:S(2)}, u32[]{:S(2)}) collective-permute-start(bf16[2,2,32,256]{3,2,1,0:T(8,128)(2,1)S(1)} %get-tuple-element.34), channel_id=1, source_target_pairs={{0,8},{8,0},{4,12},{12,4},{16,24},{24,16},{20,28},{28,20},{1,9},{9... | collective-permute-start | bytes 196616 | tf_op jit(solution)/shard_map/ppermute | solution.py:27
  12.9 0.3 collective-permute-start.4
  13.2 1.5 %collective-permute-start.5 = (bf16[2,2,32,256]{3,2,1,0:T(8,128)(2,1)S(1)}, bf16[2,2,32,256]{3,2,1,0:T(8,128)(2,1)S(1)}, u32[]{:S(2)}, u32[]{:S(2)}) collective-permute-start(bf16[2,2,32,256]{3,2,1,0:T(8,128)(2,1)S(1)} %get-tuple-element.36), channel_id=1, source_target_pairs={{0,16},{16,0},{4,20},{20,4},{8,24},{24,8},{12,28},{28,12},{1,17},{... | collective-permute-start | bytes 196616 | tf_op jit(solution)/shard_map/ppermute | solution.py:27
  14.8 0.2 collective-permute-start.6
  14.9 0.0 collective-permute-done.2.refs_1_
  14.9 2.4 %collective-permute-start.7 = (bf16[2,2,32,256]{3,2,1,0:T(8,128)(2,1)S(1)}, bf16[2,2,32,256]{3,2,1,0:T(8,128)(2,1)S(1)}, u32[]{:S(2)}, u32[]{:S(2)}) collective-permute-start(bf16[2,2,32,256]{3,2,1,0:T(8,128)(2,1)S(1)} %get-tuple-element.38), channel_id=1, source_target_pairs={{0,24},{24,0},{4,28},{28,4},{8,16},{16,8},{12,20},{20,12},{1,25},{... | collective-permute-start | bytes 196616 | tf_op jit(solution)/shard_map/ppermute | solution.py:27
  17.4 0.0 collective-permute-done.3.refs_2_
  17.4 0.3 collective-permute-start.8
  17.6 0.0 collective-permute-done.4.refs_3_
  17.6 0.0 collective-permute-done.5.refs_4_
  17.7 1.3 %collective-permute-done.6.refs_5_ = bf16[2,2,32,256]{3,2,1,0:T(8,128)(2,1)S(1)} collective-permute-done((bf16[2,2,32,256]{3,2,1,0:T(8,128)(2,1)S(1)}, bf16[2,2,32,256]{3,2,1,0:T(8,128)(2,1)S(1)}, u32[]{:S(2)}, u32[]{:S(2)}) %collective-permute-start.6) | collective-permute-done | bytes 65568 | tf_op jit(solution)/shard_map/ppermute | solution.py:27
  18.9 1.5 %collective-permute-done.7.refs_6_ = bf16[2,2,32,256]{3,2,1,0:T(8,128)(2,1)S(1)} collective-permute-done((bf16[2,2,32,256]{3,2,1,0:T(8,128)(2,1)S(1)}, bf16[2,2,32,256]{3,2,1,0:T(8,128)(2,1)S(1)}, u32[]{:S(2)}, u32[]{:S(2)}) %collective-permute-start.7) | collective-permute-done | bytes 65568 | tf_op jit(solution)/shard_map/ppermute | solution.py:27
  20.4 1.9 %collective-permute-done.8.refs_7_ = bf16[2,2,32,256]{3,2,1,0:T(8,128)(2,1)S(1)} collective-permute-done((bf16[2,2,32,256]{3,2,1,0:T(8,128)(2,1)S(1)}, bf16[2,2,32,256]{3,2,1,0:T(8,128)(2,1)S(1)}, u32[]{:S(2)}, u32[]{:S(2)}) %collective-permute-start.8) | collective-permute-done | bytes 65568 | tf_op jit(solution)/shard_map/ppermute | solution.py:27
  22.3 1.1 %looks.1 = f32[8,18,128]{2,1,0:T(8,128)S(1)} custom-call(s32[8]{0:T(128)S(4)} %get-tuple-element.23.root_ref, s32[2,16]{1,0:T(2,128)S(4)} %get-tuple-element.24.partner_ref, bf16[2,2,32,256]{3,2,1,0:T(8,128)(2,1)S(1)} %get-tuple-element.32.refs_0_, bf16[2,2,32,256]{3,2,1,0:T(8,128)(2,1)S(1)} %collective-permute-done.2.refs_1_, ...), custom_call_target="tpu_custom_call" | custom-call | tf_op jit(solution)/shard_map/looks/pallas_call | solution.py:414
  23.4 8.0 %all_to_all.5.x_ref = f32[8,18,128]{2,1,0:T(8,128)S(1)} all-to-all(f32[8,18,128]{2,1,0:T(8,128)S(1)} %looks.1), channel_id=1, replica_groups=mesh['date'=8,'range'=4] {'date'}, dimensions={0} | all-to-all | bytes 147456 | tf_op jit(solution)/shard_map/all_to_all | solution.py:432
  31.4 0.8 %place.1 = (f32[2,6,16,64]{3,2,1,0:T(8,128)}, f32[2,3,16,64]{3,2,1,0:T(8,128)}) custom-call(f32[8,18,128]{2,1,0:T(8,128)S(1)} %all_to_all.5.x_ref), custom_call_target="tpu_custom_call" | custom-call | tf_op jit(solution)/shard_map/place/pallas_call | solution.py:436
Async XLA Ops:
  3.2 6.3 %collective-permute-start = (bf16[256,64]{1,0:T(8,128)(2,1)S(1)}, bf16[256,64]{1,0:T(8,128)(2,1)S(1)}, u32[]{:S(2)}, u32[]{:S(2)}) collective-permute-start(bf16[256,64]{1,0:T(8,128)(2,1)S(1)} %get-tuple-element.26), channel_id=1, source_target_pairs={{0,1},{1,0},{2,3},{3,2},{4,5},{5,4},{6,7},{7,6},{8,9},{9,8},{10,11... | collective-permute-start | bytes 98312 | tf_op jit(solution)/shard_map/ppermute | solution.py:27
  3.3 7.3 %collective-permute-start.1 = (bf16[256,64]{1,0:T(8,128)(2,1)S(1)}, bf16[256,64]{1,0:T(8,128)(2,1)S(1)}, u32[]{:S(2)}, u32[]{:S(2)}) collective-permute-start(bf16[256,64]{1,0:T(8,128)(2,1)S(1)} %get-tuple-element.27), channel_id=1, source_target_pairs={{1,2},{2,1},{5,6},{6,5},{9,10},{10,9},{13,14},{14,13},{17,18},{18,... | collective-permute-start | bytes 98312 | tf_op jit(solution)/shard_map/ppermute | solution.py:27
  11.3 3.6 %collective-permute-start.2 = (bf16[2,2,32,256]{3,2,1,0:T(8,128)(2,1)S(1)}, bf16[2,2,32,256]{3,2,1,0:T(8,128)(2,1)S(1)}, u32[]{:S(2)}, u32[]{:S(2)}) collective-permute-start(bf16[2,2,32,256]{3,2,1,0:T(8,128)(2,1)S(1)} %get-tuple-element.33), channel_id=1, source_target_pairs={{0,4},{4,0},{8,12},{12,8},{16,20},{20,16},{24,28},{28,24},{1,5},{5... | collective-permute-start | bytes 196616 | tf_op jit(solution)/shard_map/ppermute | solution.py:27
  11.4 6.0 %collective-permute-start.3 = (bf16[2,2,32,256]{3,2,1,0:T(8,128)(2,1)S(1)}, bf16[2,2,32,256]{3,2,1,0:T(8,128)(2,1)S(1)}, u32[]{:S(2)}, u32[]{:S(2)}) collective-permute-start(bf16[2,2,32,256]{3,2,1,0:T(8,128)(2,1)S(1)} %get-tuple-element.34), channel_id=1, source_target_pairs={{0,8},{8,0},{4,12},{12,4},{16,24},{24,16},{20,28},{28,20},{1,9},{9... | collective-permute-start | bytes 196616 | tf_op jit(solution)/shard_map/ppermute | solution.py:27
  12.9 4.7 %collective-permute-start.4 = (bf16[2,2,32,256]{3,2,1,0:T(8,128)(2,1)S(1)}, bf16[2,2,32,256]{3,2,1,0:T(8,128)(2,1)S(1)}, u32[]{:S(2)}, u32[]{:S(2)}) collective-permute-start(bf16[2,2,32,256]{3,2,1,0:T(8,128)(2,1)S(1)} %get-tuple-element.35), channel_id=1, source_target_pairs={{0,12},{12,0},{4,8},{8,4},{16,28},{28,16},{20,24},{24,20},{1,13},{... | collective-permute-start | bytes 196616 | tf_op jit(solution)/shard_map/ppermute | solution.py:27
  13.2 4.4 %collective-permute-start.5 = (bf16[2,2,32,256]{3,2,1,0:T(8,128)(2,1)S(1)}, bf16[2,2,32,256]{3,2,1,0:T(8,128)(2,1)S(1)}, u32[]{:S(2)}, u32[]{:S(2)}) collective-permute-start(bf16[2,2,32,256]{3,2,1,0:T(8,128)(2,1)S(1)} %get-tuple-element.36), channel_id=1, source_target_pairs={{0,16},{16,0},{4,20},{20,4},{8,24},{24,8},{12,28},{28,12},{1,17},{... | collective-permute-start | bytes 196616 | tf_op jit(solution)/shard_map/ppermute | solution.py:27
  14.8 4.2 %collective-permute-start.6 = (bf16[2,2,32,256]{3,2,1,0:T(8,128)(2,1)S(1)}, bf16[2,2,32,256]{3,2,1,0:T(8,128)(2,1)S(1)}, u32[]{:S(2)}, u32[]{:S(2)}) collective-permute-start(bf16[2,2,32,256]{3,2,1,0:T(8,128)(2,1)S(1)} %get-tuple-element.37), channel_id=1, source_target_pairs={{0,20},{20,0},{4,16},{16,4},{8,28},{28,8},{12,24},{24,12},{1,21},{... | collective-permute-start | bytes 196616 | tf_op jit(solution)/shard_map/ppermute | solution.py:27
  14.9 5.4 %collective-permute-start.7 = (bf16[2,2,32,256]{3,2,1,0:T(8,128)(2,1)S(1)}, bf16[2,2,32,256]{3,2,1,0:T(8,128)(2,1)S(1)}, u32[]{:S(2)}, u32[]{:S(2)}) collective-permute-start(bf16[2,2,32,256]{3,2,1,0:T(8,128)(2,1)S(1)} %get-tuple-element.38), channel_id=1, source_target_pairs={{0,24},{24,0},{4,28},{28,4},{8,16},{16,8},{12,20},{20,12},{1,25},{... | collective-permute-start | bytes 196616 | tf_op jit(solution)/shard_map/ppermute | solution.py:27
  17.4 4.9 %collective-permute-start.8 = (bf16[2,2,32,256]{3,2,1,0:T(8,128)(2,1)S(1)}, bf16[2,2,32,256]{3,2,1,0:T(8,128)(2,1)S(1)}, u32[]{:S(2)}, u32[]{:S(2)}) collective-permute-start(bf16[2,2,32,256]{3,2,1,0:T(8,128)(2,1)S(1)} %get-tuple-element.39), channel_id=1, source_target_pairs={{0,28},{28,0},{4,24},{24,4},{8,20},{20,8},{12,16},{16,12},{1,29},{... | collective-permute-start | bytes 196616 | tf_op jit(solution)/shard_map/ppermute | solution.py:27

commit v5 on v3

--- a/solution.py
+++ b/solution.py
@@ -36,25 +36,6 @@
         lax.broadcasted_iota(jnp.int32, (rows, cols), 0),
         lax.broadcasted_iota(jnp.int32, (rows, cols), 1),
     )
-
-
-def edges_kernel(x_ref, near_ref, even_ref, odd_ref, sems):
-    dates, parts, _, columns = x_ref.shape
-    forward = lax.axis_index("range") % 2 == 0
-    images = [(slot, part) for slot in range(dates) for part in range(parts)]
-    copies = [
-        pltpu.make_async_copy(x_ref.at[image], near_ref.at[image], sems.at[number])
-        for number, image in enumerate(images)
-    ]
-    for copy in copies:
-        copy.start()
-    for number, (slot, part) in enumerate(images):
-        copies[number].wait()
-        spot = slice(number * MARGIN, (number + 1) * MARGIN)
-        last = near_ref[slot, part, :, columns - MARGIN :]
-        first = near_ref[slot, part, :, :MARGIN]
-        even_ref[:, spot] = jnp.where(forward, last, first)
-        odd_ref[:, spot] = jnp.where(forward, first, last)
 
 
 def weight_rows(fractions):
@@ -94,6 +75,32 @@
     )
 
 
+def start_kernel(x_ref, *refs):
+    dates, parts, _, columns = x_ref.shape
+    images = [(slot, part) for slot in range(dates) for part in range(parts)]
+    count = (len(refs) - 4) // 2
+    near_ref, even_ref, odd_ref = refs[count : count + 3]
+    sems = refs[-1]
+    small = list(zip(refs[:count], refs[count + 3 : -1]))
+    whole = [(x_ref.at[image], near_ref.at[image]) for image in images]
+    copies = [
+        pltpu.make_async_copy(source, target, sems.at[number])
+        for number, (source, target) in enumerate(whole + small)
+    ]
+    for copy in copies:
+        copy.start()
+    forward = lax.axis_index("range") % 2 == 0
+    for number, (slot, part) in enumerate(images):
+        copies[number].wait()
+        spot = slice(number * MARGIN, (number + 1) * MARGIN)
+        last = near_ref[slot, part, :, columns - MARGIN :]
+        first = near_ref[slot, part, :, :MARGIN]
+        even_ref[:, spot] = jnp.where(forward, last, first)
+        odd_ref[:, spot] = jnp.where(forward, first, last)
+    for copy in copies[len(images) :]:
+        copy.wait()
+
+
 def taps_kernel(
     tile_lines,
     az_whole,
@@ -101,22 +108,21 @@
     rg_whole,
     rg_part,
     sweeps,
-    gap_ref,
     master_ref,
     own_ref,
     low_ref,
     high_ref,
     line_ref,
-    partner_ref,
+    root_ref,
 ):
     dates, columns, _ = own_ref.shape
-    total = partner_ref.shape[1]
     lines = line_ref.shape[1]
     edge_rows = low_ref.shape[0]
     parts = edge_rows // MARGIN // dates
-    first = lax.axis_index("date") * dates
     centre = TAPS // 2 - 1
-    present = [first + slot for slot in range(dates)]
+    for number in range(root_ref.shape[0]):
+        root_ref[number] = master_ref[0]
+    present = [lax.axis_index("date") * dates + slot for slot in range(dates)]
     table = weight_rows([rg_part[d] for d in present] + [az_part[d] for d in present])
     for slot, date in enumerate(present):
         shift = centre - rg_whole[date]
@@ -139,13 +145,6 @@
         usable = row < sweeps[date] * (lines // MAX_SWEEPS)
         line_ref[slot] = jnp.where(usable, band, 0.0).astype(jnp.bfloat16)
 
-    def find(date, carry):
-        for kind, partner in enumerate(partners(date, gap_ref, master_ref, total)):
-            partner_ref[kind, date] = partner
-        return carry
-
-    lax.fori_loop(0, total, find, 0)
-
 
 def resample_kernel(split, x_ref, even_ref, odd_ref, own_ref, low_ref, high_ref, line_ref, *outs):
     dates, parts, _, columns = x_ref.shape
@@ -181,12 +180,12 @@
                         outs[i][slot, part] = tile
 
 
-def partners(date, gap_ref, master_ref, total):
+def partners(date, gap_ref, total):
     ahead = date + gap_ref[0, date]
     later = jnp.where(ahead < total, ahead, date - gap_ref[0, date])
     back = date - gap_ref[1, date]
     earlier = jnp.where(back >= 0, back, date + gap_ref[1, date])
-    return (master_ref[0], later, earlier)
+    return (later, earlier)
 
 
 def row_sums(values):
@@ -206,7 +205,7 @@
     return values[0]
 
 
-def looks_kernel(partner_ref, *refs):
+def looks_kernel(positions, root_ref, gap_ref, *refs):
     tiles, (out_ref, stack, sums, pooled, powers) = refs[:-5], refs[-5:]
     total, _, tile_lines, tile_columns = stack.shape
     owners, per_owner, lanes = out_ref.shape
@@ -214,7 +213,7 @@
     line_looks = tile_lines // LOOK_AZ
     unroll = total if total <= 16 else 1
     if len(tiles) > 1:
-        for position, tile_ref in enumerate(tiles):
+        for position, tile_ref in zip(positions, tiles):
             stack[pl.ds(tile_order(position) * dates, dates)] = tile_ref[...].astype(jnp.float32)
     else:
 
@@ -223,12 +222,15 @@
             return carry
 
         lax.fori_loop(0, owners, widen, 0)
+
+    def partner_of(kind, date):
+        return partners(date, gap_ref, total)[kind - 1] if kind else root_ref[0]
 
     def collect(date, carry):
         left0, left1 = stack[date, 0], stack[date, 1]
         values = []
         for kind in range(KINDS):
-            partner = partner_ref[kind, date]
+            partner = partner_of(kind, date)
             right0, right1 = stack[partner, 0], stack[partner, 1]
             values += [left0 * right0 + left1 * right1, left1 * right0 - left0 * right1]
         values.append(left0 * left0 + left1 * left1)
@@ -255,7 +257,7 @@
 
     def gather(date, carry):
         for kind in range(KINDS):
-            power = partner_ref[kind, date] * QUANTITIES + 2 * KINDS
+            power = partner_of(kind, date) * QUANTITIES + 2 * KINDS
             powers[kind, pl.ds(date, 1), :] = pooled[pl.ds(power, 1), :]
         return carry
 
@@ -315,46 +317,49 @@
     line_looks, column_looks = tile_lines // LOOK_AZ, tile_columns // LOOK_RG
     lanes = line_looks * column_looks
 
-    block, even, odd = pl.pallas_call(
-        edges_kernel,
+    arguments = (
+        block,
+        along_track_whole_displacement,
+        along_track_subpixel_weights,
+        slant_whole_displacement,
+        slant_subpixel_weights,
+        sweeps_each_epoch,
+        baseline_companion_gap.T,
+    )
+    block, even, odd, *small = pl.pallas_call(
+        start_kernel,
         out_shape=(
             pltpu.VMEM(block.shape, block.dtype),
             pltpu.VMEM((lines, images * MARGIN), jnp.bfloat16),
             pltpu.VMEM((lines, images * MARGIN), jnp.bfloat16),
+            *[pltpu.SMEM(array.shape, array.dtype) for array in arguments[1:]],
         ),
-        in_specs=[pl.BlockSpec(memory_space=pltpu.HBM)],
-        out_specs=(VMEM,) * 3,
-        scratch_shapes=[pltpu.SemaphoreType.DMA((images,))],
-        name="edges",
+        in_specs=[pl.BlockSpec(memory_space=pltpu.HBM)] * len(arguments),
+        out_specs=(VMEM,) * 3 + (SMEM,) * (len(arguments) - 1),
+        scratch_shapes=[pltpu.SemaphoreType.DMA((images + len(arguments) - 1,))],
+        name="start",
         compiler_params=pltpu.CompilerParams(vmem_limit_bytes=GRANT),
-    )(block)
+    )(*[pltpu.with_memory_space_constraint(array, pltpu.HBM) for array in arguments])
+    *small, gap = [pltpu.with_memory_space_constraint(array, pltpu.SMEM) for array in small]
     width = lax.axis_size("range")
     odd = exchanged(odd, "range", [(j, j + 1) for j in range(1, width - 1, 2)])
     even = exchanged(even, "range", [(j, j + 1) for j in range(0, width - 1, 2)])
 
-    *taps, table = pl.pallas_call(
+    own_taps, low_taps, high_taps, line_taps, root = pl.pallas_call(
         functools.partial(taps_kernel, tile_lines),
         out_shape=(
             pltpu.VMEM((dates, columns, columns), jnp.bfloat16),
             pltpu.VMEM((images * MARGIN, images * LANES), jnp.bfloat16),
             pltpu.VMEM((images * MARGIN, images * LANES), jnp.bfloat16),
             pltpu.VMEM((dates, lines, lines), jnp.bfloat16),
-            pltpu.SMEM((KINDS, total), jnp.int32),
+            pltpu.SMEM((8,), jnp.int32),
         ),
-        in_specs=[SMEM] * 7,
+        in_specs=[SMEM] * (len(small) + 1),
         out_specs=(VMEM,) * 4 + (SMEM,),
         cost_estimate=pl.CostEstimate(flops=4000000, bytes_accessed=800000, transcendentals=0),
         name="taps",
         compiler_params=pltpu.CompilerParams(vmem_limit_bytes=GRANT),
-    )(
-        along_track_whole_displacement,
-        along_track_subpixel_weights,
-        slant_whole_displacement,
-        slant_subpixel_weights,
-        sweeps_each_epoch,
-        baseline_companion_gap.T,
-        master_epoch_image,
-    )
+    )(*small, master_epoch_image)
     tile = (dates, parts, tile_lines, tile_columns)
     if by_pairs(owners):
         out_shape = (pltpu.VMEM(tile, jnp.bfloat16),) * owners
@@ -369,19 +374,23 @@
         out_specs=(VMEM,) * len(out_shape),
         name="resample",
         compiler_params=pltpu.CompilerParams(vmem_limit_bytes=GRANT),
-    )(near(block), near(even), near(odd), *[near(tap) for tap in taps])
+    )(*[near(array) for array in (block, even, odd, own_taps, low_taps, high_taps, line_taps)])
 
     if by_pairs(owners):
-        tiles = [tiles[0]] + [
-            exchanged(tiles[s], "date", [(i, i ^ s) for i in range(owners) if i < i ^ s])
-            for s in range(1, owners)
-        ]
+        order = [*range(owners - 2, 0, -2), *range(owners - 1, 0, -2)]
+        received = {
+            s: exchanged(tiles[s], "date", [(i, i ^ s) for i in range(owners) if i < i ^ s])
+            for s in order
+        }
+        positions = [0] + order
+        tiles = [tiles[0]] + [received[s] for s in order]
     else:
         tiles = [lax.all_to_all(tiles[0], "date", 0, 0)]
+        positions = None
     results = pl.pallas_call(
-        looks_kernel,
+        functools.partial(looks_kernel, positions),
         out_shape=pltpu.VMEM((owners, dates * CHANNELS, lanes), jnp.float32),
-        in_specs=[SMEM] + [VMEM] * len(tiles),
+        in_specs=[SMEM] * 2 + [VMEM] * len(tiles),
         out_specs=VMEM,
         scratch_shapes=[
             pltpu.VMEM((total, parts, tile_lines, tile_columns), jnp.float32),
@@ -392,7 +401,8 @@
         name="looks",
         compiler_params=pltpu.CompilerParams(vmem_limit_bytes=GRANT),
     )(
-        pltpu.with_memory_space_constraint(table, pltpu.SMEM),
+        pltpu.with_memory_space_constraint(root, pltpu.SMEM),
+        gap,
         *[near(tile) for tile in tiles],
     )
     results = lax.all_to_all(results, "date", 0, 0)

time: 33.5 us -> 31.7 us (0.946); the launches traced: 33.3 us -> 31 us
  local copies, waits for them, and re-layouts: 1.69 us -> 0 us
  Pallas kernels: 5.99 us -> 5.59 us
    unnamed x14 -> x0, local copies, waits for them, and re-layouts: 1.69 us -> none
    pallas_call x1, Pallas kernels: 1.77 us -> 1.01 us  [body(): pl.pallas_call(functools.partial(taps_kernel, tile_lines), out_shape=(plt...]
    pallas_call x2, Pallas kernels: 2.73 us -> 3.11 us  [the longest x1 2.04 us: body(): pl.pallas_call(start_kernel, out_shape=(pltpu.VMEM(block.shape, block.dty...]
  transfers between devices with their start and end apart: 9 -> 9, of which waited for: 3 -> 6; matrix products, arithmetic and copies ran while one was open for 0% -> 0% of each run, Pallas kernels for 5% -> 3%
where the time goes in v5:
time: 31.7 us; the launch traced here: 31 us
  starting transfers between devices  11.5 us (36%)
  blocking collectives  7.88 us (25%)
  Pallas kernels  5.59 us (18%)
  waiting for transfers between devices  4.72 us (15%)
  between operations  1.33 us (4%)
    ppermute x9, starting transfers between devices, exchanged(): lax.ppermute(array, axis, [route for a, b in pairs for route in ((a, b),...  11.5 us
    all_to_all x1, blocking collectives, body(): results = lax.all_to_all(results, 'date', 0, 0)  7.88 us
    ppermute x9, waiting for transfers between devices, exchanged(): lax.ppermute(array, axis, [route for a, b in pairs for route in ((a, b),...  4.72 us
    pallas_call x1, Pallas kernels, body(): pl.pallas_call(start_kernel, out_shape=(pltpu.VMEM(block.shape, block.dty...  2.04 us
    pallas_call x1, Pallas kernels, body(): pl.pallas_call(functools.partial(looks_kernel, positions), out_shape=pltp...  1.07 us
    pallas_call x1, Pallas kernels, body(): pl.pallas_call(functools.partial(taps_kernel, tile_lines), out_shape=(plt...  1.01 us
    pallas_call x1, Pallas kernels, body(): pl.pallas_call(place_kernel, out_shape=(jax.ShapeDtypeStruct((dates, 2 *...  0.76 us
    pallas_call x1, Pallas kernels, body(): pl.pallas_call(functools.partial(resample_kernel, (line_groups, column_gr...  0.72 us
  transfers between devices with their start and end apart: 9, of which 6 were waited for; matrix products, arithmetic and copies ran while one was open for 0% of the time, Pallas kernels for 3%

profile of v5, /device:TPU:8, one launch (start us, length us, event | category | flops | bytes accessed | tf_op | source)
XLA Modules:
  0.0 31.0 jit_solution(11972629305639857131)
XLA Ops:
  0.6 2.0 %start.1 = (bf16[2,2,256,256]{3,2,1,0:T(8,128)(2,1)S(1)}, bf16[256,64]{1,0:T(8,128)(2,1)S(1)}, bf16[256,64]{1,0:T(8,128)(2,1)S(1)}, s32[16]{0:T(128)S(4)}, s32[1...) custom-call(bf16[2,2,256,256]{3,2,1,0:T(8,128)(2,1)} %x_ref.1, ...), custom_call_target="tpu_custom_call" | custom-call | tf_op jit(solution)/shard_map/start/pallas_call | solution.py:329
  2.7 0.1 collective-permute-start
  2.8 5.0 %collective-permute-start.1 = (bf16[256,64]{1,0:T(8,128)(2,1)S(1)}, bf16[256,64]{1,0:T(8,128)(2,1)S(1)}, u32[]{:S(2)}, u32[]{:S(2)}) collective-permute-start(bf16[256,64]{1,0:T(8,128)(2,1)S(1)} %get-tuple-element.33), channel_id=1, source_target_pairs={{1,2},{2,1},{5,6},{6,5},{9,10},{10,9},{13,14},{14,13},{17,18},{18,... | collective-permute-start | bytes 98312 | tf_op jit(solution)/shard_map/ppermute | solution.py:27
  8.4 1.0 %taps.1 = (bf16[2,256,256]{2,1,0:T(8,128)(2,1)S(1)}, bf16[64,512]{1,0:T(8,128)(2,1)S(1)}, bf16[64,512]{1,0:T(8,128)(2,1)S(1)}, bf16[2,256,256]{2,1,0:T(8,128)(2,1)S(1)}, s32[8]{0:T(128)S(4)}) custom-call(s32[16]{0:T(128)S(4)} %get-tuple-element.24.az_whole, s32[16]{0:T(128)S(4)} %get-tuple-element.25.az_part, s32[16]{0:T(128)S(4)} %get-tuple-element.26.rg_whole, ...), custom_call_target="tpu_custom_call" | custom-call | flops 4000000 | bytes 800000 | tf_op jit(solution)/shard_map/taps/pallas_call | solution.py:348
  9.5 0.0 collective-permute-done.even_ref
  9.5 0.6 %collective-permute-done.1.odd_ref = bf16[256,64]{1,0:T(8,128)(2,1)S(1)} collective-permute-done((bf16[256,64]{1,0:T(8,128)(2,1)S(1)}, bf16[256,64]{1,0:T(8,128)(2,1)S(1)}, u32[]{:S(2)}, u32[]{:S(2)}) %collective-permute-start.1) | collective-permute-done | bytes 32800 | tf_op jit(solution)/shard_map/ppermute | solution.py:27
  10.0 0.7 %resample.1 = (bf16[2,2,32,256]{3,2,1,0:T(8,128)(2,1)S(1)}, bf16[2,2,32,256]{3,2,1,0:T(8,128)(2,1)S(1)}, bf16[2,2,32,256]{3,2,1,0:T(8,128)(2,1)S(1)}, bf16[2,2,3...) custom-call(bf16[2,2,256,256]{3,2,1,0:T(8,128)(2,1)S(1)} %get-tuple-, ...), custom_call_target="tpu_custom_call" | custom-call | tf_op jit(solution)/shard_map/resample/pallas_call | solution.py:368
  10.8 2.5 %collective-permute-start.2 = (bf16[2,2,32,256]{3,2,1,0:T(8,128)(2,1)S(1)}, bf16[2,2,32,256]{3,2,1,0:T(8,128)(2,1)S(1)}, u32[]{:S(2)}, u32[]{:S(2)}) collective-permute-start(bf16[2,2,32,256]{3,2,1,0:T(8,128)(2,1)S(1)} %get-tuple-element.39), channel_id=1, source_target_pairs={{0,24},{24,0},{4,28},{28,4},{8,16},{16,8},{12,20},{20,12},{1,25},{... | collective-permute-start | bytes 196616 | tf_op jit(solution)/shard_map/ppermute | solution.py:27
  13.3 0.5 %collective-permute-start.3 = (bf16[2,2,32,256]{3,2,1,0:T(8,128)(2,1)S(1)}, bf16[2,2,32,256]{3,2,1,0:T(8,128)(2,1)S(1)}, u32[]{:S(2)}, u32[]{:S(2)}) collective-permute-start(bf16[2,2,32,256]{3,2,1,0:T(8,128)(2,1)S(1)} %get-tuple-element.40), channel_id=1, source_target_pairs={{0,16},{16,0},{4,20},{20,4},{8,24},{24,8},{12,28},{28,12},{1,17},{... | collective-permute-start | bytes 196616 | tf_op jit(solution)/shard_map/ppermute | solution.py:27
  13.8 0.5 %collective-permute-start.4 = (bf16[2,2,32,256]{3,2,1,0:T(8,128)(2,1)S(1)}, bf16[2,2,32,256]{3,2,1,0:T(8,128)(2,1)S(1)}, u32[]{:S(2)}, u32[]{:S(2)}) collective-permute-start(bf16[2,2,32,256]{3,2,1,0:T(8,128)(2,1)S(1)} %get-tuple-element.41), channel_id=1, source_target_pairs={{0,8},{8,0},{4,12},{12,4},{16,24},{24,16},{20,28},{28,20},{1,9},{9... | collective-permute-start | bytes 196616 | tf_op jit(solution)/shard_map/ppermute | solution.py:27
  14.3 0.0 collective-permute-start.5
  14.3 2.7 %collective-permute-start.6 = (bf16[2,2,32,256]{3,2,1,0:T(8,128)(2,1)S(1)}, bf16[2,2,32,256]{3,2,1,0:T(8,128)(2,1)S(1)}, u32[]{:S(2)}, u32[]{:S(2)}) collective-permute-start(bf16[2,2,32,256]{3,2,1,0:T(8,128)(2,1)S(1)} %get-tuple-element.43), channel_id=1, source_target_pairs={{0,20},{20,0},{4,16},{16,4},{8,28},{28,8},{12,24},{24,12},{1,21},{... | collective-permute-start | bytes 196616 | tf_op jit(solution)/shard_map/ppermute | solution.py:27
  17.0 0.0 collective-permute-done.2.refs_1_
  17.0 0.1 collective-permute-start.7
  17.0 0.5 %collective-permute-done.3.refs_2_ = bf16[2,2,32,256]{3,2,1,0:T(8,128)(2,1)S(1)} collective-permute-done((bf16[2,2,32,256]{3,2,1,0:T(8,128)(2,1)S(1)}, bf16[2,2,32,256]{3,2,1,0:T(8,128)(2,1)S(1)}, u32[]{:S(2)}, u32[]{:S(2)}) %collective-permute-start.3) | collective-permute-done | bytes 65568 | tf_op jit(solution)/shard_map/ppermute | solution.py:27
  17.5 0.1 collective-permute-start.8
  17.6 0.4 %collective-permute-done.4.refs_3_ = bf16[2,2,32,256]{3,2,1,0:T(8,128)(2,1)S(1)} collective-permute-done((bf16[2,2,32,256]{3,2,1,0:T(8,128)(2,1)S(1)}, bf16[2,2,32,256]{3,2,1,0:T(8,128)(2,1)S(1)}, u32[]{:S(2)}, u32[]{:S(2)}) %collective-permute-start.4) | collective-permute-done | bytes 65568 | tf_op jit(solution)/shard_map/ppermute | solution.py:27
  18.0 1.5 %collective-permute-done.5.refs_4_ = bf16[2,2,32,256]{3,2,1,0:T(8,128)(2,1)S(1)} collective-permute-done((bf16[2,2,32,256]{3,2,1,0:T(8,128)(2,1)S(1)}, bf16[2,2,32,256]{3,2,1,0:T(8,128)(2,1)S(1)}, u32[]{:S(2)}, u32[]{:S(2)}) %collective-permute-start.5) | collective-permute-done | bytes 65568 | tf_op jit(solution)/shard_map/ppermute | solution.py:27
  19.5 0.3 %collective-permute-done.6.refs_5_ = bf16[2,2,32,256]{3,2,1,0:T(8,128)(2,1)S(1)} collective-permute-done((bf16[2,2,32,256]{3,2,1,0:T(8,128)(2,1)S(1)}, bf16[2,2,32,256]{3,2,1,0:T(8,128)(2,1)S(1)}, u32[]{:S(2)}, u32[]{:S(2)}) %collective-permute-start.6) | collective-permute-done | bytes 65568 | tf_op jit(solution)/shard_map/ppermute | solution.py:27
  19.8 1.5 %collective-permute-done.7.refs_6_ = bf16[2,2,32,256]{3,2,1,0:T(8,128)(2,1)S(1)} collective-permute-done((bf16[2,2,32,256]{3,2,1,0:T(8,128)(2,1)S(1)}, bf16[2,2,32,256]{3,2,1,0:T(8,128)(2,1)S(1)}, u32[]{:S(2)}, u32[]{:S(2)}) %collective-permute-start.7) | collective-permute-done | bytes 65568 | tf_op jit(solution)/shard_map/ppermute | solution.py:27
  21.3 0.0 collective-permute-done.8.refs_7_
  21.3 1.1 %looks.1 = f32[8,18,128]{2,1,0:T(8,128)S(1)} custom-call(s32[8]{0:T(128)S(4)} %get-tuple-element.29.root_ref, s32[2,16]{1,0:T(2,128)S(4)} %get-tuple-element.30.gap_ref, bf16[2,2,32,256]{3,2,1,0:T(8,128)(2,1)S(1)} %get-tuple-element.38.refs_0_, bf16[2,2,32,256]{3,2,1,0:T(8,128)(2,1)S(1)} %collective-permute-done.2.refs_1_, ...), custom_call_target="tpu_custom_call" | custom-call | tf_op jit(solution)/shard_map/looks/pallas_call | solution.py:390
  22.4 7.9 %all_to_all.5.x_ref = f32[8,18,128]{2,1,0:T(8,128)S(1)} all-to-all(f32[8,18,128]{2,1,0:T(8,128)S(1)} %looks.1), channel_id=1, replica_groups=mesh['date'=8,'range'=4] {'date'}, dimensions={0} | all-to-all | bytes 147456 | tf_op jit(solution)/shard_map/all_to_all | solution.py:408
  30.3 0.8 %place.1 = (f32[2,6,16,64]{3,2,1,0:T(8,128)}, f32[2,3,16,64]{3,2,1,0:T(8,128)}) custom-call(f32[8,18,128]{2,1,0:T(8,128)S(1)} %all_to_all.5.x_ref), custom_call_target="tpu_custom_call" | custom-call | tf_op jit(solution)/shard_map/place/pallas_call | solution.py:412
Async XLA Ops:
  2.7 6.8 %collective-permute-start = (bf16[256,64]{1,0:T(8,128)(2,1)S(1)}, bf16[256,64]{1,0:T(8,128)(2,1)S(1)}, u32[]{:S(2)}, u32[]{:S(2)}) collective-permute-start(bf16[256,64]{1,0:T(8,128)(2,1)S(1)} %get-tuple-element.32), channel_id=1, source_target_pairs={{0,1},{1,0},{2,3},{3,2},{4,5},{5,4},{6,7},{7,6},{8,9},{9,8},{10,11... | collective-permute-start | bytes 98312 | tf_op jit(solution)/shard_map/ppermute | solution.py:27
  2.8 7.3 %collective-permute-start.1 = (bf16[256,64]{1,0:T(8,128)(2,1)S(1)}, bf16[256,64]{1,0:T(8,128)(2,1)S(1)}, u32[]{:S(2)}, u32[]{:S(2)}) collective-permute-start(bf16[256,64]{1,0:T(8,128)(2,1)S(1)} %get-tuple-element.33), channel_id=1, source_target_pairs={{1,2},{2,1},{5,6},{6,5},{9,10},{10,9},{13,14},{14,13},{17,18},{18,... | collective-permute-start | bytes 98312 | tf_op jit(solution)/shard_map/ppermute | solution.py:27
  10.8 6.2 %collective-permute-start.2 = (bf16[2,2,32,256]{3,2,1,0:T(8,128)(2,1)S(1)}, bf16[2,2,32,256]{3,2,1,0:T(8,128)(2,1)S(1)}, u32[]{:S(2)}, u32[]{:S(2)}) collective-permute-start(bf16[2,2,32,256]{3,2,1,0:T(8,128)(2,1)S(1)} %get-tuple-element.39), channel_id=1, source_target_pairs={{0,24},{24,0},{4,28},{28,4},{8,16},{16,8},{12,20},{20,12},{1,25},{... | collective-permute-start | bytes 196616 | tf_op jit(solution)/shard_map/ppermute | solution.py:27
  13.3 4.3 %collective-permute-start.3 = (bf16[2,2,32,256]{3,2,1,0:T(8,128)(2,1)S(1)}, bf16[2,2,32,256]{3,2,1,0:T(8,128)(2,1)S(1)}, u32[]{:S(2)}, u32[]{:S(2)}) collective-permute-start(bf16[2,2,32,256]{3,2,1,0:T(8,128)(2,1)S(1)} %get-tuple-element.40), channel_id=1, source_target_pairs={{0,16},{16,0},{4,20},{20,4},{8,24},{24,8},{12,28},{28,12},{1,17},{... | collective-permute-start | bytes 196616 | tf_op jit(solution)/shard_map/ppermute | solution.py:27
  13.8 4.3 %collective-permute-start.4 = (bf16[2,2,32,256]{3,2,1,0:T(8,128)(2,1)S(1)}, bf16[2,2,32,256]{3,2,1,0:T(8,128)(2,1)S(1)}, u32[]{:S(2)}, u32[]{:S(2)}) collective-permute-start(bf16[2,2,32,256]{3,2,1,0:T(8,128)(2,1)S(1)} %get-tuple-element.41), channel_id=1, source_target_pairs={{0,8},{8,0},{4,12},{12,4},{16,24},{24,16},{20,28},{28,20},{1,9},{9... | collective-permute-start | bytes 196616 | tf_op jit(solution)/shard_map/ppermute | solution.py:27
  14.3 5.2 %collective-permute-start.5 = (bf16[2,2,32,256]{3,2,1,0:T(8,128)(2,1)S(1)}, bf16[2,2,32,256]{3,2,1,0:T(8,128)(2,1)S(1)}, u32[]{:S(2)}, u32[]{:S(2)}) collective-permute-start(bf16[2,2,32,256]{3,2,1,0:T(8,128)(2,1)S(1)} %get-tuple-element.42), channel_id=1, source_target_pairs={{0,28},{28,0},{4,24},{24,4},{8,20},{20,8},{12,16},{16,12},{1,29},{... | collective-permute-start | bytes 196616 | tf_op jit(solution)/shard_map/ppermute | solution.py:27
  14.3 5.5 %collective-permute-start.6 = (bf16[2,2,32,256]{3,2,1,0:T(8,128)(2,1)S(1)}, bf16[2,2,32,256]{3,2,1,0:T(8,128)(2,1)S(1)}, u32[]{:S(2)}, u32[]{:S(2)}) collective-permute-start(bf16[2,2,32,256]{3,2,1,0:T(8,128)(2,1)S(1)} %get-tuple-element.43), channel_id=1, source_target_pairs={{0,20},{20,0},{4,16},{16,4},{8,28},{28,8},{12,24},{24,12},{1,21},{... | collective-permute-start | bytes 196616 | tf_op jit(solution)/shard_map/ppermute | solution.py:27
  17.0 4.3 %collective-permute-start.7 = (bf16[2,2,32,256]{3,2,1,0:T(8,128)(2,1)S(1)}, bf16[2,2,32,256]{3,2,1,0:T(8,128)(2,1)S(1)}, u32[]{:S(2)}, u32[]{:S(2)}) collective-permute-start(bf16[2,2,32,256]{3,2,1,0:T(8,128)(2,1)S(1)} %get-tuple-element.44), channel_id=1, source_target_pairs={{0,12},{12,0},{4,8},{8,4},{16,28},{28,16},{20,24},{24,20},{1,13},{... | collective-permute-start | bytes 196616 | tf_op jit(solution)/shard_map/ppermute | solution.py:27
  17.5 3.8 %collective-permute-start.8 = (bf16[2,2,32,256]{3,2,1,0:T(8,128)(2,1)S(1)}, bf16[2,2,32,256]{3,2,1,0:T(8,128)(2,1)S(1)}, u32[]{:S(2)}, u32[]{:S(2)}) collective-permute-start(bf16[2,2,32,256]{3,2,1,0:T(8,128)(2,1)S(1)} %get-tuple-element.45), channel_id=1, source_target_pairs={{0,4},{4,0},{8,12},{12,8},{16,20},{20,16},{24,28},{28,24},{1,5},{5... | collective-permute-start | bytes 196616 | tf_op jit(solution)/shard_map/ppermute | solution.py:27

commit v6 on v5

--- a/solution.py
+++ b/solution.py
@@ -93,10 +93,16 @@
     for number, (slot, part) in enumerate(images):
         copies[number].wait()
         spot = slice(number * MARGIN, (number + 1) * MARGIN)
-        last = near_ref[slot, part, :, columns - MARGIN :]
-        first = near_ref[slot, part, :, :MARGIN]
-        even_ref[:, spot] = jnp.where(forward, last, first)
-        odd_ref[:, spot] = jnp.where(forward, first, last)
+        for parity, last_ref, first_ref in (
+            (forward, even_ref, odd_ref),
+            (jnp.logical_not(forward), odd_ref, even_ref),
+        ):
+
+            @pl.when(parity)
+            def _():
+                last_ref[:, spot] = near_ref[slot, part, :, columns - MARGIN :]
+                first_ref[:, spot] = near_ref[slot, part, :, :MARGIN]
+
     for copy in copies[len(images) :]:
         copy.wait()
 
@@ -146,17 +152,15 @@
         line_ref[slot] = jnp.where(usable, band, 0.0).astype(jnp.bfloat16)
 
 
-def resample_kernel(split, x_ref, even_ref, odd_ref, own_ref, low_ref, high_ref, line_ref, *outs):
+def resample_kernel(split, x_ref, even_ref, odd_ref, own_ref, low_ref, high_ref, line_ref, *refs):
+    *outs, edges = refs
     dates, parts, _, columns = x_ref.shape
     line_groups, column_groups, tile_lines, tile_columns = split
-    forward = lax.axis_index("range") % 2 == 0
-    even, odd = even_ref[...], odd_ref[...]
-    low = jnp.dot(
-        jnp.where(forward, odd, even), low_ref[...], preferred_element_type=jnp.float32
-    )
-    high = jnp.dot(
-        jnp.where(forward, even, odd), high_ref[...], preferred_element_type=jnp.float32
-    )
+    backward = lax.axis_index("range") % 2
+    edges[1 - backward] = even_ref[...]
+    edges[backward] = odd_ref[...]
+    low = jnp.dot(edges[0], low_ref[...], preferred_element_type=jnp.float32)
+    high = jnp.dot(edges[1], high_ref[...], preferred_element_type=jnp.float32)
     for slot in range(dates):
         for part in range(parts):
             spot = slice((slot * parts + part) * LANES, (slot * parts + part + 1) * LANES)
@@ -372,6 +376,7 @@
         out_shape=out_shape,
         in_specs=[VMEM] * 7,
         out_specs=(VMEM,) * len(out_shape),
+        scratch_shapes=[pltpu.VMEM((2,) + even.shape, even.dtype)],
         name="resample",
         compiler_params=pltpu.CompilerParams(vmem_limit_bytes=GRANT),
     )(*[near(array) for array in (block, even, odd, own_taps, low_taps, high_taps, line_taps)])

time: 31.7 us -> 31.2 us (0.984)
  the two profiles are of different devices: /device:TPU:8 before, /device:TPU:16 now
where the time goes in v6:
time: 31.2 us; the launch traced here: 31 us
  starting transfers between devices  9.95 us (32%)
  blocking collectives  7.87 us (25%)
  waiting for transfers between devices  6.72 us (22%)
  Pallas kernels  5.13 us (16%)
  between operations  1.32 us (4%)
    ppermute x9, starting transfers between devices, exchanged(): lax.ppermute(array, axis, [route for a, b in pairs for route in ((a, b),...  9.95 us
    all_to_all x1, blocking collectives, body(): results = lax.all_to_all(results, 'date', 0, 0)  7.87 us
    ppermute x9, waiting for transfers between devices, exchanged(): lax.ppermute(array, axis, [route for a, b in pairs for route in ((a, b),...  6.72 us
    pallas_call x1, Pallas kernels, body(): pl.pallas_call(start_kernel, out_shape=(pltpu.VMEM(block.shape, block.dty...  1.55 us
    pallas_call x1, Pallas kernels, body(): pl.pallas_call(functools.partial(looks_kernel, positions), out_shape=pltp...  1.07 us
    pallas_call x1, Pallas kernels, body(): pl.pallas_call(functools.partial(taps_kernel, tile_lines), out_shape=(plt...  1.01 us
    pallas_call x1, Pallas kernels, body(): pl.pallas_call(place_kernel, out_shape=(jax.ShapeDtypeStruct((dates, 2 *...  0.76 us
    pallas_call x1, Pallas kernels, body(): pl.pallas_call(functools.partial(resample_kernel, (line_groups, column_gr...  0.74 us
  transfers between devices with their start and end apart: 9, of which 6 were waited for; matrix products, arithmetic and copies ran while one was open for 0% of the time, Pallas kernels for 3%

profile of v6, /device:TPU:16, one launch (start us, length us, event | category | flops | bytes accessed | tf_op | source)
XLA Modules:
  0.0 31.0 jit_solution(8789154307789117513)
XLA Ops:
  0.6 1.6 %start.1 = (bf16[2,2,256,256]{3,2,1,0:T(8,128)(2,1)S(1)}, bf16[256,64]{1,0:T(8,128)(2,1)S(1)}, bf16[256,64]{1,0:T(8,128)(2,1)S(1)}, s32[16]{0:T(128)S(4)}, s32[1...) custom-call(bf16[2,2,256,256]{3,2,1,0:T(8,128)(2,1)} %x_ref.1, ...), custom_call_target="tpu_custom_call" | custom-call | tf_op jit(solution)/shard_map/start/pallas_call | solution.py:333
  2.2 1.6 %collective-permute-start = (bf16[256,64]{1,0:T(8,128)(2,1)S(1)}, bf16[256,64]{1,0:T(8,128)(2,1)S(1)}, u32[]{:S(2)}, u32[]{:S(2)}) collective-permute-start(bf16[256,64]{1,0:T(8,128)(2,1)S(1)} %get-tuple-element.32), channel_id=1, source_target_pairs={{0,1},{1,0},{2,3},{3,2},{4,5},{5,4},{6,7},{7,6},{8,9},{9,8},{10,11... | collective-permute-start | bytes 98312 | tf_op jit(solution)/shard_map/ppermute | solution.py:27
  3.8 1.9 %collective-permute-start.1 = (bf16[256,64]{1,0:T(8,128)(2,1)S(1)}, bf16[256,64]{1,0:T(8,128)(2,1)S(1)}, u32[]{:S(2)}, u32[]{:S(2)}) collective-permute-start(bf16[256,64]{1,0:T(8,128)(2,1)S(1)} %get-tuple-element.33), channel_id=1, source_target_pairs={{1,2},{2,1},{5,6},{6,5},{9,10},{10,9},{13,14},{14,13},{17,18},{18,... | collective-permute-start | bytes 98312 | tf_op jit(solution)/shard_map/ppermute | solution.py:27
  6.4 1.0 %taps.1 = (bf16[2,256,256]{2,1,0:T(8,128)(2,1)S(1)}, bf16[64,512]{1,0:T(8,128)(2,1)S(1)}, bf16[64,512]{1,0:T(8,128)(2,1)S(1)}, bf16[2,256,256]{2,1,0:T(8,128)(2,1)S(1)}, s32[8]{0:T(128)S(4)}) custom-call(s32[16]{0:T(128)S(4)} %get-tuple-element.24.az_whole, s32[16]{0:T(128)S(4)} %get-tuple-element.25.az_part, s32[16]{0:T(128)S(4)} %get-tuple-element.26.rg_whole, ...), custom_call_target="tpu_custom_call" | custom-call | flops 4000000 | bytes 800000 | tf_op jit(solution)/shard_map/taps/pallas_call | solution.py:352
  7.4 0.0 collective-permute-done.even_ref
  7.4 2.6 %collective-permute-done.1.odd_ref = bf16[256,64]{1,0:T(8,128)(2,1)S(1)} collective-permute-done((bf16[256,64]{1,0:T(8,128)(2,1)S(1)}, bf16[256,64]{1,0:T(8,128)(2,1)S(1)}, u32[]{:S(2)}, u32[]{:S(2)}) %collective-permute-start.1) | collective-permute-done | bytes 32800 | tf_op jit(solution)/shard_map/ppermute | solution.py:27
  10.0 0.7 %resample.1 = (bf16[2,2,32,256]{3,2,1,0:T(8,128)(2,1)S(1)}, bf16[2,2,32,256]{3,2,1,0:T(8,128)(2,1)S(1)}, bf16[2,2,32,256]{3,2,1,0:T(8,128)(2,1)S(1)}, bf16[2,2,3...) custom-call(bf16[2,2,256,256]{3,2,1,0:T(8,128)(2,1)S(1)} %get-tuple-, ...), custom_call_target="tpu_custom_call" | custom-call | tf_op jit(solution)/shard_map/resample/pallas_call | solution.py:372
  10.7 2.5 %collective-permute-start.2 = (bf16[2,2,32,256]{3,2,1,0:T(8,128)(2,1)S(1)}, bf16[2,2,32,256]{3,2,1,0:T(8,128)(2,1)S(1)}, u32[]{:S(2)}, u32[]{:S(2)}) collective-permute-start(bf16[2,2,32,256]{3,2,1,0:T(8,128)(2,1)S(1)} %get-tuple-element.39), channel_id=1, source_target_pairs={{0,24},{24,0},{4,28},{28,4},{8,16},{16,8},{12,20},{20,12},{1,25},{... | collective-permute-start | bytes 196616 | tf_op jit(solution)/shard_map/ppermute | solution.py:27
  13.2 0.5 %collective-permute-start.3 = (bf16[2,2,32,256]{3,2,1,0:T(8,128)(2,1)S(1)}, bf16[2,2,32,256]{3,2,1,0:T(8,128)(2,1)S(1)}, u32[]{:S(2)}, u32[]{:S(2)}) collective-permute-start(bf16[2,2,32,256]{3,2,1,0:T(8,128)(2,1)S(1)} %get-tuple-element.40), channel_id=1, source_target_pairs={{0,16},{16,0},{4,20},{20,4},{8,24},{24,8},{12,28},{28,12},{1,17},{... | collective-permute-start | bytes 196616 | tf_op jit(solution)/shard_map/ppermute | solution.py:27
  13.7 0.5 %collective-permute-start.4 = (bf16[2,2,32,256]{3,2,1,0:T(8,128)(2,1)S(1)}, bf16[2,2,32,256]{3,2,1,0:T(8,128)(2,1)S(1)}, u32[]{:S(2)}, u32[]{:S(2)}) collective-permute-start(bf16[2,2,32,256]{3,2,1,0:T(8,128)(2,1)S(1)} %get-tuple-element.41), channel_id=1, source_target_pairs={{0,8},{8,0},{4,12},{12,4},{16,24},{24,16},{20,28},{28,20},{1,9},{9... | collective-permute-start | bytes 196616 | tf_op jit(solution)/shard_map/ppermute | solution.py:27
  14.3 0.0 collective-permute-start.5
  14.3 2.7 %collective-permute-start.6 = (bf16[2,2,32,256]{3,2,1,0:T(8,128)(2,1)S(1)}, bf16[2,2,32,256]{3,2,1,0:T(8,128)(2,1)S(1)}, u32[]{:S(2)}, u32[]{:S(2)}) collective-permute-start(bf16[2,2,32,256]{3,2,1,0:T(8,128)(2,1)S(1)} %get-tuple-element.43), channel_id=1, source_target_pairs={{0,20},{20,0},{4,16},{16,4},{8,28},{28,8},{12,24},{24,12},{1,21},{... | collective-permute-start | bytes 196616 | tf_op jit(solution)/shard_map/ppermute | solution.py:27
  17.0 0.0 collective-permute-done.2.refs_1_
  17.0 0.1 collective-permute-start.7
  17.0 0.5 %collective-permute-done.3.refs_2_ = bf16[2,2,32,256]{3,2,1,0:T(8,128)(2,1)S(1)} collective-permute-done((bf16[2,2,32,256]{3,2,1,0:T(8,128)(2,1)S(1)}, bf16[2,2,32,256]{3,2,1,0:T(8,128)(2,1)S(1)}, u32[]{:S(2)}, u32[]{:S(2)}) %collective-permute-start.3) | collective-permute-done | bytes 65568 | tf_op jit(solution)/shard_map/ppermute | solution.py:27
  17.5 0.1 collective-permute-start.8
  17.6 0.4 %collective-permute-done.4.refs_3_ = bf16[2,2,32,256]{3,2,1,0:T(8,128)(2,1)S(1)} collective-permute-done((bf16[2,2,32,256]{3,2,1,0:T(8,128)(2,1)S(1)}, bf16[2,2,32,256]{3,2,1,0:T(8,128)(2,1)S(1)}, u32[]{:S(2)}, u32[]{:S(2)}) %collective-permute-start.4) | collective-permute-done | bytes 65568 | tf_op jit(solution)/shard_map/ppermute | solution.py:27
  18.0 1.5 %collective-permute-done.5.refs_4_ = bf16[2,2,32,256]{3,2,1,0:T(8,128)(2,1)S(1)} collective-permute-done((bf16[2,2,32,256]{3,2,1,0:T(8,128)(2,1)S(1)}, bf16[2,2,32,256]{3,2,1,0:T(8,128)(2,1)S(1)}, u32[]{:S(2)}, u32[]{:S(2)}) %collective-permute-start.5) | collective-permute-done | bytes 65568 | tf_op jit(solution)/shard_map/ppermute | solution.py:27
  19.5 0.3 %collective-permute-done.6.refs_5_ = bf16[2,2,32,256]{3,2,1,0:T(8,128)(2,1)S(1)} collective-permute-done((bf16[2,2,32,256]{3,2,1,0:T(8,128)(2,1)S(1)}, bf16[2,2,32,256]{3,2,1,0:T(8,128)(2,1)S(1)}, u32[]{:S(2)}, u32[]{:S(2)}) %collective-permute-start.6) | collective-permute-done | bytes 65568 | tf_op jit(solution)/shard_map/ppermute | solution.py:27
  19.8 1.5 %collective-permute-done.7.refs_6_ = bf16[2,2,32,256]{3,2,1,0:T(8,128)(2,1)S(1)} collective-permute-done((bf16[2,2,32,256]{3,2,1,0:T(8,128)(2,1)S(1)}, bf16[2,2,32,256]{3,2,1,0:T(8,128)(2,1)S(1)}, u32[]{:S(2)}, u32[]{:S(2)}) %collective-permute-start.7) | collective-permute-done | bytes 65568 | tf_op jit(solution)/shard_map/ppermute | solution.py:27
  21.3 0.0 collective-permute-done.8.refs_7_
  21.3 1.1 %looks.1 = f32[8,18,128]{2,1,0:T(8,128)S(1)} custom-call(s32[8]{0:T(128)S(4)} %get-tuple-element.29.root_ref, s32[2,16]{1,0:T(2,128)S(4)} %get-tuple-element.30.gap_ref, bf16[2,2,32,256]{3,2,1,0:T(8,128)(2,1)S(1)} %get-tuple-element.38.refs_0_, bf16[2,2,32,256]{3,2,1,0:T(8,128)(2,1)S(1)} %collective-permute-done.2.refs_1_, ...), custom_call_target="tpu_custom_call" | custom-call | tf_op jit(solution)/shard_map/looks/pallas_call | solution.py:395
  22.4 7.9 %all_to_all.5.x_ref = f32[8,18,128]{2,1,0:T(8,128)S(1)} all-to-all(f32[8,18,128]{2,1,0:T(8,128)S(1)} %looks.1), channel_id=1, replica_groups=mesh['date'=8,'range'=4] {'date'}, dimensions={0} | all-to-all | bytes 147456 | tf_op jit(solution)/shard_map/all_to_all | solution.py:413
  30.2 0.8 %place.1 = (f32[2,6,16,64]{3,2,1,0:T(8,128)}, f32[2,3,16,64]{3,2,1,0:T(8,128)}) custom-call(f32[8,18,128]{2,1,0:T(8,128)S(1)} %all_to_all.5.x_ref), custom_call_target="tpu_custom_call" | custom-call | tf_op jit(solution)/shard_map/place/pallas_call | solution.py:417
Async XLA Ops:
  2.2 5.2 %collective-permute-start = (bf16[256,64]{1,0:T(8,128)(2,1)S(1)}, bf16[256,64]{1,0:T(8,128)(2,1)S(1)}, u32[]{:S(2)}, u32[]{:S(2)}) collective-permute-start(bf16[256,64]{1,0:T(8,128)(2,1)S(1)} %get-tuple-element.32), channel_id=1, source_target_pairs={{0,1},{1,0},{2,3},{3,2},{4,5},{5,4},{6,7},{7,6},{8,9},{9,8},{10,11... | collective-permute-start | bytes 98312 | tf_op jit(solution)/shard_map/ppermute | solution.py:27
  3.8 6.1 %collective-permute-start.1 = (bf16[256,64]{1,0:T(8,128)(2,1)S(1)}, bf16[256,64]{1,0:T(8,128)(2,1)S(1)}, u32[]{:S(2)}, u32[]{:S(2)}) collective-permute-start(bf16[256,64]{1,0:T(8,128)(2,1)S(1)} %get-tuple-element.33), channel_id=1, source_target_pairs={{1,2},{2,1},{5,6},{6,5},{9,10},{10,9},{13,14},{14,13},{17,18},{18,... | collective-permute-start | bytes 98312 | tf_op jit(solution)/shard_map/ppermute | solution.py:27
  10.7 6.2 %collective-permute-start.2 = (bf16[2,2,32,256]{3,2,1,0:T(8,128)(2,1)S(1)}, bf16[2,2,32,256]{3,2,1,0:T(8,128)(2,1)S(1)}, u32[]{:S(2)}, u32[]{:S(2)}) collective-permute-start(bf16[2,2,32,256]{3,2,1,0:T(8,128)(2,1)S(1)} %get-tuple-element.39), channel_id=1, source_target_pairs={{0,24},{24,0},{4,28},{28,4},{8,16},{16,8},{12,20},{20,12},{1,25},{... | collective-permute-start | bytes 196616 | tf_op jit(solution)/shard_map/ppermute | solution.py:27
  13.2 4.3 %collective-permute-start.3 = (bf16[2,2,32,256]{3,2,1,0:T(8,128)(2,1)S(1)}, bf16[2,2,32,256]{3,2,1,0:T(8,128)(2,1)S(1)}, u32[]{:S(2)}, u32[]{:S(2)}) collective-permute-start(bf16[2,2,32,256]{3,2,1,0:T(8,128)(2,1)S(1)} %get-tuple-element.40), channel_id=1, source_target_pairs={{0,16},{16,0},{4,20},{20,4},{8,24},{24,8},{12,28},{28,12},{1,17},{... | collective-permute-start | bytes 196616 | tf_op jit(solution)/shard_map/ppermute | solution.py:27
  13.7 4.3 %collective-permute-start.4 = (bf16[2,2,32,256]{3,2,1,0:T(8,128)(2,1)S(1)}, bf16[2,2,32,256]{3,2,1,0:T(8,128)(2,1)S(1)}, u32[]{:S(2)}, u32[]{:S(2)}) collective-permute-start(bf16[2,2,32,256]{3,2,1,0:T(8,128)(2,1)S(1)} %get-tuple-element.41), channel_id=1, source_target_pairs={{0,8},{8,0},{4,12},{12,4},{16,24},{24,16},{20,28},{28,20},{1,9},{9... | collective-permute-start | bytes 196616 | tf_op jit(solution)/shard_map/ppermute | solution.py:27
  14.3 5.2 %collective-permute-start.5 = (bf16[2,2,32,256]{3,2,1,0:T(8,128)(2,1)S(1)}, bf16[2,2,32,256]{3,2,1,0:T(8,128)(2,1)S(1)}, u32[]{:S(2)}, u32[]{:S(2)}) collective-permute-start(bf16[2,2,32,256]{3,2,1,0:T(8,128)(2,1)S(1)} %get-tuple-element.42), channel_id=1, source_target_pairs={{0,28},{28,0},{4,24},{24,4},{8,20},{20,8},{12,16},{16,12},{1,29},{... | collective-permute-start | bytes 196616 | tf_op jit(solution)/shard_map/ppermute | solution.py:27
  14.3 5.5 %collective-permute-start.6 = (bf16[2,2,32,256]{3,2,1,0:T(8,128)(2,1)S(1)}, bf16[2,2,32,256]{3,2,1,0:T(8,128)(2,1)S(1)}, u32[]{:S(2)}, u32[]{:S(2)}) collective-permute-start(bf16[2,2,32,256]{3,2,1,0:T(8,128)(2,1)S(1)} %get-tuple-element.43), channel_id=1, source_target_pairs={{0,20},{20,0},{4,16},{16,4},{8,28},{28,8},{12,24},{24,12},{1,21},{... | collective-permute-start | bytes 196616 | tf_op jit(solution)/shard_map/ppermute | solution.py:27
  17.0 4.3 %collective-permute-start.7 = (bf16[2,2,32,256]{3,2,1,0:T(8,128)(2,1)S(1)}, bf16[2,2,32,256]{3,2,1,0:T(8,128)(2,1)S(1)}, u32[]{:S(2)}, u32[]{:S(2)}) collective-permute-start(bf16[2,2,32,256]{3,2,1,0:T(8,128)(2,1)S(1)} %get-tuple-element.44), channel_id=1, source_target_pairs={{0,12},{12,0},{4,8},{8,4},{16,28},{28,16},{20,24},{24,20},{1,13},{... | collective-permute-start | bytes 196616 | tf_op jit(solution)/shard_map/ppermute | solution.py:27
  17.5 3.8 %collective-permute-start.8 = (bf16[2,2,32,256]{3,2,1,0:T(8,128)(2,1)S(1)}, bf16[2,2,32,256]{3,2,1,0:T(8,128)(2,1)S(1)}, u32[]{:S(2)}, u32[]{:S(2)}) collective-permute-start(bf16[2,2,32,256]{3,2,1,0:T(8,128)(2,1)S(1)} %get-tuple-element.45), channel_id=1, source_target_pairs={{0,4},{4,0},{8,12},{12,8},{16,20},{20,16},{24,28},{28,24},{1,5},{5... | collective-permute-start | bytes 196616 | tf_op jit(solution)/shard_map/ppermute | solution.py:27

commit v7 on v6

--- a/solution.py
+++ b/solution.py
@@ -152,7 +152,7 @@
         line_ref[slot] = jnp.where(usable, band, 0.0).astype(jnp.bfloat16)
 
 
-def resample_kernel(split, x_ref, even_ref, odd_ref, own_ref, low_ref, high_ref, line_ref, *refs):
+def resample_kernel(split, x_ref, odd_ref, even_ref, own_ref, low_ref, high_ref, line_ref, *refs):
     *outs, edges = refs
     dates, parts, _, columns = x_ref.shape
     line_groups, column_groups, tile_lines, tile_columns = split
@@ -379,7 +379,7 @@
         scratch_shapes=[pltpu.VMEM((2,) + even.shape, even.dtype)],
         name="resample",
         compiler_params=pltpu.CompilerParams(vmem_limit_bytes=GRANT),
-    )(*[near(array) for array in (block, even, odd, own_taps, low_taps, high_taps, line_taps)])
+    )(*[near(array) for array in (block, odd, even, own_taps, low_taps, high_taps, line_taps)])
 
     if by_pairs(owners):
         order = [*range(owners - 2, 0, -2), *range(owners - 1, 0, -2)]

time: 31.2 us -> 32.2 us (1.032)
  the two profiles are of different devices: /device:TPU:16 before, /device:TPU:0 now
where the time goes in v7:
time: 32.2 us; the launch traced here: 32 us
  starting transfers between devices  13 us (40%)
  blocking collectives  7.88 us (24%)
  Pallas kernels  5.13 us (16%)
  waiting for transfers between devices  4.73 us (15%)
  between operations  1.33 us (4%)
    ppermute x9, starting transfers between devices, exchanged(): lax.ppermute(array, axis, [route for a, b in pairs for route in ((a, b),...  13 us
    all_to_all x1, blocking collectives, body(): results = lax.all_to_all(results, 'date', 0, 0)  7.88 us
    ppermute x9, waiting for transfers between devices, exchanged(): lax.ppermute(array, axis, [route for a, b in pairs for route in ((a, b),...  4.73 us
    pallas_call x1, Pallas kernels, body(): pl.pallas_call(start_kernel, out_shape=(pltpu.VMEM(block.shape, block.dty...  1.55 us
    pallas_call x1, Pallas kernels, body(): pl.pallas_call(functools.partial(looks_kernel, positions), out_shape=pltp...  1.07 us
    pallas_call x1, Pallas kernels, body(): pl.pallas_call(functools.partial(taps_kernel, tile_lines), out_shape=(plt...  1.01 us
    pallas_call x1, Pallas kernels, body(): pl.pallas_call(place_kernel, out_shape=(jax.ShapeDtypeStruct((dates, 2 *...  0.76 us
    pallas_call x1, Pallas kernels, body(): pl.pallas_call(functools.partial(resample_kernel, (line_groups, column_gr...  0.73 us
  transfers between devices with their start and end apart: 9, of which 6 were waited for; matrix products, arithmetic and copies ran while one was open for 0% of the time, Pallas kernels for 3%

profile of v7, /device:TPU:0, one launch (start us, length us, event | category | flops | bytes accessed | tf_op | source)
XLA Modules:
  0.0 32.0 jit_solution(1477894592714209633)
XLA Ops:
  0.6 1.6 %start.1 = (bf16[2,2,256,256]{3,2,1,0:T(8,128)(2,1)S(1)}, bf16[256,64]{1,0:T(8,128)(2,1)S(1)}, bf16[256,64]{1,0:T(8,128)(2,1)S(1)}, s32[16]{0:T(128)S(4)}, s32[1...) custom-call(bf16[2,2,256,256]{3,2,1,0:T(8,128)(2,1)} %x_ref.1, ...), custom_call_target="tpu_custom_call" | custom-call | tf_op jit(solution)/shard_map/start/pallas_call | solution.py:333
  2.2 0.7 %collective-permute-start = (bf16[256,64]{1,0:T(8,128)(2,1)S(1)}, bf16[256,64]{1,0:T(8,128)(2,1)S(1)}, u32[]{:S(2)}, u32[]{:S(2)}) collective-permute-start(bf16[256,64]{1,0:T(8,128)(2,1)S(1)} %get-tuple-element.32), channel_id=1, source_target_pairs={{1,2},{2,1},{5,6},{6,5},{9,10},{10,9},{13,14},{14,13},{17,18},{18,... | collective-permute-start | bytes 98312 | tf_op jit(solution)/shard_map/ppermute | solution.py:27
  2.9 5.9 %collective-permute-start.1 = (bf16[256,64]{1,0:T(8,128)(2,1)S(1)}, bf16[256,64]{1,0:T(8,128)(2,1)S(1)}, u32[]{:S(2)}, u32[]{:S(2)}) collective-permute-start(bf16[256,64]{1,0:T(8,128)(2,1)S(1)} %get-tuple-element.33), channel_id=1, source_target_pairs={{0,1},{1,0},{2,3},{3,2},{4,5},{5,4},{6,7},{7,6},{8,9},{9,8},{10,11... | collective-permute-start | bytes 98312 | tf_op jit(solution)/shard_map/ppermute | solution.py:27
  9.4 1.0 %taps.1 = (bf16[2,256,256]{2,1,0:T(8,128)(2,1)S(1)}, bf16[64,512]{1,0:T(8,128)(2,1)S(1)}, bf16[64,512]{1,0:T(8,128)(2,1)S(1)}, bf16[2,256,256]{2,1,0:T(8,128)(2,1)S(1)}, s32[8]{0:T(128)S(4)}) custom-call(s32[16]{0:T(128)S(4)} %get-tuple-element.24.az_whole, s32[16]{0:T(128)S(4)} %get-tuple-element.25.az_part, s32[16]{0:T(128)S(4)} %get-tuple-element.26.rg_whole, ...), custom_call_target="tpu_custom_call" | custom-call | flops 4000000 | bytes 800000 | tf_op jit(solution)/shard_map/taps/pallas_call | solution.py:352
  10.4 0.0 collective-permute-done.odd_ref
  10.4 0.6 %collective-permute-done.1.even_ref = bf16[256,64]{1,0:T(8,128)(2,1)S(1)} collective-permute-done((bf16[256,64]{1,0:T(8,128)(2,1)S(1)}, bf16[256,64]{1,0:T(8,128)(2,1)S(1)}, u32[]{:S(2)}, u32[]{:S(2)}) %collective-permute-start.1) | collective-permute-done | bytes 32800 | tf_op jit(solution)/shard_map/ppermute | solution.py:27
  11.0 0.7 %resample.1 = (bf16[2,2,32,256]{3,2,1,0:T(8,128)(2,1)S(1)}, bf16[2,2,32,256]{3,2,1,0:T(8,128)(2,1)S(1)}, bf16[2,2,32,256]{3,2,1,0:T(8,128)(2,1)S(1)}, bf16[2,2,3...) custom-call(bf16[2,2,256,256]{3,2,1,0:T(8,128)(2,1)S(1)} %get-tuple-, ...), custom_call_target="tpu_custom_call" | custom-call | tf_op jit(solution)/shard_map/resample/pallas_call | solution.py:372
  11.8 2.5 %collective-permute-start.2 = (bf16[2,2,32,256]{3,2,1,0:T(8,128)(2,1)S(1)}, bf16[2,2,32,256]{3,2,1,0:T(8,128)(2,1)S(1)}, u32[]{:S(2)}, u32[]{:S(2)}) collective-permute-start(bf16[2,2,32,256]{3,2,1,0:T(8,128)(2,1)S(1)} %get-tuple-element.39), channel_id=1, source_target_pairs={{0,24},{24,0},{4,28},{28,4},{8,16},{16,8},{12,20},{20,12},{1,25},{... | collective-permute-start | bytes 196616 | tf_op jit(solution)/shard_map/ppermute | solution.py:27
  14.3 0.5 %collective-permute-start.3 = (bf16[2,2,32,256]{3,2,1,0:T(8,128)(2,1)S(1)}, bf16[2,2,32,256]{3,2,1,0:T(8,128)(2,1)S(1)}, u32[]{:S(2)}, u32[]{:S(2)}) collective-permute-start(bf16[2,2,32,256]{3,2,1,0:T(8,128)(2,1)S(1)} %get-tuple-element.40), channel_id=1, source_target_pairs={{0,16},{16,0},{4,20},{20,4},{8,24},{24,8},{12,28},{28,12},{1,17},{... | collective-permute-start | bytes 196616 | tf_op jit(solution)/shard_map/ppermute | solution.py:27
  14.8 0.5 %collective-permute-start.4 = (bf16[2,2,32,256]{3,2,1,0:T(8,128)(2,1)S(1)}, bf16[2,2,32,256]{3,2,1,0:T(8,128)(2,1)S(1)}, u32[]{:S(2)}, u32[]{:S(2)}) collective-permute-start(bf16[2,2,32,256]{3,2,1,0:T(8,128)(2,1)S(1)} %get-tuple-element.41), channel_id=1, source_target_pairs={{0,8},{8,0},{4,12},{12,4},{16,24},{24,16},{20,28},{28,20},{1,9},{9... | collective-permute-start | bytes 196616 | tf_op jit(solution)/shard_map/ppermute | solution.py:27
  15.3 0.0 collective-permute-start.5
  15.3 2.7 %collective-permute-start.6 = (bf16[2,2,32,256]{3,2,1,0:T(8,128)(2,1)S(1)}, bf16[2,2,32,256]{3,2,1,0:T(8,128)(2,1)S(1)}, u32[]{:S(2)}, u32[]{:S(2)}) collective-permute-start(bf16[2,2,32,256]{3,2,1,0:T(8,128)(2,1)S(1)} %get-tuple-element.43), channel_id=1, source_target_pairs={{0,20},{20,0},{4,16},{16,4},{8,28},{28,8},{12,24},{24,12},{1,21},{... | collective-permute-start | bytes 196616 | tf_op jit(solution)/shard_map/ppermute | solution.py:27
  18.0 0.0 collective-permute-done.2.refs_1_
  18.0 0.1 collective-permute-start.7
  18.1 0.5 %collective-permute-done.3.refs_2_ = bf16[2,2,32,256]{3,2,1,0:T(8,128)(2,1)S(1)} collective-permute-done((bf16[2,2,32,256]{3,2,1,0:T(8,128)(2,1)S(1)}, bf16[2,2,32,256]{3,2,1,0:T(8,128)(2,1)S(1)}, u32[]{:S(2)}, u32[]{:S(2)}) %collective-permute-start.3) | collective-permute-done | bytes 65568 | tf_op jit(solution)/shard_map/ppermute | solution.py:27
  18.5 0.1 collective-permute-start.8
  18.7 0.4 %collective-permute-done.4.refs_3_ = bf16[2,2,32,256]{3,2,1,0:T(8,128)(2,1)S(1)} collective-permute-done((bf16[2,2,32,256]{3,2,1,0:T(8,128)(2,1)S(1)}, bf16[2,2,32,256]{3,2,1,0:T(8,128)(2,1)S(1)}, u32[]{:S(2)}, u32[]{:S(2)}) %collective-permute-start.4) | collective-permute-done | bytes 65568 | tf_op jit(solution)/shard_map/ppermute | solution.py:27
  19.1 1.5 %collective-permute-done.5.refs_4_ = bf16[2,2,32,256]{3,2,1,0:T(8,128)(2,1)S(1)} collective-permute-done((bf16[2,2,32,256]{3,2,1,0:T(8,128)(2,1)S(1)}, bf16[2,2,32,256]{3,2,1,0:T(8,128)(2,1)S(1)}, u32[]{:S(2)}, u32[]{:S(2)}) %collective-permute-start.5) | collective-permute-done | bytes 65568 | tf_op jit(solution)/shard_map/ppermute | solution.py:27
  20.5 0.3 %collective-permute-done.6.refs_5_ = bf16[2,2,32,256]{3,2,1,0:T(8,128)(2,1)S(1)} collective-permute-done((bf16[2,2,32,256]{3,2,1,0:T(8,128)(2,1)S(1)}, bf16[2,2,32,256]{3,2,1,0:T(8,128)(2,1)S(1)}, u32[]{:S(2)}, u32[]{:S(2)}) %collective-permute-start.6) | collective-permute-done | bytes 65568 | tf_op jit(solution)/shard_map/ppermute | solution.py:27
  20.9 1.5 %collective-permute-done.7.refs_6_ = bf16[2,2,32,256]{3,2,1,0:T(8,128)(2,1)S(1)} collective-permute-done((bf16[2,2,32,256]{3,2,1,0:T(8,128)(2,1)S(1)}, bf16[2,2,32,256]{3,2,1,0:T(8,128)(2,1)S(1)}, u32[]{:S(2)}, u32[]{:S(2)}) %collective-permute-start.7) | collective-permute-done | bytes 65568 | tf_op jit(solution)/shard_map/ppermute | solution.py:27
  22.3 0.0 collective-permute-done.8.refs_7_
  22.3 1.1 %looks.1 = f32[8,18,128]{2,1,0:T(8,128)S(1)} custom-call(s32[8]{0:T(128)S(4)} %get-tuple-element.29.root_ref, s32[2,16]{1,0:T(2,128)S(4)} %get-tuple-element.30.gap_ref, bf16[2,2,32,256]{3,2,1,0:T(8,128)(2,1)S(1)} %get-tuple-element.38.refs_0_, bf16[2,2,32,256]{3,2,1,0:T(8,128)(2,1)S(1)} %collective-permute-done.2.refs_1_, ...), custom_call_target="tpu_custom_call" | custom-call | tf_op jit(solution)/shard_map/looks/pallas_call | solution.py:395
  23.4 7.9 %all_to_all.5.x_ref = f32[8,18,128]{2,1,0:T(8,128)S(1)} all-to-all(f32[8,18,128]{2,1,0:T(8,128)S(1)} %looks.1), channel_id=1, replica_groups=mesh['date'=8,'range'=4] {'date'}, dimensions={0} | all-to-all | bytes 147456 | tf_op jit(solution)/shard_map/all_to_all | solution.py:413
  31.3 0.8 %place.1 = (f32[2,6,16,64]{3,2,1,0:T(8,128)}, f32[2,3,16,64]{3,2,1,0:T(8,128)}) custom-call(f32[8,18,128]{2,1,0:T(8,128)S(1)} %all_to_all.5.x_ref), custom_call_target="tpu_custom_call" | custom-call | tf_op jit(solution)/shard_map/place/pallas_call | solution.py:417
Async XLA Ops:
  2.2 8.2 %collective-permute-start = (bf16[256,64]{1,0:T(8,128)(2,1)S(1)}, bf16[256,64]{1,0:T(8,128)(2,1)S(1)}, u32[]{:S(2)}, u32[]{:S(2)}) collective-permute-start(bf16[256,64]{1,0:T(8,128)(2,1)S(1)} %get-tuple-element.32), channel_id=1, source_target_pairs={{1,2},{2,1},{5,6},{6,5},{9,10},{10,9},{13,14},{14,13},{17,18},{18,... | collective-permute-start | bytes 98312 | tf_op jit(solution)/shard_map/ppermute | solution.py:27
  2.9 8.2 %collective-permute-start.1 = (bf16[256,64]{1,0:T(8,128)(2,1)S(1)}, bf16[256,64]{1,0:T(8,128)(2,1)S(1)}, u32[]{:S(2)}, u32[]{:S(2)}) collective-permute-start(bf16[256,64]{1,0:T(8,128)(2,1)S(1)} %get-tuple-element.33), channel_id=1, source_target_pairs={{0,1},{1,0},{2,3},{3,2},{4,5},{5,4},{6,7},{7,6},{8,9},{9,8},{10,11... | collective-permute-start | bytes 98312 | tf_op jit(solution)/shard_map/ppermute | solution.py:27
  11.8 6.2 %collective-permute-start.2 = (bf16[2,2,32,256]{3,2,1,0:T(8,128)(2,1)S(1)}, bf16[2,2,32,256]{3,2,1,0:T(8,128)(2,1)S(1)}, u32[]{:S(2)}, u32[]{:S(2)}) collective-permute-start(bf16[2,2,32,256]{3,2,1,0:T(8,128)(2,1)S(1)} %get-tuple-element.39), channel_id=1, source_target_pairs={{0,24},{24,0},{4,28},{28,4},{8,16},{16,8},{12,20},{20,12},{1,25},{... | collective-permute-start | bytes 196616 | tf_op jit(solution)/shard_map/ppermute | solution.py:27
  14.3 4.3 %collective-permute-start.3 = (bf16[2,2,32,256]{3,2,1,0:T(8,128)(2,1)S(1)}, bf16[2,2,32,256]{3,2,1,0:T(8,128)(2,1)S(1)}, u32[]{:S(2)}, u32[]{:S(2)}) collective-permute-start(bf16[2,2,32,256]{3,2,1,0:T(8,128)(2,1)S(1)} %get-tuple-element.40), channel_id=1, source_target_pairs={{0,16},{16,0},{4,20},{20,4},{8,24},{24,8},{12,28},{28,12},{1,17},{... | collective-permute-start | bytes 196616 | tf_op jit(solution)/shard_map/ppermute | solution.py:27
  14.8 4.3 %collective-permute-start.4 = (bf16[2,2,32,256]{3,2,1,0:T(8,128)(2,1)S(1)}, bf16[2,2,32,256]{3,2,1,0:T(8,128)(2,1)S(1)}, u32[]{:S(2)}, u32[]{:S(2)}) collective-permute-start(bf16[2,2,32,256]{3,2,1,0:T(8,128)(2,1)S(1)} %get-tuple-element.41), channel_id=1, source_target_pairs={{0,8},{8,0},{4,12},{12,4},{16,24},{24,16},{20,28},{28,20},{1,9},{9... | collective-permute-start | bytes 196616 | tf_op jit(solution)/shard_map/ppermute | solution.py:27
  15.3 5.2 %collective-permute-start.5 = (bf16[2,2,32,256]{3,2,1,0:T(8,128)(2,1)S(1)}, bf16[2,2,32,256]{3,2,1,0:T(8,128)(2,1)S(1)}, u32[]{:S(2)}, u32[]{:S(2)}) collective-permute-start(bf16[2,2,32,256]{3,2,1,0:T(8,128)(2,1)S(1)} %get-tuple-element.42), channel_id=1, source_target_pairs={{0,28},{28,0},{4,24},{24,4},{8,20},{20,8},{12,16},{16,12},{1,29},{... | collective-permute-start | bytes 196616 | tf_op jit(solution)/shard_map/ppermute | solution.py:27
  15.3 5.5 %collective-permute-start.6 = (bf16[2,2,32,256]{3,2,1,0:T(8,128)(2,1)S(1)}, bf16[2,2,32,256]{3,2,1,0:T(8,128)(2,1)S(1)}, u32[]{:S(2)}, u32[]{:S(2)}) collective-permute-start(bf16[2,2,32,256]{3,2,1,0:T(8,128)(2,1)S(1)} %get-tuple-element.43), channel_id=1, source_target_pairs={{0,20},{20,0},{4,16},{16,4},{8,28},{28,8},{12,24},{24,12},{1,21},{... | collective-permute-start | bytes 196616 | tf_op jit(solution)/shard_map/ppermute | solution.py:27
  18.0 4.3 %collective-permute-start.7 = (bf16[2,2,32,256]{3,2,1,0:T(8,128)(2,1)S(1)}, bf16[2,2,32,256]{3,2,1,0:T(8,128)(2,1)S(1)}, u32[]{:S(2)}, u32[]{:S(2)}) collective-permute-start(bf16[2,2,32,256]{3,2,1,0:T(8,128)(2,1)S(1)} %get-tuple-element.44), channel_id=1, source_target_pairs={{0,12},{12,0},{4,8},{8,4},{16,28},{28,16},{20,24},{24,20},{1,13},{... | collective-permute-start | bytes 196616 | tf_op jit(solution)/shard_map/ppermute | solution.py:27
  18.5 3.8 %collective-permute-start.8 = (bf16[2,2,32,256]{3,2,1,0:T(8,128)(2,1)S(1)}, bf16[2,2,32,256]{3,2,1,0:T(8,128)(2,1)S(1)}, u32[]{:S(2)}, u32[]{:S(2)}) collective-permute-start(bf16[2,2,32,256]{3,2,1,0:T(8,128)(2,1)S(1)} %get-tuple-element.45), channel_id=1, source_target_pairs={{0,4},{4,0},{8,12},{12,8},{16,20},{20,16},{24,28},{28,24},{1,5},{5... | collective-permute-start | bytes 196616 | tf_op jit(solution)/shard_map/ppermute | solution.py:27

commit v8 on v6

--- a/solution.py
+++ b/solution.py
@@ -18,6 +18,9 @@
 CHANNELS = 9
 LANES = 128
 GRANT = 24 * 2**20
+CORES = 2
+CHIPS = 4
+CHIP_LOOKS = 4
 
 SMEM = pl.BlockSpec(memory_space=pltpu.SMEM)
 VMEM = pl.BlockSpec(memory_space=pltpu.VMEM)
@@ -52,14 +55,18 @@
     return weights.astype(jnp.bfloat16).astype(jnp.float32)
 
 
-def by_pairs(owners):
-    return owners in (2, 4, 8)
-
-
-def tile_order(position):
-    if by_pairs(lax.axis_size("date")):
-        return position ^ lax.axis_index("date")
-    return position
+def by_chips(block, owners):
+    dates, parts, lines, columns = block.shape
+    return (
+        owners == CHIPS * CORES
+        and (dates, parts) == (2, 2)
+        and lines == CHIPS * CHIP_LOOKS * LOOK_AZ
+        and columns == 2 * LANES
+    )
+
+
+def tile_order(position, chips):
+    return position ^ (lax.axis_index("date") // CORES) if chips else position
 
 
 def banded(offsets, weights):
@@ -108,6 +115,7 @@
 
 
 def taps_kernel(
+    chips,
     tile_lines,
     az_whole,
     az_part,
@@ -145,7 +153,7 @@
             low_ref[:, spot] = jnp.where(held, low, 0.0).astype(jnp.bfloat16)
             high_ref[:, spot] = jnp.where(held, high, 0.0).astype(jnp.bfloat16)
         row, col = iotas(lines, lines)
-        row = tile_order(row // tile_lines) * tile_lines + row % tile_lines
+        row = tile_order(row // tile_lines, chips) * tile_lines + row % tile_lines
         weights = table[dates + slot : dates + slot + 1]
         band = banded(col - row + (centre - az_whole[date]), weights)
         usable = row < sweeps[date] * (lines // MAX_SWEEPS)
@@ -209,23 +217,28 @@
     return values[0]
 
 
-def looks_kernel(positions, root_ref, gap_ref, *refs):
-    tiles, (out_ref, stack, sums, pooled, powers) = refs[:-5], refs[-5:]
+def pool_columns(sums, lanes):
+    row, col = iotas(sums.shape[1], lanes)
+    pool = jnp.where(row // LOOK_RG == col, 1.0, 0.0).astype(jnp.bfloat16)
+    coarse = sums.astype(jnp.bfloat16)
+    fine = (sums - coarse.astype(jnp.float32)).astype(jnp.bfloat16)
+    return jnp.dot(coarse, pool, preferred_element_type=jnp.float32) + jnp.dot(
+        fine, pool, preferred_element_type=jnp.float32
+    )
+
+
+def looks_kernel(root_ref, gap_ref, tiles_ref, out_ref, stack, sums, pooled, powers):
     total, _, tile_lines, tile_columns = stack.shape
     owners, per_owner, lanes = out_ref.shape
     dates = per_owner // CHANNELS
     line_looks = tile_lines // LOOK_AZ
     unroll = total if total <= 16 else 1
-    if len(tiles) > 1:
-        for position, tile_ref in zip(positions, tiles):
-            stack[pl.ds(tile_order(position) * dates, dates)] = tile_ref[...].astype(jnp.float32)
-    else:
-
-        def widen(owner, carry):
-            stack[pl.ds(owner * dates, dates)] = tiles[0][owner].astype(jnp.float32)
-            return carry
-
-        lax.fori_loop(0, owners, widen, 0)
+
+    def widen(owner, carry):
+        stack[pl.ds(owner * dates, dates)] = tiles_ref[owner].astype(jnp.float32)
+        return carry
+
+    lax.fori_loop(0, owners, widen, 0)
 
     def partner_of(kind, date):
         return partners(date, gap_ref, total)[kind - 1] if kind else root_ref[0]
@@ -248,16 +261,7 @@
         return carry
 
     lax.fori_loop(0, total, collect, 0, unroll=unroll)
-    shape = (line_looks * tile_columns, lanes)
-    row = lax.broadcasted_iota(jnp.int32, shape, 0)
-    col = lax.broadcasted_iota(jnp.int32, shape, 1)
-    pool = jnp.where(row // LOOK_RG == col, 1.0, 0.0).astype(jnp.bfloat16)
-    whole = sums[...]
-    coarse = whole.astype(jnp.bfloat16)
-    fine = (whole - coarse.astype(jnp.float32)).astype(jnp.bfloat16)
-    pooled[...] = jnp.dot(coarse, pool, preferred_element_type=jnp.float32) + jnp.dot(
-        fine, pool, preferred_element_type=jnp.float32
-    )
+    pooled[...] = pool_columns(sums[...], lanes)
 
     def gather(date, carry):
         for kind in range(KINDS):
@@ -282,6 +286,106 @@
             out_ref[:, slot * CHANNELS + 2 * KINDS + kind, :] = jnp.sqrt(
                 real * real + imag * imag
             ) / jnp.sqrt(power_left * power_right + 1e-06)
+
+
+def chip_looks_kernel(root_ref, gap_ref, *refs):
+    tiles, outs, (stack, sums, pooled) = refs[: CHIPS * CORES], refs[CHIPS * CORES : -3], refs[-3:]
+    dates, _, _, columns = tiles[0].shape
+    me = lax.axis_index("date")
+    total = len(tiles) * dates
+    scale = 1.0 / (LOOK_AZ * LOOK_RG) ** 0.5
+    for position, tile_ref in enumerate(tiles):
+        stack[position * dates : (position + 1) * dates] = tile_ref[...].astype(jnp.float32)
+
+    def partner_of(kind, date):
+        partner = partners(date, gap_ref, total)[kind - 1] if kind else root_ref[0]
+        return lax.div(partner, dates) ^ me, lax.rem(partner, dates)
+
+    def part(spot, number, look):
+        return stack[spot, number, look * LOOK_AZ : (look + 1) * LOOK_AZ, :]
+
+    def folded(value):
+        return value[: LOOK_AZ // 2] + value[LOOK_AZ // 2 :]
+
+    block = QUANTITIES * CHIP_LOOKS
+    for chip in range(CHIPS):
+        for slot in range(dates):
+            date = (me ^ (CORES * chip)) * dates + slot
+            own = CORES * chip * dates + slot
+            spot = slice(slot * columns, (slot + 1) * columns)
+            for kind in range(KINDS):
+                position, number = partner_of(kind, date)
+                other = position * dates + number
+                reals, imags = [], []
+                for look in range(CHIP_LOOKS):
+                    left0, left1 = part(own, 0, look), part(own, 1, look)
+                    right0, right1 = part(other, 0, look), part(other, 1, look)
+                    reals.append(folded(left0 * right0 + left1 * right1))
+                    imags.append(folded(left1 * right0 - left0 * right1))
+                start = chip * block + kind * 2 * CHIP_LOOKS
+                sums[start : start + 2 * CHIP_LOOKS, spot] = row_sums(reals + imags)
+            powers = []
+            for core in range(CORES):
+                for look in range(CHIP_LOOKS):
+                    left0 = part(own + core * dates, 0, look)
+                    left1 = part(own + core * dates, 1, look)
+                    powers.append(folded(left0 * left0 + left1 * left1))
+            start = chip * block + KINDS * 2 * CHIP_LOOKS
+            sums[start : start + 2 * CHIP_LOOKS, spot] = row_sums(powers)
+    pooled[...] = pool_columns(sums[...], LANES)
+
+    row, lane = iotas(2 * CHIP_LOOKS, LANES)
+    upper, first = row < CHIP_LOOKS, lane < LANES // 2
+    for chip in range(CHIPS):
+        base = chip * block
+        views = [pooled[base + 8 * number : base + 8 * (number + 1), :] for number in range(4)]
+        squares = [view * view for view in views[:KINDS]]
+        squares = [square + pltpu.roll(square, CHIP_LOOKS, 0) for square in squares]
+        power_left = jnp.where(upper, views[KINDS], pltpu.roll(views[KINDS], CHIP_LOOKS, 0))
+        power_right = []
+        for kind in range(KINDS):
+            halves = []
+            for slot in range(dates):
+                position, number = partner_of(kind, (me ^ (CORES * chip)) * dates + slot)
+                start = lax.div(position, CORES) * block + KINDS * 2 * CHIP_LOOKS
+                power = pooled[pl.ds(pl.multiple_of(start, 8), 8), :]
+                power = pltpu.roll(power, CHIP_LOOKS * (lax.rem(position, CORES) ^ (kind % 2)), 0)
+                halves.append(pltpu.roll(power, LANES // 2 * (number ^ slot), 1))
+            power_right.append(jnp.where(first, halves[0], halves[1]))
+        outs[chip][: 2 * KINDS * CHIP_LOOKS, :] = (
+            pooled[base : base + 2 * KINDS * CHIP_LOOKS, :] * scale
+        )
+        pairs = (
+            (jnp.where(upper, squares[0], squares[1]), jnp.where(upper, *power_right[:2])),
+            (squares[2], power_right[2]),
+        )
+        start = 2 * KINDS * CHIP_LOOKS
+        for square, power in pairs:
+            coherent = jnp.sqrt(square) / jnp.sqrt(power_left * power + 1e-06)
+            rows = min(8, outs[chip].shape[0] - start)
+            outs[chip][start : start + rows, :] = coherent[:rows]
+            start += rows
+
+
+def chip_place_kernel(*refs):
+    pieces, (ifg_ref, coh_ref) = refs[:CHIPS], refs[CHIPS:]
+    dates, _, _, columns = ifg_ref.shape
+    mine = lax.axis_index("date") // CORES
+    for chip in range(CHIPS):
+
+        @pl.when(mine == chip)
+        def _():
+            for position, piece_ref in enumerate(pieces):
+                start = (chip ^ position) * CHIP_LOOKS
+                where = slice(start, start + CHIP_LOOKS)
+                for channel in range(CHANNELS):
+                    rows = piece_ref[channel * CHIP_LOOKS : (channel + 1) * CHIP_LOOKS, :]
+                    for slot in range(dates):
+                        part = rows[:, slot * columns : (slot + 1) * columns]
+                        if channel < 2 * KINDS:
+                            ifg_ref[slot, channel, where, :] = part
+                        else:
+                            coh_ref[slot, channel - 2 * KINDS, where, :] = part
 
 
 def place_kernel(x_ref, ifg_ref, coh_ref):
@@ -315,8 +419,9 @@
     owners = lax.axis_size("date")
     total = owners * dates
     images = dates * parts
-    line_groups = min(owners, lines // LOOK_AZ)
-    column_groups = owners // line_groups
+    chips = by_chips(block, owners)
+    line_groups = CHIPS if chips else min(owners, lines // LOOK_AZ)
+    column_groups = 1 if chips else owners // line_groups
     tile_lines, tile_columns = lines // line_groups, columns // column_groups
     line_looks, column_looks = tile_lines // LOOK_AZ, tile_columns // LOOK_RG
     lanes = line_looks * column_looks
@@ -350,7 +455,7 @@
     even = exchanged(even, "range", [(j, j + 1) for j in range(0, width - 1, 2)])
 
     own_taps, low_taps, high_taps, line_taps, root = pl.pallas_call(
-        functools.partial(taps_kernel, tile_lines),
+        functools.partial(taps_kernel, chips, tile_lines),
         out_shape=(
             pltpu.VMEM((dates, columns, columns), jnp.bfloat16),
             pltpu.VMEM((images * MARGIN, images * LANES), jnp.bfloat16),
@@ -365,8 +470,8 @@
         compiler_params=pltpu.CompilerParams(vmem_limit_bytes=GRANT),
     )(*small, master_epoch_image)
     tile = (dates, parts, tile_lines, tile_columns)
-    if by_pairs(owners):
-        out_shape = (pltpu.VMEM(tile, jnp.bfloat16),) * owners
+    if chips:
+        out_shape = (pltpu.VMEM(tile, jnp.bfloat16),) * CHIPS
     else:
         out_shape = (pltpu.VMEM((owners,) + tile, jnp.bfloat16),)
     tiles = pl.pallas_call(
@@ -381,21 +486,55 @@
         compiler_params=pltpu.CompilerParams(vmem_limit_bytes=GRANT),
     )(*[near(array) for array in (block, even, odd, own_taps, low_taps, high_taps, line_taps)])
 
-    if by_pairs(owners):
-        order = [*range(owners - 2, 0, -2), *range(owners - 1, 0, -2)]
-        received = {
-            s: exchanged(tiles[s], "date", [(i, i ^ s) for i in range(owners) if i < i ^ s])
-            for s in order
-        }
-        positions = [0] + order
-        tiles = [tiles[0]] + [received[s] for s in order]
-    else:
-        tiles = [lax.all_to_all(tiles[0], "date", 0, 0)]
-        positions = None
+    root = pltpu.with_memory_space_constraint(root, pltpu.SMEM)
+    rows, cols = lines // LOOK_AZ, columns // LOOK_RG
+    out_shape = (
+        jax.ShapeDtypeStruct((dates, 2 * KINDS, rows, cols), jnp.float32),
+        jax.ShapeDtypeStruct((dates, KINDS, rows, cols), jnp.float32),
+    )
+    if chips:
+
+        def swapped(array, bits):
+            pairs = [(i, i ^ bits) for i in range(owners) if i < i ^ bits]
+            return exchanged(array, "date", pairs)
+
+        order = [3, 2, 1]
+        own = tiles[0]
+        direct = {number: swapped(tiles[number], CORES * number) for number in order}
+        other = swapped(own, 1)
+        passed = {number: swapped(direct[number], 1) for number in order}
+        held = [own, other]
+        for number in range(1, CHIPS):
+            held += [direct[number], passed[number]]
+        results = pl.pallas_call(
+            chip_looks_kernel,
+            out_shape=(pltpu.VMEM((CHANNELS * CHIP_LOOKS, LANES), jnp.float32),) * CHIPS,
+            in_specs=[SMEM] * 2 + [VMEM] * len(held),
+            out_specs=(VMEM,) * CHIPS,
+            scratch_shapes=[
+                pltpu.VMEM((total, parts, tile_lines, tile_columns), jnp.float32),
+                pltpu.VMEM((CHIPS * QUANTITIES * CHIP_LOOKS, dates * columns), jnp.float32),
+                pltpu.VMEM((CHIPS * QUANTITIES * CHIP_LOOKS, LANES), jnp.float32),
+            ],
+            name="looks",
+            compiler_params=pltpu.CompilerParams(vmem_limit_bytes=GRANT),
+        )(root, gap, *[near(tile) for tile in held])
+        back = {number: swapped(results[number], CORES * number) for number in order}
+        pieces = [results[0]] + [back[number] for number in range(1, CHIPS)]
+        return pl.pallas_call(
+            chip_place_kernel,
+            out_shape=out_shape,
+            in_specs=[VMEM] * CHIPS,
+            out_specs=(VMEM, VMEM),
+            name="place",
+            compiler_params=pltpu.CompilerParams(vmem_limit_bytes=GRANT),
+        )(*[near(piece) for piece in pieces])
+
+    tiles = lax.all_to_all(tiles[0], "date", 0, 0)
     results = pl.pallas_call(
-        functools.partial(looks_kernel, positions),
+        looks_kernel,
         out_shape=pltpu.VMEM((owners, dates * CHANNELS, lanes), jnp.float32),
-        in_specs=[SMEM] * 2 + [VMEM] * len(tiles),
+        in_specs=[SMEM] * 2 + [VMEM],
         out_specs=VMEM,
         scratch_shapes=[
             pltpu.VMEM((total, parts, tile_lines, tile_columns), jnp.float32),
@@ -405,21 +544,13 @@
         ],
         name="looks",
         compiler_params=pltpu.CompilerParams(vmem_limit_bytes=GRANT),
-    )(
-        pltpu.with_memory_space_constraint(root, pltpu.SMEM),
-        gap,
-        *[near(tile) for tile in tiles],
-    )
+    )(root, gap, near(tiles))
     results = lax.all_to_all(results, "date", 0, 0)
 
-    rows, cols = lines // LOOK_AZ, columns // LOOK_RG
     if column_groups == 1:
         return pl.pallas_call(
             place_kernel,
-            out_shape=(
-                jax.ShapeDtypeStruct((dates, 2 * KINDS, rows, cols), jnp.float32),
-                jax.ShapeDtypeStruct((dates, KINDS, rows, cols), jnp.float32),
-            ),
+            out_shape=out_shape,
             in_specs=[VMEM],
             out_specs=(VMEM, VMEM),
             name="place",

time: 31.2 us -> 29.6 us (0.949)
  the two profiles are of different devices: /device:TPU:16 before, /device:TPU:18 now
where the time goes in v8:
time: 29.6 us; the launch traced here: 29.5 us
  waiting for transfers between devices  12.2 us (41%)
  starting transfers between devices  10.7 us (36%)
  Pallas kernels  5.32 us (18%)
  between operations  1.34 us (5%)
    ppermute x12, waiting for transfers between devices, exchanged(): lax.ppermute(array, axis, [route for a, b in pairs for route in ((a, b),...  12.2 us
    ppermute x12, starting transfers between devices, exchanged(): lax.ppermute(array, axis, [route for a, b in pairs for route in ((a, b),...  10.7 us
    pallas_call x1, Pallas kernels, body(): pl.pallas_call(start_kernel, out_shape=(pltpu.VMEM(block.shape, block.dty...  1.55 us
    pallas_call x1, Pallas kernels, body(): pl.pallas_call(chip_looks_kernel, out_shape=(pltpu.VMEM((CHANNELS * CHIP_...  1.26 us
    pallas_call x1, Pallas kernels, body(): pl.pallas_call(functools.partial(taps_kernel, chips, tile_lines), out_sha...  1.01 us
    pallas_call x1, Pallas kernels, body(): pl.pallas_call(chip_place_kernel, out_shape=out_shape, in_specs=[VMEM] *...  0.76 us
    pallas_call x1, Pallas kernels, body(): pl.pallas_call(functools.partial(resample_kernel, (line_groups, column_gr...  0.74 us
  transfers between devices with their start and end apart: 12, of which 8 were waited for; matrix products, arithmetic and copies ran while one was open for 0% of the time, Pallas kernels for 3%

profile of v8, /device:TPU:18, one launch (start us, length us, event | category | flops | bytes accessed | tf_op | source)
XLA Modules:
  0.0 29.5 jit_solution(9383898011737114861)
XLA Ops:
  0.6 1.6 %start.1 = (bf16[2,2,256,256]{3,2,1,0:T(8,128)(2,1)S(1)}, bf16[256,64]{1,0:T(8,128)(2,1)S(1)}, bf16[256,64]{1,0:T(8,128)(2,1)S(1)}, s32[16]{0:T(128)S(4)}, s32[1...) custom-call(bf16[2,2,256,256]{3,2,1,0:T(8,128)(2,1)} %x_ref.1, ...), custom_call_target="tpu_custom_call" | custom-call | tf_op jit(solution)/shard_map/start/pallas_call | solution.py:438
  2.2 1.6 %collective-permute-start = (bf16[256,64]{1,0:T(8,128)(2,1)S(1)}, bf16[256,64]{1,0:T(8,128)(2,1)S(1)}, u32[]{:S(2)}, u32[]{:S(2)}) collective-permute-start(bf16[256,64]{1,0:T(8,128)(2,1)S(1)} %get-tuple-element.32), channel_id=1, source_target_pairs={{0,1},{1,0},{2,3},{3,2},{4,5},{5,4},{6,7},{7,6},{8,9},{9,8},{10,11... | collective-permute-start | bytes 98312 | tf_op jit(solution)/shard_map/ppermute | solution.py:30
  3.8 1.9 %collective-permute-start.1 = (bf16[256,64]{1,0:T(8,128)(2,1)S(1)}, bf16[256,64]{1,0:T(8,128)(2,1)S(1)}, u32[]{:S(2)}, u32[]{:S(2)}) collective-permute-start(bf16[256,64]{1,0:T(8,128)(2,1)S(1)} %get-tuple-element.33), channel_id=1, source_target_pairs={{1,2},{2,1},{5,6},{6,5},{9,10},{10,9},{13,14},{14,13},{17,18},{18,... | collective-permute-start | bytes 98312 | tf_op jit(solution)/shard_map/ppermute | solution.py:30
  6.4 1.0 %taps.1 = (bf16[2,256,256]{2,1,0:T(8,128)(2,1)S(1)}, bf16[64,512]{1,0:T(8,128)(2,1)S(1)}, bf16[64,512]{1,0:T(8,128)(2,1)S(1)}, bf16[2,256,256]{2,1,0:T(8,128)(2,1)S(1)}, s32[8]{0:T(128)S(4)}) custom-call(s32[16]{0:T(128)S(4)} %get-tuple-element.24.az_whole, s32[16]{0:T(128)S(4)} %get-tuple-element.25.az_part, s32[16]{0:T(128)S(4)} %get-tuple-element.26.rg_whole, ...), custom_call_target="tpu_custom_call" | custom-call | flops 4000000 | bytes 800000 | tf_op jit(solution)/shard_map/taps/pallas_call | solution.py:457
  7.4 0.0 collective-permute-done.even_ref
  7.4 2.6 %collective-permute-done.1.odd_ref = bf16[256,64]{1,0:T(8,128)(2,1)S(1)} collective-permute-done((bf16[256,64]{1,0:T(8,128)(2,1)S(1)}, bf16[256,64]{1,0:T(8,128)(2,1)S(1)}, u32[]{:S(2)}, u32[]{:S(2)}) %collective-permute-start.1) | collective-permute-done | bytes 32800 | tf_op jit(solution)/shard_map/ppermute | solution.py:30
  10.0 0.7 %resample.1 = (bf16[2,2,64,256]{3,2,1,0:T(8,128)(2,1)S(1)}, bf16[2,2,64,256]{3,2,1,0:T(8,128)(2,1)S(1)}, bf16[2,2,64,256]{3,2,1,0:T(8,128)(2,1)S(1)}, bf16[2,2,64,256]{3,2,1,0:T(8,128)(2,1)S(1)}) custom-call(bf16[2,2,256,256]{3,2,1,0:T(8,128)(2,1)S(1)} %get-tuple-element.31.x_ref, bf16[256,64]{1,0:T(8,128)(2,1)S(1)} %collective-permute-done.even_ref, ...), custom_call_target="tpu_custom_call" | custom-call | tf_op jit(solution)/shard_map/resample/pallas_call | solution.py:477
  10.7 0.6 %collective-permute-start.3 = (bf16[2,2,64,256]{3,2,1,0:T(8,128)(2,1)S(1)}, bf16[2,2,64,256]{3,2,1,0:T(8,128)(2,1)S(1)}, u32[]{:S(2)}, u32[]{:S(2)}) collective-permute-start(bf16[2,2,64,256]{3,2,1,0:T(8,128)(2,1)S(1)} %get-tuple-element.39), channel_id=1, source_target_pairs={{0,8},{8,0},{4,12},{12,4},{16,24},{24,16},{20,28},{28,20},{1,9},{9... | collective-permute-start | bytes 393224 | tf_op jit(solution)/shard_map/ppermute | solution.py:30
  11.3 1.5 %collective-permute-start.5 = (bf16[2,2,64,256]{3,2,1,0:T(8,128)(2,1)S(1)}, bf16[2,2,64,256]{3,2,1,0:T(8,128)(2,1)S(1)}, u32[]{:S(2)}, u32[]{:S(2)}) collective-permute-start(bf16[2,2,64,256]{3,2,1,0:T(8,128)(2,1)S(1)} %get-tuple-element.40), channel_id=1, source_target_pairs={{0,16},{16,0},{4,20},{20,4},{8,24},{24,8},{12,28},{28,12},{1,17},{... | collective-permute-start | bytes 393224 | tf_op jit(solution)/shard_map/ppermute | solution.py:30
  12.8 1.4 %collective-permute-start.7 = (bf16[2,2,64,256]{3,2,1,0:T(8,128)(2,1)S(1)}, bf16[2,2,64,256]{3,2,1,0:T(8,128)(2,1)S(1)}, u32[]{:S(2)}, u32[]{:S(2)}) collective-permute-start(bf16[2,2,64,256]{3,2,1,0:T(8,128)(2,1)S(1)} %get-tuple-element.41), channel_id=1, source_target_pairs={{0,24},{24,0},{4,28},{28,4},{8,16},{16,8},{12,20},{20,12},{1,25},{... | collective-permute-start | bytes 393224 | tf_op jit(solution)/shard_map/ppermute | solution.py:30
  14.3 1.8 %collective-permute-done.3.refs_2_ = bf16[2,2,64,256]{3,2,1,0:T(8,128)(2,1)S(1)} collective-permute-done((bf16[2,2,64,256]{3,2,1,0:T(8,128)(2,1)S(1)}, bf16[2,2,64,256]{3,2,1,0:T(8,128)(2,1)S(1)}, u32[]{:S(2)}, u32[]{:S(2)}) %collective-permute-start.3) | collective-permute-done | bytes 131104 | tf_op jit(solution)/shard_map/ppermute | solution.py:30
  16.1 0.9 %collective-permute-done.5.refs_4_ = bf16[2,2,64,256]{3,2,1,0:T(8,128)(2,1)S(1)} collective-permute-done((bf16[2,2,64,256]{3,2,1,0:T(8,128)(2,1)S(1)}, bf16[2,2,64,256]{3,2,1,0:T(8,128)(2,1)S(1)}, u32[]{:S(2)}, u32[]{:S(2)}) %collective-permute-start.5) | collective-permute-done | bytes 131104 | tf_op jit(solution)/shard_map/ppermute | solution.py:30
  17.0 0.0 collective-permute-start.6
  17.0 1.7 %collective-permute-done.7.refs_6_ = bf16[2,2,64,256]{3,2,1,0:T(8,128)(2,1)S(1)} collective-permute-done((bf16[2,2,64,256]{3,2,1,0:T(8,128)(2,1)S(1)}, bf16[2,2,64,256]{3,2,1,0:T(8,128)(2,1)S(1)}, u32[]{:S(2)}, u32[]{:S(2)}) %collective-permute-start.7) | collective-permute-done | bytes 131104 | tf_op jit(solution)/shard_map/ppermute | solution.py:30
  18.7 0.0 collective-permute-start.8
  18.7 1.3 %collective-permute-done.8.refs_7_ = bf16[2,2,64,256]{3,2,1,0:T(8,128)(2,1)S(1)} collective-permute-done((bf16[2,2,64,256]{3,2,1,0:T(8,128)(2,1)S(1)}, bf16[2,2,64,256]{3,2,1,0:T(8,128)(2,1)S(1)}, u32[]{:S(2)}, u32[]{:S(2)}) %collective-permute-start.8) | collective-permute-done | bytes 131104 | tf_op jit(solution)/shard_map/ppermute | solution.py:30
  20.1 1.3 %looks.1 = (f32[36,128]{1,0:T(8,128)S(1)}, f32[36,128]{1,0:T(8,128)S(1)}, f32[36,128]{1,0:T(8,128)S(1)}, f32[36,128]{1,0:T(8,128)S(1)}) custom-call(s32[8]{0:T(128)S(4)} %get-tuple-element.29.root_ref, s32[2,16]{1,0:T(2,128)S(4)} %get-tuple-element.30.gap_ref, bf16[2,2,64,256]{3,2,1,0:T(8,128)(2,1)S(1)} %get-tuple-element.38.refs_0_, ...), custom_call_target="tpu_custom_call" | custom-call | tf_op jit(solution)/shard_map/looks/pallas_call | solution.py:509
  21.3 1.6 %collective-permute-start.9 = (f32[36,128]{1,0:T(8,128)S(1)}, f32[36,128]{1,0:T(8,128)S(1)}, u32[]{:S(2)}, u32[]{:S(2)}) collective-permute-start(f32[36,128]{1,0:T(8,128)S(1)} %get-tuple-element.43), channel_id=1, source_target_pairs={{0,8},{8,0},{4,12},{12,4},{16,24},{24,16},{20,28},{28,20},{1,9},{9... | collective-permute-start | bytes 55304 | tf_op jit(solution)/shard_map/ppermute | solution.py:30
  22.9 1.1 %collective-permute-start.10 = (f32[36,128]{1,0:T(8,128)S(1)}, f32[36,128]{1,0:T(8,128)S(1)}, u32[]{:S(2)}, u32[]{:S(2)}) collective-permute-start(f32[36,128]{1,0:T(8,128)S(1)} %get-tuple-element.44), channel_id=1, source_target_pairs={{0,16},{16,0},{4,20},{20,4},{8,24},{24,8},{12,28},{28,12},{1,17},{... | collective-permute-start | bytes 55304 | tf_op jit(solution)/shard_map/ppermute | solution.py:30
  24.0 0.8 %collective-permute-start.11 = (f32[36,128]{1,0:T(8,128)S(1)}, f32[36,128]{1,0:T(8,128)S(1)}, u32[]{:S(2)}, u32[]{:S(2)}) collective-permute-start(f32[36,128]{1,0:T(8,128)S(1)} %get-tuple-element.45), channel_id=1, source_target_pairs={{0,24},{24,0},{4,28},{28,4},{8,16},{16,8},{12,20},{20,12},{1,25},{... | collective-permute-start | bytes 55304 | tf_op jit(solution)/shard_map/ppermute | solution.py:30
  24.9 0.3 collective-permute-done.9.refs_1_
  25.2 1.5 %collective-permute-done.10.refs_2_ = f32[36,128]{1,0:T(8,128)S(1)} collective-permute-done((f32[36,128]{1,0:T(8,128)S(1)}, f32[36,128]{1,0:T(8,128)S(1)}, u32[]{:S(2)}, u32[]{:S(2)}) %collective-permute-start.10) | collective-permute-done | bytes 18464 | tf_op jit(solution)/shard_map/ppermute | solution.py:30
  26.7 2.0 %collective-permute-done.11.refs_3_ = f32[36,128]{1,0:T(8,128)S(1)} collective-permute-done((f32[36,128]{1,0:T(8,128)S(1)}, f32[36,128]{1,0:T(8,128)S(1)}, u32[]{:S(2)}, u32[]{:S(2)}) %collective-permute-start.11) | collective-permute-done | bytes 18464 | tf_op jit(solution)/shard_map/ppermute | solution.py:30
  28.7 0.8 %place.1 = (f32[2,6,16,64]{3,2,1,0:T(8,128)}, f32[2,3,16,64]{3,2,1,0:T(8,128)}) custom-call(f32[36,128]{1,0:T(8,128)S(1)} %get-tuple-element.42.refs_0_, f32[36,128]{1,0:T(8,128)S(1)} %collective-permute-done.9.refs_1_, f32[36,128]{1,0:T(8,128)S(1)} %collective-permute-done.10.refs_2_, f32[36,128]{1,0:T(8,128)S(1)} %collective-permute-done.11.refs_3_), custom_call_target="tpu_custom_call" | custom-call | tf_op jit(solution)/shard_map/place/pallas_call | solution.py:524
  (5 shorter events, 0.0 us)
Async XLA Ops:
  2.2 5.2 %collective-permute-start = (bf16[256,64]{1,0:T(8,128)(2,1)S(1)}, bf16[256,64]{1,0:T(8,128)(2,1)S(1)}, u32[]{:S(2)}, u32[]{:S(2)}) collective-permute-start(bf16[256,64]{1,0:T(8,128)(2,1)S(1)} %get-tuple-element.32), channel_id=1, source_target_pairs={{0,1},{1,0},{2,3},{3,2},{4,5},{5,4},{6,7},{7,6},{8,9},{9,8},{10,11... | collective-permute-start | bytes 98312 | tf_op jit(solution)/shard_map/ppermute | solution.py:30
  3.8 6.1 %collective-permute-start.1 = (bf16[256,64]{1,0:T(8,128)(2,1)S(1)}, bf16[256,64]{1,0:T(8,128)(2,1)S(1)}, u32[]{:S(2)}, u32[]{:S(2)}) collective-permute-start(bf16[256,64]{1,0:T(8,128)(2,1)S(1)} %get-tuple-element.33), channel_id=1, source_target_pairs={{1,2},{2,1},{5,6},{6,5},{9,10},{10,9},{13,14},{14,13},{17,18},{18,... | collective-permute-start | bytes 98312 | tf_op jit(solution)/shard_map/ppermute | solution.py:30
  10.7 5.4 %collective-permute-start.3 = (bf16[2,2,64,256]{3,2,1,0:T(8,128)(2,1)S(1)}, bf16[2,2,64,256]{3,2,1,0:T(8,128)(2,1)S(1)}, u32[]{:S(2)}, u32[]{:S(2)}) collective-permute-start(bf16[2,2,64,256]{3,2,1,0:T(8,128)(2,1)S(1)} %get-tuple-element.39), channel_id=1, source_target_pairs={{0,8},{8,0},{4,12},{12,4},{16,24},{24,16},{20,28},{28,20},{1,9},{9... | collective-permute-start | bytes 393224 | tf_op jit(solution)/shard_map/ppermute | solution.py:30
  11.3 5.7 %collective-permute-start.5 = (bf16[2,2,64,256]{3,2,1,0:T(8,128)(2,1)S(1)}, bf16[2,2,64,256]{3,2,1,0:T(8,128)(2,1)S(1)}, u32[]{:S(2)}, u32[]{:S(2)}) collective-permute-start(bf16[2,2,64,256]{3,2,1,0:T(8,128)(2,1)S(1)} %get-tuple-element.40), channel_id=1, source_target_pairs={{0,16},{16,0},{4,20},{20,4},{8,24},{24,8},{12,28},{28,12},{1,17},{... | collective-permute-start | bytes 393224 | tf_op jit(solution)/shard_map/ppermute | solution.py:30
  12.8 5.9 %collective-permute-start.7 = (bf16[2,2,64,256]{3,2,1,0:T(8,128)(2,1)S(1)}, bf16[2,2,64,256]{3,2,1,0:T(8,128)(2,1)S(1)}, u32[]{:S(2)}, u32[]{:S(2)}) collective-permute-start(bf16[2,2,64,256]{3,2,1,0:T(8,128)(2,1)S(1)} %get-tuple-element.41), channel_id=1, source_target_pairs={{0,24},{24,0},{4,28},{28,4},{8,16},{16,8},{12,20},{20,12},{1,25},{... | collective-permute-start | bytes 393224 | tf_op jit(solution)/shard_map/ppermute | solution.py:30
  14.3 4.4 %collective-permute-start.2 = (bf16[2,2,64,256]{3,2,1,0:T(8,128)(2,1)S(1)}, bf16[2,2,64,256]{3,2,1,0:T(8,128)(2,1)S(1)}, u32[]{:S(2)}, u32[]{:S(2)}) collective-permute-start(bf16[2,2,64,256]{3,2,1,0:T(8,128)(2,1)S(1)} %get-tuple-element.38.refs_0_), channel_id=1, source_target_pairs={{0,4},{4,0},{8,12},{12,8},{16,20},{20,16},{24,28},{28,24},{1,5},{5... | collective-permute-start | bytes 393224 | tf_op jit(solution)/shard_map/ppermute | solution.py:30
  16.1 2.6 %collective-permute-start.4 = (bf16[2,2,64,256]{3,2,1,0:T(8,128)(2,1)S(1)}, bf16[2,2,64,256]{3,2,1,0:T(8,128)(2,1)S(1)}, u32[]{:S(2)}, u32[]{:S(2)}) collective-permute-start(bf16[2,2,64,256]{3,2,1,0:T(8,128)(2,1)S(1)} %collective-permute-done.3.refs_2_), channel_id=1, source_target_pairs={{0,4},{4,0},{8,12},{12,8},{16,20},{20,16},{24,28},{28,24},{1,5},{5... | collective-permute-start | bytes 393224 | tf_op jit(solution)/shard_map/ppermute | solution.py:30
  17.0 1.7 %collective-permute-start.6 = (bf16[2,2,64,256]{3,2,1,0:T(8,128)(2,1)S(1)}, bf16[2,2,64,256]{3,2,1,0:T(8,128)(2,1)S(1)}, u32[]{:S(2)}, u32[]{:S(2)}) collective-permute-start(bf16[2,2,64,256]{3,2,1,0:T(8,128)(2,1)S(1)} %collective-permute-done.5.refs_4_), channel_id=1, source_target_pairs={{0,4},{4,0},{8,12},{12,8},{16,20},{20,16},{24,28},{28,24},{1,5},{5... | collective-permute-start | bytes 393224 | tf_op jit(solution)/shard_map/ppermute | solution.py:30
  18.7 1.3 %collective-permute-start.8 = (bf16[2,2,64,256]{3,2,1,0:T(8,128)(2,1)S(1)}, bf16[2,2,64,256]{3,2,1,0:T(8,128)(2,1)S(1)}, u32[]{:S(2)}, u32[]{:S(2)}) collective-permute-start(bf16[2,2,64,256]{3,2,1,0:T(8,128)(2,1)S(1)} %collective-permute-done.7.refs_6_), channel_id=1, source_target_pairs={{0,4},{4,0},{8,12},{12,8},{16,20},{20,16},{24,28},{28,24},{1,5},{5... | collective-permute-start | bytes 393224 | tf_op jit(solution)/shard_map/ppermute | solution.py:30
  21.3 3.8 %collective-permute-start.9 = (f32[36,128]{1,0:T(8,128)S(1)}, f32[36,128]{1,0:T(8,128)S(1)}, u32[]{:S(2)}, u32[]{:S(2)}) collective-permute-start(f32[36,128]{1,0:T(8,128)S(1)} %get-tuple-element.43), channel_id=1, source_target_pairs={{0,8},{8,0},{4,12},{12,4},{16,24},{24,16},{20,28},{28,20},{1,9},{9... | collective-permute-start | bytes 55304 | tf_op jit(solution)/shard_map/ppermute | solution.py:30
  22.9 3.8 %collective-permute-start.10 = (f32[36,128]{1,0:T(8,128)S(1)}, f32[36,128]{1,0:T(8,128)S(1)}, u32[]{:S(2)}, u32[]{:S(2)}) collective-permute-start(f32[36,128]{1,0:T(8,128)S(1)} %get-tuple-element.44), channel_id=1, source_target_pairs={{0,16},{16,0},{4,20},{20,4},{8,24},{24,8},{12,28},{28,12},{1,17},{... | collective-permute-start | bytes 55304 | tf_op jit(solution)/shard_map/ppermute | solution.py:30
  24.0 4.7 %collective-permute-start.11 = (f32[36,128]{1,0:T(8,128)S(1)}, f32[36,128]{1,0:T(8,128)S(1)}, u32[]{:S(2)}, u32[]{:S(2)}) collective-permute-start(f32[36,128]{1,0:T(8,128)S(1)} %get-tuple-element.45), channel_id=1, source_target_pairs={{0,24},{24,0},{4,28},{28,4},{8,16},{16,8},{12,20},{20,12},{1,25},{... | collective-permute-start | bytes 55304 | tf_op jit(solution)/shard_map/ppermute | solution.py:30

commit v9 on v8

--- a/solution.py
+++ b/solution.py
@@ -288,13 +288,13 @@
             ) / jnp.sqrt(power_left * power_right + 1e-06)
 
 
-def chip_looks_kernel(root_ref, gap_ref, *refs):
+def chip_looks_kernel(positions, root_ref, gap_ref, *refs):
     tiles, outs, (stack, sums, pooled) = refs[: CHIPS * CORES], refs[CHIPS * CORES : -3], refs[-3:]
     dates, _, _, columns = tiles[0].shape
     me = lax.axis_index("date")
     total = len(tiles) * dates
     scale = 1.0 / (LOOK_AZ * LOOK_RG) ** 0.5
-    for position, tile_ref in enumerate(tiles):
+    for position, tile_ref in zip(positions, tiles):
         stack[position * dates : (position + 1) * dates] = tile_ref[...].astype(jnp.float32)
 
     def partner_of(kind, date):
@@ -367,7 +367,7 @@
             start += rows
 
 
-def chip_place_kernel(*refs):
+def chip_place_kernel(positions, *refs):
     pieces, (ifg_ref, coh_ref) = refs[:CHIPS], refs[CHIPS:]
     dates, _, _, columns = ifg_ref.shape
     mine = lax.axis_index("date") // CORES
@@ -375,7 +375,7 @@
 
         @pl.when(mine == chip)
         def _():
-            for position, piece_ref in enumerate(pieces):
+            for position, piece_ref in zip(positions, pieces):
                 start = (chip ^ position) * CHIP_LOOKS
                 where = slice(start, start + CHIP_LOOKS)
                 for channel in range(CHANNELS):
@@ -503,11 +503,12 @@
         direct = {number: swapped(tiles[number], CORES * number) for number in order}
         other = swapped(own, 1)
         passed = {number: swapped(direct[number], 1) for number in order}
-        held = [own, other]
-        for number in range(1, CHIPS):
+        held, positions = [own, other], [0, 1]
+        for number in order:
             held += [direct[number], passed[number]]
+            positions += [CORES * number, CORES * number + 1]
         results = pl.pallas_call(
-            chip_looks_kernel,
+            functools.partial(chip_looks_kernel, positions),
             out_shape=(pltpu.VMEM((CHANNELS * CHIP_LOOKS, LANES), jnp.float32),) * CHIPS,
             in_specs=[SMEM] * 2 + [VMEM] * len(held),
             out_specs=(VMEM,) * CHIPS,
@@ -520,9 +521,9 @@
             compiler_params=pltpu.CompilerParams(vmem_limit_bytes=GRANT),
         )(root, gap, *[near(tile) for tile in held])
         back = {number: swapped(results[number], CORES * number) for number in order}
-        pieces = [results[0]] + [back[number] for number in range(1, CHIPS)]
+        pieces = [results[0]] + [back[number] for number in order]
         return pl.pallas_call(
-            chip_place_kernel,
+            functools.partial(chip_place_kernel, [0] + order),
             out_shape=out_shape,
             in_specs=[VMEM] * CHIPS,
             out_specs=(VMEM, VMEM),

time: 29.6 us -> 28.9 us (0.976)
  the two profiles are of different devices: /device:TPU:18 before, /device:TPU:8 now
where the time goes in v9:
time: 28.9 us; the launch traced here: 28.6 us
  starting transfers between devices  12.7 us (44%)
  waiting for transfers between devices  9.17 us (32%)
  Pallas kernels  5.32 us (18%)
  between operations  1.34 us (5%)
    ppermute x12, starting transfers between devices, exchanged(): lax.ppermute(array, axis, [route for a, b in pairs for route in ((a, b),...  12.7 us
    ppermute x12, waiting for transfers between devices, exchanged(): lax.ppermute(array, axis, [route for a, b in pairs for route in ((a, b),...  9.17 us
    pallas_call x1, Pallas kernels, body(): pl.pallas_call(start_kernel, out_shape=(pltpu.VMEM(block.shape, block.dty...  1.55 us
    pallas_call x1, Pallas kernels, body(): pl.pallas_call(functools.partial(chip_looks_kernel, positions), out_shape...  1.26 us
    pallas_call x1, Pallas kernels, body(): pl.pallas_call(functools.partial(taps_kernel, chips, tile_lines), out_sha...  1.01 us
    pallas_call x1, Pallas kernels, body(): pl.pallas_call(functools.partial(chip_place_kernel, [0] + order), out_sha...  0.76 us
    pallas_call x1, Pallas kernels, body(): pl.pallas_call(functools.partial(resample_kernel, (line_groups, column_gr...  0.74 us
  transfers between devices with their start and end apart: 12, of which 8 were waited for; matrix products, arithmetic and copies ran while one was open for 0% of the time, Pallas kernels for 4%

profile of v9, /device:TPU:8, one launch (start us, length us, event | category | flops | bytes accessed | tf_op | source)
XLA Modules:
  0.0 28.6 jit_solution(12762535711105660862)
XLA Ops:
  0.6 1.6 %start.1 = (bf16[2,2,256,256]{3,2,1,0:T(8,128)(2,1)S(1)}, bf16[256,64]{1,0:T(8,128)(2,1)S(1)}, bf16[256,64]{1,0:T(8,128)(2,1)S(1)}, s32[16]{0:T(128)S(4)}, s32[1...) custom-call(bf16[2,2,256,256]{3,2,1,0:T(8,128)(2,1)} %x_ref.1, ...), custom_call_target="tpu_custom_call" | custom-call | tf_op jit(solution)/shard_map/start/pallas_call | solution.py:438
  2.2 0.1 collective-permute-start
  2.3 5.0 %collective-permute-start.1 = (bf16[256,64]{1,0:T(8,128)(2,1)S(1)}, bf16[256,64]{1,0:T(8,128)(2,1)S(1)}, u32[]{:S(2)}, u32[]{:S(2)}) collective-permute-start(bf16[256,64]{1,0:T(8,128)(2,1)S(1)} %get-tuple-element.33), channel_id=1, source_target_pairs={{1,2},{2,1},{5,6},{6,5},{9,10},{10,9},{13,14},{14,13},{17,18},{18,... | collective-permute-start | bytes 98312 | tf_op jit(solution)/shard_map/ppermute | solution.py:30
  8.0 1.0 %taps.1 = (bf16[2,256,256]{2,1,0:T(8,128)(2,1)S(1)}, bf16[64,512]{1,0:T(8,128)(2,1)S(1)}, bf16[64,512]{1,0:T(8,128)(2,1)S(1)}, bf16[2,256,256]{2,1,0:T(8,128)(2,1)S(1)}, s32[8]{0:T(128)S(4)}) custom-call(s32[16]{0:T(128)S(4)} %get-tuple-element.24.az_whole, s32[16]{0:T(128)S(4)} %get-tuple-element.25.az_part, s32[16]{0:T(128)S(4)} %get-tuple-element.26.rg_whole, ...), custom_call_target="tpu_custom_call" | custom-call | flops 4000000 | bytes 800000 | tf_op jit(solution)/shard_map/taps/pallas_call | solution.py:457
  9.0 0.0 collective-permute-done.even_ref
  9.0 0.6 %collective-permute-done.1.odd_ref = bf16[256,64]{1,0:T(8,128)(2,1)S(1)} collective-permute-done((bf16[256,64]{1,0:T(8,128)(2,1)S(1)}, bf16[256,64]{1,0:T(8,128)(2,1)S(1)}, u32[]{:S(2)}, u32[]{:S(2)}) %collective-permute-start.1) | collective-permute-done | bytes 32800 | tf_op jit(solution)/shard_map/ppermute | solution.py:30
  9.5 0.7 %resample.1 = (bf16[2,2,64,256]{3,2,1,0:T(8,128)(2,1)S(1)}, bf16[2,2,64,256]{3,2,1,0:T(8,128)(2,1)S(1)}, bf16[2,2,64,256]{3,2,1,0:T(8,128)(2,1)S(1)}, bf16[2,2,64,256]{3,2,1,0:T(8,128)(2,1)S(1)}) custom-call(bf16[2,2,256,256]{3,2,1,0:T(8,128)(2,1)S(1)} %get-tuple-element.31.x_ref, bf16[256,64]{1,0:T(8,128)(2,1)S(1)} %collective-permute-done.even_ref, ...), custom_call_target="tpu_custom_call" | custom-call | tf_op jit(solution)/shard_map/resample/pallas_call | solution.py:477
  10.3 2.5 %collective-permute-start.3 = (bf16[2,2,64,256]{3,2,1,0:T(8,128)(2,1)S(1)}, bf16[2,2,64,256]{3,2,1,0:T(8,128)(2,1)S(1)}, u32[]{:S(2)}, u32[]{:S(2)}) collective-permute-start(bf16[2,2,64,256]{3,2,1,0:T(8,128)(2,1)S(1)} %get-tuple-element.39), channel_id=1, source_target_pairs={{0,24},{24,0},{4,28},{28,4},{8,16},{16,8},{12,20},{20,12},{1,25},{... | collective-permute-start | bytes 393224 | tf_op jit(solution)/shard_map/ppermute | solution.py:30
  12.8 0.5 %collective-permute-start.5 = (bf16[2,2,64,256]{3,2,1,0:T(8,128)(2,1)S(1)}, bf16[2,2,64,256]{3,2,1,0:T(8,128)(2,1)S(1)}, u32[]{:S(2)}, u32[]{:S(2)}) collective-permute-start(bf16[2,2,64,256]{3,2,1,0:T(8,128)(2,1)S(1)} %get-tuple-element.40), channel_id=1, source_target_pairs={{0,16},{16,0},{4,20},{20,4},{8,24},{24,8},{12,28},{28,12},{1,17},{... | collective-permute-start | bytes 393224 | tf_op jit(solution)/shard_map/ppermute | solution.py:30
  13.3 0.5 %collective-permute-start.7 = (bf16[2,2,64,256]{3,2,1,0:T(8,128)(2,1)S(1)}, bf16[2,2,64,256]{3,2,1,0:T(8,128)(2,1)S(1)}, u32[]{:S(2)}, u32[]{:S(2)}) collective-permute-start(bf16[2,2,64,256]{3,2,1,0:T(8,128)(2,1)S(1)} %get-tuple-element.41), channel_id=1, source_target_pairs={{0,8},{8,0},{4,12},{12,4},{16,24},{24,16},{20,28},{28,20},{1,9},{9... | collective-permute-start | bytes 393224 | tf_op jit(solution)/shard_map/ppermute | solution.py:30
  13.8 0.0 collective-permute-start.2
  13.8 3.6 %collective-permute-done.3.refs_2_ = bf16[2,2,64,256]{3,2,1,0:T(8,128)(2,1)S(1)} collective-permute-done((bf16[2,2,64,256]{3,2,1,0:T(8,128)(2,1)S(1)}, bf16[2,2,64,256]{3,2,1,0:T(8,128)(2,1)S(1)}, u32[]{:S(2)}, u32[]{:S(2)}) %collective-permute-start.3) | collective-permute-done | bytes 131104 | tf_op jit(solution)/shard_map/ppermute | solution.py:30
  17.4 0.9 %collective-permute-done.5.refs_4_ = bf16[2,2,64,256]{3,2,1,0:T(8,128)(2,1)S(1)} collective-permute-done((bf16[2,2,64,256]{3,2,1,0:T(8,128)(2,1)S(1)}, bf16[2,2,64,256]{3,2,1,0:T(8,128)(2,1)S(1)}, u32[]{:S(2)}, u32[]{:S(2)}) %collective-permute-start.5) | collective-permute-done | bytes 131104 | tf_op jit(solution)/shard_map/ppermute | solution.py:30
  18.3 0.5 %collective-permute-start.8 = (bf16[2,2,64,256]{3,2,1,0:T(8,128)(2,1)S(1)}, bf16[2,2,64,256]{3,2,1,0:T(8,128)(2,1)S(1)}, u32[]{:S(2)}, u32[]{:S(2)}) collective-permute-start(bf16[2,2,64,256]{3,2,1,0:T(8,128)(2,1)S(1)} %collective-permute-done.7.refs_6_), channel_id=1, source_target_pairs={{0,4},{4,0},{8,12},{12,8},{16,20},{20,16},{24,28},{28,24},{1,5},{5... | collective-permute-start | bytes 393224 | tf_op jit(solution)/shard_map/ppermute | solution.py:30
  18.8 0.8 %collective-permute-done.6.refs_5_ = bf16[2,2,64,256]{3,2,1,0:T(8,128)(2,1)S(1)} collective-permute-done((bf16[2,2,64,256]{3,2,1,0:T(8,128)(2,1)S(1)}, bf16[2,2,64,256]{3,2,1,0:T(8,128)(2,1)S(1)}, u32[]{:S(2)}, u32[]{:S(2)}) %collective-permute-start.6) | collective-permute-done | bytes 131104 | tf_op jit(solution)/shard_map/ppermute | solution.py:30
  19.6 0.2 collective-permute-done.8.refs_7_
  19.8 1.3 %looks.1 = (f32[36,128]{1,0:T(8,128)S(1)}, f32[36,128]{1,0:T(8,128)S(1)}, f32[36,128]{1,0:T(8,128)S(1)}, f32[36,128]{1,0:T(8,128)S(1)}) custom-call(s32[8]{0:T(128)S(4)} %get-tuple-element.29.root_ref, s32[2,16]{1,0:T(2,128)S(4)} %get-tuple-element.30.gap_ref, bf16[2,2,64,256]{3,2,1,0:T(8,128)(2,1)S(1)} %get-tuple-element.38.refs_0_, ...), custom_call_target="tpu_custom_call" | custom-call | tf_op jit(solution)/shard_map/looks/pallas_call | solution.py:510
  21.1 1.7 %collective-permute-start.9 = (f32[36,128]{1,0:T(8,128)S(1)}, f32[36,128]{1,0:T(8,128)S(1)}, u32[]{:S(2)}, u32[]{:S(2)}) collective-permute-start(f32[36,128]{1,0:T(8,128)S(1)} %get-tuple-element.43), channel_id=1, source_target_pairs={{0,24},{24,0},{4,28},{28,4},{8,16},{16,8},{12,20},{20,12},{1,25},{... | collective-permute-start | bytes 55304 | tf_op jit(solution)/shard_map/ppermute | solution.py:30
  22.8 1.2 %collective-permute-start.10 = (f32[36,128]{1,0:T(8,128)S(1)}, f32[36,128]{1,0:T(8,128)S(1)}, u32[]{:S(2)}, u32[]{:S(2)}) collective-permute-start(f32[36,128]{1,0:T(8,128)S(1)} %get-tuple-element.44), channel_id=1, source_target_pairs={{0,16},{16,0},{4,20},{20,4},{8,24},{24,8},{12,28},{28,12},{1,17},{... | collective-permute-start | bytes 55304 | tf_op jit(solution)/shard_map/ppermute | solution.py:30
  24.0 0.6 %collective-permute-start.11 = (f32[36,128]{1,0:T(8,128)S(1)}, f32[36,128]{1,0:T(8,128)S(1)}, u32[]{:S(2)}, u32[]{:S(2)}) collective-permute-start(f32[36,128]{1,0:T(8,128)S(1)} %get-tuple-element.45), channel_id=1, source_target_pairs={{0,8},{8,0},{4,12},{12,4},{16,24},{24,16},{20,28},{28,20},{1,9},{9... | collective-permute-start | bytes 55304 | tf_op jit(solution)/shard_map/ppermute | solution.py:30
  24.7 1.2 %collective-permute-done.9.refs_1_ = f32[36,128]{1,0:T(8,128)S(1)} collective-permute-done((f32[36,128]{1,0:T(8,128)S(1)}, f32[36,128]{1,0:T(8,128)S(1)}, u32[]{:S(2)}, u32[]{:S(2)}) %collective-permute-start.9) | collective-permute-done | bytes 18464 | tf_op jit(solution)/shard_map/ppermute | solution.py:30
  25.9 0.7 %collective-permute-done.10.refs_2_ = f32[36,128]{1,0:T(8,128)S(1)} collective-permute-done((f32[36,128]{1,0:T(8,128)S(1)}, f32[36,128]{1,0:T(8,128)S(1)}, u32[]{:S(2)}, u32[]{:S(2)}) %collective-permute-start.10) | collective-permute-done | bytes 18464 | tf_op jit(solution)/shard_map/ppermute | solution.py:30
  26.6 1.2 %collective-permute-done.11.refs_3_ = f32[36,128]{1,0:T(8,128)S(1)} collective-permute-done((f32[36,128]{1,0:T(8,128)S(1)}, f32[36,128]{1,0:T(8,128)S(1)}, u32[]{:S(2)}, u32[]{:S(2)}) %collective-permute-start.11) | collective-permute-done | bytes 18464 | tf_op jit(solution)/shard_map/ppermute | solution.py:30
  27.8 0.8 %place.1 = (f32[2,6,16,64]{3,2,1,0:T(8,128)}, f32[2,3,16,64]{3,2,1,0:T(8,128)}) custom-call(f32[36,128]{1,0:T(8,128)S(1)} %get-tuple-element.42.refs_0_, f32[36,128]{1,0:T(8,128)S(1)} %collective-permute-done.9.refs_1_, f32[36,128]{1,0:T(8,128)S(1)} %collective-permute-done.10.refs_2_, f32[36,128]{1,0:T(8,128)S(1)} %collective-permute-done.11.refs_3_), custom_call_target="tpu_custom_call" | custom-call | tf_op jit(solution)/shard_map/place/pallas_call | solution.py:525
  (5 shorter events, 0.0 us)
Async XLA Ops:
  2.2 6.8 %collective-permute-start = (bf16[256,64]{1,0:T(8,128)(2,1)S(1)}, bf16[256,64]{1,0:T(8,128)(2,1)S(1)}, u32[]{:S(2)}, u32[]{:S(2)}) collective-permute-start(bf16[256,64]{1,0:T(8,128)(2,1)S(1)} %get-tuple-element.32), channel_id=1, source_target_pairs={{0,1},{1,0},{2,3},{3,2},{4,5},{5,4},{6,7},{7,6},{8,9},{9,8},{10,11... | collective-permute-start | bytes 98312 | tf_op jit(solution)/shard_map/ppermute | solution.py:30
  2.3 7.3 %collective-permute-start.1 = (bf16[256,64]{1,0:T(8,128)(2,1)S(1)}, bf16[256,64]{1,0:T(8,128)(2,1)S(1)}, u32[]{:S(2)}, u32[]{:S(2)}) collective-permute-start(bf16[256,64]{1,0:T(8,128)(2,1)S(1)} %get-tuple-element.33), channel_id=1, source_target_pairs={{1,2},{2,1},{5,6},{6,5},{9,10},{10,9},{13,14},{14,13},{17,18},{18,... | collective-permute-start | bytes 98312 | tf_op jit(solution)/shard_map/ppermute | solution.py:30
  10.3 7.1 %collective-permute-start.3 = (bf16[2,2,64,256]{3,2,1,0:T(8,128)(2,1)S(1)}, bf16[2,2,64,256]{3,2,1,0:T(8,128)(2,1)S(1)}, u32[]{:S(2)}, u32[]{:S(2)}) collective-permute-start(bf16[2,2,64,256]{3,2,1,0:T(8,128)(2,1)S(1)} %get-tuple-element.39), channel_id=1, source_target_pairs={{0,24},{24,0},{4,28},{28,4},{8,16},{16,8},{12,20},{20,12},{1,25},{... | collective-permute-start | bytes 393224 | tf_op jit(solution)/shard_map/ppermute | solution.py:30
  12.8 5.5 %collective-permute-start.5 = (bf16[2,2,64,256]{3,2,1,0:T(8,128)(2,1)S(1)}, bf16[2,2,64,256]{3,2,1,0:T(8,128)(2,1)S(1)}, u32[]{:S(2)}, u32[]{:S(2)}) collective-permute-start(bf16[2,2,64,256]{3,2,1,0:T(8,128)(2,1)S(1)} %get-tuple-element.40), channel_id=1, source_target_pairs={{0,16},{16,0},{4,20},{20,4},{8,24},{24,8},{12,28},{28,12},{1,17},{... | collective-permute-start | bytes 393224 | tf_op jit(solution)/shard_map/ppermute | solution.py:30
  13.3 5.0 %collective-permute-start.7 = (bf16[2,2,64,256]{3,2,1,0:T(8,128)(2,1)S(1)}, bf16[2,2,64,256]{3,2,1,0:T(8,128)(2,1)S(1)}, u32[]{:S(2)}, u32[]{:S(2)}) collective-permute-start(bf16[2,2,64,256]{3,2,1,0:T(8,128)(2,1)S(1)} %get-tuple-element.41), channel_id=1, source_target_pairs={{0,8},{8,0},{4,12},{12,4},{16,24},{24,16},{20,28},{28,20},{1,9},{9... | collective-permute-start | bytes 393224 | tf_op jit(solution)/shard_map/ppermute | solution.py:30
  13.8 5.0 %collective-permute-start.2 = (bf16[2,2,64,256]{3,2,1,0:T(8,128)(2,1)S(1)}, bf16[2,2,64,256]{3,2,1,0:T(8,128)(2,1)S(1)}, u32[]{:S(2)}, u32[]{:S(2)}) collective-permute-start(bf16[2,2,64,256]{3,2,1,0:T(8,128)(2,1)S(1)} %get-tuple-element.38.refs_0_), channel_id=1, source_target_pairs={{0,4},{4,0},{8,12},{12,8},{16,20},{20,16},{24,28},{28,24},{1,5},{5... | collective-permute-start | bytes 393224 | tf_op jit(solution)/shard_map/ppermute | solution.py:30
  17.4 1.4 %collective-permute-start.4 = (bf16[2,2,64,256]{3,2,1,0:T(8,128)(2,1)S(1)}, bf16[2,2,64,256]{3,2,1,0:T(8,128)(2,1)S(1)}, u32[]{:S(2)}, u32[]{:S(2)}) collective-permute-start(bf16[2,2,64,256]{3,2,1,0:T(8,128)(2,1)S(1)} %collective-permute-done.3.refs_2_), channel_id=1, source_target_pairs={{0,4},{4,0},{8,12},{12,8},{16,20},{20,16},{24,28},{28,24},{1,5},{5... | collective-permute-start | bytes 393224 | tf_op jit(solution)/shard_map/ppermute | solution.py:30
  18.3 1.3 %collective-permute-start.6 = (bf16[2,2,64,256]{3,2,1,0:T(8,128)(2,1)S(1)}, bf16[2,2,64,256]{3,2,1,0:T(8,128)(2,1)S(1)}, u32[]{:S(2)}, u32[]{:S(2)}) collective-permute-start(bf16[2,2,64,256]{3,2,1,0:T(8,128)(2,1)S(1)} %collective-permute-done.5.refs_4_), channel_id=1, source_target_pairs={{0,4},{4,0},{8,12},{12,8},{16,20},{20,16},{24,28},{28,24},{1,5},{5... | collective-permute-start | bytes 393224 | tf_op jit(solution)/shard_map/ppermute | solution.py:30
  18.3 1.5 %collective-permute-start.8 = (bf16[2,2,64,256]{3,2,1,0:T(8,128)(2,1)S(1)}, bf16[2,2,64,256]{3,2,1,0:T(8,128)(2,1)S(1)}, u32[]{:S(2)}, u32[]{:S(2)}) collective-permute-start(bf16[2,2,64,256]{3,2,1,0:T(8,128)(2,1)S(1)} %collective-permute-done.7.refs_6_), channel_id=1, source_target_pairs={{0,4},{4,0},{8,12},{12,8},{16,20},{20,16},{24,28},{28,24},{1,5},{5... | collective-permute-start | bytes 393224 | tf_op jit(solution)/shard_map/ppermute | solution.py:30
  21.1 4.8 %collective-permute-start.9 = (f32[36,128]{1,0:T(8,128)S(1)}, f32[36,128]{1,0:T(8,128)S(1)}, u32[]{:S(2)}, u32[]{:S(2)}) collective-permute-start(f32[36,128]{1,0:T(8,128)S(1)} %get-tuple-element.43), channel_id=1, source_target_pairs={{0,24},{24,0},{4,28},{28,4},{8,16},{16,8},{12,20},{20,12},{1,25},{... | collective-permute-start | bytes 55304 | tf_op jit(solution)/shard_map/ppermute | solution.py:30
  22.8 3.8 %collective-permute-start.10 = (f32[36,128]{1,0:T(8,128)S(1)}, f32[36,128]{1,0:T(8,128)S(1)}, u32[]{:S(2)}, u32[]{:S(2)}) collective-permute-start(f32[36,128]{1,0:T(8,128)S(1)} %get-tuple-element.44), channel_id=1, source_target_pairs={{0,16},{16,0},{4,20},{20,4},{8,24},{24,8},{12,28},{28,12},{1,17},{... | collective-permute-start | bytes 55304 | tf_op jit(solution)/shard_map/ppermute | solution.py:30
  24.0 3.8 %collective-permute-start.11 = (f32[36,128]{1,0:T(8,128)S(1)}, f32[36,128]{1,0:T(8,128)S(1)}, u32[]{:S(2)}, u32[]{:S(2)}) collective-permute-start(f32[36,128]{1,0:T(8,128)S(1)} %get-tuple-element.45), channel_id=1, source_target_pairs={{0,8},{8,0},{4,12},{12,4},{16,24},{24,16},{20,28},{28,20},{1,9},{9... | collective-permute-start | bytes 55304 | tf_op jit(solution)/shard_map/ppermute | solution.py:30

commit v10 on v9

--- a/solution.py
+++ b/solution.py
@@ -122,27 +122,26 @@
     rg_whole,
     rg_part,
     sweeps,
-    master_ref,
-    own_ref,
+    x_ref,
+    inner_ref,
     low_ref,
     high_ref,
     line_ref,
-    root_ref,
 ):
-    dates, columns, _ = own_ref.shape
-    lines = line_ref.shape[1]
+    dates, parts, lines, columns = x_ref.shape
     edge_rows = low_ref.shape[0]
-    parts = edge_rows // MARGIN // dates
     centre = TAPS // 2 - 1
-    for number in range(root_ref.shape[0]):
-        root_ref[number] = master_ref[0]
     present = [lax.axis_index("date") * dates + slot for slot in range(dates)]
     table = weight_rows([rg_part[d] for d in present] + [az_part[d] for d in present])
     for slot, date in enumerate(present):
         shift = centre - rg_whole[date]
         weights = table[slot : slot + 1]
         row, col = iotas(columns, columns)
-        own_ref[slot] = banded(row - col + shift, weights).astype(jnp.bfloat16)
+        own = banded(row - col + shift, weights).astype(jnp.bfloat16)
+        for part in range(parts):
+            inner_ref[slot, part] = jnp.dot(
+                x_ref[slot, part], own, preferred_element_type=jnp.float32
+            )
         row, col = iotas(edge_rows, LANES)
         low = banded(row % MARGIN - MARGIN - col + shift, weights)
         high = banded(row % MARGIN + LANES - col + shift, weights)
@@ -160,9 +159,9 @@
         line_ref[slot] = jnp.where(usable, band, 0.0).astype(jnp.bfloat16)
 
 
-def resample_kernel(split, x_ref, even_ref, odd_ref, own_ref, low_ref, high_ref, line_ref, *refs):
+def resample_kernel(split, inner_ref, even_ref, odd_ref, low_ref, high_ref, line_ref, *refs):
     *outs, edges = refs
-    dates, parts, _, columns = x_ref.shape
+    dates, parts, _, columns = inner_ref.shape
     line_groups, column_groups, tile_lines, tile_columns = split
     backward = lax.axis_index("range") % 2
     edges[1 - backward] = even_ref[...]
@@ -172,8 +171,10 @@
     for slot in range(dates):
         for part in range(parts):
             spot = slice((slot * parts + part) * LANES, (slot * parts + part + 1) * LANES)
-            ranged = jnp.dot(x_ref[slot, part], own_ref[slot], preferred_element_type=jnp.float32)
-            pieces = [ranged[:, start : start + LANES] for start in range(0, columns, LANES)]
+            pieces = [
+                inner_ref[slot, part, :, start : start + LANES]
+                for start in range(0, columns, LANES)
+            ]
             pieces[0] += low[:, spot]
             pieces[-1] += high[:, spot]
             ranged = jnp.concatenate(pieces, axis=1)
@@ -454,21 +455,20 @@
     odd = exchanged(odd, "range", [(j, j + 1) for j in range(1, width - 1, 2)])
     even = exchanged(even, "range", [(j, j + 1) for j in range(0, width - 1, 2)])
 
-    own_taps, low_taps, high_taps, line_taps, root = pl.pallas_call(
+    inner, low_taps, high_taps, line_taps = pl.pallas_call(
         functools.partial(taps_kernel, chips, tile_lines),
         out_shape=(
-            pltpu.VMEM((dates, columns, columns), jnp.bfloat16),
+            pltpu.VMEM(block.shape, jnp.float32),
             pltpu.VMEM((images * MARGIN, images * LANES), jnp.bfloat16),
             pltpu.VMEM((images * MARGIN, images * LANES), jnp.bfloat16),
             pltpu.VMEM((dates, lines, lines), jnp.bfloat16),
-            pltpu.SMEM((8,), jnp.int32),
         ),
-        in_specs=[SMEM] * (len(small) + 1),
-        out_specs=(VMEM,) * 4 + (SMEM,),
+        in_specs=[SMEM] * len(small) + [VMEM],
+        out_specs=(VMEM,) * 4,
         cost_estimate=pl.CostEstimate(flops=4000000, bytes_accessed=800000, transcendentals=0),
         name="taps",
         compiler_params=pltpu.CompilerParams(vmem_limit_bytes=GRANT),
-    )(*small, master_epoch_image)
+    )(*small, near(block))
     tile = (dates, parts, tile_lines, tile_columns)
     if chips:
         out_shape = (pltpu.VMEM(tile, jnp.bfloat16),) * CHIPS
@@ -479,14 +479,13 @@
             resample_kernel, (line_groups, column_groups, tile_lines, tile_columns)
         ),
         out_shape=out_shape,
-        in_specs=[VMEM] * 7,
+        in_specs=[VMEM] * 6,
         out_specs=(VMEM,) * len(out_shape),
         scratch_shapes=[pltpu.VMEM((2,) + even.shape, even.dtype)],
         name="resample",
         compiler_params=pltpu.CompilerParams(vmem_limit_bytes=GRANT),
-    )(*[near(array) for array in (block, even, odd, own_taps, low_taps, high_taps, line_taps)])
-
-    root = pltpu.with_memory_space_constraint(root, pltpu.SMEM)
+    )(*[near(array) for array in (inner, even, odd, low_taps, high_taps, line_taps)])
+
     rows, cols = lines // LOOK_AZ, columns // LOOK_RG
     out_shape = (
         jax.ShapeDtypeStruct((dates, 2 * KINDS, rows, cols), jnp.float32),
@@ -519,7 +518,7 @@
             ],
             name="looks",
             compiler_params=pltpu.CompilerParams(vmem_limit_bytes=GRANT),
-        )(root, gap, *[near(tile) for tile in held])
+        )(master_epoch_image, gap, *[near(tile) for tile in held])
         back = {number: swapped(results[number], CORES * number) for number in order}
         pieces = [results[0]] + [back[number] for number in order]
         return pl.pallas_call(
@@ -545,7 +544,7 @@
         ],
         name="looks",
         compiler_params=pltpu.CompilerParams(vmem_limit_bytes=GRANT),
-    )(root, gap, near(tiles))
+    )(master_epoch_image, gap, near(tiles))
     results = lax.all_to_all(results, "date", 0, 0)
 
     if column_groups == 1:

time: 28.9 us -> 28.9 us (level)
  no operation moved by 1% of the time
where the time goes in v10:
time: 28.9 us; the launch traced here: 28.6 us
  starting transfers between devices  12.7 us (44%)
  waiting for transfers between devices  9.34 us (32%)
  Pallas kernels  5.17 us (18%)
  between operations  1.36 us (5%)
    ppermute x12, starting transfers between devices, exchanged(): lax.ppermute(array, axis, [route for a, b in pairs for route in ((a, b),...  12.7 us
    ppermute x12, waiting for transfers between devices, exchanged(): lax.ppermute(array, axis, [route for a, b in pairs for route in ((a, b),...  9.34 us
    pallas_call x1, Pallas kernels, body(): pl.pallas_call(start_kernel, out_shape=(pltpu.VMEM(block.shape, block.dty...  1.55 us
    pallas_call x1, Pallas kernels, body(): pl.pallas_call(functools.partial(chip_looks_kernel, positions), out_shape...  1.26 us
    pallas_call x1, Pallas kernels, body(): pl.pallas_call(functools.partial(taps_kernel, chips, tile_lines), out_sha...  1.04 us
    pallas_call x1, Pallas kernels, body(): pl.pallas_call(functools.partial(chip_place_kernel, [0] + order), out_sha...  0.76 us
  transfers between devices with their start and end apart: 12, of which 8 were waited for; matrix products, arithmetic and copies ran while one was open for 0% of the time, Pallas kernels for 4%

profile of v10, /device:TPU:8, one launch (start us, length us, event | category | flops | bytes accessed | tf_op | source)
XLA Modules:
  0.0 28.6 jit_solution(8726898542196821805)
XLA Ops:
  0.6 1.6 %start.1 = (bf16[2,2,256,256]{3,2,1,0:T(8,128)(2,1)S(1)}, bf16[256,64]{1,0:T(8,128)(2,1)S(1)}, bf16[256,64]{1,0:T(8,128)(2,1)S(1)}, s32[16]{0:T(128)S(4)}, s32[1...) custom-call(bf16[2,2,256,256]{3,2,1,0:T(8,128)(2,1)} %x_ref.1, ...), custom_call_target="tpu_custom_call" | custom-call | tf_op jit(solution)/shard_map/start/pallas_call | solution.py:439
  2.2 0.1 collective-permute-start
  2.3 5.0 %collective-permute-start.1 = (bf16[256,64]{1,0:T(8,128)(2,1)S(1)}, bf16[256,64]{1,0:T(8,128)(2,1)S(1)}, u32[]{:S(2)}, u32[]{:S(2)}) collective-permute-start(bf16[256,64]{1,0:T(8,128)(2,1)S(1)} %get-tuple-element.32), channel_id=1, source_target_pairs={{1,2},{2,1},{5,6},{6,5},{9,10},{10,9},{13,14},{14,13},{17,18},{18,... | collective-permute-start | bytes 98312 | tf_op jit(solution)/shard_map/ppermute | solution.py:30
  7.3 1.0 %taps.1 = (f32[2,2,256,256]{3,2,1,0:T(8,128)S(1)}, bf16[64,512]{1,0:T(8,128)(2,1)S(1)}, bf16[64,512]{1,0:T(8,128)(2,1)S(1)}, bf16[2,256,256]{2,1,0:T(8,128)(2,1)S(1)}) custom-call(s32[16]{0:T(128)S(4)} %get-tuple-element.24.az_whole, s32[16]{0:T(128)S(4)} %get-tuple-element.25.az_part, s32[16]{0:T(128)S(4)} %get-tuple-element.26.rg_whole, ...), custom_call_target="tpu_custom_call" | custom-call | flops 4000000 | bytes 800000 | tf_op jit(solution)/shard_map/taps/pallas_call | solution.py:458
  8.4 0.0 collective-permute-done.even_ref
  8.4 1.2 %collective-permute-done.1.odd_ref = bf16[256,64]{1,0:T(8,128)(2,1)S(1)} collective-permute-done((bf16[256,64]{1,0:T(8,128)(2,1)S(1)}, bf16[256,64]{1,0:T(8,128)(2,1)S(1)}, u32[]{:S(2)}, u32[]{:S(2)}) %collective-permute-start.1) | collective-permute-done | bytes 32800 | tf_op jit(solution)/shard_map/ppermute | solution.py:30
  9.5 0.6 %resample.1 = (bf16[2,2,64,256]{3,2,1,0:T(8,128)(2,1)S(1)}, bf16[2,2,64,256]{3,2,1,0:T(8,128)(2,1)S(1)}, bf16[2,2,64,256]{3,2,1,0:T(8,128)(2,1)S(1)}, bf16[2,2,64,256]{3,2,1,0:T(8,128)(2,1)S(1)}) custom-call(f32[2,2,256,256]{3,2,1,0:T(8,128)S(1)} %get-tuple-element.30.inner_ref, bf16[256,64]{1,0:T(8,128)(2,1)S(1)} %collective-permute-done.even_ref, ...), custom_call_target="tpu_custom_call" | custom-call | tf_op jit(solution)/shard_map/resample/pallas_call | solution.py:477
  10.1 2.5 %collective-permute-start.3 = (bf16[2,2,64,256]{3,2,1,0:T(8,128)(2,1)S(1)}, bf16[2,2,64,256]{3,2,1,0:T(8,128)(2,1)S(1)}, u32[]{:S(2)}, u32[]{:S(2)}) collective-permute-start(bf16[2,2,64,256]{3,2,1,0:T(8,128)(2,1)S(1)} %get-tuple-element.37), channel_id=1, source_target_pairs={{0,24},{24,0},{4,28},{28,4},{8,16},{16,8},{12,20},{20,12},{1,25},{... | collective-permute-start | bytes 393224 | tf_op jit(solution)/shard_map/ppermute | solution.py:30
  12.6 0.5 %collective-permute-start.5 = (bf16[2,2,64,256]{3,2,1,0:T(8,128)(2,1)S(1)}, bf16[2,2,64,256]{3,2,1,0:T(8,128)(2,1)S(1)}, u32[]{:S(2)}, u32[]{:S(2)}) collective-permute-start(bf16[2,2,64,256]{3,2,1,0:T(8,128)(2,1)S(1)} %get-tuple-element.38), channel_id=1, source_target_pairs={{0,16},{16,0},{4,20},{20,4},{8,24},{24,8},{12,28},{28,12},{1,17},{... | collective-permute-start | bytes 393224 | tf_op jit(solution)/shard_map/ppermute | solution.py:30
  13.1 0.5 %collective-permute-start.7 = (bf16[2,2,64,256]{3,2,1,0:T(8,128)(2,1)S(1)}, bf16[2,2,64,256]{3,2,1,0:T(8,128)(2,1)S(1)}, u32[]{:S(2)}, u32[]{:S(2)}) collective-permute-start(bf16[2,2,64,256]{3,2,1,0:T(8,128)(2,1)S(1)} %get-tuple-element.39), channel_id=1, source_target_pairs={{0,8},{8,0},{4,12},{12,4},{16,24},{24,16},{20,28},{28,20},{1,9},{9... | collective-permute-start | bytes 393224 | tf_op jit(solution)/shard_map/ppermute | solution.py:30
  13.7 0.0 collective-permute-start.2
  13.7 3.6 %collective-permute-done.3.refs_2_ = bf16[2,2,64,256]{3,2,1,0:T(8,128)(2,1)S(1)} collective-permute-done((bf16[2,2,64,256]{3,2,1,0:T(8,128)(2,1)S(1)}, bf16[2,2,64,256]{3,2,1,0:T(8,128)(2,1)S(1)}, u32[]{:S(2)}, u32[]{:S(2)}) %collective-permute-start.3) | collective-permute-done | bytes 131104 | tf_op jit(solution)/shard_map/ppermute | solution.py:30
  17.3 0.9 %collective-permute-done.5.refs_4_ = bf16[2,2,64,256]{3,2,1,0:T(8,128)(2,1)S(1)} collective-permute-done((bf16[2,2,64,256]{3,2,1,0:T(8,128)(2,1)S(1)}, bf16[2,2,64,256]{3,2,1,0:T(8,128)(2,1)S(1)}, u32[]{:S(2)}, u32[]{:S(2)}) %collective-permute-start.5) | collective-permute-done | bytes 131104 | tf_op jit(solution)/shard_map/ppermute | solution.py:30
  18.1 0.5 %collective-permute-start.8 = (bf16[2,2,64,256]{3,2,1,0:T(8,128)(2,1)S(1)}, bf16[2,2,64,256]{3,2,1,0:T(8,128)(2,1)S(1)}, u32[]{:S(2)}, u32[]{:S(2)}) collective-permute-start(bf16[2,2,64,256]{3,2,1,0:T(8,128)(2,1)S(1)} %collective-permute-done.7.refs_6_), channel_id=1, source_target_pairs={{0,4},{4,0},{8,12},{12,8},{16,20},{20,16},{24,28},{28,24},{1,5},{5... | collective-permute-start | bytes 393224 | tf_op jit(solution)/shard_map/ppermute | solution.py:30
  19.3 0.2 collective-permute-done.6.refs_5_
  19.5 0.2 collective-permute-done.8.refs_7_
  19.7 1.3 %looks.1 = (f32[36,128]{1,0:T(8,128)S(1)}, f32[36,128]{1,0:T(8,128)S(1)}, f32[36,128]{1,0:T(8,128)S(1)}, f32[36,128]{1,0:T(8,128)S(1)}) custom-call(s32[1]{0:T(128)S(6)} %copy.10.root_ref, s32[2,16]{1,0:T(2,128)S(4)} %get-tuple-element.23.gap_ref, bf16[2,2,64,256]{3,2,1,0:T(8,128)(2,1)S(1)} %get-tuple-element.36.refs_0_, ...), custom_call_target="tpu_custom_call" | custom-call | tf_op jit(solution)/shard_map/looks/pallas_call | solution.py:509
  20.9 1.4 %collective-permute-start.10 = (f32[36,128]{1,0:T(8,128)S(1)}, f32[36,128]{1,0:T(8,128)S(1)}, u32[]{:S(2)}, u32[]{:S(2)}) collective-permute-start(f32[36,128]{1,0:T(8,128)S(1)} %get-tuple-element.42), channel_id=1, source_target_pairs={{0,16},{16,0},{4,20},{20,4},{8,24},{24,8},{12,28},{28,12},{1,17},{... | collective-permute-start | bytes 55304 | tf_op jit(solution)/shard_map/ppermute | solution.py:30
  22.4 0.8 %collective-permute-start.11 = (f32[36,128]{1,0:T(8,128)S(1)}, f32[36,128]{1,0:T(8,128)S(1)}, u32[]{:S(2)}, u32[]{:S(2)}) collective-permute-start(f32[36,128]{1,0:T(8,128)S(1)} %get-tuple-element.43), channel_id=1, source_target_pairs={{0,8},{8,0},{4,12},{12,4},{16,24},{24,16},{20,28},{28,20},{1,9},{9... | collective-permute-start | bytes 55304 | tf_op jit(solution)/shard_map/ppermute | solution.py:30
  23.2 1.3 %collective-permute-start.9 = (f32[36,128]{1,0:T(8,128)S(1)}, f32[36,128]{1,0:T(8,128)S(1)}, u32[]{:S(2)}, u32[]{:S(2)}) collective-permute-start(f32[36,128]{1,0:T(8,128)S(1)} %get-tuple-element.41), channel_id=1, source_target_pairs={{0,24},{24,0},{4,28},{28,4},{8,16},{16,8},{12,20},{20,12},{1,25},{... | collective-permute-start | bytes 55304 | tf_op jit(solution)/shard_map/ppermute | solution.py:30
  24.5 0.3 %collective-permute-done.10.refs_2_ = f32[36,128]{1,0:T(8,128)S(1)} collective-permute-done((f32[36,128]{1,0:T(8,128)S(1)}, f32[36,128]{1,0:T(8,128)S(1)}, u32[]{:S(2)}, u32[]{:S(2)}) %collective-permute-start.10) | collective-permute-done | bytes 18464 | tf_op jit(solution)/shard_map/ppermute | solution.py:30
  24.8 1.4 %collective-permute-done.11.refs_3_ = f32[36,128]{1,0:T(8,128)S(1)} collective-permute-done((f32[36,128]{1,0:T(8,128)S(1)}, f32[36,128]{1,0:T(8,128)S(1)}, u32[]{:S(2)}, u32[]{:S(2)}) %collective-permute-start.11) | collective-permute-done | bytes 18464 | tf_op jit(solution)/shard_map/ppermute | solution.py:30
  26.1 1.7 %collective-permute-done.9.refs_1_ = f32[36,128]{1,0:T(8,128)S(1)} collective-permute-done((f32[36,128]{1,0:T(8,128)S(1)}, f32[36,128]{1,0:T(8,128)S(1)}, u32[]{:S(2)}, u32[]{:S(2)}) %collective-permute-start.9) | collective-permute-done | bytes 18464 | tf_op jit(solution)/shard_map/ppermute | solution.py:30
  27.8 0.8 %place.1 = (f32[2,6,16,64]{3,2,1,0:T(8,128)}, f32[2,3,16,64]{3,2,1,0:T(8,128)}) custom-call(f32[36,128]{1,0:T(8,128)S(1)} %get-tuple-element.40.refs_0_, f32[36,128]{1,0:T(8,128)S(1)} %collective-permute-done.9.refs_1_, f32[36,128]{1,0:T(8,128)S(1)} %collective-permute-done.10.refs_2_, f32[36,128]{1,0:T(8,128)S(1)} %collective-permute-done.11.refs_3_), custom_call_target="tpu_custom_call" | custom-call | tf_op jit(solution)/shard_map/place/pallas_call | solution.py:524
  (5 shorter events, 0.0 us)
Async XLA Ops:
  2.2 6.2 %collective-permute-start = (bf16[256,64]{1,0:T(8,128)(2,1)S(1)}, bf16[256,64]{1,0:T(8,128)(2,1)S(1)}, u32[]{:S(2)}, u32[]{:S(2)}) collective-permute-start(bf16[256,64]{1,0:T(8,128)(2,1)S(1)} %get-tuple-element.31), channel_id=1, source_target_pairs={{0,1},{1,0},{2,3},{3,2},{4,5},{5,4},{6,7},{7,6},{8,9},{9,8},{10,11... | collective-permute-start | bytes 98312 | tf_op jit(solution)/shard_map/ppermute | solution.py:30
  2.3 7.3 %collective-permute-start.1 = (bf16[256,64]{1,0:T(8,128)(2,1)S(1)}, bf16[256,64]{1,0:T(8,128)(2,1)S(1)}, u32[]{:S(2)}, u32[]{:S(2)}) collective-permute-start(bf16[256,64]{1,0:T(8,128)(2,1)S(1)} %get-tuple-element.32), channel_id=1, source_target_pairs={{1,2},{2,1},{5,6},{6,5},{9,10},{10,9},{13,14},{14,13},{17,18},{18,... | collective-permute-start | bytes 98312 | tf_op jit(solution)/shard_map/ppermute | solution.py:30
  10.1 7.2 %collective-permute-start.3 = (bf16[2,2,64,256]{3,2,1,0:T(8,128)(2,1)S(1)}, bf16[2,2,64,256]{3,2,1,0:T(8,128)(2,1)S(1)}, u32[]{:S(2)}, u32[]{:S(2)}) collective-permute-start(bf16[2,2,64,256]{3,2,1,0:T(8,128)(2,1)S(1)} %get-tuple-element.37), channel_id=1, source_target_pairs={{0,24},{24,0},{4,28},{28,4},{8,16},{16,8},{12,20},{20,12},{1,25},{... | collective-permute-start | bytes 393224 | tf_op jit(solution)/shard_map/ppermute | solution.py:30
  12.6 5.5 %collective-permute-start.5 = (bf16[2,2,64,256]{3,2,1,0:T(8,128)(2,1)S(1)}, bf16[2,2,64,256]{3,2,1,0:T(8,128)(2,1)S(1)}, u32[]{:S(2)}, u32[]{:S(2)}) collective-permute-start(bf16[2,2,64,256]{3,2,1,0:T(8,128)(2,1)S(1)} %get-tuple-element.38), channel_id=1, source_target_pairs={{0,16},{16,0},{4,20},{20,4},{8,24},{24,8},{12,28},{28,12},{1,17},{... | collective-permute-start | bytes 393224 | tf_op jit(solution)/shard_map/ppermute | solution.py:30
  13.1 5.0 %collective-permute-start.7 = (bf16[2,2,64,256]{3,2,1,0:T(8,128)(2,1)S(1)}, bf16[2,2,64,256]{3,2,1,0:T(8,128)(2,1)S(1)}, u32[]{:S(2)}, u32[]{:S(2)}) collective-permute-start(bf16[2,2,64,256]{3,2,1,0:T(8,128)(2,1)S(1)} %get-tuple-element.39), channel_id=1, source_target_pairs={{0,8},{8,0},{4,12},{12,4},{16,24},{24,16},{20,28},{28,20},{1,9},{9... | collective-permute-start | bytes 393224 | tf_op jit(solution)/shard_map/ppermute | solution.py:30
  13.7 5.6 %collective-permute-start.2 = (bf16[2,2,64,256]{3,2,1,0:T(8,128)(2,1)S(1)}, bf16[2,2,64,256]{3,2,1,0:T(8,128)(2,1)S(1)}, u32[]{:S(2)}, u32[]{:S(2)}) collective-permute-start(bf16[2,2,64,256]{3,2,1,0:T(8,128)(2,1)S(1)} %get-tuple-element.36.refs_0_), channel_id=1, source_target_pairs={{0,4},{4,0},{8,12},{12,8},{16,20},{20,16},{24,28},{28,24},{1,5},{5... | collective-permute-start | bytes 393224 | tf_op jit(solution)/shard_map/ppermute | solution.py:30
  17.3 2.0 %collective-permute-start.4 = (bf16[2,2,64,256]{3,2,1,0:T(8,128)(2,1)S(1)}, bf16[2,2,64,256]{3,2,1,0:T(8,128)(2,1)S(1)}, u32[]{:S(2)}, u32[]{:S(2)}) collective-permute-start(bf16[2,2,64,256]{3,2,1,0:T(8,128)(2,1)S(1)} %collective-permute-done.3.refs_2_), channel_id=1, source_target_pairs={{0,4},{4,0},{8,12},{12,8},{16,20},{20,16},{24,28},{28,24},{1,5},{5... | collective-permute-start | bytes 393224 | tf_op jit(solution)/shard_map/ppermute | solution.py:30
  18.1 1.3 %collective-permute-start.6 = (bf16[2,2,64,256]{3,2,1,0:T(8,128)(2,1)S(1)}, bf16[2,2,64,256]{3,2,1,0:T(8,128)(2,1)S(1)}, u32[]{:S(2)}, u32[]{:S(2)}) collective-permute-start(bf16[2,2,64,256]{3,2,1,0:T(8,128)(2,1)S(1)} %collective-permute-done.5.refs_4_), channel_id=1, source_target_pairs={{0,4},{4,0},{8,12},{12,8},{16,20},{20,16},{24,28},{28,24},{1,5},{5... | collective-permute-start | bytes 393224 | tf_op jit(solution)/shard_map/ppermute | solution.py:30
  18.1 1.5 %collective-permute-start.8 = (bf16[2,2,64,256]{3,2,1,0:T(8,128)(2,1)S(1)}, bf16[2,2,64,256]{3,2,1,0:T(8,128)(2,1)S(1)}, u32[]{:S(2)}, u32[]{:S(2)}) collective-permute-start(bf16[2,2,64,256]{3,2,1,0:T(8,128)(2,1)S(1)} %collective-permute-done.7.refs_6_), channel_id=1, source_target_pairs={{0,4},{4,0},{8,12},{12,8},{16,20},{20,16},{24,28},{28,24},{1,5},{5... | collective-permute-start | bytes 393224 | tf_op jit(solution)/shard_map/ppermute | solution.py:30
  20.9 3.8 %collective-permute-start.10 = (f32[36,128]{1,0:T(8,128)S(1)}, f32[36,128]{1,0:T(8,128)S(1)}, u32[]{:S(2)}, u32[]{:S(2)}) collective-permute-start(f32[36,128]{1,0:T(8,128)S(1)} %get-tuple-element.42), channel_id=1, source_target_pairs={{0,16},{16,0},{4,20},{20,4},{8,24},{24,8},{12,28},{28,12},{1,17},{... | collective-permute-start | bytes 55304 | tf_op jit(solution)/shard_map/ppermute | solution.py:30
  22.4 3.8 %collective-permute-start.11 = (f32[36,128]{1,0:T(8,128)S(1)}, f32[36,128]{1,0:T(8,128)S(1)}, u32[]{:S(2)}, u32[]{:S(2)}) collective-permute-start(f32[36,128]{1,0:T(8,128)S(1)} %get-tuple-element.43), channel_id=1, source_target_pairs={{0,8},{8,0},{4,12},{12,4},{16,24},{24,16},{20,28},{28,20},{1,9},{9... | collective-permute-start | bytes 55304 | tf_op jit(solution)/shard_map/ppermute | solution.py:30
  23.2 4.7 %collective-permute-start.9 = (f32[36,128]{1,0:T(8,128)S(1)}, f32[36,128]{1,0:T(8,128)S(1)}, u32[]{:S(2)}, u32[]{:S(2)}) collective-permute-start(f32[36,128]{1,0:T(8,128)S(1)} %get-tuple-element.41), channel_id=1, source_target_pairs={{0,24},{24,0},{4,28},{28,4},{8,16},{16,8},{12,20},{20,12},{1,25},{... | collective-permute-start | bytes 55304 | tf_op jit(solution)/shard_map/ppermute | solution.py:30

commit v11 on v10

--- a/solution.py
+++ b/solution.py
@@ -83,7 +83,7 @@
 
 
 def start_kernel(x_ref, *refs):
-    dates, parts, _, columns = x_ref.shape
+    dates, parts, lines, columns = x_ref.shape
     images = [(slot, part) for slot in range(dates) for part in range(parts)]
     count = (len(refs) - 4) // 2
     near_ref, even_ref, odd_ref = refs[count : count + 3]
@@ -99,7 +99,6 @@
     forward = lax.axis_index("range") % 2 == 0
     for number, (slot, part) in enumerate(images):
         copies[number].wait()
-        spot = slice(number * MARGIN, (number + 1) * MARGIN)
         for parity, last_ref, first_ref in (
             (forward, even_ref, odd_ref),
             (jnp.logical_not(forward), odd_ref, even_ref),
@@ -107,8 +106,12 @@
 
             @pl.when(parity)
             def _():
-                last_ref[:, spot] = near_ref[slot, part, :, columns - MARGIN :]
-                first_ref[:, spot] = near_ref[slot, part, :, :MARGIN]
+                for half in range(2):
+                    rows = slice(half * (lines // 2), (half + 1) * (lines // 2))
+                    start = (half * len(images) + number) * MARGIN
+                    spot = slice(start, start + MARGIN)
+                    last_ref[:, spot] = near_ref[slot, part, rows, columns - MARGIN :]
+                    first_ref[:, spot] = near_ref[slot, part, rows, :MARGIN]
 
     for copy in copies[len(images) :]:
         copy.wait()
@@ -164,8 +167,12 @@
     dates, parts, _, columns = inner_ref.shape
     line_groups, column_groups, tile_lines, tile_columns = split
     backward = lax.axis_index("range") % 2
-    edges[1 - backward] = even_ref[...]
-    edges[backward] = odd_ref[...]
+    height, width = even_ref.shape
+    for half in range(2):
+        rows = slice(half * height, (half + 1) * height)
+        spot = slice(half * (width // 2), (half + 1) * (width // 2))
+        edges[1 - backward, rows, :] = even_ref[:, spot]
+        edges[backward, rows, :] = odd_ref[:, spot]
     low = jnp.dot(edges[0], low_ref[...], preferred_element_type=jnp.float32)
     high = jnp.dot(edges[1], high_ref[...], preferred_element_type=jnp.float32)
     for slot in range(dates):
@@ -440,8 +447,8 @@
         start_kernel,
         out_shape=(
             pltpu.VMEM(block.shape, block.dtype),
-            pltpu.VMEM((lines, images * MARGIN), jnp.bfloat16),
-            pltpu.VMEM((lines, images * MARGIN), jnp.bfloat16),
+            pltpu.VMEM((lines // 2, 2 * images * MARGIN), jnp.bfloat16),
+            pltpu.VMEM((lines // 2, 2 * images * MARGIN), jnp.bfloat16),
             *[pltpu.SMEM(array.shape, array.dtype) for array in arguments[1:]],
         ),
         in_specs=[pl.BlockSpec(memory_space=pltpu.HBM)] * len(arguments),
@@ -481,7 +488,7 @@
         out_shape=out_shape,
         in_specs=[VMEM] * 6,
         out_specs=(VMEM,) * len(out_shape),
-        scratch_shapes=[pltpu.VMEM((2,) + even.shape, even.dtype)],
+        scratch_shapes=[pltpu.VMEM((2, lines, images * MARGIN), jnp.bfloat16)],
         name="resample",
         compiler_params=pltpu.CompilerParams(vmem_limit_bytes=GRANT),
     )(*[near(array) for array in (inner, even, odd, low_taps, high_taps, line_taps)])
@@ -520,9 +527,10 @@
             compiler_params=pltpu.CompilerParams(vmem_limit_bytes=GRANT),
         )(master_epoch_image, gap, *[near(tile) for tile in held])
         back = {number: swapped(results[number], CORES * number) for number in order}
-        pieces = [results[0]] + [back[number] for number in order]
+        last = [1, 3, 2]
+        pieces = [results[0]] + [back[number] for number in last]
         return pl.pallas_call(
-            functools.partial(chip_place_kernel, [0] + order),
+            functools.partial(chip_place_kernel, [0] + last),
             out_shape=out_shape,
             in_specs=[VMEM] * CHIPS,
             out_specs=(VMEM, VMEM),

time: 28.9 us -> 28.4 us (0.983)
  waiting for transfers between devices: 9.34 us -> 8.73 us
    ppermute x12, waiting for transfers between devices: 9.34 us -> 8.73 us  [exchanged(): lax.ppermute(array, axis, [route for a, b in pairs for route in ((a, b),...]
where the time goes in v11:
time: 28.4 us; the launch traced here: 28 us
  starting transfers between devices  12.7 us (45%)
  waiting for transfers between devices  8.73 us (31%)
  Pallas kernels  5.2 us (18%)
  between operations  1.36 us (5%)
    ppermute x12, starting transfers between devices, exchanged(): lax.ppermute(array, axis, [route for a, b in pairs for route in ((a, b),...  12.7 us
    ppermute x12, waiting for transfers between devices, exchanged(): lax.ppermute(array, axis, [route for a, b in pairs for route in ((a, b),...  8.73 us
    pallas_call x1, Pallas kernels, body(): pl.pallas_call(start_kernel, out_shape=(pltpu.VMEM(block.shape, block.dty...  1.55 us
    pallas_call x1, Pallas kernels, body(): pl.pallas_call(functools.partial(chip_looks_kernel, positions), out_shape...  1.26 us
    pallas_call x1, Pallas kernels, body(): pl.pallas_call(functools.partial(taps_kernel, chips, tile_lines), out_sha...  1.04 us
    pallas_call x1, Pallas kernels, body(): pl.pallas_call(functools.partial(chip_place_kernel, [0] + last), out_shap...  0.76 us
    pallas_call x1, Pallas kernels, body(): pl.pallas_call(functools.partial(resample_kernel, (line_groups, column_gr...  0.58 us
  transfers between devices with their start and end apart: 12, of which 8 were waited for; matrix products, arithmetic and copies ran while one was open for 0% of the time, Pallas kernels for 4%

profile of v11, /device:TPU:8, one launch (start us, length us, event | category | flops | bytes accessed | tf_op | source)
XLA Modules:
  0.0 28.0 jit_solution(15032054635525645954)
XLA Ops:
  0.6 1.6 %start.1 = (bf16[2,2,256,256]{3,2,1,0:T(8,128)(2,1)S(1)}, bf16[128,128]{1,0:T(8,128)(2,1)S(1)}, bf16[128,128]{1,0:T(8,128)(2,1)S(1)}, s32[16]{0:T(128)S(4)}, s32...) custom-call(bf16[2,2,256,256]{3,2,1,0:T(8,128)(2,1)} %x_ref.1, ...), custom_call_target="tpu_custom_call" | custom-call | tf_op jit(solution)/shard_map/start/pallas_call | solution.py:446
  2.2 0.1 collective-permute-start
  2.3 5.0 %collective-permute-start.1 = (bf16[128,128]{1,0:T(8,128)(2,1)S(1)}, bf16[128,128]{1,0:T(8,128)(2,1)S(1)}, u32[]{:S(2)}, u32[]{:S(2)}) collective-permute-start(bf16[128,128]{1,0:T(8,128)(2,1)S(1)} %get-tuple-element.32), channel_id=1, source_target_pairs={{1,2},{2,1},{5,6},{6,5},{9,10},{10,9},{13,14},{14,13},{17,18},{18,... | collective-permute-start | bytes 98312 | tf_op jit(solution)/shard_map/ppermute | solution.py:30
  7.3 1.0 %taps.1 = (f32[2,2,256,256]{3,2,1,0:T(8,128)S(1)}, bf16[64,512]{1,0:T(8,128)(2,1)S(1)}, bf16[64,512]{1,0:T(8,128)(2,1)S(1)}, bf16[2,256,256]{2,1,0:T(8,128)(2,1)S(1)}) custom-call(s32[16]{0:T(128)S(4)} %get-tuple-element.24.az_whole, s32[16]{0:T(128)S(4)} %get-tuple-element.25.az_part, s32[16]{0:T(128)S(4)} %get-tuple-element.26.rg_whole, ...), custom_call_target="tpu_custom_call" | custom-call | flops 4000000 | bytes 800000 | tf_op jit(solution)/shard_map/taps/pallas_call | solution.py:465
  8.4 0.0 collective-permute-done.even_ref
  8.4 0.8 %collective-permute-done.1.odd_ref = bf16[128,128]{1,0:T(8,128)(2,1)S(1)} collective-permute-done((bf16[128,128]{1,0:T(8,128)(2,1)S(1)}, bf16[128,128]{1,0:T(8,128)(2,1)S(1)}, u32[]{:S(2)}, u32[]{:S(2)}) %collective-permute-start.1) | collective-permute-done | bytes 32800 | tf_op jit(solution)/shard_map/ppermute | solution.py:30
  9.2 0.6 %resample.1 = (bf16[2,2,64,256]{3,2,1,0:T(8,128)(2,1)S(1)}, bf16[2,2,64,256]{3,2,1,0:T(8,128)(2,1)S(1)}, bf16[2,2,64,256]{3,2,1,0:T(8,128)(2,1)S(1)}, bf16[2,2,64,256]{3,2,1,0:T(8,128)(2,1)S(1)}) custom-call(f32[2,2,256,256]{3,2,1,0:T(8,128)S(1)} %get-tuple-element.30.inner_ref, bf16[128,128]{1,0:T(8,128)(2,1)S(1)} %collective-permute-done.even_ref, ...), custom_call_target="tpu_custom_call" | custom-call | tf_op jit(solution)/shard_map/resample/pallas_call | solution.py:484
  9.8 2.5 %collective-permute-start.3 = (bf16[2,2,64,256]{3,2,1,0:T(8,128)(2,1)S(1)}, bf16[2,2,64,256]{3,2,1,0:T(8,128)(2,1)S(1)}, u32[]{:S(2)}, u32[]{:S(2)}) collective-permute-start(bf16[2,2,64,256]{3,2,1,0:T(8,128)(2,1)S(1)} %get-tuple-element.37), channel_id=1, source_target_pairs={{0,24},{24,0},{4,28},{28,4},{8,16},{16,8},{12,20},{20,12},{1,25},{... | collective-permute-start | bytes 393224 | tf_op jit(solution)/shard_map/ppermute | solution.py:30
  12.3 0.5 %collective-permute-start.5 = (bf16[2,2,64,256]{3,2,1,0:T(8,128)(2,1)S(1)}, bf16[2,2,64,256]{3,2,1,0:T(8,128)(2,1)S(1)}, u32[]{:S(2)}, u32[]{:S(2)}) collective-permute-start(bf16[2,2,64,256]{3,2,1,0:T(8,128)(2,1)S(1)} %get-tuple-element.38), channel_id=1, source_target_pairs={{0,16},{16,0},{4,20},{20,4},{8,24},{24,8},{12,28},{28,12},{1,17},{... | collective-permute-start | bytes 393224 | tf_op jit(solution)/shard_map/ppermute | solution.py:30
  12.8 0.5 %collective-permute-start.7 = (bf16[2,2,64,256]{3,2,1,0:T(8,128)(2,1)S(1)}, bf16[2,2,64,256]{3,2,1,0:T(8,128)(2,1)S(1)}, u32[]{:S(2)}, u32[]{:S(2)}) collective-permute-start(bf16[2,2,64,256]{3,2,1,0:T(8,128)(2,1)S(1)} %get-tuple-element.39), channel_id=1, source_target_pairs={{0,8},{8,0},{4,12},{12,4},{16,24},{24,16},{20,28},{28,20},{1,9},{9... | collective-permute-start | bytes 393224 | tf_op jit(solution)/shard_map/ppermute | solution.py:30
  13.3 3.6 %collective-permute-done.3.refs_2_ = bf16[2,2,64,256]{3,2,1,0:T(8,128)(2,1)S(1)} collective-permute-done((bf16[2,2,64,256]{3,2,1,0:T(8,128)(2,1)S(1)}, bf16[2,2,64,256]{3,2,1,0:T(8,128)(2,1)S(1)}, u32[]{:S(2)}, u32[]{:S(2)}) %collective-permute-start.3) | collective-permute-done | bytes 131104 | tf_op jit(solution)/shard_map/ppermute | solution.py:30
  17.0 0.0 collective-permute-start.4
  17.0 0.9 %collective-permute-done.5.refs_4_ = bf16[2,2,64,256]{3,2,1,0:T(8,128)(2,1)S(1)} collective-permute-done((bf16[2,2,64,256]{3,2,1,0:T(8,128)(2,1)S(1)}, bf16[2,2,64,256]{3,2,1,0:T(8,128)(2,1)S(1)}, u32[]{:S(2)}, u32[]{:S(2)}) %collective-permute-start.5) | collective-permute-done | bytes 131104 | tf_op jit(solution)/shard_map/ppermute | solution.py:30
  17.8 0.5 %collective-permute-start.8 = (bf16[2,2,64,256]{3,2,1,0:T(8,128)(2,1)S(1)}, bf16[2,2,64,256]{3,2,1,0:T(8,128)(2,1)S(1)}, u32[]{:S(2)}, u32[]{:S(2)}) collective-permute-start(bf16[2,2,64,256]{3,2,1,0:T(8,128)(2,1)S(1)} %collective-permute-done.7.refs_6_), channel_id=1, source_target_pairs={{0,4},{4,0},{8,12},{12,8},{16,20},{20,16},{24,28},{28,24},{1,5},{5... | collective-permute-start | bytes 393224 | tf_op jit(solution)/shard_map/ppermute | solution.py:30
  19.0 0.2 collective-permute-done.6.refs_5_
  19.2 0.2 collective-permute-done.8.refs_7_
  19.3 1.3 %looks.1 = (f32[36,128]{1,0:T(8,128)S(1)}, f32[36,128]{1,0:T(8,128)S(1)}, f32[36,128]{1,0:T(8,128)S(1)}, f32[36,128]{1,0:T(8,128)S(1)}) custom-call(s32[1]{0:T(128)S(6)} %copy.10.root_ref, s32[2,16]{1,0:T(2,128)S(4)} %get-tuple-element.23.gap_ref, bf16[2,2,64,256]{3,2,1,0:T(8,128)(2,1)S(1)} %get-tuple-element.36.refs_0_, ...), custom_call_target="tpu_custom_call" | custom-call | tf_op jit(solution)/shard_map/looks/pallas_call | solution.py:516
  20.6 1.6 %collective-permute-start.10 = (f32[36,128]{1,0:T(8,128)S(1)}, f32[36,128]{1,0:T(8,128)S(1)}, u32[]{:S(2)}, u32[]{:S(2)}) collective-permute-start(f32[36,128]{1,0:T(8,128)S(1)} %get-tuple-element.42), channel_id=1, source_target_pairs={{0,24},{24,0},{4,28},{28,4},{8,16},{16,8},{12,20},{20,12},{1,25},{... | collective-permute-start | bytes 55304 | tf_op jit(solution)/shard_map/ppermute | solution.py:30
  22.3 1.2 %collective-permute-start.11 = (f32[36,128]{1,0:T(8,128)S(1)}, f32[36,128]{1,0:T(8,128)S(1)}, u32[]{:S(2)}, u32[]{:S(2)}) collective-permute-start(f32[36,128]{1,0:T(8,128)S(1)} %get-tuple-element.43), channel_id=1, source_target_pairs={{0,16},{16,0},{4,20},{20,4},{8,24},{24,8},{12,28},{28,12},{1,17},{... | collective-permute-start | bytes 55304 | tf_op jit(solution)/shard_map/ppermute | solution.py:30
  23.5 0.7 %collective-permute-start.9 = (f32[36,128]{1,0:T(8,128)S(1)}, f32[36,128]{1,0:T(8,128)S(1)}, u32[]{:S(2)}, u32[]{:S(2)}) collective-permute-start(f32[36,128]{1,0:T(8,128)S(1)} %get-tuple-element.41), channel_id=1, source_target_pairs={{0,8},{8,0},{4,12},{12,4},{16,24},{24,16},{20,28},{28,20},{1,9},{9... | collective-permute-start | bytes 55304 | tf_op jit(solution)/shard_map/ppermute | solution.py:30
  24.2 1.2 %collective-permute-done.10.refs_2_ = f32[36,128]{1,0:T(8,128)S(1)} collective-permute-done((f32[36,128]{1,0:T(8,128)S(1)}, f32[36,128]{1,0:T(8,128)S(1)}, u32[]{:S(2)}, u32[]{:S(2)}) %collective-permute-start.10) | collective-permute-done | bytes 18464 | tf_op jit(solution)/shard_map/ppermute | solution.py:30
  25.4 0.7 %collective-permute-done.11.refs_3_ = f32[36,128]{1,0:T(8,128)S(1)} collective-permute-done((f32[36,128]{1,0:T(8,128)S(1)}, f32[36,128]{1,0:T(8,128)S(1)}, u32[]{:S(2)}, u32[]{:S(2)}) %collective-permute-start.11) | collective-permute-done | bytes 18464 | tf_op jit(solution)/shard_map/ppermute | solution.py:30
  26.0 1.2 %collective-permute-done.9.refs_1_ = f32[36,128]{1,0:T(8,128)S(1)} collective-permute-done((f32[36,128]{1,0:T(8,128)S(1)}, f32[36,128]{1,0:T(8,128)S(1)}, u32[]{:S(2)}, u32[]{:S(2)}) %collective-permute-start.9) | collective-permute-done | bytes 18464 | tf_op jit(solution)/shard_map/ppermute | solution.py:30
  27.2 0.8 %place.1 = (f32[2,6,16,64]{3,2,1,0:T(8,128)}, f32[2,3,16,64]{3,2,1,0:T(8,128)}) custom-call(f32[36,128]{1,0:T(8,128)S(1)} %get-tuple-element.40.refs_0_, f32[36,128]{1,0:T(8,128)S(1)} %collective-permute-done.9.refs_1_, f32[36,128]{1,0:T(8,128)S(1)} %collective-permute-done.10.refs_2_, f32[36,128]{1,0:T(8,128)S(1)} %collective-permute-done.11.refs_3_), custom_call_target="tpu_custom_call" | custom-call | tf_op jit(solution)/shard_map/place/pallas_call | solution.py:532
  (5 shorter events, 0.0 us)
Async XLA Ops:
  2.2 6.2 %collective-permute-start = (bf16[128,128]{1,0:T(8,128)(2,1)S(1)}, bf16[128,128]{1,0:T(8,128)(2,1)S(1)}, u32[]{:S(2)}, u32[]{:S(2)}) collective-permute-start(bf16[128,128]{1,0:T(8,128)(2,1)S(1)} %get-tuple-element.31), channel_id=1, source_target_pairs={{0,1},{1,0},{2,3},{3,2},{4,5},{5,4},{6,7},{7,6},{8,9},{9,8},{10,11... | collective-permute-start | bytes 98312 | tf_op jit(solution)/shard_map/ppermute | solution.py:30
  2.3 6.9 %collective-permute-start.1 = (bf16[128,128]{1,0:T(8,128)(2,1)S(1)}, bf16[128,128]{1,0:T(8,128)(2,1)S(1)}, u32[]{:S(2)}, u32[]{:S(2)}) collective-permute-start(bf16[128,128]{1,0:T(8,128)(2,1)S(1)} %get-tuple-element.32), channel_id=1, source_target_pairs={{1,2},{2,1},{5,6},{6,5},{9,10},{10,9},{13,14},{14,13},{17,18},{18,... | collective-permute-start | bytes 98312 | tf_op jit(solution)/shard_map/ppermute | solution.py:30
  9.8 7.2 %collective-permute-start.3 = (bf16[2,2,64,256]{3,2,1,0:T(8,128)(2,1)S(1)}, bf16[2,2,64,256]{3,2,1,0:T(8,128)(2,1)S(1)}, u32[]{:S(2)}, u32[]{:S(2)}) collective-permute-start(bf16[2,2,64,256]{3,2,1,0:T(8,128)(2,1)S(1)} %get-tuple-element.37), channel_id=1, source_target_pairs={{0,24},{24,0},{4,28},{28,4},{8,16},{16,8},{12,20},{20,12},{1,25},{... | collective-permute-start | bytes 393224 | tf_op jit(solution)/shard_map/ppermute | solution.py:30
  12.3 5.5 %collective-permute-start.5 = (bf16[2,2,64,256]{3,2,1,0:T(8,128)(2,1)S(1)}, bf16[2,2,64,256]{3,2,1,0:T(8,128)(2,1)S(1)}, u32[]{:S(2)}, u32[]{:S(2)}) collective-permute-start(bf16[2,2,64,256]{3,2,1,0:T(8,128)(2,1)S(1)} %get-tuple-element.38), channel_id=1, source_target_pairs={{0,16},{16,0},{4,20},{20,4},{8,24},{24,8},{12,28},{28,12},{1,17},{... | collective-permute-start | bytes 393224 | tf_op jit(solution)/shard_map/ppermute | solution.py:30
  12.8 5.0 %collective-permute-start.7 = (bf16[2,2,64,256]{3,2,1,0:T(8,128)(2,1)S(1)}, bf16[2,2,64,256]{3,2,1,0:T(8,128)(2,1)S(1)}, u32[]{:S(2)}, u32[]{:S(2)}) collective-permute-start(bf16[2,2,64,256]{3,2,1,0:T(8,128)(2,1)S(1)} %get-tuple-element.39), channel_id=1, source_target_pairs={{0,8},{8,0},{4,12},{12,4},{16,24},{24,16},{20,28},{28,20},{1,9},{9... | collective-permute-start | bytes 393224 | tf_op jit(solution)/shard_map/ppermute | solution.py:30
  13.3 5.6 %collective-permute-start.2 = (bf16[2,2,64,256]{3,2,1,0:T(8,128)(2,1)S(1)}, bf16[2,2,64,256]{3,2,1,0:T(8,128)(2,1)S(1)}, u32[]{:S(2)}, u32[]{:S(2)}) collective-permute-start(bf16[2,2,64,256]{3,2,1,0:T(8,128)(2,1)S(1)} %get-tuple-element.36.refs_0_), channel_id=1, source_target_pairs={{0,4},{4,0},{8,12},{12,8},{16,20},{20,16},{24,28},{28,24},{1,5},{5... | collective-permute-start | bytes 393224 | tf_op jit(solution)/shard_map/ppermute | solution.py:30
  17.0 2.0 %collective-permute-start.4 = (bf16[2,2,64,256]{3,2,1,0:T(8,128)(2,1)S(1)}, bf16[2,2,64,256]{3,2,1,0:T(8,128)(2,1)S(1)}, u32[]{:S(2)}, u32[]{:S(2)}) collective-permute-start(bf16[2,2,64,256]{3,2,1,0:T(8,128)(2,1)S(1)} %collective-permute-done.3.refs_2_), channel_id=1, source_target_pairs={{0,4},{4,0},{8,12},{12,8},{16,20},{20,16},{24,28},{28,24},{1,5},{5... | collective-permute-start | bytes 393224 | tf_op jit(solution)/shard_map/ppermute | solution.py:30
  17.8 1.3 %collective-permute-start.6 = (bf16[2,2,64,256]{3,2,1,0:T(8,128)(2,1)S(1)}, bf16[2,2,64,256]{3,2,1,0:T(8,128)(2,1)S(1)}, u32[]{:S(2)}, u32[]{:S(2)}) collective-permute-start(bf16[2,2,64,256]{3,2,1,0:T(8,128)(2,1)S(1)} %collective-permute-done.5.refs_4_), channel_id=1, source_target_pairs={{0,4},{4,0},{8,12},{12,8},{16,20},{20,16},{24,28},{28,24},{1,5},{5... | collective-permute-start | bytes 393224 | tf_op jit(solution)/shard_map/ppermute | solution.py:30
  17.8 1.5 %collective-permute-start.8 = (bf16[2,2,64,256]{3,2,1,0:T(8,128)(2,1)S(1)}, bf16[2,2,64,256]{3,2,1,0:T(8,128)(2,1)S(1)}, u32[]{:S(2)}, u32[]{:S(2)}) collective-permute-start(bf16[2,2,64,256]{3,2,1,0:T(8,128)(2,1)S(1)} %collective-permute-done.7.refs_6_), channel_id=1, source_target_pairs={{0,4},{4,0},{8,12},{12,8},{16,20},{20,16},{24,28},{28,24},{1,5},{5... | collective-permute-start | bytes 393224 | tf_op jit(solution)/shard_map/ppermute | solution.py:30
  20.6 4.7 %collective-permute-start.10 = (f32[36,128]{1,0:T(8,128)S(1)}, f32[36,128]{1,0:T(8,128)S(1)}, u32[]{:S(2)}, u32[]{:S(2)}) collective-permute-start(f32[36,128]{1,0:T(8,128)S(1)} %get-tuple-element.42), channel_id=1, source_target_pairs={{0,24},{24,0},{4,28},{28,4},{8,16},{16,8},{12,20},{20,12},{1,25},{... | collective-permute-start | bytes 55304 | tf_op jit(solution)/shard_map/ppermute | solution.py:30
  22.3 3.8 %collective-permute-start.11 = (f32[36,128]{1,0:T(8,128)S(1)}, f32[36,128]{1,0:T(8,128)S(1)}, u32[]{:S(2)}, u32[]{:S(2)}) collective-permute-start(f32[36,128]{1,0:T(8,128)S(1)} %get-tuple-element.43), channel_id=1, source_target_pairs={{0,16},{16,0},{4,20},{20,4},{8,24},{24,8},{12,28},{28,12},{1,17},{... | collective-permute-start | bytes 55304 | tf_op jit(solution)/shard_map/ppermute | solution.py:30
  23.5 3.8 %collective-permute-start.9 = (f32[36,128]{1,0:T(8,128)S(1)}, f32[36,128]{1,0:T(8,128)S(1)}, u32[]{:S(2)}, u32[]{:S(2)}) collective-permute-start(f32[36,128]{1,0:T(8,128)S(1)} %get-tuple-element.41), channel_id=1, source_target_pairs={{0,8},{8,0},{4,12},{12,4},{16,24},{24,16},{20,28},{28,20},{1,9},{9... | collective-permute-start | bytes 55304 | tf_op jit(solution)/shard_map/ppermute | solution.py:30

commit v12 on v11

--- a/solution.py
+++ b/solution.py
@@ -318,61 +318,48 @@
     block = QUANTITIES * CHIP_LOOKS
     for chip in range(CHIPS):
         for slot in range(dates):
-            date = (me ^ (CORES * chip)) * dates + slot
             own = CORES * chip * dates + slot
-            spot = slice(slot * columns, (slot + 1) * columns)
+            others = []
             for kind in range(KINDS):
-                position, number = partner_of(kind, date)
-                other = position * dates + number
-                reals, imags = [], []
-                for look in range(CHIP_LOOKS):
-                    left0, left1 = part(own, 0, look), part(own, 1, look)
+                position, number = partner_of(kind, (me ^ (CORES * chip)) * dates + slot)
+                others.append(position * dates + number)
+            for look in range(CHIP_LOOKS):
+                left0, left1 = part(own, 0, look), part(own, 1, look)
+                values = []
+                for other in others:
                     right0, right1 = part(other, 0, look), part(other, 1, look)
-                    reals.append(folded(left0 * right0 + left1 * right1))
-                    imags.append(folded(left1 * right0 - left0 * right1))
-                start = chip * block + kind * 2 * CHIP_LOOKS
-                sums[start : start + 2 * CHIP_LOOKS, spot] = row_sums(reals + imags)
-            powers = []
-            for core in range(CORES):
-                for look in range(CHIP_LOOKS):
-                    left0 = part(own + core * dates, 0, look)
-                    left1 = part(own + core * dates, 1, look)
-                    powers.append(folded(left0 * left0 + left1 * left1))
-            start = chip * block + KINDS * 2 * CHIP_LOOKS
-            sums[start : start + 2 * CHIP_LOOKS, spot] = row_sums(powers)
+                    values.append(folded(left0 * right0 + left1 * right1))
+                    values.append(folded(left1 * right0 - left0 * right1))
+                values.append(folded(left0 * left0 + left1 * left1))
+                right0, right1 = part(own + dates, 0, look), part(own + dates, 1, look)
+                values.append(folded(right0 * right0 + right1 * right1))
+                start = chip * block + look * QUANTITIES
+                sums[start : start + QUANTITIES, slot * columns : (slot + 1) * columns] = (
+                    row_sums(values)
+                )
     pooled[...] = pool_columns(sums[...], LANES)
 
-    row, lane = iotas(2 * CHIP_LOOKS, LANES)
-    upper, first = row < CHIP_LOOKS, lane < LANES // 2
+    def every_look(start):
+        return pooled[pl.ds(start, CHIP_LOOKS, stride=QUANTITIES), :]
+
+    first = lax.broadcasted_iota(jnp.int32, (CHIP_LOOKS, LANES), 1) < LANES // 2
     for chip in range(CHIPS):
         base = chip * block
-        views = [pooled[base + 8 * number : base + 8 * (number + 1), :] for number in range(4)]
-        squares = [view * view for view in views[:KINDS]]
-        squares = [square + pltpu.roll(square, CHIP_LOOKS, 0) for square in squares]
-        power_left = jnp.where(upper, views[KINDS], pltpu.roll(views[KINDS], CHIP_LOOKS, 0))
-        power_right = []
+        power_left = every_look(base + 2 * KINDS)
         for kind in range(KINDS):
             halves = []
             for slot in range(dates):
                 position, number = partner_of(kind, (me ^ (CORES * chip)) * dates + slot)
-                start = lax.div(position, CORES) * block + KINDS * 2 * CHIP_LOOKS
-                power = pooled[pl.ds(pl.multiple_of(start, 8), 8), :]
-                power = pltpu.roll(power, CHIP_LOOKS * (lax.rem(position, CORES) ^ (kind % 2)), 0)
-                halves.append(pltpu.roll(power, LANES // 2 * (number ^ slot), 1))
-            power_right.append(jnp.where(first, halves[0], halves[1]))
-        outs[chip][: 2 * KINDS * CHIP_LOOKS, :] = (
-            pooled[base : base + 2 * KINDS * CHIP_LOOKS, :] * scale
-        )
-        pairs = (
-            (jnp.where(upper, squares[0], squares[1]), jnp.where(upper, *power_right[:2])),
-            (squares[2], power_right[2]),
-        )
-        start = 2 * KINDS * CHIP_LOOKS
-        for square, power in pairs:
-            coherent = jnp.sqrt(square) / jnp.sqrt(power_left * power + 1e-06)
-            rows = min(8, outs[chip].shape[0] - start)
-            outs[chip][start : start + rows, :] = coherent[:rows]
-            start += rows
+                start = lax.div(position, CORES) * block + 2 * KINDS + lax.rem(position, CORES)
+                halves.append(pltpu.roll(every_look(start), LANES // 2 * (number ^ slot), 1))
+            power = power_left * jnp.where(first, halves[0], halves[1])
+            real, imag = every_look(base + 2 * kind), every_look(base + 2 * kind + 1)
+            for channel, value in (
+                (2 * kind, real * scale),
+                (2 * kind + 1, imag * scale),
+                (2 * KINDS + kind, jnp.sqrt(real * real + imag * imag) / jnp.sqrt(power + 1e-06)),
+            ):
+                outs[chip][channel * CHIP_LOOKS : (channel + 1) * CHIP_LOOKS, :] = value
 
 
 def chip_place_kernel(positions, *refs):

time: 28.4 us -> 28.4 us (level)
  no operation moved by 1% of the time
where the time goes in v12:
time: 28.4 us; the launch traced here: 28 us
  starting transfers between devices  12.7 us (45%)
  waiting for transfers between devices  8.73 us (31%)
  Pallas kernels  5.19 us (18%)
  between operations  1.36 us (5%)
    ppermute x12, starting transfers between devices, exchanged(): lax.ppermute(array, axis, [route for a, b in pairs for route in ((a, b),...  12.7 us
    ppermute x12, waiting for transfers between devices, exchanged(): lax.ppermute(array, axis, [route for a, b in pairs for route in ((a, b),...  8.73 us
    pallas_call x1, Pallas kernels, body(): pl.pallas_call(start_kernel, out_shape=(pltpu.VMEM(block.shape, block.dty...  1.55 us
    pallas_call x1, Pallas kernels, body(): pl.pallas_call(functools.partial(chip_looks_kernel, positions), out_shape...  1.25 us
    pallas_call x1, Pallas kernels, body(): pl.pallas_call(functools.partial(taps_kernel, chips, tile_lines), out_sha...  1.04 us
    pallas_call x1, Pallas kernels, body(): pl.pallas_call(functools.partial(chip_place_kernel, [0] + last), out_shap...  0.76 us
    pallas_call x1, Pallas kernels, body(): pl.pallas_call(functools.partial(resample_kernel, (line_groups, column_gr...  0.58 us
  transfers between devices with their start and end apart: 12, of which 8 were waited for; matrix products, arithmetic and copies ran while one was open for 0% of the time, Pallas kernels for 4%

profile of v12, /device:TPU:8, one launch (start us, length us, event | category | flops | bytes accessed | tf_op | source)
XLA Modules:
  0.0 28.0 jit_solution(3388915636869394293)
XLA Ops:
  0.6 1.6 %start.1 = (bf16[2,2,256,256]{3,2,1,0:T(8,128)(2,1)S(1)}, bf16[128,128]{1,0:T(8,128)(2,1)S(1)}, bf16[128,128]{1,0:T(8,128)(2,1)S(1)}, s32[16]{0:T(128)S(4)}, s32...) custom-call(bf16[2,2,256,256]{3,2,1,0:T(8,128)(2,1)} %x_ref.1, ...), custom_call_target="tpu_custom_call" | custom-call | tf_op jit(solution)/shard_map/start/pallas_call | solution.py:433
  2.2 0.1 collective-permute-start
  2.3 5.0 %collective-permute-start.1 = (bf16[128,128]{1,0:T(8,128)(2,1)S(1)}, bf16[128,128]{1,0:T(8,128)(2,1)S(1)}, u32[]{:S(2)}, u32[]{:S(2)}) collective-permute-start(bf16[128,128]{1,0:T(8,128)(2,1)S(1)} %get-tuple-element.32), channel_id=1, source_target_pairs={{1,2},{2,1},{5,6},{6,5},{9,10},{10,9},{13,14},{14,13},{17,18},{18,... | collective-permute-start | bytes 98312 | tf_op jit(solution)/shard_map/ppermute | solution.py:30
  7.3 1.0 %taps.1 = (f32[2,2,256,256]{3,2,1,0:T(8,128)S(1)}, bf16[64,512]{1,0:T(8,128)(2,1)S(1)}, bf16[64,512]{1,0:T(8,128)(2,1)S(1)}, bf16[2,256,256]{2,1,0:T(8,128)(2,1)S(1)}) custom-call(s32[16]{0:T(128)S(4)} %get-tuple-element.24.az_whole, s32[16]{0:T(128)S(4)} %get-tuple-element.25.az_part, s32[16]{0:T(128)S(4)} %get-tuple-element.26.rg_whole, ...), custom_call_target="tpu_custom_call" | custom-call | flops 4000000 | bytes 800000 | tf_op jit(solution)/shard_map/taps/pallas_call | solution.py:452
  8.4 0.8 %collective-permute-done.1.odd_ref = bf16[128,128]{1,0:T(8,128)(2,1)S(1)} collective-permute-done((bf16[128,128]{1,0:T(8,128)(2,1)S(1)}, bf16[128,128]{1,0:T(8,128)(2,1)S(1)}, u32[]{:S(2)}, u32[]{:S(2)}) %collective-permute-start.1) | collective-permute-done | bytes 32800 | tf_op jit(solution)/shard_map/ppermute | solution.py:30
  9.2 0.6 %resample.1 = (bf16[2,2,64,256]{3,2,1,0:T(8,128)(2,1)S(1)}, bf16[2,2,64,256]{3,2,1,0:T(8,128)(2,1)S(1)}, bf16[2,2,64,256]{3,2,1,0:T(8,128)(2,1)S(1)}, bf16[2,2,64,256]{3,2,1,0:T(8,128)(2,1)S(1)}) custom-call(f32[2,2,256,256]{3,2,1,0:T(8,128)S(1)} %get-tuple-element.30.inner_ref, bf16[128,128]{1,0:T(8,128)(2,1)S(1)} %collective-permute-done.even_ref, ...), custom_call_target="tpu_custom_call" | custom-call | tf_op jit(solution)/shard_map/resample/pallas_call | solution.py:471
  9.8 2.5 %collective-permute-start.3 = (bf16[2,2,64,256]{3,2,1,0:T(8,128)(2,1)S(1)}, bf16[2,2,64,256]{3,2,1,0:T(8,128)(2,1)S(1)}, u32[]{:S(2)}, u32[]{:S(2)}) collective-permute-start(bf16[2,2,64,256]{3,2,1,0:T(8,128)(2,1)S(1)} %get-tuple-element.37), channel_id=1, source_target_pairs={{0,24},{24,0},{4,28},{28,4},{8,16},{16,8},{12,20},{20,12},{1,25},{... | collective-permute-start | bytes 393224 | tf_op jit(solution)/shard_map/ppermute | solution.py:30
  12.3 0.5 %collective-permute-start.5 = (bf16[2,2,64,256]{3,2,1,0:T(8,128)(2,1)S(1)}, bf16[2,2,64,256]{3,2,1,0:T(8,128)(2,1)S(1)}, u32[]{:S(2)}, u32[]{:S(2)}) collective-permute-start(bf16[2,2,64,256]{3,2,1,0:T(8,128)(2,1)S(1)} %get-tuple-element.38), channel_id=1, source_target_pairs={{0,16},{16,0},{4,20},{20,4},{8,24},{24,8},{12,28},{28,12},{1,17},{... | collective-permute-start | bytes 393224 | tf_op jit(solution)/shard_map/ppermute | solution.py:30
  12.8 0.5 %collective-permute-start.7 = (bf16[2,2,64,256]{3,2,1,0:T(8,128)(2,1)S(1)}, bf16[2,2,64,256]{3,2,1,0:T(8,128)(2,1)S(1)}, u32[]{:S(2)}, u32[]{:S(2)}) collective-permute-start(bf16[2,2,64,256]{3,2,1,0:T(8,128)(2,1)S(1)} %get-tuple-element.39), channel_id=1, source_target_pairs={{0,8},{8,0},{4,12},{12,4},{16,24},{24,16},{20,28},{28,20},{1,9},{9... | collective-permute-start | bytes 393224 | tf_op jit(solution)/shard_map/ppermute | solution.py:30
  13.3 0.0 collective-permute-start.2
  13.3 3.6 %collective-permute-done.3.refs_2_ = bf16[2,2,64,256]{3,2,1,0:T(8,128)(2,1)S(1)} collective-permute-done((bf16[2,2,64,256]{3,2,1,0:T(8,128)(2,1)S(1)}, bf16[2,2,64,256]{3,2,1,0:T(8,128)(2,1)S(1)}, u32[]{:S(2)}, u32[]{:S(2)}) %collective-permute-start.3) | collective-permute-done | bytes 131104 | tf_op jit(solution)/shard_map/ppermute | solution.py:30
  17.0 0.9 %collective-permute-done.5.refs_4_ = bf16[2,2,64,256]{3,2,1,0:T(8,128)(2,1)S(1)} collective-permute-done((bf16[2,2,64,256]{3,2,1,0:T(8,128)(2,1)S(1)}, bf16[2,2,64,256]{3,2,1,0:T(8,128)(2,1)S(1)}, u32[]{:S(2)}, u32[]{:S(2)}) %collective-permute-start.5) | collective-permute-done | bytes 131104 | tf_op jit(solution)/shard_map/ppermute | solution.py:30
  17.8 0.0 collective-permute-start.6
  17.8 0.5 %collective-permute-start.8 = (bf16[2,2,64,256]{3,2,1,0:T(8,128)(2,1)S(1)}, bf16[2,2,64,256]{3,2,1,0:T(8,128)(2,1)S(1)}, u32[]{:S(2)}, u32[]{:S(2)}) collective-permute-start(bf16[2,2,64,256]{3,2,1,0:T(8,128)(2,1)S(1)} %collective-permute-done.7.refs_6_), channel_id=1, source_target_pairs={{0,4},{4,0},{8,12},{12,8},{16,20},{20,16},{24,28},{28,24},{1,5},{5... | collective-permute-start | bytes 393224 | tf_op jit(solution)/shard_map/ppermute | solution.py:30
  19.0 0.2 collective-permute-done.6.refs_5_
  19.2 0.2 collective-permute-done.8.refs_7_
  19.3 1.2 %looks.1 = (f32[36,128]{1,0:T(8,128)S(1)}, f32[36,128]{1,0:T(8,128)S(1)}, f32[36,128]{1,0:T(8,128)S(1)}, f32[36,128]{1,0:T(8,128)S(1)}) custom-call(s32[1]{0:T(128)S(6)} %copy.10.root_ref, s32[2,16]{1,0:T(2,128)S(4)} %get-tuple-element.23.gap_ref, bf16[2,2,64,256]{3,2,1,0:T(8,128)(2,1)S(1)} %get-tuple-element.36.refs_0_, ...), custom_call_target="tpu_custom_call" | custom-call | tf_op jit(solution)/shard_map/looks/pallas_call | solution.py:503
  20.6 1.6 %collective-permute-start.10 = (f32[36,128]{1,0:T(8,128)S(1)}, f32[36,128]{1,0:T(8,128)S(1)}, u32[]{:S(2)}, u32[]{:S(2)}) collective-permute-start(f32[36,128]{1,0:T(8,128)S(1)} %get-tuple-element.42), channel_id=1, source_target_pairs={{0,24},{24,0},{4,28},{28,4},{8,16},{16,8},{12,20},{20,12},{1,25},{... | collective-permute-start | bytes 55304 | tf_op jit(solution)/shard_map/ppermute | solution.py:30
  22.2 1.2 %collective-permute-start.11 = (f32[36,128]{1,0:T(8,128)S(1)}, f32[36,128]{1,0:T(8,128)S(1)}, u32[]{:S(2)}, u32[]{:S(2)}) collective-permute-start(f32[36,128]{1,0:T(8,128)S(1)} %get-tuple-element.43), channel_id=1, source_target_pairs={{0,16},{16,0},{4,20},{20,4},{8,24},{24,8},{12,28},{28,12},{1,17},{... | collective-permute-start | bytes 55304 | tf_op jit(solution)/shard_map/ppermute | solution.py:30
  23.5 0.7 %collective-permute-start.9 = (f32[36,128]{1,0:T(8,128)S(1)}, f32[36,128]{1,0:T(8,128)S(1)}, u32[]{:S(2)}, u32[]{:S(2)}) collective-permute-start(f32[36,128]{1,0:T(8,128)S(1)} %get-tuple-element.41), channel_id=1, source_target_pairs={{0,8},{8,0},{4,12},{12,4},{16,24},{24,16},{20,28},{28,20},{1,9},{9... | collective-permute-start | bytes 55304 | tf_op jit(solution)/shard_map/ppermute | solution.py:30
  24.2 1.2 %collective-permute-done.10.refs_2_ = f32[36,128]{1,0:T(8,128)S(1)} collective-permute-done((f32[36,128]{1,0:T(8,128)S(1)}, f32[36,128]{1,0:T(8,128)S(1)}, u32[]{:S(2)}, u32[]{:S(2)}) %collective-permute-start.10) | collective-permute-done | bytes 18464 | tf_op jit(solution)/shard_map/ppermute | solution.py:30
  25.4 0.7 %collective-permute-done.11.refs_3_ = f32[36,128]{1,0:T(8,128)S(1)} collective-permute-done((f32[36,128]{1,0:T(8,128)S(1)}, f32[36,128]{1,0:T(8,128)S(1)}, u32[]{:S(2)}, u32[]{:S(2)}) %collective-permute-start.11) | collective-permute-done | bytes 18464 | tf_op jit(solution)/shard_map/ppermute | solution.py:30
  26.0 1.2 %collective-permute-done.9.refs_1_ = f32[36,128]{1,0:T(8,128)S(1)} collective-permute-done((f32[36,128]{1,0:T(8,128)S(1)}, f32[36,128]{1,0:T(8,128)S(1)}, u32[]{:S(2)}, u32[]{:S(2)}) %collective-permute-start.9) | collective-permute-done | bytes 18464 | tf_op jit(solution)/shard_map/ppermute | solution.py:30
  27.2 0.8 %place.1 = (f32[2,6,16,64]{3,2,1,0:T(8,128)}, f32[2,3,16,64]{3,2,1,0:T(8,128)}) custom-call(f32[36,128]{1,0:T(8,128)S(1)} %get-tuple-element.40.refs_0_, f32[36,128]{1,0:T(8,128)S(1)} %collective-permute-done.9.refs_1_, f32[36,128]{1,0:T(8,128)S(1)} %collective-permute-done.10.refs_2_, f32[36,128]{1,0:T(8,128)S(1)} %collective-permute-done.11.refs_3_), custom_call_target="tpu_custom_call" | custom-call | tf_op jit(solution)/shard_map/place/pallas_call | solution.py:519
  (5 shorter events, 0.0 us)
Async XLA Ops:
  2.2 6.2 %collective-permute-start = (bf16[128,128]{1,0:T(8,128)(2,1)S(1)}, bf16[128,128]{1,0:T(8,128)(2,1)S(1)}, u32[]{:S(2)}, u32[]{:S(2)}) collective-permute-start(bf16[128,128]{1,0:T(8,128)(2,1)S(1)} %get-tuple-element.31), channel_id=1, source_target_pairs={{0,1},{1,0},{2,3},{3,2},{4,5},{5,4},{6,7},{7,6},{8,9},{9,8},{10,11... | collective-permute-start | bytes 98312 | tf_op jit(solution)/shard_map/ppermute | solution.py:30
  2.3 6.9 %collective-permute-start.1 = (bf16[128,128]{1,0:T(8,128)(2,1)S(1)}, bf16[128,128]{1,0:T(8,128)(2,1)S(1)}, u32[]{:S(2)}, u32[]{:S(2)}) collective-permute-start(bf16[128,128]{1,0:T(8,128)(2,1)S(1)} %get-tuple-element.32), channel_id=1, source_target_pairs={{1,2},{2,1},{5,6},{6,5},{9,10},{10,9},{13,14},{14,13},{17,18},{18,... | collective-permute-start | bytes 98312 | tf_op jit(solution)/shard_map/ppermute | solution.py:30
  9.8 7.2 %collective-permute-start.3 = (bf16[2,2,64,256]{3,2,1,0:T(8,128)(2,1)S(1)}, bf16[2,2,64,256]{3,2,1,0:T(8,128)(2,1)S(1)}, u32[]{:S(2)}, u32[]{:S(2)}) collective-permute-start(bf16[2,2,64,256]{3,2,1,0:T(8,128)(2,1)S(1)} %get-tuple-element.37), channel_id=1, source_target_pairs={{0,24},{24,0},{4,28},{28,4},{8,16},{16,8},{12,20},{20,12},{1,25},{... | collective-permute-start | bytes 393224 | tf_op jit(solution)/shard_map/ppermute | solution.py:30
  12.3 5.5 %collective-permute-start.5 = (bf16[2,2,64,256]{3,2,1,0:T(8,128)(2,1)S(1)}, bf16[2,2,64,256]{3,2,1,0:T(8,128)(2,1)S(1)}, u32[]{:S(2)}, u32[]{:S(2)}) collective-permute-start(bf16[2,2,64,256]{3,2,1,0:T(8,128)(2,1)S(1)} %get-tuple-element.38), channel_id=1, source_target_pairs={{0,16},{16,0},{4,20},{20,4},{8,24},{24,8},{12,28},{28,12},{1,17},{... | collective-permute-start | bytes 393224 | tf_op jit(solution)/shard_map/ppermute | solution.py:30
  12.8 5.0 %collective-permute-start.7 = (bf16[2,2,64,256]{3,2,1,0:T(8,128)(2,1)S(1)}, bf16[2,2,64,256]{3,2,1,0:T(8,128)(2,1)S(1)}, u32[]{:S(2)}, u32[]{:S(2)}) collective-permute-start(bf16[2,2,64,256]{3,2,1,0:T(8,128)(2,1)S(1)} %get-tuple-element.39), channel_id=1, source_target_pairs={{0,8},{8,0},{4,12},{12,4},{16,24},{24,16},{20,28},{28,20},{1,9},{9... | collective-permute-start | bytes 393224 | tf_op jit(solution)/shard_map/ppermute | solution.py:30
  13.3 5.6 %collective-permute-start.2 = (bf16[2,2,64,256]{3,2,1,0:T(8,128)(2,1)S(1)}, bf16[2,2,64,256]{3,2,1,0:T(8,128)(2,1)S(1)}, u32[]{:S(2)}, u32[]{:S(2)}) collective-permute-start(bf16[2,2,64,256]{3,2,1,0:T(8,128)(2,1)S(1)} %get-tuple-element.36.refs_0_), channel_id=1, source_target_pairs={{0,4},{4,0},{8,12},{12,8},{16,20},{20,16},{24,28},{28,24},{1,5},{5... | collective-permute-start | bytes 393224 | tf_op jit(solution)/shard_map/ppermute | solution.py:30
  17.0 2.0 %collective-permute-start.4 = (bf16[2,2,64,256]{3,2,1,0:T(8,128)(2,1)S(1)}, bf16[2,2,64,256]{3,2,1,0:T(8,128)(2,1)S(1)}, u32[]{:S(2)}, u32[]{:S(2)}) collective-permute-start(bf16[2,2,64,256]{3,2,1,0:T(8,128)(2,1)S(1)} %collective-permute-done.3.refs_2_), channel_id=1, source_target_pairs={{0,4},{4,0},{8,12},{12,8},{16,20},{20,16},{24,28},{28,24},{1,5},{5... | collective-permute-start | bytes 393224 | tf_op jit(solution)/shard_map/ppermute | solution.py:30
  17.8 1.3 %collective-permute-start.6 = (bf16[2,2,64,256]{3,2,1,0:T(8,128)(2,1)S(1)}, bf16[2,2,64,256]{3,2,1,0:T(8,128)(2,1)S(1)}, u32[]{:S(2)}, u32[]{:S(2)}) collective-permute-start(bf16[2,2,64,256]{3,2,1,0:T(8,128)(2,1)S(1)} %collective-permute-done.5.refs_4_), channel_id=1, source_target_pairs={{0,4},{4,0},{8,12},{12,8},{16,20},{20,16},{24,28},{28,24},{1,5},{5... | collective-permute-start | bytes 393224 | tf_op jit(solution)/shard_map/ppermute | solution.py:30
  17.8 1.5 %collective-permute-start.8 = (bf16[2,2,64,256]{3,2,1,0:T(8,128)(2,1)S(1)}, bf16[2,2,64,256]{3,2,1,0:T(8,128)(2,1)S(1)}, u32[]{:S(2)}, u32[]{:S(2)}) collective-permute-start(bf16[2,2,64,256]{3,2,1,0:T(8,128)(2,1)S(1)} %collective-permute-done.7.refs_6_), channel_id=1, source_target_pairs={{0,4},{4,0},{8,12},{12,8},{16,20},{20,16},{24,28},{28,24},{1,5},{5... | collective-permute-start | bytes 393224 | tf_op jit(solution)/shard_map/ppermute | solution.py:30
  20.6 4.7 %collective-permute-start.10 = (f32[36,128]{1,0:T(8,128)S(1)}, f32[36,128]{1,0:T(8,128)S(1)}, u32[]{:S(2)}, u32[]{:S(2)}) collective-permute-start(f32[36,128]{1,0:T(8,128)S(1)} %get-tuple-element.42), channel_id=1, source_target_pairs={{0,24},{24,0},{4,28},{28,4},{8,16},{16,8},{12,20},{20,12},{1,25},{... | collective-permute-start | bytes 55304 | tf_op jit(solution)/shard_map/ppermute | solution.py:30
  22.2 3.8 %collective-permute-start.11 = (f32[36,128]{1,0:T(8,128)S(1)}, f32[36,128]{1,0:T(8,128)S(1)}, u32[]{:S(2)}, u32[]{:S(2)}) collective-permute-start(f32[36,128]{1,0:T(8,128)S(1)} %get-tuple-element.43), channel_id=1, source_target_pairs={{0,16},{16,0},{4,20},{20,4},{8,24},{24,8},{12,28},{28,12},{1,17},{... | collective-permute-start | bytes 55304 | tf_op jit(solution)/shard_map/ppermute | solution.py:30
  23.5 3.8 %collective-permute-start.9 = (f32[36,128]{1,0:T(8,128)S(1)}, f32[36,128]{1,0:T(8,128)S(1)}, u32[]{:S(2)}, u32[]{:S(2)}) collective-permute-start(f32[36,128]{1,0:T(8,128)S(1)} %get-tuple-element.41), channel_id=1, source_target_pairs={{0,8},{8,0},{4,12},{12,4},{16,24},{24,16},{20,28},{28,20},{1,9},{9... | collective-permute-start | bytes 55304 | tf_op jit(solution)/shard_map/ppermute | solution.py:30

commit v13 on v12

--- a/solution.py
+++ b/solution.py
@@ -117,6 +117,11 @@
         copy.wait()
 
 
+def pool_matrix(columns, lanes):
+    row, col = iotas(columns, lanes)
+    return jnp.where(row // LOOK_RG == col, 1.0, 0.0).astype(jnp.bfloat16)
+
+
 def taps_kernel(
     chips,
     tile_lines,
@@ -130,8 +135,10 @@
     low_ref,
     high_ref,
     line_ref,
+    pool_ref,
 ):
     dates, parts, lines, columns = x_ref.shape
+    pool_ref[...] = pool_matrix(*pool_ref.shape)
     edge_rows = low_ref.shape[0]
     centre = TAPS // 2 - 1
     present = [lax.axis_index("date") * dates + slot for slot in range(dates)]
@@ -225,9 +232,7 @@
     return values[0]
 
 
-def pool_columns(sums, lanes):
-    row, col = iotas(sums.shape[1], lanes)
-    pool = jnp.where(row // LOOK_RG == col, 1.0, 0.0).astype(jnp.bfloat16)
+def pool_columns(sums, pool):
     coarse = sums.astype(jnp.bfloat16)
     fine = (sums - coarse.astype(jnp.float32)).astype(jnp.bfloat16)
     return jnp.dot(coarse, pool, preferred_element_type=jnp.float32) + jnp.dot(
@@ -269,7 +274,7 @@
         return carry
 
     lax.fori_loop(0, total, collect, 0, unroll=unroll)
-    pooled[...] = pool_columns(sums[...], lanes)
+    pooled[...] = pool_columns(sums[...], pool_matrix(sums.shape[1], lanes))
 
     def gather(date, carry):
         for kind in range(KINDS):
@@ -296,7 +301,7 @@
             ) / jnp.sqrt(power_left * power_right + 1e-06)
 
 
-def chip_looks_kernel(positions, root_ref, gap_ref, *refs):
+def chip_looks_kernel(positions, root_ref, gap_ref, pool_ref, *refs):
     tiles, outs, (stack, sums, pooled) = refs[: CHIPS * CORES], refs[CHIPS * CORES : -3], refs[-3:]
     dates, _, _, columns = tiles[0].shape
     me = lax.axis_index("date")
@@ -337,7 +342,8 @@
                 sums[start : start + QUANTITIES, slot * columns : (slot + 1) * columns] = (
                     row_sums(values)
                 )
-    pooled[...] = pool_columns(sums[...], LANES)
+        rows = slice(chip * block, (chip + 1) * block)
+        pooled[rows] = pool_columns(sums[rows], pool_ref[...])
 
     def every_look(start):
         return pooled[pl.ds(start, CHIP_LOOKS, stride=QUANTITIES), :]
@@ -449,16 +455,17 @@
     odd = exchanged(odd, "range", [(j, j + 1) for j in range(1, width - 1, 2)])
     even = exchanged(even, "range", [(j, j + 1) for j in range(0, width - 1, 2)])
 
-    inner, low_taps, high_taps, line_taps = pl.pallas_call(
+    inner, low_taps, high_taps, line_taps, pool = pl.pallas_call(
         functools.partial(taps_kernel, chips, tile_lines),
         out_shape=(
             pltpu.VMEM(block.shape, jnp.float32),
             pltpu.VMEM((images * MARGIN, images * LANES), jnp.bfloat16),
             pltpu.VMEM((images * MARGIN, images * LANES), jnp.bfloat16),
             pltpu.VMEM((dates, lines, lines), jnp.bfloat16),
+            pltpu.VMEM((dates * columns, LANES), jnp.bfloat16),
         ),
         in_specs=[SMEM] * len(small) + [VMEM],
-        out_specs=(VMEM,) * 4,
+        out_specs=(VMEM,) * 5,
         cost_estimate=pl.CostEstimate(flops=4000000, bytes_accessed=800000, transcendentals=0),
         name="taps",
         compiler_params=pltpu.CompilerParams(vmem_limit_bytes=GRANT),
@@ -503,7 +510,7 @@
         results = pl.pallas_call(
             functools.partial(chip_looks_kernel, positions),
             out_shape=(pltpu.VMEM((CHANNELS * CHIP_LOOKS, LANES), jnp.float32),) * CHIPS,
-            in_specs=[SMEM] * 2 + [VMEM] * len(held),
+            in_specs=[SMEM] * 2 + [VMEM] * (1 + len(held)),
             out_specs=(VMEM,) * CHIPS,
             scratch_shapes=[
                 pltpu.VMEM((total, parts, tile_lines, tile_columns), jnp.float32),
@@ -512,7 +519,7 @@
             ],
             name="looks",
             compiler_params=pltpu.CompilerParams(vmem_limit_bytes=GRANT),
-        )(master_epoch_image, gap, *[near(tile) for tile in held])
+        )(master_epoch_image, gap, near(pool), *[near(tile) for tile in held])
         back = {number: swapped(results[number], CORES * number) for number in order}
         last = [1, 3, 2]
         pieces = [results[0]] + [back[number] for number in last]

time: 28.4 us -> 28.3 us (level)
  no operation moved by 1% of the time
where the time goes in v13:
time: 28.3 us; the launch traced here: 27.9 us
  starting transfers between devices  12.7 us (45%)
  waiting for transfers between devices  8.7 us (31%)
  Pallas kernels  5.14 us (18%)
  between operations  1.36 us (5%)
    ppermute x12, starting transfers between devices, exchanged(): lax.ppermute(array, axis, [route for a, b in pairs for route in ((a, b),...  12.7 us
    ppermute x12, waiting for transfers between devices, exchanged(): lax.ppermute(array, axis, [route for a, b in pairs for route in ((a, b),...  8.7 us
    pallas_call x1, Pallas kernels, body(): pl.pallas_call(start_kernel, out_shape=(pltpu.VMEM(block.shape, block.dty...  1.55 us
    pallas_call x1, Pallas kernels, body(): pl.pallas_call(functools.partial(chip_looks_kernel, positions), out_shape...  1.18 us
    pallas_call x1, Pallas kernels, body(): pl.pallas_call(functools.partial(taps_kernel, chips, tile_lines), out_sha...  1.06 us
    pallas_call x1, Pallas kernels, body(): pl.pallas_call(functools.partial(chip_place_kernel, [0] + last), out_shap...  0.76 us
    pallas_call x1, Pallas kernels, body(): pl.pallas_call(functools.partial(resample_kernel, (line_groups, column_gr...  0.58 us
  transfers between devices with their start and end apart: 12, of which 8 were waited for; matrix products, arithmetic and copies ran while one was open for 0% of the time, Pallas kernels for 4%

profile of v13, /device:TPU:8, one launch (start us, length us, event | category | flops | bytes accessed | tf_op | source)
XLA Modules:
  0.0 27.9 jit_solution(530708554249016757)
XLA Ops:
  0.6 1.6 %start.1 = (bf16[2,2,256,256]{3,2,1,0:T(8,128)(2,1)S(1)}, bf16[128,128]{1,0:T(8,128)(2,1)S(1)}, bf16[128,128]{1,0:T(8,128)(2,1)S(1)}, s32[16]{0:T(128)S(4)}, s32...) custom-call(bf16[2,2,256,256]{3,2,1,0:T(8,128)(2,1)} %x_ref.1, ...), custom_call_target="tpu_custom_call" | custom-call | tf_op jit(solution)/shard_map/start/pallas_call | solution.py:439
  2.2 0.1 collective-permute-start
  2.3 5.0 %collective-permute-start.1 = (bf16[128,128]{1,0:T(8,128)(2,1)S(1)}, bf16[128,128]{1,0:T(8,128)(2,1)S(1)}, u32[]{:S(2)}, u32[]{:S(2)}) collective-permute-start(bf16[128,128]{1,0:T(8,128)(2,1)S(1)} %get-tuple-element.34), channel_id=1, source_target_pairs={{1,2},{2,1},{5,6},{6,5},{9,10},{10,9},{13,14},{14,13},{17,18},{18,... | collective-permute-start | bytes 98312 | tf_op jit(solution)/shard_map/ppermute | solution.py:30
  7.3 1.1 %taps.1 = (f32[2,2,256,256]{3,2,1,0:T(8,128)S(1)}, bf16[64,512]{1,0:T(8,128)(2,1)S(1)}, bf16[64,512]{1,0:T(8,128)(2,1)S(1)}, bf16[2,256,256]{2,1,0:T(8,128)(2,1)S(1)}, bf16[512,128]{1,0:T(8,128)(2,1)S(1)}) custom-call(s32[16]{0:T(128)S(4)} %get-tuple-element.25.az_whole, s32[16]{0:T(128)S(4)} %get-tuple-element.26.az_part, ...), custom_call_target="tpu_custom_call" | custom-call | flops 4000000 | bytes 800000 | tf_op jit(solution)/shard_map/taps/pallas_call | solution.py:458
  8.4 0.0 collective-permute-done.even_ref
  8.4 0.8 %collective-permute-done.1.odd_ref = bf16[128,128]{1,0:T(8,128)(2,1)S(1)} collective-permute-done((bf16[128,128]{1,0:T(8,128)(2,1)S(1)}, bf16[128,128]{1,0:T(8,128)(2,1)S(1)}, u32[]{:S(2)}, u32[]{:S(2)}) %collective-permute-start.1) | collective-permute-done | bytes 32800 | tf_op jit(solution)/shard_map/ppermute | solution.py:30
  9.2 0.6 %resample.1 = (bf16[2,2,64,256]{3,2,1,0:T(8,128)(2,1)S(1)}, bf16[2,2,64,256]{3,2,1,0:T(8,128)(2,1)S(1)}, bf16[2,2,64,256]{3,2,1,0:T(8,128)(2,1)S(1)}, bf16[2,2,64,256]{3,2,1,0:T(8,128)(2,1)S(1)}) custom-call(f32[2,2,256,256]{3,2,1,0:T(8,128)S(1)} %get-tuple-element.32.inner_ref, bf16[128,128]{1,0:T(8,128)(2,1)S(1)} %collective-permute-done.even_ref, ...), custom_call_target="tpu_custom_call" | custom-call | tf_op jit(solution)/shard_map/resample/pallas_call | solution.py:478
  9.8 2.5 %collective-permute-start.3 = (bf16[2,2,64,256]{3,2,1,0:T(8,128)(2,1)S(1)}, bf16[2,2,64,256]{3,2,1,0:T(8,128)(2,1)S(1)}, u32[]{:S(2)}, u32[]{:S(2)}) collective-permute-start(bf16[2,2,64,256]{3,2,1,0:T(8,128)(2,1)S(1)} %get-tuple-element.39), channel_id=1, source_target_pairs={{0,24},{24,0},{4,28},{28,4},{8,16},{16,8},{12,20},{20,12},{1,25},{... | collective-permute-start | bytes 393224 | tf_op jit(solution)/shard_map/ppermute | solution.py:30
  12.3 0.5 %collective-permute-start.5 = (bf16[2,2,64,256]{3,2,1,0:T(8,128)(2,1)S(1)}, bf16[2,2,64,256]{3,2,1,0:T(8,128)(2,1)S(1)}, u32[]{:S(2)}, u32[]{:S(2)}) collective-permute-start(bf16[2,2,64,256]{3,2,1,0:T(8,128)(2,1)S(1)} %get-tuple-element.40), channel_id=1, source_target_pairs={{0,16},{16,0},{4,20},{20,4},{8,24},{24,8},{12,28},{28,12},{1,17},{... | collective-permute-start | bytes 393224 | tf_op jit(solution)/shard_map/ppermute | solution.py:30
  12.8 0.5 %collective-permute-start.7 = (bf16[2,2,64,256]{3,2,1,0:T(8,128)(2,1)S(1)}, bf16[2,2,64,256]{3,2,1,0:T(8,128)(2,1)S(1)}, u32[]{:S(2)}, u32[]{:S(2)}) collective-permute-start(bf16[2,2,64,256]{3,2,1,0:T(8,128)(2,1)S(1)} %get-tuple-element.41), channel_id=1, source_target_pairs={{0,8},{8,0},{4,12},{12,4},{16,24},{24,16},{20,28},{28,20},{1,9},{9... | collective-permute-start | bytes 393224 | tf_op jit(solution)/shard_map/ppermute | solution.py:30
  13.3 3.6 %collective-permute-done.3.refs_2_ = bf16[2,2,64,256]{3,2,1,0:T(8,128)(2,1)S(1)} collective-permute-done((bf16[2,2,64,256]{3,2,1,0:T(8,128)(2,1)S(1)}, bf16[2,2,64,256]{3,2,1,0:T(8,128)(2,1)S(1)}, u32[]{:S(2)}, u32[]{:S(2)}) %collective-permute-start.3) | collective-permute-done | bytes 131104 | tf_op jit(solution)/shard_map/ppermute | solution.py:30
  17.0 0.0 collective-permute-start.4
  17.0 0.9 %collective-permute-done.5.refs_4_ = bf16[2,2,64,256]{3,2,1,0:T(8,128)(2,1)S(1)} collective-permute-done((bf16[2,2,64,256]{3,2,1,0:T(8,128)(2,1)S(1)}, bf16[2,2,64,256]{3,2,1,0:T(8,128)(2,1)S(1)}, u32[]{:S(2)}, u32[]{:S(2)}) %collective-permute-start.5) | collective-permute-done | bytes 131104 | tf_op jit(solution)/shard_map/ppermute | solution.py:30
  17.8 0.5 %collective-permute-start.8 = (bf16[2,2,64,256]{3,2,1,0:T(8,128)(2,1)S(1)}, bf16[2,2,64,256]{3,2,1,0:T(8,128)(2,1)S(1)}, u32[]{:S(2)}, u32[]{:S(2)}) collective-permute-start(bf16[2,2,64,256]{3,2,1,0:T(8,128)(2,1)S(1)} %collective-permute-done.7.refs_6_), channel_id=1, source_target_pairs={{0,4},{4,0},{8,12},{12,8},{16,20},{20,16},{24,28},{28,24},{1,5},{5... | collective-permute-start | bytes 393224 | tf_op jit(solution)/shard_map/ppermute | solution.py:30
  19.0 0.2 collective-permute-done.6.refs_5_
  19.2 0.2 collective-permute-done.8.refs_7_
  19.3 1.2 %looks.1 = (f32[36,128]{1,0:T(8,128)S(1)}, f32[36,128]{1,0:T(8,128)S(1)}, f32[36,128]{1,0:T(8,128)S(1)}, f32[36,128]{1,0:T(8,128)S(1)}) custom-call(s32[1]{0:T(128)S(6)} %copy.10.root_ref, s32[2,16]{1,0:T(2,128)S(4)} %get-tuple-element.24.gap_ref, bf16[512,128]{1,0:T(8,128)(2,1)S(1)} %get-tuple-element.31.pool_ref, ...), custom_call_target="tpu_custom_call" | custom-call | tf_op jit(solution)/shard_map/looks/pallas_call | solution.py:510
  20.5 1.6 %collective-permute-start.10 = (f32[36,128]{1,0:T(8,128)S(1)}, f32[36,128]{1,0:T(8,128)S(1)}, u32[]{:S(2)}, u32[]{:S(2)}) collective-permute-start(f32[36,128]{1,0:T(8,128)S(1)} %get-tuple-element.44), channel_id=1, source_target_pairs={{0,24},{24,0},{4,28},{28,4},{8,16},{16,8},{12,20},{20,12},{1,25},{... | collective-permute-start | bytes 55304 | tf_op jit(solution)/shard_map/ppermute | solution.py:30
  22.2 1.2 %collective-permute-start.11 = (f32[36,128]{1,0:T(8,128)S(1)}, f32[36,128]{1,0:T(8,128)S(1)}, u32[]{:S(2)}, u32[]{:S(2)}) collective-permute-start(f32[36,128]{1,0:T(8,128)S(1)} %get-tuple-element.45), channel_id=1, source_target_pairs={{0,16},{16,0},{4,20},{20,4},{8,24},{24,8},{12,28},{28,12},{1,17},{... | collective-permute-start | bytes 55304 | tf_op jit(solution)/shard_map/ppermute | solution.py:30
  23.4 0.7 %collective-permute-start.9 = (f32[36,128]{1,0:T(8,128)S(1)}, f32[36,128]{1,0:T(8,128)S(1)}, u32[]{:S(2)}, u32[]{:S(2)}) collective-permute-start(f32[36,128]{1,0:T(8,128)S(1)} %get-tuple-element.43), channel_id=1, source_target_pairs={{0,8},{8,0},{4,12},{12,4},{16,24},{24,16},{20,28},{28,20},{1,9},{9... | collective-permute-start | bytes 55304 | tf_op jit(solution)/shard_map/ppermute | solution.py:30
  24.1 1.2 %collective-permute-done.10.refs_2_ = f32[36,128]{1,0:T(8,128)S(1)} collective-permute-done((f32[36,128]{1,0:T(8,128)S(1)}, f32[36,128]{1,0:T(8,128)S(1)}, u32[]{:S(2)}, u32[]{:S(2)}) %collective-permute-start.10) | collective-permute-done | bytes 18464 | tf_op jit(solution)/shard_map/ppermute | solution.py:30
  25.3 0.7 %collective-permute-done.11.refs_3_ = f32[36,128]{1,0:T(8,128)S(1)} collective-permute-done((f32[36,128]{1,0:T(8,128)S(1)}, f32[36,128]{1,0:T(8,128)S(1)}, u32[]{:S(2)}, u32[]{:S(2)}) %collective-permute-start.11) | collective-permute-done | bytes 18464 | tf_op jit(solution)/shard_map/ppermute | solution.py:30
  26.0 1.2 %collective-permute-done.9.refs_1_ = f32[36,128]{1,0:T(8,128)S(1)} collective-permute-done((f32[36,128]{1,0:T(8,128)S(1)}, f32[36,128]{1,0:T(8,128)S(1)}, u32[]{:S(2)}, u32[]{:S(2)}) %collective-permute-start.9) | collective-permute-done | bytes 18464 | tf_op jit(solution)/shard_map/ppermute | solution.py:30
  27.2 0.8 %place.1 = (f32[2,6,16,64]{3,2,1,0:T(8,128)}, f32[2,3,16,64]{3,2,1,0:T(8,128)}) custom-call(f32[36,128]{1,0:T(8,128)S(1)} %get-tuple-element.42.refs_0_, f32[36,128]{1,0:T(8,128)S(1)} %collective-permute-done.9.refs_1_, f32[36,128]{1,0:T(8,128)S(1)} %collective-permute-done.10.refs_2_, f32[36,128]{1,0:T(8,128)S(1)} %collective-permute-done.11.refs_3_), custom_call_target="tpu_custom_call" | custom-call | tf_op jit(solution)/shard_map/place/pallas_call | solution.py:526
  (5 shorter events, 0.0 us)
Async XLA Ops:
  2.2 6.2 %collective-permute-start = (bf16[128,128]{1,0:T(8,128)(2,1)S(1)}, bf16[128,128]{1,0:T(8,128)(2,1)S(1)}, u32[]{:S(2)}, u32[]{:S(2)}) collective-permute-start(bf16[128,128]{1,0:T(8,128)(2,1)S(1)} %get-tuple-element.33), channel_id=1, source_target_pairs={{0,1},{1,0},{2,3},{3,2},{4,5},{5,4},{6,7},{7,6},{8,9},{9,8},{10,11... | collective-permute-start | bytes 98312 | tf_op jit(solution)/shard_map/ppermute | solution.py:30
  2.3 6.9 %collective-permute-start.1 = (bf16[128,128]{1,0:T(8,128)(2,1)S(1)}, bf16[128,128]{1,0:T(8,128)(2,1)S(1)}, u32[]{:S(2)}, u32[]{:S(2)}) collective-permute-start(bf16[128,128]{1,0:T(8,128)(2,1)S(1)} %get-tuple-element.34), channel_id=1, source_target_pairs={{1,2},{2,1},{5,6},{6,5},{9,10},{10,9},{13,14},{14,13},{17,18},{18,... | collective-permute-start | bytes 98312 | tf_op jit(solution)/shard_map/ppermute | solution.py:30
  9.8 7.2 %collective-permute-start.3 = (bf16[2,2,64,256]{3,2,1,0:T(8,128)(2,1)S(1)}, bf16[2,2,64,256]{3,2,1,0:T(8,128)(2,1)S(1)}, u32[]{:S(2)}, u32[]{:S(2)}) collective-permute-start(bf16[2,2,64,256]{3,2,1,0:T(8,128)(2,1)S(1)} %get-tuple-element.39), channel_id=1, source_target_pairs={{0,24},{24,0},{4,28},{28,4},{8,16},{16,8},{12,20},{20,12},{1,25},{... | collective-permute-start | bytes 393224 | tf_op jit(solution)/shard_map/ppermute | solution.py:30
  12.3 5.5 %collective-permute-start.5 = (bf16[2,2,64,256]{3,2,1,0:T(8,128)(2,1)S(1)}, bf16[2,2,64,256]{3,2,1,0:T(8,128)(2,1)S(1)}, u32[]{:S(2)}, u32[]{:S(2)}) collective-permute-start(bf16[2,2,64,256]{3,2,1,0:T(8,128)(2,1)S(1)} %get-tuple-element.40), channel_id=1, source_target_pairs={{0,16},{16,0},{4,20},{20,4},{8,24},{24,8},{12,28},{28,12},{1,17},{... | collective-permute-start | bytes 393224 | tf_op jit(solution)/shard_map/ppermute | solution.py:30
  12.8 5.0 %collective-permute-start.7 = (bf16[2,2,64,256]{3,2,1,0:T(8,128)(2,1)S(1)}, bf16[2,2,64,256]{3,2,1,0:T(8,128)(2,1)S(1)}, u32[]{:S(2)}, u32[]{:S(2)}) collective-permute-start(bf16[2,2,64,256]{3,2,1,0:T(8,128)(2,1)S(1)} %get-tuple-element.41), channel_id=1, source_target_pairs={{0,8},{8,0},{4,12},{12,4},{16,24},{24,16},{20,28},{28,20},{1,9},{9... | collective-permute-start | bytes 393224 | tf_op jit(solution)/shard_map/ppermute | solution.py:30
  13.3 5.6 %collective-permute-start.2 = (bf16[2,2,64,256]{3,2,1,0:T(8,128)(2,1)S(1)}, bf16[2,2,64,256]{3,2,1,0:T(8,128)(2,1)S(1)}, u32[]{:S(2)}, u32[]{:S(2)}) collective-permute-start(bf16[2,2,64,256]{3,2,1,0:T(8,128)(2,1)S(1)} %get-tuple-element.38.refs_0_), channel_id=1, source_target_pairs={{0,4},{4,0},{8,12},{12,8},{16,20},{20,16},{24,28},{28,24},{1,5},{5... | collective-permute-start | bytes 393224 | tf_op jit(solution)/shard_map/ppermute | solution.py:30
  17.0 2.0 %collective-permute-start.4 = (bf16[2,2,64,256]{3,2,1,0:T(8,128)(2,1)S(1)}, bf16[2,2,64,256]{3,2,1,0:T(8,128)(2,1)S(1)}, u32[]{:S(2)}, u32[]{:S(2)}) collective-permute-start(bf16[2,2,64,256]{3,2,1,0:T(8,128)(2,1)S(1)} %collective-permute-done.3.refs_2_), channel_id=1, source_target_pairs={{0,4},{4,0},{8,12},{12,8},{16,20},{20,16},{24,28},{28,24},{1,5},{5... | collective-permute-start | bytes 393224 | tf_op jit(solution)/shard_map/ppermute | solution.py:30
  17.8 1.3 %collective-permute-start.6 = (bf16[2,2,64,256]{3,2,1,0:T(8,128)(2,1)S(1)}, bf16[2,2,64,256]{3,2,1,0:T(8,128)(2,1)S(1)}, u32[]{:S(2)}, u32[]{:S(2)}) collective-permute-start(bf16[2,2,64,256]{3,2,1,0:T(8,128)(2,1)S(1)} %collective-permute-done.5.refs_4_), channel_id=1, source_target_pairs={{0,4},{4,0},{8,12},{12,8},{16,20},{20,16},{24,28},{28,24},{1,5},{5... | collective-permute-start | bytes 393224 | tf_op jit(solution)/shard_map/ppermute | solution.py:30
  17.8 1.5 %collective-permute-start.8 = (bf16[2,2,64,256]{3,2,1,0:T(8,128)(2,1)S(1)}, bf16[2,2,64,256]{3,2,1,0:T(8,128)(2,1)S(1)}, u32[]{:S(2)}, u32[]{:S(2)}) collective-permute-start(bf16[2,2,64,256]{3,2,1,0:T(8,128)(2,1)S(1)} %collective-permute-done.7.refs_6_), channel_id=1, source_target_pairs={{0,4},{4,0},{8,12},{12,8},{16,20},{20,16},{24,28},{28,24},{1,5},{5... | collective-permute-start | bytes 393224 | tf_op jit(solution)/shard_map/ppermute | solution.py:30
  20.5 4.7 %collective-permute-start.10 = (f32[36,128]{1,0:T(8,128)S(1)}, f32[36,128]{1,0:T(8,128)S(1)}, u32[]{:S(2)}, u32[]{:S(2)}) collective-permute-start(f32[36,128]{1,0:T(8,128)S(1)} %get-tuple-element.44), channel_id=1, source_target_pairs={{0,24},{24,0},{4,28},{28,4},{8,16},{16,8},{12,20},{20,12},{1,25},{... | collective-permute-start | bytes 55304 | tf_op jit(solution)/shard_map/ppermute | solution.py:30
  22.2 3.8 %collective-permute-start.11 = (f32[36,128]{1,0:T(8,128)S(1)}, f32[36,128]{1,0:T(8,128)S(1)}, u32[]{:S(2)}, u32[]{:S(2)}) collective-permute-start(f32[36,128]{1,0:T(8,128)S(1)} %get-tuple-element.45), channel_id=1, source_target_pairs={{0,16},{16,0},{4,20},{20,4},{8,24},{24,8},{12,28},{28,12},{1,17},{... | collective-permute-start | bytes 55304 | tf_op jit(solution)/shard_map/ppermute | solution.py:30
  23.4 3.8 %collective-permute-start.9 = (f32[36,128]{1,0:T(8,128)S(1)}, f32[36,128]{1,0:T(8,128)S(1)}, u32[]{:S(2)}, u32[]{:S(2)}) collective-permute-start(f32[36,128]{1,0:T(8,128)S(1)} %get-tuple-element.43), channel_id=1, source_target_pairs={{0,8},{8,0},{4,12},{12,4},{16,24},{24,16},{20,28},{28,20},{1,9},{9... | collective-permute-start | bytes 55304 | tf_op jit(solution)/shard_map/ppermute | solution.py:30

commit v14 on v13

--- a/solution.py
+++ b/solution.py
@@ -65,8 +65,8 @@
     )
 
 
-def tile_order(position, chips):
-    return position ^ (lax.axis_index("date") // CORES) if chips else position
+def tile_order(position):
+    return position ^ (lax.axis_index("date") // CORES)
 
 
 def banded(offsets, weights):
@@ -123,8 +123,6 @@
 
 
 def taps_kernel(
-    chips,
-    tile_lines,
     az_whole,
     az_part,
     rg_whole,
@@ -135,10 +133,8 @@
     low_ref,
     high_ref,
     line_ref,
-    pool_ref,
 ):
     dates, parts, lines, columns = x_ref.shape
-    pool_ref[...] = pool_matrix(*pool_ref.shape)
     edge_rows = low_ref.shape[0]
     centre = TAPS // 2 - 1
     present = [lax.axis_index("date") * dates + slot for slot in range(dates)]
@@ -162,17 +158,72 @@
             low_ref[:, spot] = jnp.where(held, low, 0.0).astype(jnp.bfloat16)
             high_ref[:, spot] = jnp.where(held, high, 0.0).astype(jnp.bfloat16)
         row, col = iotas(lines, lines)
-        row = tile_order(row // tile_lines, chips) * tile_lines + row % tile_lines
         weights = table[dates + slot : dates + slot + 1]
         band = banded(col - row + (centre - az_whole[date]), weights)
         usable = row < sweeps[date] * (lines // MAX_SWEEPS)
         line_ref[slot] = jnp.where(usable, band, 0.0).astype(jnp.bfloat16)
 
 
-def resample_kernel(split, inner_ref, even_ref, odd_ref, low_ref, high_ref, line_ref, *refs):
-    *outs, edges = refs
-    dates, parts, _, columns = inner_ref.shape
-    line_groups, column_groups, tile_lines, tile_columns = split
+def main_kernel(
+    az_whole,
+    az_part,
+    rg_whole,
+    rg_part,
+    sweeps,
+    x_ref,
+    line_ref,
+    inner_ref,
+    low_ref,
+    high_ref,
+    pool_ref,
+    *outs,
+):
+    dates, parts, lines, columns = x_ref.shape
+    edge_rows = low_ref.shape[0]
+    tile_lines = lines // len(outs)
+    centre = TAPS // 2 - 1
+    pool_ref[...] = pool_matrix(*pool_ref.shape)
+    present = [lax.axis_index("date") * dates + slot for slot in range(dates)]
+    table = weight_rows([rg_part[d] for d in present] + [az_part[d] for d in present])
+    lows, highs = [], []
+    for slot, date in enumerate(present):
+        shift = centre - rg_whole[date]
+        weights = table[slot : slot + 1]
+        row, col = iotas(lines, lines)
+        row = tile_order(row // tile_lines) * tile_lines + row % tile_lines
+        band = banded(
+            col - row + (centre - az_whole[date]), table[dates + slot : dates + slot + 1]
+        )
+        usable = row < sweeps[date] * (lines // MAX_SWEEPS)
+        line = jnp.where(usable, band, 0.0).astype(jnp.bfloat16)
+        line_ref[slot] = line
+        row, col = iotas(columns, columns)
+        own = banded(row - col + shift, weights).astype(jnp.bfloat16)
+        for part in range(parts):
+            inner = jnp.dot(x_ref[slot, part], own, preferred_element_type=jnp.float32)
+            start = (slot * parts + part) * 2 * MARGIN
+            inner_ref[:, start : start + MARGIN] = inner[:, :MARGIN]
+            inner_ref[:, start + MARGIN : start + 2 * MARGIN] = inner[:, columns - MARGIN :]
+            moved = jnp.dot(
+                line, inner.astype(jnp.bfloat16), preferred_element_type=jnp.float32
+            ).astype(jnp.bfloat16)
+            for group, out_ref in enumerate(outs):
+                out_ref[slot, part] = moved[group * tile_lines : (group + 1) * tile_lines]
+        row, col = iotas(edge_rows, LANES)
+        offset = row % MARGIN - col % MARGIN + shift
+        lows.append(banded(offset - MARGIN, weights))
+        highs.append(banded(offset + MARGIN, weights))
+    row, col = iotas(edge_rows, LANES)
+    same = row // MARGIN == col // (2 * MARGIN)
+    upper = (col // MARGIN) % 2 == 1
+    first = col < LANES // 2
+    low = jnp.where(first, lows[0], lows[1])
+    high = jnp.where(first, highs[0], highs[1])
+    low_ref[...] = jnp.where(same & jnp.logical_not(upper), low, 0.0).astype(jnp.bfloat16)
+    high_ref[...] = jnp.where(same & upper, high, 0.0).astype(jnp.bfloat16)
+
+
+def spread_edges(even_ref, odd_ref, edges):
     backward = lax.axis_index("range") % 2
     height, width = even_ref.shape
     for half in range(2):
@@ -180,6 +231,57 @@
         spot = slice(half * (width // 2), (half + 1) * (width // 2))
         edges[1 - backward, rows, :] = even_ref[:, spot]
         edges[backward, rows, :] = odd_ref[:, spot]
+
+
+def patched(tile, border, image):
+    start = image * 2 * MARGIN
+    lane = lax.broadcasted_iota(jnp.int32, border.shape, 1)
+    low = pltpu.roll(border, (LANES - start) % LANES, 1) if start else border
+    high = pltpu.roll(border, (LANES - 2 * MARGIN - start) % LANES, 1)
+    return (
+        jnp.where(lane < MARGIN, low, tile[:, :LANES]),
+        jnp.where(lane >= LANES - MARGIN, high, tile[:, LANES:]),
+    )
+
+
+def border_kernel(inner_ref, even_ref, odd_ref, low_ref, high_ref, line_ref, *refs):
+    *refs, edges = refs
+    tiles, wholes, outs = refs[: CHIPS // 2], refs[CHIPS // 2 : CHIPS], refs[CHIPS:]
+    spread_edges(even_ref, odd_ref, edges)
+    ranged = inner_ref[...]
+    ranged += jnp.dot(edges[0], low_ref[...], preferred_element_type=jnp.float32)
+    ranged += jnp.dot(edges[1], high_ref[...], preferred_element_type=jnp.float32)
+    ranged = ranged.astype(jnp.bfloat16)
+    moved = [
+        jnp.dot(line_ref[slot], ranged, preferred_element_type=jnp.float32) for slot in range(2)
+    ]
+    lane = lax.broadcasted_iota(jnp.int32, moved[0].shape, 1)
+    border = jnp.where(lane < LANES // 2, moved[0], moved[1])
+    dates, parts, height, _ = wholes[0].shape
+    for group, (tile_ref, whole_ref) in enumerate(zip(tiles, wholes)):
+        own = border[group * height : (group + 1) * height]
+        for slot in range(dates):
+            for part in range(parts):
+                tile = tile_ref[slot, part].astype(jnp.float32)
+                low, high = patched(tile, own, slot * parts + part)
+                whole_ref[slot, part, :, :LANES] = low.astype(jnp.bfloat16)
+                whole_ref[slot, part, :, LANES:] = high.astype(jnp.bfloat16)
+    for group, out_ref in enumerate(outs):
+        start = (CHIPS // 2 + group) * height
+        out_ref[...] = border[start : start + height].astype(jnp.bfloat16)
+
+
+def bundle_kernel(*refs):
+    *pieces, out_ref = refs
+    for number, piece_ref in enumerate(pieces):
+        out_ref[number] = piece_ref[...]
+
+
+def resample_kernel(split, inner_ref, even_ref, odd_ref, low_ref, high_ref, line_ref, *refs):
+    out_ref, edges = refs
+    dates, parts, _, columns = inner_ref.shape
+    line_groups, column_groups, tile_lines, tile_columns = split
+    spread_edges(even_ref, odd_ref, edges)
     low = jnp.dot(edges[0], low_ref[...], preferred_element_type=jnp.float32)
     high = jnp.dot(edges[1], high_ref[...], preferred_element_type=jnp.float32)
     for slot in range(dates):
@@ -201,10 +303,7 @@
                         i * tile_lines : (i + 1) * tile_lines,
                         j * tile_columns : (j + 1) * tile_columns,
                     ]
-                    if len(outs) == 1:
-                        outs[0][i * column_groups + j, slot, part] = tile
-                    else:
-                        outs[i][slot, part] = tile
+                    out_ref[i * column_groups + j, slot, part] = tile
 
 
 def partners(date, gap_ref, total):
@@ -302,13 +401,26 @@
 
 
 def chip_looks_kernel(positions, root_ref, gap_ref, pool_ref, *refs):
-    tiles, outs, (stack, sums, pooled) = refs[: CHIPS * CORES], refs[CHIPS * CORES : -3], refs[-3:]
-    dates, _, _, columns = tiles[0].shape
+    count = CHIPS * CORES
+    tiles, refs = refs[:count], refs[count:]
+    half = CHIPS // 2
+    borders, (passed_ref, *outs), (stack, sums, pooled) = refs[:half], refs[half:-3], refs[-3:]
+    dates, parts, _, columns = tiles[0].shape
     me = lax.axis_index("date")
     total = len(tiles) * dates
     scale = 1.0 / (LOOK_AZ * LOOK_RG) ** 0.5
     for position, tile_ref in zip(positions, tiles):
-        stack[position * dates : (position + 1) * dates] = tile_ref[...].astype(jnp.float32)
+        chip = position // CORES - half
+        if chip < 0:
+            stack[position * dates : (position + 1) * dates] = tile_ref[...].astype(jnp.float32)
+            continue
+        border = (passed_ref[chip] if position % CORES else borders[chip][...]).astype(jnp.float32)
+        for slot in range(dates):
+            for number in range(parts):
+                tile = tile_ref[slot, number].astype(jnp.float32)
+                low, high = patched(tile, border, slot * parts + number)
+                stack[position * dates + slot, number, :, :LANES] = low
+                stack[position * dates + slot, number, :, LANES:] = high
 
     def partner_of(kind, date):
         partner = partners(date, gap_ref, total)[kind - 1] if kind else root_ref[0]
@@ -455,38 +567,7 @@
     odd = exchanged(odd, "range", [(j, j + 1) for j in range(1, width - 1, 2)])
     even = exchanged(even, "range", [(j, j + 1) for j in range(0, width - 1, 2)])
 
-    inner, low_taps, high_taps, line_taps, pool = pl.pallas_call(
-        functools.partial(taps_kernel, chips, tile_lines),
-        out_shape=(
-            pltpu.VMEM(block.shape, jnp.float32),
-            pltpu.VMEM((images * MARGIN, images * LANES), jnp.bfloat16),
-            pltpu.VMEM((images * MARGIN, images * LANES), jnp.bfloat16),
-            pltpu.VMEM((dates, lines, lines), jnp.bfloat16),
-            pltpu.VMEM((dates * columns, LANES), jnp.bfloat16),
-        ),
-        in_specs=[SMEM] * len(small) + [VMEM],
-        out_specs=(VMEM,) * 5,
-        cost_estimate=pl.CostEstimate(flops=4000000, bytes_accessed=800000, transcendentals=0),
-        name="taps",
-        compiler_params=pltpu.CompilerParams(vmem_limit_bytes=GRANT),
-    )(*small, near(block))
     tile = (dates, parts, tile_lines, tile_columns)
-    if chips:
-        out_shape = (pltpu.VMEM(tile, jnp.bfloat16),) * CHIPS
-    else:
-        out_shape = (pltpu.VMEM((owners,) + tile, jnp.bfloat16),)
-    tiles = pl.pallas_call(
-        functools.partial(
-            resample_kernel, (line_groups, column_groups, tile_lines, tile_columns)
-        ),
-        out_shape=out_shape,
-        in_specs=[VMEM] * 6,
-        out_specs=(VMEM,) * len(out_shape),
-        scratch_shapes=[pltpu.VMEM((2, lines, images * MARGIN), jnp.bfloat16)],
-        name="resample",
-        compiler_params=pltpu.CompilerParams(vmem_limit_bytes=GRANT),
-    )(*[near(array) for array in (inner, even, odd, low_taps, high_taps, line_taps)])
-
     rows, cols = lines // LOOK_AZ, columns // LOOK_RG
     out_shape = (
         jax.ShapeDtypeStruct((dates, 2 * KINDS, rows, cols), jnp.float32),
@@ -498,15 +579,58 @@
             pairs = [(i, i ^ bits) for i in range(owners) if i < i ^ bits]
             return exchanged(array, "date", pairs)
 
+        line_taps, inner, low_taps, high_taps, pool, *tiles = pl.pallas_call(
+            main_kernel,
+            out_shape=(
+                pltpu.VMEM((dates, lines, lines), jnp.bfloat16),
+                pltpu.VMEM((lines, LANES), jnp.float32),
+                pltpu.VMEM((images * MARGIN, LANES), jnp.bfloat16),
+                pltpu.VMEM((images * MARGIN, LANES), jnp.bfloat16),
+                pltpu.VMEM((dates * columns, LANES), jnp.bfloat16),
+                *[pltpu.VMEM(tile, jnp.bfloat16)] * CHIPS,
+            ),
+            in_specs=[SMEM] * len(small) + [VMEM],
+            out_specs=(VMEM,) * (5 + CHIPS),
+            cost_estimate=pl.CostEstimate(
+                flops=400000000, bytes_accessed=2000000, transcendentals=0
+            ),
+            name="main",
+            compiler_params=pltpu.CompilerParams(vmem_limit_bytes=GRANT),
+        )(*small, near(block))
+        half = CHIPS // 2
+        tiles[0], tiles[1], *borders = pl.pallas_call(
+            border_kernel,
+            out_shape=(pltpu.VMEM(tile, jnp.bfloat16),) * half
+            + (pltpu.VMEM((tile_lines, LANES), jnp.bfloat16),) * half,
+            in_specs=[VMEM] * (6 + half),
+            out_specs=(VMEM,) * CHIPS,
+            scratch_shapes=[pltpu.VMEM((2, lines, images * MARGIN), jnp.bfloat16)],
+            name="border",
+            compiler_params=pltpu.CompilerParams(vmem_limit_bytes=GRANT),
+        )(
+            *[near(array) for array in (inner, even, odd, low_taps, high_taps, line_taps)],
+            *[near(array) for array in tiles[:half]],
+        )
         order = [3, 2, 1]
         own = tiles[0]
         direct = {number: swapped(tiles[number], CORES * number) for number in order}
+        borders = [swapped(borders[n], CORES * (half + n)) for n in range(half)]
         other = swapped(own, 1)
+        direct[1], *borders = lax.optimization_barrier((direct[1], *borders))
         passed = {number: swapped(direct[number], 1) for number in order}
         held, positions = [own, other], [0, 1]
         for number in order:
             held += [direct[number], passed[number]]
             positions += [CORES * number, CORES * number + 1]
+        bundle = pl.pallas_call(
+            bundle_kernel,
+            out_shape=pltpu.VMEM((half, tile_lines, LANES), jnp.bfloat16),
+            in_specs=[VMEM] * half,
+            out_specs=VMEM,
+            name="bundle",
+            compiler_params=pltpu.CompilerParams(vmem_limit_bytes=GRANT),
+        )(*[near(border) for border in borders])
+        held += borders + [swapped(bundle, 1)]
         results = pl.pallas_call(
             functools.partial(chip_looks_kernel, positions),
             out_shape=(pltpu.VMEM((CHANNELS * CHIP_LOOKS, LANES), jnp.float32),) * CHIPS,
@@ -521,7 +645,7 @@
             compiler_params=pltpu.CompilerParams(vmem_limit_bytes=GRANT),
         )(master_epoch_image, gap, near(pool), *[near(tile) for tile in held])
         back = {number: swapped(results[number], CORES * number) for number in order}
-        last = [1, 3, 2]
+        last = [3, 2, 1]
         pieces = [results[0]] + [back[number] for number in last]
         return pl.pallas_call(
             functools.partial(chip_place_kernel, [0] + last),
@@ -532,7 +656,33 @@
             compiler_params=pltpu.CompilerParams(vmem_limit_bytes=GRANT),
         )(*[near(piece) for piece in pieces])
 
-    tiles = lax.all_to_all(tiles[0], "date", 0, 0)
+    inner, low_taps, high_taps, line_taps = pl.pallas_call(
+        taps_kernel,
+        out_shape=(
+            pltpu.VMEM(block.shape, jnp.float32),
+            pltpu.VMEM((images * MARGIN, images * LANES), jnp.bfloat16),
+            pltpu.VMEM((images * MARGIN, images * LANES), jnp.bfloat16),
+            pltpu.VMEM((dates, lines, lines), jnp.bfloat16),
+        ),
+        in_specs=[SMEM] * len(small) + [VMEM],
+        out_specs=(VMEM,) * 4,
+        cost_estimate=pl.CostEstimate(flops=4000000, bytes_accessed=800000, transcendentals=0),
+        name="taps",
+        compiler_params=pltpu.CompilerParams(vmem_limit_bytes=GRANT),
+    )(*small, near(block))
+    tiles = pl.pallas_call(
+        functools.partial(
+            resample_kernel, (line_groups, column_groups, tile_lines, tile_columns)
+        ),
+        out_shape=pltpu.VMEM((owners,) + tile, jnp.bfloat16),
+        in_specs=[VMEM] * 6,
+        out_specs=VMEM,
+        scratch_shapes=[pltpu.VMEM((2, lines, images * MARGIN), jnp.bfloat16)],
+        name="resample",
+        compiler_params=pltpu.CompilerParams(vmem_limit_bytes=GRANT),
+    )(*[near(array) for array in (inner, even, odd, low_taps, high_taps, line_taps)])
+
+    tiles = lax.all_to_all(tiles, "date", 0, 0)
     results = pl.pallas_call(
         looks_kernel,
         out_shape=pltpu.VMEM((owners, dates * CHANNELS, lanes), jnp.float32),

time: 28.3 us -> 29.3 us (1.035)
  starting transfers between devices: 12.7 us -> 16.3 us
  waiting for transfers between devices: 8.7 us -> 6.1 us
    ppermute x12 -> x15, starting transfers between devices: 12.7 us -> 16.3 us  [exchanged(): lax.ppermute(array, axis, [route for a, b in pairs for route in ((a, b),...]
    ppermute x12 -> x15, waiting for transfers between devices: 8.7 us -> 6.1 us  [exchanged(): lax.ppermute(array, axis, [route for a, b in pairs for route in ((a, b),...]
    pallas_call x2 -> x3, Pallas kernels: 1.65 us -> 1.79 us  [the longest x1 1.3 us: body(): pl.pallas_call(main_kernel, out_shape=(pltpu.VMEM((dates, lines, lines),...]
  transfers between devices with their start and end apart: 12 -> 15, of which waited for: 8 -> 6; matrix products, arithmetic and copies ran while one was open for 0% -> 0% of each run, Pallas kernels for 4% -> 6%
where the time goes in v14:
time: 29.3 us; the launch traced here: 29.1 us
  starting transfers between devices  16.3 us (56%)
  waiting for transfers between devices  6.1 us (21%)
  Pallas kernels  5.36 us (18%)
  between operations  1.35 us (5%)
    ppermute x15, starting transfers between devices, exchanged(): lax.ppermute(array, axis, [route for a, b in pairs for route in ((a, b),...  16.3 us
    ppermute x15, waiting for transfers between devices, exchanged(): lax.ppermute(array, axis, [route for a, b in pairs for route in ((a, b),...  6.1 us
    pallas_call x1, Pallas kernels, body(): pl.pallas_call(start_kernel, out_shape=(pltpu.VMEM(block.shape, block.dty...  1.55 us
    pallas_call x1, Pallas kernels, body(): pl.pallas_call(main_kernel, out_shape=(pltpu.VMEM((dates, lines, lines),...  1.3 us
    pallas_call x1, Pallas kernels, body(): pl.pallas_call(functools.partial(chip_looks_kernel, positions), out_shape...  1.25 us
    pallas_call x1, Pallas kernels, body(): pl.pallas_call(functools.partial(chip_place_kernel, [0] + last), out_shap...  0.76 us
  transfers between devices with their start and end apart: 15, of which 6 were waited for; matrix products, arithmetic and copies ran while one was open for 0% of the time, Pallas kernels for 6%

profile of v14, /device:TPU:8, one launch (start us, length us, event | category | flops | bytes accessed | tf_op | source)
XLA Modules:
  0.0 29.1 jit_solution(7837965020733114442)
XLA Ops:
  0.6 1.6 %start.1 = (bf16[2,2,256,256]{3,2,1,0:T(8,128)(2,1)S(1)}, bf16[128,128]{1,0:T(8,128)(2,1)S(1)}, bf16[128,128]{1,0:T(8,128)(2,1)S(1)}, s32[16]{0:T(128)S(4)}, s32...) custom-call(bf16[2,2,256,256]{3,2,1,0:T(8,128)(2,1)} %x_ref.1, ...), custom_call_target="tpu_custom_call" | custom-call | tf_op jit(solution)/shard_map/start/pallas_call | solution.py:551
  2.2 0.1 collective-permute-start
  2.3 5.0 %collective-permute-start.1 = (bf16[128,128]{1,0:T(8,128)(2,1)S(1)}, bf16[128,128]{1,0:T(8,128)(2,1)S(1)}, u32[]{:S(2)}, u32[]{:S(2)}) collective-permute-start(bf16[128,128]{1,0:T(8,128)(2,1)S(1)} %get-tuple-element.41), channel_id=1, source_target_pairs={{1,2},{2,1},{5,6},{6,5},{9,10},{10,9},{13,14},{14,13},{17,18},{18,... | collective-permute-start | bytes 98312 | tf_op jit(solution)/shard_map/ppermute | solution.py:30
  7.3 1.3 %main.1 = (bf16[2,256,256]{2,1,0:T(8,128)(2,1)S(1)}, f32[256,128]{1,0:T(8,128)S(1)}, bf16[64,128]{1,0:T(8,128)(2,1)S(1)}, bf16[64,128]{1,0:T(8,128)(2,1)S(1)}, b...) custom-call(s32[16]{0:T(128)S(4)} %get-tuple-element.32.az_whole, ...), custom_call_target="tpu_custom_call" | custom-call | flops 400000000 | bytes 2000000 | tf_op jit(solution)/shard_map/main/pallas_call | solution.py:582
  8.6 2.5 %collective-permute-start.3 = (bf16[2,2,64,256]{3,2,1,0:T(8,128)(2,1)S(1)}, bf16[2,2,64,256]{3,2,1,0:T(8,128)(2,1)S(1)}, u32[]{:S(2)}, u32[]{:S(2)}) collective-permute-start(bf16[2,2,64,256]{3,2,1,0:T(8,128)(2,1)S(1)} %get-tuple-element.48), channel_id=1, source_target_pairs={{0,24},{24,0},{4,28},{28,4},{8,16},{16,8},{12,20},{20,12},{1,25},{... | collective-permute-start | bytes 393224 | tf_op jit(solution)/shard_map/ppermute | solution.py:30
  11.1 0.5 %collective-permute-start.5 = (bf16[2,2,64,256]{3,2,1,0:T(8,128)(2,1)S(1)}, bf16[2,2,64,256]{3,2,1,0:T(8,128)(2,1)S(1)}, u32[]{:S(2)}, u32[]{:S(2)}) collective-permute-start(bf16[2,2,64,256]{3,2,1,0:T(8,128)(2,1)S(1)} %get-tuple-element.49), channel_id=1, source_target_pairs={{0,16},{16,0},{4,20},{20,4},{8,24},{24,8},{12,28},{28,12},{1,17},{... | collective-permute-start | bytes 393224 | tf_op jit(solution)/shard_map/ppermute | solution.py:30
  11.6 0.5 %border.1 = (bf16[2,2,64,256]{3,2,1,0:T(8,128)(2,1)S(1)}, bf16[2,2,64,256]{3,2,1,0:T(8,128)(2,1)S(1)}, bf16[64,128]{1,0:T(8,128)(2,1)S(1)}, bf16[64,128]{1,0:T(8,128)(2,1)S(1)}) custom-call(f32[256,128]{1,0:T(8,128)S(1)} %get-tuple-element.39.inner_ref, bf16[128,128]{1,0:T(8,128)(2,1)S(1)} %collective-permute-done.even_ref, ...), custom_call_target="tpu_custom_call" | custom-call | tf_op jit(solution)/shard_map/border/pallas_call | solution.py:601
  12.1 0.6 %collective-permute-start.7 = (bf16[2,2,64,256]{3,2,1,0:T(8,128)(2,1)S(1)}, bf16[2,2,64,256]{3,2,1,0:T(8,128)(2,1)S(1)}, u32[]{:S(2)}, u32[]{:S(2)}) collective-permute-start(bf16[2,2,64,256]{3,2,1,0:T(8,128)(2,1)S(1)} %get-tuple-element.50), channel_id=1, source_target_pairs={{0,8},{8,0},{4,12},{12,4},{16,24},{24,16},{20,28},{28,20},{1,9},{9... | collective-permute-start | bytes 393224 | tf_op jit(solution)/shard_map/ppermute | solution.py:30
  12.7 1.5 %collective-permute-start.8 = (bf16[64,128]{1,0:T(8,128)(2,1)S(1)}, bf16[64,128]{1,0:T(8,128)(2,1)S(1)}, u32[]{:S(2)}, u32[]{:S(2)}) collective-permute-start(bf16[64,128]{1,0:T(8,128)(2,1)S(1)} %get-tuple-element.51), channel_id=1, source_target_pairs={{0,16},{16,0},{4,20},{20,4},{8,24},{24,8},{12,28},{28,12},{1,17},{... | collective-permute-start | bytes 49160 | tf_op jit(solution)/shard_map/ppermute | solution.py:30
  14.3 1.4 %collective-permute-start.9 = (bf16[64,128]{1,0:T(8,128)(2,1)S(1)}, bf16[64,128]{1,0:T(8,128)(2,1)S(1)}, u32[]{:S(2)}, u32[]{:S(2)}) collective-permute-start(bf16[64,128]{1,0:T(8,128)(2,1)S(1)} %get-tuple-element.52), channel_id=1, source_target_pairs={{0,24},{24,0},{4,28},{28,4},{8,16},{16,8},{12,20},{20,12},{1,25},{... | collective-permute-start | bytes 49160 | tf_op jit(solution)/shard_map/ppermute | solution.py:30
  15.7 1.9 %collective-permute-done.8.refs_0_.refs_8_ = bf16[64,128]{1,0:T(8,128)(2,1)S(1)} collective-permute-done((bf16[64,128]{1,0:T(8,128)(2,1)S(1)}, bf16[64,128]{1,0:T(8,128)(2,1)S(1)}, u32[]{:S(2)}, u32[]{:S(2)}) %collective-permute-start.8) | collective-permute-done | bytes 16416 | tf_op jit(solution)/shard_map/ppermute | solution.py:30
  17.6 0.5 %collective-permute-start.4 = (bf16[2,2,64,256]{3,2,1,0:T(8,128)(2,1)S(1)}, bf16[2,2,64,256]{3,2,1,0:T(8,128)(2,1)S(1)}, u32[]{:S(2)}, u32[]{:S(2)}) collective-permute-start(bf16[2,2,64,256]{3,2,1,0:T(8,128)(2,1)S(1)} %collective-permute-done.3.refs_2_), channel_id=1, source_target_pairs={{0,4},{4,0},{8,12},{12,8},{16,20},{20,16},{24,28},{28,24},{1,5},{5... | collective-permute-start | bytes 393224 | tf_op jit(solution)/shard_map/ppermute | solution.py:30
  18.1 0.1 collective-permute-start.6
  18.2 0.7 %collective-permute-done.9.refs_1_.refs_9_ = bf16[64,128]{1,0:T(8,128)(2,1)S(1)} collective-permute-done((bf16[64,128]{1,0:T(8,128)(2,1)S(1)}, bf16[64,128]{1,0:T(8,128)(2,1)S(1)}, u32[]{:S(2)}, u32[]{:S(2)}) %collective-permute-start.9) | collective-permute-done | bytes 16416 | tf_op jit(solution)/shard_map/ppermute | solution.py:30
  18.9 0.5 %collective-permute-start.11 = (bf16[2,64,128]{2,1,0:T(8,128)(2,1)S(1)}, bf16[2,64,128]{2,1,0:T(8,128)(2,1)S(1)}, u32[]{:S(2)}, u32[]{:S(2)}) collective-permute-start(bf16[2,64,128]{2,1,0:T(8,128)(2,1)S(1)} %bundle.1), channel_id=1, source_target_pairs={{0,4},{4,0},{8,12},{12,8},{16,20},{20,16},{24,28},{28,24},{1,5},{5... | collective-permute-start | bytes 98312 | tf_op jit(solution)/shard_map/ppermute | solution.py:30
  20.1 0.2 collective-permute-done.11.refs_10_
  20.3 1.3 %looks.1 = (f32[36,128]{1,0:T(8,128)S(1)}, f32[36,128]{1,0:T(8,128)S(1)}, f32[36,128]{1,0:T(8,128)S(1)}, f32[36,128]{1,0:T(8,128)S(1)}) custom-call(s32[1]{0:T(128)S(6)} %copy.10.root_ref, s32[2,16]{1,0:T(2,128)S(4)} %get-tuple-element.31.gap_ref, bf16[512,128]{1,0:T(8,128)(2,1)S(1)} %get-tuple-element.38.pool_ref, ...), custom_call_target="tpu_custom_call" | custom-call | tf_op jit(solution)/shard_map/looks/pallas_call | solution.py:634
  21.6 1.5 %collective-permute-start.12 = (f32[36,128]{1,0:T(8,128)S(1)}, f32[36,128]{1,0:T(8,128)S(1)}, u32[]{:S(2)}, u32[]{:S(2)}) collective-permute-start(f32[36,128]{1,0:T(8,128)S(1)} %get-tuple-element.57), channel_id=1, source_target_pairs={{0,24},{24,0},{4,28},{28,4},{8,16},{16,8},{12,20},{20,12},{1,25},{... | collective-permute-start | bytes 55304 | tf_op jit(solution)/shard_map/ppermute | solution.py:30
  23.1 1.5 %collective-permute-start.13 = (f32[36,128]{1,0:T(8,128)S(1)}, f32[36,128]{1,0:T(8,128)S(1)}, u32[]{:S(2)}, u32[]{:S(2)}) collective-permute-start(f32[36,128]{1,0:T(8,128)S(1)} %get-tuple-element.58), channel_id=1, source_target_pairs={{0,16},{16,0},{4,20},{20,4},{8,24},{24,8},{12,28},{28,12},{1,17},{... | collective-permute-start | bytes 55304 | tf_op jit(solution)/shard_map/ppermute | solution.py:30
  24.6 0.5 %collective-permute-start.14 = (f32[36,128]{1,0:T(8,128)S(1)}, f32[36,128]{1,0:T(8,128)S(1)}, u32[]{:S(2)}, u32[]{:S(2)}) collective-permute-start(f32[36,128]{1,0:T(8,128)S(1)} %get-tuple-element.59), channel_id=1, source_target_pairs={{0,8},{8,0},{4,12},{12,4},{16,24},{24,16},{20,28},{28,20},{1,9},{9... | collective-permute-start | bytes 55304 | tf_op jit(solution)/shard_map/ppermute | solution.py:30
  25.1 1.2 %collective-permute-done.12.refs_1_ = f32[36,128]{1,0:T(8,128)S(1)} collective-permute-done((f32[36,128]{1,0:T(8,128)S(1)}, f32[36,128]{1,0:T(8,128)S(1)}, u32[]{:S(2)}, u32[]{:S(2)}) %collective-permute-start.12) | collective-permute-done | bytes 18464 | tf_op jit(solution)/shard_map/ppermute | solution.py:30
  26.3 0.5 %collective-permute-done.13.refs_2_ = f32[36,128]{1,0:T(8,128)S(1)} collective-permute-done((f32[36,128]{1,0:T(8,128)S(1)}, f32[36,128]{1,0:T(8,128)S(1)}, u32[]{:S(2)}, u32[]{:S(2)}) %collective-permute-start.13) | collective-permute-done | bytes 18464 | tf_op jit(solution)/shard_map/ppermute | solution.py:30
  26.8 1.5 %collective-permute-done.14.refs_3_ = f32[36,128]{1,0:T(8,128)S(1)} collective-permute-done((f32[36,128]{1,0:T(8,128)S(1)}, f32[36,128]{1,0:T(8,128)S(1)}, u32[]{:S(2)}, u32[]{:S(2)}) %collective-permute-start.14) | collective-permute-done | bytes 18464 | tf_op jit(solution)/shard_map/ppermute | solution.py:30
  28.4 0.8 %place.1 = (f32[2,6,16,64]{3,2,1,0:T(8,128)}, f32[2,3,16,64]{3,2,1,0:T(8,128)}) custom-call(f32[36,128]{1,0:T(8,128)S(1)} %get-tuple-element.56.refs_0_, f32[36,128]{1,0:T(8,128)S(1)} %collective-permute-done.12.refs_1_, f32[36,128]{1,0:T(8,128)S(1)} %collective-permute-done.13.refs_2_, f32[36,128]{1,0:T(8,128)S(1)} %collective-permute-done.14.refs_3_), custom_call_target="tpu_custom_call" | custom-call | tf_op jit(solution)/shard_map/place/pallas_call | solution.py:650
  (12 shorter events, 0.0 us)
Async XLA Ops:
  2.2 9.4 %collective-permute-start = (bf16[128,128]{1,0:T(8,128)(2,1)S(1)}, bf16[128,128]{1,0:T(8,128)(2,1)S(1)}, u32[]{:S(2)}, u32[]{:S(2)}) collective-permute-start(bf16[128,128]{1,0:T(8,128)(2,1)S(1)} %get-tuple-element.40), channel_id=1, source_target_pairs={{0,1},{1,0},{2,3},{3,2},{4,5},{5,4},{6,7},{7,6},{8,9},{9,8},{10,11... | collective-permute-start | bytes 98312 | tf_op jit(solution)/shard_map/ppermute | solution.py:30
  2.3 9.4 %collective-permute-start.1 = (bf16[128,128]{1,0:T(8,128)(2,1)S(1)}, bf16[128,128]{1,0:T(8,128)(2,1)S(1)}, u32[]{:S(2)}, u32[]{:S(2)}) collective-permute-start(bf16[128,128]{1,0:T(8,128)(2,1)S(1)} %get-tuple-element.41), channel_id=1, source_target_pairs={{1,2},{2,1},{5,6},{6,5},{9,10},{10,9},{13,14},{14,13},{17,18},{18,... | collective-permute-start | bytes 98312 | tf_op jit(solution)/shard_map/ppermute | solution.py:30
  8.6 9.0 %collective-permute-start.3 = (bf16[2,2,64,256]{3,2,1,0:T(8,128)(2,1)S(1)}, bf16[2,2,64,256]{3,2,1,0:T(8,128)(2,1)S(1)}, u32[]{:S(2)}, u32[]{:S(2)}) collective-permute-start(bf16[2,2,64,256]{3,2,1,0:T(8,128)(2,1)S(1)} %get-tuple-element.48), channel_id=1, source_target_pairs={{0,24},{24,0},{4,28},{28,4},{8,16},{16,8},{12,20},{20,12},{1,25},{... | collective-permute-start | bytes 393224 | tf_op jit(solution)/shard_map/ppermute | solution.py:30
  11.1 7.0 %collective-permute-start.5 = (bf16[2,2,64,256]{3,2,1,0:T(8,128)(2,1)S(1)}, bf16[2,2,64,256]{3,2,1,0:T(8,128)(2,1)S(1)}, u32[]{:S(2)}, u32[]{:S(2)}) collective-permute-start(bf16[2,2,64,256]{3,2,1,0:T(8,128)(2,1)S(1)} %get-tuple-element.49), channel_id=1, source_target_pairs={{0,16},{16,0},{4,20},{20,4},{8,24},{24,8},{12,28},{28,12},{1,17},{... | collective-permute-start | bytes 393224 | tf_op jit(solution)/shard_map/ppermute | solution.py:30
  12.1 6.8 %collective-permute-start.7 = (bf16[2,2,64,256]{3,2,1,0:T(8,128)(2,1)S(1)}, bf16[2,2,64,256]{3,2,1,0:T(8,128)(2,1)S(1)}, u32[]{:S(2)}, u32[]{:S(2)}) collective-permute-start(bf16[2,2,64,256]{3,2,1,0:T(8,128)(2,1)S(1)} %get-tuple-element.50), channel_id=1, source_target_pairs={{0,8},{8,0},{4,12},{12,4},{16,24},{24,16},{20,28},{28,20},{1,9},{9... | collective-permute-start | bytes 393224 | tf_op jit(solution)/shard_map/ppermute | solution.py:30
  12.7 4.9 %collective-permute-start.8 = (bf16[64,128]{1,0:T(8,128)(2,1)S(1)}, bf16[64,128]{1,0:T(8,128)(2,1)S(1)}, u32[]{:S(2)}, u32[]{:S(2)}) collective-permute-start(bf16[64,128]{1,0:T(8,128)(2,1)S(1)} %get-tuple-element.51), channel_id=1, source_target_pairs={{0,16},{16,0},{4,20},{20,4},{8,24},{24,8},{12,28},{28,12},{1,17},{... | collective-permute-start | bytes 49160 | tf_op jit(solution)/shard_map/ppermute | solution.py:30
  14.3 4.6 %collective-permute-start.9 = (bf16[64,128]{1,0:T(8,128)(2,1)S(1)}, bf16[64,128]{1,0:T(8,128)(2,1)S(1)}, u32[]{:S(2)}, u32[]{:S(2)}) collective-permute-start(bf16[64,128]{1,0:T(8,128)(2,1)S(1)} %get-tuple-element.52), channel_id=1, source_target_pairs={{0,24},{24,0},{4,28},{28,4},{8,16},{16,8},{12,20},{20,12},{1,25},{... | collective-permute-start | bytes 49160 | tf_op jit(solution)/shard_map/ppermute | solution.py:30
  17.6 2.5 %collective-permute-start.2 = (bf16[2,2,64,256]{3,2,1,0:T(8,128)(2,1)S(1)}, bf16[2,2,64,256]{3,2,1,0:T(8,128)(2,1)S(1)}, u32[]{:S(2)}, u32[]{:S(2)}) collective-permute-start(bf16[2,2,64,256]{3,2,1,0:T(8,128)(2,1)S(1)} %get-tuple-element.47.refs_0_), channel_id=1, source_target_pairs={{0,4},{4,0},{8,12},{12,8},{16,20},{20,16},{24,28},{28,24},{1,5},{5... | collective-permute-start | bytes 393224 | tf_op jit(solution)/shard_map/ppermute | solution.py:30
  17.6 2.7 %collective-permute-start.4 = (bf16[2,2,64,256]{3,2,1,0:T(8,128)(2,1)S(1)}, bf16[2,2,64,256]{3,2,1,0:T(8,128)(2,1)S(1)}, u32[]{:S(2)}, u32[]{:S(2)}) collective-permute-start(bf16[2,2,64,256]{3,2,1,0:T(8,128)(2,1)S(1)} %collective-permute-done.3.refs_2_), channel_id=1, source_target_pairs={{0,4},{4,0},{8,12},{12,8},{16,20},{20,16},{24,28},{28,24},{1,5},{5... | collective-permute-start | bytes 393224 | tf_op jit(solution)/shard_map/ppermute | solution.py:30
  18.1 2.2 %collective-permute-start.6 = (bf16[2,2,64,256]{3,2,1,0:T(8,128)(2,1)S(1)}, bf16[2,2,64,256]{3,2,1,0:T(8,128)(2,1)S(1)}, u32[]{:S(2)}, u32[]{:S(2)}) collective-permute-start(bf16[2,2,64,256]{3,2,1,0:T(8,128)(2,1)S(1)} %collective-permute-done.5.refs_4_), channel_id=1, source_target_pairs={{0,4},{4,0},{8,12},{12,8},{16,20},{20,16},{24,28},{28,24},{1,5},{5... | collective-permute-start | bytes 393224 | tf_op jit(solution)/shard_map/ppermute | solution.py:30
  18.9 1.4 %collective-permute-start.10 = (bf16[2,2,64,256]{3,2,1,0:T(8,128)(2,1)S(1)}, bf16[2,2,64,256]{3,2,1,0:T(8,128)(2,1)S(1)}, u32[]{:S(2)}, u32[]{:S(2)}) collective-permute-start(bf16[2,2,64,256]{3,2,1,0:T(8,128)(2,1)S(1)} %collective-permute-done.7.refs_6_), channel_id=1, source_target_pairs={{0,4},{4,0},{8,12},{12,8},{16,20},{20,16},{24,28},{28,24},{1,5},{5... | collective-permute-start | bytes 393224 | tf_op jit(solution)/shard_map/ppermute | solution.py:30
  18.9 1.4 %collective-permute-start.11 = (bf16[2,64,128]{2,1,0:T(8,128)(2,1)S(1)}, bf16[2,64,128]{2,1,0:T(8,128)(2,1)S(1)}, u32[]{:S(2)}, u32[]{:S(2)}) collective-permute-start(bf16[2,64,128]{2,1,0:T(8,128)(2,1)S(1)} %bundle.1), channel_id=1, source_target_pairs={{0,4},{4,0},{8,12},{12,8},{16,20},{20,16},{24,28},{28,24},{1,5},{5... | collective-permute-start | bytes 98312 | tf_op jit(solution)/shard_map/ppermute | solution.py:30
  21.6 4.7 %collective-permute-start.12 = (f32[36,128]{1,0:T(8,128)S(1)}, f32[36,128]{1,0:T(8,128)S(1)}, u32[]{:S(2)}, u32[]{:S(2)}) collective-permute-start(f32[36,128]{1,0:T(8,128)S(1)} %get-tuple-element.57), channel_id=1, source_target_pairs={{0,24},{24,0},{4,28},{28,4},{8,16},{16,8},{12,20},{20,12},{1,25},{... | collective-permute-start | bytes 55304 | tf_op jit(solution)/shard_map/ppermute | solution.py:30
  23.1 3.8 %collective-permute-start.13 = (f32[36,128]{1,0:T(8,128)S(1)}, f32[36,128]{1,0:T(8,128)S(1)}, u32[]{:S(2)}, u32[]{:S(2)}) collective-permute-start(f32[36,128]{1,0:T(8,128)S(1)} %get-tuple-element.58), channel_id=1, source_target_pairs={{0,16},{16,0},{4,20},{20,4},{8,24},{24,8},{12,28},{28,12},{1,17},{... | collective-permute-start | bytes 55304 | tf_op jit(solution)/shard_map/ppermute | solution.py:30
  24.6 3.8 %collective-permute-start.14 = (f32[36,128]{1,0:T(8,128)S(1)}, f32[36,128]{1,0:T(8,128)S(1)}, u32[]{:S(2)}, u32[]{:S(2)}) collective-permute-start(f32[36,128]{1,0:T(8,128)S(1)} %get-tuple-element.59), channel_id=1, source_target_pairs={{0,8},{8,0},{4,12},{12,4},{16,24},{24,16},{20,28},{28,20},{1,9},{9... | collective-permute-start | bytes 55304 | tf_op jit(solution)/shard_map/ppermute | solution.py:30

commit v15 on v13

--- a/solution.py
+++ b/solution.py
@@ -363,7 +363,7 @@
             for channel, value in (
                 (2 * kind, real * scale),
                 (2 * kind + 1, imag * scale),
-                (2 * KINDS + kind, jnp.sqrt(real * real + imag * imag) / jnp.sqrt(power + 1e-06)),
+                (2 * KINDS + kind, jnp.sqrt((real * real + imag * imag) / (power + 1e-06))),
             ):
                 outs[chip][channel * CHIP_LOOKS : (channel + 1) * CHIP_LOOKS, :] = value
 
@@ -515,7 +515,7 @@
             scratch_shapes=[
                 pltpu.VMEM((total, parts, tile_lines, tile_columns), jnp.float32),
                 pltpu.VMEM((CHIPS * QUANTITIES * CHIP_LOOKS, dates * columns), jnp.float32),
-                pltpu.VMEM((CHIPS * QUANTITIES * CHIP_LOOKS, LANES), jnp.float32),
+                pltpu.VMEM(((CHIPS + 1) * QUANTITIES * CHIP_LOOKS, LANES), jnp.float32),
             ],
             name="looks",
             compiler_params=pltpu.CompilerParams(vmem_limit_bytes=GRANT),

time: 28.3 us -> 28.3 us (level)
  no operation moved by 1% of the time
where the time goes in v15:
time: 28.3 us; the launch traced here: 27.9 us
  starting transfers between devices  12.7 us (45%)
  waiting for transfers between devices  8.7 us (31%)
  Pallas kernels  5.13 us (18%)
  between operations  1.36 us (5%)
    ppermute x12, starting transfers between devices, exchanged(): lax.ppermute(array, axis, [route for a, b in pairs for route in ((a, b),...  12.7 us
    ppermute x12, waiting for transfers between devices, exchanged(): lax.ppermute(array, axis, [route for a, b in pairs for route in ((a, b),...  8.7 us
    pallas_call x1, Pallas kernels, body(): pl.pallas_call(start_kernel, out_shape=(pltpu.VMEM(block.shape, block.dty...  1.55 us
    pallas_call x1, Pallas kernels, body(): pl.pallas_call(functools.partial(chip_looks_kernel, positions), out_shape...  1.17 us
    pallas_call x1, Pallas kernels, body(): pl.pallas_call(functools.partial(taps_kernel, chips, tile_lines), out_sha...  1.06 us
    pallas_call x1, Pallas kernels, body(): pl.pallas_call(functools.partial(chip_place_kernel, [0] + last), out_shap...  0.76 us
    pallas_call x1, Pallas kernels, body(): pl.pallas_call(functools.partial(resample_kernel, (line_groups, column_gr...  0.58 us
  transfers between devices with their start and end apart: 12, of which 8 were waited for; matrix products, arithmetic and copies ran while one was open for 0% of the time, Pallas kernels for 4%

profile of v15, /device:TPU:8, one launch (start us, length us, event | category | flops | bytes accessed | tf_op | source)
XLA Modules:
  0.0 27.9 jit_solution(3594998079697015968)
XLA Ops:
  0.6 1.6 %start.1 = (bf16[2,2,256,256]{3,2,1,0:T(8,128)(2,1)S(1)}, bf16[128,128]{1,0:T(8,128)(2,1)S(1)}, bf16[128,128]{1,0:T(8,128)(2,1)S(1)}, s32[16]{0:T(128)S(4)}, s32...) custom-call(bf16[2,2,256,256]{3,2,1,0:T(8,128)(2,1)} %x_ref.1, ...), custom_call_target="tpu_custom_call" | custom-call | tf_op jit(solution)/shard_map/start/pallas_call | solution.py:439
  2.2 0.1 collective-permute-start
  2.3 5.0 %collective-permute-start.1 = (bf16[128,128]{1,0:T(8,128)(2,1)S(1)}, bf16[128,128]{1,0:T(8,128)(2,1)S(1)}, u32[]{:S(2)}, u32[]{:S(2)}) collective-permute-start(bf16[128,128]{1,0:T(8,128)(2,1)S(1)} %get-tuple-element.34), channel_id=1, source_target_pairs={{1,2},{2,1},{5,6},{6,5},{9,10},{10,9},{13,14},{14,13},{17,18},{18,... | collective-permute-start | bytes 98312 | tf_op jit(solution)/shard_map/ppermute | solution.py:30
  7.3 1.1 %taps.1 = (f32[2,2,256,256]{3,2,1,0:T(8,128)S(1)}, bf16[64,512]{1,0:T(8,128)(2,1)S(1)}, bf16[64,512]{1,0:T(8,128)(2,1)S(1)}, bf16[2,256,256]{2,1,0:T(8,128)(2,1)S(1)}, bf16[512,128]{1,0:T(8,128)(2,1)S(1)}) custom-call(s32[16]{0:T(128)S(4)} %get-tuple-element.25.az_whole, s32[16]{0:T(128)S(4)} %get-tuple-element.26.az_part, ...), custom_call_target="tpu_custom_call" | custom-call | flops 4000000 | bytes 800000 | tf_op jit(solution)/shard_map/taps/pallas_call | solution.py:458
  8.4 0.0 collective-permute-done.even_ref
  8.4 0.8 %collective-permute-done.1.odd_ref = bf16[128,128]{1,0:T(8,128)(2,1)S(1)} collective-permute-done((bf16[128,128]{1,0:T(8,128)(2,1)S(1)}, bf16[128,128]{1,0:T(8,128)(2,1)S(1)}, u32[]{:S(2)}, u32[]{:S(2)}) %collective-permute-start.1) | collective-permute-done | bytes 32800 | tf_op jit(solution)/shard_map/ppermute | solution.py:30
  9.2 0.6 %resample.1 = (bf16[2,2,64,256]{3,2,1,0:T(8,128)(2,1)S(1)}, bf16[2,2,64,256]{3,2,1,0:T(8,128)(2,1)S(1)}, bf16[2,2,64,256]{3,2,1,0:T(8,128)(2,1)S(1)}, bf16[2,2,64,256]{3,2,1,0:T(8,128)(2,1)S(1)}) custom-call(f32[2,2,256,256]{3,2,1,0:T(8,128)S(1)} %get-tuple-element.32.inner_ref, bf16[128,128]{1,0:T(8,128)(2,1)S(1)} %collective-permute-done.even_ref, ...), custom_call_target="tpu_custom_call" | custom-call | tf_op jit(solution)/shard_map/resample/pallas_call | solution.py:478
  9.8 2.5 %collective-permute-start.3 = (bf16[2,2,64,256]{3,2,1,0:T(8,128)(2,1)S(1)}, bf16[2,2,64,256]{3,2,1,0:T(8,128)(2,1)S(1)}, u32[]{:S(2)}, u32[]{:S(2)}) collective-permute-start(bf16[2,2,64,256]{3,2,1,0:T(8,128)(2,1)S(1)} %get-tuple-element.39), channel_id=1, source_target_pairs={{0,24},{24,0},{4,28},{28,4},{8,16},{16,8},{12,20},{20,12},{1,25},{... | collective-permute-start | bytes 393224 | tf_op jit(solution)/shard_map/ppermute | solution.py:30
  12.3 0.5 %collective-permute-start.5 = (bf16[2,2,64,256]{3,2,1,0:T(8,128)(2,1)S(1)}, bf16[2,2,64,256]{3,2,1,0:T(8,128)(2,1)S(1)}, u32[]{:S(2)}, u32[]{:S(2)}) collective-permute-start(bf16[2,2,64,256]{3,2,1,0:T(8,128)(2,1)S(1)} %get-tuple-element.40), channel_id=1, source_target_pairs={{0,16},{16,0},{4,20},{20,4},{8,24},{24,8},{12,28},{28,12},{1,17},{... | collective-permute-start | bytes 393224 | tf_op jit(solution)/shard_map/ppermute | solution.py:30
  12.8 0.5 %collective-permute-start.7 = (bf16[2,2,64,256]{3,2,1,0:T(8,128)(2,1)S(1)}, bf16[2,2,64,256]{3,2,1,0:T(8,128)(2,1)S(1)}, u32[]{:S(2)}, u32[]{:S(2)}) collective-permute-start(bf16[2,2,64,256]{3,2,1,0:T(8,128)(2,1)S(1)} %get-tuple-element.41), channel_id=1, source_target_pairs={{0,8},{8,0},{4,12},{12,4},{16,24},{24,16},{20,28},{28,20},{1,9},{9... | collective-permute-start | bytes 393224 | tf_op jit(solution)/shard_map/ppermute | solution.py:30
  13.3 3.6 %collective-permute-done.3.refs_2_ = bf16[2,2,64,256]{3,2,1,0:T(8,128)(2,1)S(1)} collective-permute-done((bf16[2,2,64,256]{3,2,1,0:T(8,128)(2,1)S(1)}, bf16[2,2,64,256]{3,2,1,0:T(8,128)(2,1)S(1)}, u32[]{:S(2)}, u32[]{:S(2)}) %collective-permute-start.3) | collective-permute-done | bytes 131104 | tf_op jit(solution)/shard_map/ppermute | solution.py:30
  17.0 0.0 collective-permute-start.4
  17.0 0.9 %collective-permute-done.5.refs_4_ = bf16[2,2,64,256]{3,2,1,0:T(8,128)(2,1)S(1)} collective-permute-done((bf16[2,2,64,256]{3,2,1,0:T(8,128)(2,1)S(1)}, bf16[2,2,64,256]{3,2,1,0:T(8,128)(2,1)S(1)}, u32[]{:S(2)}, u32[]{:S(2)}) %collective-permute-start.5) | collective-permute-done | bytes 131104 | tf_op jit(solution)/shard_map/ppermute | solution.py:30
  17.8 0.5 %collective-permute-start.8 = (bf16[2,2,64,256]{3,2,1,0:T(8,128)(2,1)S(1)}, bf16[2,2,64,256]{3,2,1,0:T(8,128)(2,1)S(1)}, u32[]{:S(2)}, u32[]{:S(2)}) collective-permute-start(bf16[2,2,64,256]{3,2,1,0:T(8,128)(2,1)S(1)} %collective-permute-done.7.refs_6_), channel_id=1, source_target_pairs={{0,4},{4,0},{8,12},{12,8},{16,20},{20,16},{24,28},{28,24},{1,5},{5... | collective-permute-start | bytes 393224 | tf_op jit(solution)/shard_map/ppermute | solution.py:30
  19.0 0.2 collective-permute-done.6.refs_5_
  19.2 0.2 collective-permute-done.8.refs_7_
  19.3 1.2 %looks.1 = (f32[36,128]{1,0:T(8,128)S(1)}, f32[36,128]{1,0:T(8,128)S(1)}, f32[36,128]{1,0:T(8,128)S(1)}, f32[36,128]{1,0:T(8,128)S(1)}) custom-call(s32[1]{0:T(128)S(6)} %copy.10.root_ref, s32[2,16]{1,0:T(2,128)S(4)} %get-tuple-element.24.gap_ref, bf16[512,128]{1,0:T(8,128)(2,1)S(1)} %get-tuple-element.31.pool_ref, ...), custom_call_target="tpu_custom_call" | custom-call | tf_op jit(solution)/shard_map/looks/pallas_call | solution.py:510
  20.5 1.6 %collective-permute-start.10 = (f32[36,128]{1,0:T(8,128)S(1)}, f32[36,128]{1,0:T(8,128)S(1)}, u32[]{:S(2)}, u32[]{:S(2)}) collective-permute-start(f32[36,128]{1,0:T(8,128)S(1)} %get-tuple-element.44), channel_id=1, source_target_pairs={{0,24},{24,0},{4,28},{28,4},{8,16},{16,8},{12,20},{20,12},{1,25},{... | collective-permute-start | bytes 55304 | tf_op jit(solution)/shard_map/ppermute | solution.py:30
  22.2 1.2 %collective-permute-start.11 = (f32[36,128]{1,0:T(8,128)S(1)}, f32[36,128]{1,0:T(8,128)S(1)}, u32[]{:S(2)}, u32[]{:S(2)}) collective-permute-start(f32[36,128]{1,0:T(8,128)S(1)} %get-tuple-element.45), channel_id=1, source_target_pairs={{0,16},{16,0},{4,20},{20,4},{8,24},{24,8},{12,28},{28,12},{1,17},{... | collective-permute-start | bytes 55304 | tf_op jit(solution)/shard_map/ppermute | solution.py:30
  23.4 0.7 %collective-permute-start.9 = (f32[36,128]{1,0:T(8,128)S(1)}, f32[36,128]{1,0:T(8,128)S(1)}, u32[]{:S(2)}, u32[]{:S(2)}) collective-permute-start(f32[36,128]{1,0:T(8,128)S(1)} %get-tuple-element.43), channel_id=1, source_target_pairs={{0,8},{8,0},{4,12},{12,4},{16,24},{24,16},{20,28},{28,20},{1,9},{9... | collective-permute-start | bytes 55304 | tf_op jit(solution)/shard_map/ppermute | solution.py:30
  24.1 1.2 %collective-permute-done.10.refs_2_ = f32[36,128]{1,0:T(8,128)S(1)} collective-permute-done((f32[36,128]{1,0:T(8,128)S(1)}, f32[36,128]{1,0:T(8,128)S(1)}, u32[]{:S(2)}, u32[]{:S(2)}) %collective-permute-start.10) | collective-permute-done | bytes 18464 | tf_op jit(solution)/shard_map/ppermute | solution.py:30
  25.3 0.7 %collective-permute-done.11.refs_3_ = f32[36,128]{1,0:T(8,128)S(1)} collective-permute-done((f32[36,128]{1,0:T(8,128)S(1)}, f32[36,128]{1,0:T(8,128)S(1)}, u32[]{:S(2)}, u32[]{:S(2)}) %collective-permute-start.11) | collective-permute-done | bytes 18464 | tf_op jit(solution)/shard_map/ppermute | solution.py:30
  26.0 1.2 %collective-permute-done.9.refs_1_ = f32[36,128]{1,0:T(8,128)S(1)} collective-permute-done((f32[36,128]{1,0:T(8,128)S(1)}, f32[36,128]{1,0:T(8,128)S(1)}, u32[]{:S(2)}, u32[]{:S(2)}) %collective-permute-start.9) | collective-permute-done | bytes 18464 | tf_op jit(solution)/shard_map/ppermute | solution.py:30
  27.2 0.8 %place.1 = (f32[2,6,16,64]{3,2,1,0:T(8,128)}, f32[2,3,16,64]{3,2,1,0:T(8,128)}) custom-call(f32[36,128]{1,0:T(8,128)S(1)} %get-tuple-element.42.refs_0_, f32[36,128]{1,0:T(8,128)S(1)} %collective-permute-done.9.refs_1_, f32[36,128]{1,0:T(8,128)S(1)} %collective-permute-done.10.refs_2_, f32[36,128]{1,0:T(8,128)S(1)} %collective-permute-done.11.refs_3_), custom_call_target="tpu_custom_call" | custom-call | tf_op jit(solution)/shard_map/place/pallas_call | solution.py:526
  (5 shorter events, 0.0 us)
Async XLA Ops:
  2.2 6.2 %collective-permute-start = (bf16[128,128]{1,0:T(8,128)(2,1)S(1)}, bf16[128,128]{1,0:T(8,128)(2,1)S(1)}, u32[]{:S(2)}, u32[]{:S(2)}) collective-permute-start(bf16[128,128]{1,0:T(8,128)(2,1)S(1)} %get-tuple-element.33), channel_id=1, source_target_pairs={{0,1},{1,0},{2,3},{3,2},{4,5},{5,4},{6,7},{7,6},{8,9},{9,8},{10,11... | collective-permute-start | bytes 98312 | tf_op jit(solution)/shard_map/ppermute | solution.py:30
  2.3 6.9 %collective-permute-start.1 = (bf16[128,128]{1,0:T(8,128)(2,1)S(1)}, bf16[128,128]{1,0:T(8,128)(2,1)S(1)}, u32[]{:S(2)}, u32[]{:S(2)}) collective-permute-start(bf16[128,128]{1,0:T(8,128)(2,1)S(1)} %get-tuple-element.34), channel_id=1, source_target_pairs={{1,2},{2,1},{5,6},{6,5},{9,10},{10,9},{13,14},{14,13},{17,18},{18,... | collective-permute-start | bytes 98312 | tf_op jit(solution)/shard_map/ppermute | solution.py:30
  9.8 7.2 %collective-permute-start.3 = (bf16[2,2,64,256]{3,2,1,0:T(8,128)(2,1)S(1)}, bf16[2,2,64,256]{3,2,1,0:T(8,128)(2,1)S(1)}, u32[]{:S(2)}, u32[]{:S(2)}) collective-permute-start(bf16[2,2,64,256]{3,2,1,0:T(8,128)(2,1)S(1)} %get-tuple-element.39), channel_id=1, source_target_pairs={{0,24},{24,0},{4,28},{28,4},{8,16},{16,8},{12,20},{20,12},{1,25},{... | collective-permute-start | bytes 393224 | tf_op jit(solution)/shard_map/ppermute | solution.py:30
  12.3 5.5 %collective-permute-start.5 = (bf16[2,2,64,256]{3,2,1,0:T(8,128)(2,1)S(1)}, bf16[2,2,64,256]{3,2,1,0:T(8,128)(2,1)S(1)}, u32[]{:S(2)}, u32[]{:S(2)}) collective-permute-start(bf16[2,2,64,256]{3,2,1,0:T(8,128)(2,1)S(1)} %get-tuple-element.40), channel_id=1, source_target_pairs={{0,16},{16,0},{4,20},{20,4},{8,24},{24,8},{12,28},{28,12},{1,17},{... | collective-permute-start | bytes 393224 | tf_op jit(solution)/shard_map/ppermute | solution.py:30
  12.8 5.0 %collective-permute-start.7 = (bf16[2,2,64,256]{3,2,1,0:T(8,128)(2,1)S(1)}, bf16[2,2,64,256]{3,2,1,0:T(8,128)(2,1)S(1)}, u32[]{:S(2)}, u32[]{:S(2)}) collective-permute-start(bf16[2,2,64,256]{3,2,1,0:T(8,128)(2,1)S(1)} %get-tuple-element.41), channel_id=1, source_target_pairs={{0,8},{8,0},{4,12},{12,4},{16,24},{24,16},{20,28},{28,20},{1,9},{9... | collective-permute-start | bytes 393224 | tf_op jit(solution)/shard_map/ppermute | solution.py:30
  13.3 5.6 %collective-permute-start.2 = (bf16[2,2,64,256]{3,2,1,0:T(8,128)(2,1)S(1)}, bf16[2,2,64,256]{3,2,1,0:T(8,128)(2,1)S(1)}, u32[]{:S(2)}, u32[]{:S(2)}) collective-permute-start(bf16[2,2,64,256]{3,2,1,0:T(8,128)(2,1)S(1)} %get-tuple-element.38.refs_0_), channel_id=1, source_target_pairs={{0,4},{4,0},{8,12},{12,8},{16,20},{20,16},{24,28},{28,24},{1,5},{5... | collective-permute-start | bytes 393224 | tf_op jit(solution)/shard_map/ppermute | solution.py:30
  17.0 2.0 %collective-permute-start.4 = (bf16[2,2,64,256]{3,2,1,0:T(8,128)(2,1)S(1)}, bf16[2,2,64,256]{3,2,1,0:T(8,128)(2,1)S(1)}, u32[]{:S(2)}, u32[]{:S(2)}) collective-permute-start(bf16[2,2,64,256]{3,2,1,0:T(8,128)(2,1)S(1)} %collective-permute-done.3.refs_2_), channel_id=1, source_target_pairs={{0,4},{4,0},{8,12},{12,8},{16,20},{20,16},{24,28},{28,24},{1,5},{5... | collective-permute-start | bytes 393224 | tf_op jit(solution)/shard_map/ppermute | solution.py:30
  17.8 1.3 %collective-permute-start.6 = (bf16[2,2,64,256]{3,2,1,0:T(8,128)(2,1)S(1)}, bf16[2,2,64,256]{3,2,1,0:T(8,128)(2,1)S(1)}, u32[]{:S(2)}, u32[]{:S(2)}) collective-permute-start(bf16[2,2,64,256]{3,2,1,0:T(8,128)(2,1)S(1)} %collective-permute-done.5.refs_4_), channel_id=1, source_target_pairs={{0,4},{4,0},{8,12},{12,8},{16,20},{20,16},{24,28},{28,24},{1,5},{5... | collective-permute-start | bytes 393224 | tf_op jit(solution)/shard_map/ppermute | solution.py:30
  17.8 1.5 %collective-permute-start.8 = (bf16[2,2,64,256]{3,2,1,0:T(8,128)(2,1)S(1)}, bf16[2,2,64,256]{3,2,1,0:T(8,128)(2,1)S(1)}, u32[]{:S(2)}, u32[]{:S(2)}) collective-permute-start(bf16[2,2,64,256]{3,2,1,0:T(8,128)(2,1)S(1)} %collective-permute-done.7.refs_6_), channel_id=1, source_target_pairs={{0,4},{4,0},{8,12},{12,8},{16,20},{20,16},{24,28},{28,24},{1,5},{5... | collective-permute-start | bytes 393224 | tf_op jit(solution)/shard_map/ppermute | solution.py:30
  20.5 4.7 %collective-permute-start.10 = (f32[36,128]{1,0:T(8,128)S(1)}, f32[36,128]{1,0:T(8,128)S(1)}, u32[]{:S(2)}, u32[]{:S(2)}) collective-permute-start(f32[36,128]{1,0:T(8,128)S(1)} %get-tuple-element.44), channel_id=1, source_target_pairs={{0,24},{24,0},{4,28},{28,4},{8,16},{16,8},{12,20},{20,12},{1,25},{... | collective-permute-start | bytes 55304 | tf_op jit(solution)/shard_map/ppermute | solution.py:30
  22.2 3.8 %collective-permute-start.11 = (f32[36,128]{1,0:T(8,128)S(1)}, f32[36,128]{1,0:T(8,128)S(1)}, u32[]{:S(2)}, u32[]{:S(2)}) collective-permute-start(f32[36,128]{1,0:T(8,128)S(1)} %get-tuple-element.45), channel_id=1, source_target_pairs={{0,16},{16,0},{4,20},{20,4},{8,24},{24,8},{12,28},{28,12},{1,17},{... | collective-permute-start | bytes 55304 | tf_op jit(solution)/shard_map/ppermute | solution.py:30
  23.4 3.8 %collective-permute-start.9 = (f32[36,128]{1,0:T(8,128)S(1)}, f32[36,128]{1,0:T(8,128)S(1)}, u32[]{:S(2)}, u32[]{:S(2)}) collective-permute-start(f32[36,128]{1,0:T(8,128)S(1)} %get-tuple-element.43), channel_id=1, source_target_pairs={{0,8},{8,0},{4,12},{12,4},{16,24},{24,16},{20,28},{28,20},{1,9},{9... | collective-permute-start | bytes 55304 | tf_op jit(solution)/shard_map/ppermute | solution.py:30

commit v16 on v15

--- a/solution.py
+++ b/solution.py
@@ -498,7 +498,7 @@
             pairs = [(i, i ^ bits) for i in range(owners) if i < i ^ bits]
             return exchanged(array, "date", pairs)
 
-        order = [3, 2, 1]
+        order = [3, 1, 2]
         own = tiles[0]
         direct = {number: swapped(tiles[number], CORES * number) for number in order}
         other = swapped(own, 1)

time: 28.3 us -> 28.5 us (level)
  transfers between devices with their start and end apart: 12 -> 12, of which waited for: 8 -> 9; matrix products, arithmetic and copies ran while one was open for 0% -> 0% of each run, Pallas kernels for 4% -> 4%
where the time goes in v16:
time: 28.5 us; the launch traced here: 28 us
  starting transfers between devices  12.6 us (44%)
  waiting for transfers between devices  8.86 us (31%)
  Pallas kernels  5.13 us (18%)
  between operations  1.36 us (5%)
    ppermute x12, starting transfers between devices, exchanged(): lax.ppermute(array, axis, [route for a, b in pairs for route in ((a, b),...  12.6 us
    ppermute x12, waiting for transfers between devices, exchanged(): lax.ppermute(array, axis, [route for a, b in pairs for route in ((a, b),...  8.86 us
    pallas_call x1, Pallas kernels, body(): pl.pallas_call(start_kernel, out_shape=(pltpu.VMEM(block.shape, block.dty...  1.55 us
    pallas_call x1, Pallas kernels, body(): pl.pallas_call(functools.partial(chip_looks_kernel, positions), out_shape...  1.17 us
    pallas_call x1, Pallas kernels, body(): pl.pallas_call(functools.partial(taps_kernel, chips, tile_lines), out_sha...  1.06 us
    pallas_call x1, Pallas kernels, body(): pl.pallas_call(functools.partial(chip_place_kernel, [0] + last), out_shap...  0.76 us
    pallas_call x1, Pallas kernels, body(): pl.pallas_call(functools.partial(resample_kernel, (line_groups, column_gr...  0.58 us
  transfers between devices with their start and end apart: 12, of which 9 were waited for; matrix products, arithmetic and copies ran while one was open for 0% of the time, Pallas kernels for 4%

profile of v16, /device:TPU:8, one launch (start us, length us, event | category | flops | bytes accessed | tf_op | source)
XLA Modules:
  0.0 28.0 jit_solution(6740155348297696357)
XLA Ops:
  0.6 1.6 %start.1 = (bf16[2,2,256,256]{3,2,1,0:T(8,128)(2,1)S(1)}, bf16[128,128]{1,0:T(8,128)(2,1)S(1)}, bf16[128,128]{1,0:T(8,128)(2,1)S(1)}, s32[16]{0:T(128)S(4)}, s32...) custom-call(bf16[2,2,256,256]{3,2,1,0:T(8,128)(2,1)} %x_ref.1, ...), custom_call_target="tpu_custom_call" | custom-call | tf_op jit(solution)/shard_map/start/pallas_call | solution.py:439
  2.2 0.1 collective-permute-start
  2.3 5.0 %collective-permute-start.1 = (bf16[128,128]{1,0:T(8,128)(2,1)S(1)}, bf16[128,128]{1,0:T(8,128)(2,1)S(1)}, u32[]{:S(2)}, u32[]{:S(2)}) collective-permute-start(bf16[128,128]{1,0:T(8,128)(2,1)S(1)} %get-tuple-element.34), channel_id=1, source_target_pairs={{1,2},{2,1},{5,6},{6,5},{9,10},{10,9},{13,14},{14,13},{17,18},{18,... | collective-permute-start | bytes 98312 | tf_op jit(solution)/shard_map/ppermute | solution.py:30
  7.3 1.1 %taps.1 = (f32[2,2,256,256]{3,2,1,0:T(8,128)S(1)}, bf16[64,512]{1,0:T(8,128)(2,1)S(1)}, bf16[64,512]{1,0:T(8,128)(2,1)S(1)}, bf16[2,256,256]{2,1,0:T(8,128)(2,1)S(1)}, bf16[512,128]{1,0:T(8,128)(2,1)S(1)}) custom-call(s32[16]{0:T(128)S(4)} %get-tuple-element.25.az_whole, s32[16]{0:T(128)S(4)} %get-tuple-element.26.az_part, ...), custom_call_target="tpu_custom_call" | custom-call | flops 4000000 | bytes 800000 | tf_op jit(solution)/shard_map/taps/pallas_call | solution.py:458
  8.4 0.0 collective-permute-done.even_ref
  8.4 0.8 %collective-permute-done.1.odd_ref = bf16[128,128]{1,0:T(8,128)(2,1)S(1)} collective-permute-done((bf16[128,128]{1,0:T(8,128)(2,1)S(1)}, bf16[128,128]{1,0:T(8,128)(2,1)S(1)}, u32[]{:S(2)}, u32[]{:S(2)}) %collective-permute-start.1) | collective-permute-done | bytes 32800 | tf_op jit(solution)/shard_map/ppermute | solution.py:30
  9.2 0.6 %resample.1 = (bf16[2,2,64,256]{3,2,1,0:T(8,128)(2,1)S(1)}, bf16[2,2,64,256]{3,2,1,0:T(8,128)(2,1)S(1)}, bf16[2,2,64,256]{3,2,1,0:T(8,128)(2,1)S(1)}, bf16[2,2,64,256]{3,2,1,0:T(8,128)(2,1)S(1)}) custom-call(f32[2,2,256,256]{3,2,1,0:T(8,128)S(1)} %get-tuple-element.32.inner_ref, bf16[128,128]{1,0:T(8,128)(2,1)S(1)} %collective-permute-done.even_ref, ...), custom_call_target="tpu_custom_call" | custom-call | tf_op jit(solution)/shard_map/resample/pallas_call | solution.py:478
  9.8 2.5 %collective-permute-start.3 = (bf16[2,2,64,256]{3,2,1,0:T(8,128)(2,1)S(1)}, bf16[2,2,64,256]{3,2,1,0:T(8,128)(2,1)S(1)}, u32[]{:S(2)}, u32[]{:S(2)}) collective-permute-start(bf16[2,2,64,256]{3,2,1,0:T(8,128)(2,1)S(1)} %get-tuple-element.39), channel_id=1, source_target_pairs={{0,24},{24,0},{4,28},{28,4},{8,16},{16,8},{12,20},{20,12},{1,25},{... | collective-permute-start | bytes 393224 | tf_op jit(solution)/shard_map/ppermute | solution.py:30
  12.3 0.5 %collective-permute-start.5 = (bf16[2,2,64,256]{3,2,1,0:T(8,128)(2,1)S(1)}, bf16[2,2,64,256]{3,2,1,0:T(8,128)(2,1)S(1)}, u32[]{:S(2)}, u32[]{:S(2)}) collective-permute-start(bf16[2,2,64,256]{3,2,1,0:T(8,128)(2,1)S(1)} %get-tuple-element.40), channel_id=1, source_target_pairs={{0,8},{8,0},{4,12},{12,4},{16,24},{24,16},{20,28},{28,20},{1,9},{9... | collective-permute-start | bytes 393224 | tf_op jit(solution)/shard_map/ppermute | solution.py:30
  12.8 0.5 %collective-permute-start.7 = (bf16[2,2,64,256]{3,2,1,0:T(8,128)(2,1)S(1)}, bf16[2,2,64,256]{3,2,1,0:T(8,128)(2,1)S(1)}, u32[]{:S(2)}, u32[]{:S(2)}) collective-permute-start(bf16[2,2,64,256]{3,2,1,0:T(8,128)(2,1)S(1)} %get-tuple-element.41), channel_id=1, source_target_pairs={{0,16},{16,0},{4,20},{20,4},{8,24},{24,8},{12,28},{28,12},{1,17},{... | collective-permute-start | bytes 393224 | tf_op jit(solution)/shard_map/ppermute | solution.py:30
  13.3 3.0 %collective-permute-done.3.refs_2_ = bf16[2,2,64,256]{3,2,1,0:T(8,128)(2,1)S(1)} collective-permute-done((bf16[2,2,64,256]{3,2,1,0:T(8,128)(2,1)S(1)}, bf16[2,2,64,256]{3,2,1,0:T(8,128)(2,1)S(1)}, u32[]{:S(2)}, u32[]{:S(2)}) %collective-permute-start.3) | collective-permute-done | bytes 131104 | tf_op jit(solution)/shard_map/ppermute | solution.py:30
  16.3 1.3 %collective-permute-done.5.refs_4_ = bf16[2,2,64,256]{3,2,1,0:T(8,128)(2,1)S(1)} collective-permute-done((bf16[2,2,64,256]{3,2,1,0:T(8,128)(2,1)S(1)}, bf16[2,2,64,256]{3,2,1,0:T(8,128)(2,1)S(1)}, u32[]{:S(2)}, u32[]{:S(2)}) %collective-permute-start.5) | collective-permute-done | bytes 131104 | tf_op jit(solution)/shard_map/ppermute | solution.py:30
  17.7 0.1 collective-permute-done.7.refs_6_
  17.8 0.4 %collective-permute-start.8 = (bf16[2,2,64,256]{3,2,1,0:T(8,128)(2,1)S(1)}, bf16[2,2,64,256]{3,2,1,0:T(8,128)(2,1)S(1)}, u32[]{:S(2)}, u32[]{:S(2)}) collective-permute-start(bf16[2,2,64,256]{3,2,1,0:T(8,128)(2,1)S(1)} %collective-permute-done.7.refs_6_), channel_id=1, source_target_pairs={{0,4},{4,0},{8,12},{12,8},{16,20},{20,16},{24,28},{28,24},{1,5},{5... | collective-permute-start | bytes 393224 | tf_op jit(solution)/shard_map/ppermute | solution.py:30
  18.9 0.2 collective-permute-done.6.refs_5_
  19.0 0.2 collective-permute-done.8.refs_7_
  19.2 1.2 %looks.1 = (f32[36,128]{1,0:T(8,128)S(1)}, f32[36,128]{1,0:T(8,128)S(1)}, f32[36,128]{1,0:T(8,128)S(1)}, f32[36,128]{1,0:T(8,128)S(1)}) custom-call(s32[1]{0:T(128)S(6)} %copy.10.root_ref, s32[2,16]{1,0:T(2,128)S(4)} %get-tuple-element.24.gap_ref, bf16[512,128]{1,0:T(8,128)(2,1)S(1)} %get-tuple-element.31.pool_ref, ...), custom_call_target="tpu_custom_call" | custom-call | tf_op jit(solution)/shard_map/looks/pallas_call | solution.py:510
  20.4 2.3 %collective-permute-start.10 = (f32[36,128]{1,0:T(8,128)S(1)}, f32[36,128]{1,0:T(8,128)S(1)}, u32[]{:S(2)}, u32[]{:S(2)}) collective-permute-start(f32[36,128]{1,0:T(8,128)S(1)} %get-tuple-element.44), channel_id=1, source_target_pairs={{0,24},{24,0},{4,28},{28,4},{8,16},{16,8},{12,20},{20,12},{1,25},{... | collective-permute-start | bytes 55304 | tf_op jit(solution)/shard_map/ppermute | solution.py:30
  22.7 0.7 %collective-permute-start.11 = (f32[36,128]{1,0:T(8,128)S(1)}, f32[36,128]{1,0:T(8,128)S(1)}, u32[]{:S(2)}, u32[]{:S(2)}) collective-permute-start(f32[36,128]{1,0:T(8,128)S(1)} %get-tuple-element.45), channel_id=1, source_target_pairs={{0,16},{16,0},{4,20},{20,4},{8,24},{24,8},{12,28},{28,12},{1,17},{... | collective-permute-start | bytes 55304 | tf_op jit(solution)/shard_map/ppermute | solution.py:30
  23.4 0.5 %collective-permute-start.9 = (f32[36,128]{1,0:T(8,128)S(1)}, f32[36,128]{1,0:T(8,128)S(1)}, u32[]{:S(2)}, u32[]{:S(2)}) collective-permute-start(f32[36,128]{1,0:T(8,128)S(1)} %get-tuple-element.43), channel_id=1, source_target_pairs={{0,8},{8,0},{4,12},{12,4},{16,24},{24,16},{20,28},{28,20},{1,9},{9... | collective-permute-start | bytes 55304 | tf_op jit(solution)/shard_map/ppermute | solution.py:30
  24.0 1.2 %collective-permute-done.10.refs_2_ = f32[36,128]{1,0:T(8,128)S(1)} collective-permute-done((f32[36,128]{1,0:T(8,128)S(1)}, f32[36,128]{1,0:T(8,128)S(1)}, u32[]{:S(2)}, u32[]{:S(2)}) %collective-permute-start.10) | collective-permute-done | bytes 18464 | tf_op jit(solution)/shard_map/ppermute | solution.py:30
  25.2 1.3 %collective-permute-done.11.refs_3_ = f32[36,128]{1,0:T(8,128)S(1)} collective-permute-done((f32[36,128]{1,0:T(8,128)S(1)}, f32[36,128]{1,0:T(8,128)S(1)}, u32[]{:S(2)}, u32[]{:S(2)}) %collective-permute-start.11) | collective-permute-done | bytes 18464 | tf_op jit(solution)/shard_map/ppermute | solution.py:30
  26.5 0.7 %collective-permute-done.9.refs_1_ = f32[36,128]{1,0:T(8,128)S(1)} collective-permute-done((f32[36,128]{1,0:T(8,128)S(1)}, f32[36,128]{1,0:T(8,128)S(1)}, u32[]{:S(2)}, u32[]{:S(2)}) %collective-permute-start.9) | collective-permute-done | bytes 18464 | tf_op jit(solution)/shard_map/ppermute | solution.py:30
  27.2 0.8 %place.1 = (f32[2,6,16,64]{3,2,1,0:T(8,128)}, f32[2,3,16,64]{3,2,1,0:T(8,128)}) custom-call(f32[36,128]{1,0:T(8,128)S(1)} %get-tuple-element.42.refs_0_, f32[36,128]{1,0:T(8,128)S(1)} %collective-permute-done.9.refs_1_, f32[36,128]{1,0:T(8,128)S(1)} %collective-permute-done.10.refs_2_, f32[36,128]{1,0:T(8,128)S(1)} %collective-permute-done.11.refs_3_), custom_call_target="tpu_custom_call" | custom-call | tf_op jit(solution)/shard_map/place/pallas_call | solution.py:526
  (5 shorter events, 0.0 us)
Async XLA Ops:
  2.2 6.2 %collective-permute-start = (bf16[128,128]{1,0:T(8,128)(2,1)S(1)}, bf16[128,128]{1,0:T(8,128)(2,1)S(1)}, u32[]{:S(2)}, u32[]{:S(2)}) collective-permute-start(bf16[128,128]{1,0:T(8,128)(2,1)S(1)} %get-tuple-element.33), channel_id=1, source_target_pairs={{0,1},{1,0},{2,3},{3,2},{4,5},{5,4},{6,7},{7,6},{8,9},{9,8},{10,11... | collective-permute-start | bytes 98312 | tf_op jit(solution)/shard_map/ppermute | solution.py:30
  2.3 6.9 %collective-permute-start.1 = (bf16[128,128]{1,0:T(8,128)(2,1)S(1)}, bf16[128,128]{1,0:T(8,128)(2,1)S(1)}, u32[]{:S(2)}, u32[]{:S(2)}) collective-permute-start(bf16[128,128]{1,0:T(8,128)(2,1)S(1)} %get-tuple-element.34), channel_id=1, source_target_pairs={{1,2},{2,1},{5,6},{6,5},{9,10},{10,9},{13,14},{14,13},{17,18},{18,... | collective-permute-start | bytes 98312 | tf_op jit(solution)/shard_map/ppermute | solution.py:30
  9.8 6.6 %collective-permute-start.3 = (bf16[2,2,64,256]{3,2,1,0:T(8,128)(2,1)S(1)}, bf16[2,2,64,256]{3,2,1,0:T(8,128)(2,1)S(1)}, u32[]{:S(2)}, u32[]{:S(2)}) collective-permute-start(bf16[2,2,64,256]{3,2,1,0:T(8,128)(2,1)S(1)} %get-tuple-element.39), channel_id=1, source_target_pairs={{0,24},{24,0},{4,28},{28,4},{8,16},{16,8},{12,20},{20,12},{1,25},{... | collective-permute-start | bytes 393224 | tf_op jit(solution)/shard_map/ppermute | solution.py:30
  12.3 5.4 %collective-permute-start.5 = (bf16[2,2,64,256]{3,2,1,0:T(8,128)(2,1)S(1)}, bf16[2,2,64,256]{3,2,1,0:T(8,128)(2,1)S(1)}, u32[]{:S(2)}, u32[]{:S(2)}) collective-permute-start(bf16[2,2,64,256]{3,2,1,0:T(8,128)(2,1)S(1)} %get-tuple-element.40), channel_id=1, source_target_pairs={{0,8},{8,0},{4,12},{12,4},{16,24},{24,16},{20,28},{28,20},{1,9},{9... | collective-permute-start | bytes 393224 | tf_op jit(solution)/shard_map/ppermute | solution.py:30
  12.8 5.0 %collective-permute-start.7 = (bf16[2,2,64,256]{3,2,1,0:T(8,128)(2,1)S(1)}, bf16[2,2,64,256]{3,2,1,0:T(8,128)(2,1)S(1)}, u32[]{:S(2)}, u32[]{:S(2)}) collective-permute-start(bf16[2,2,64,256]{3,2,1,0:T(8,128)(2,1)S(1)} %get-tuple-element.41), channel_id=1, source_target_pairs={{0,16},{16,0},{4,20},{20,4},{8,24},{24,8},{12,28},{28,12},{1,17},{... | collective-permute-start | bytes 393224 | tf_op jit(solution)/shard_map/ppermute | solution.py:30
  13.3 5.5 %collective-permute-start.2 = (bf16[2,2,64,256]{3,2,1,0:T(8,128)(2,1)S(1)}, bf16[2,2,64,256]{3,2,1,0:T(8,128)(2,1)S(1)}, u32[]{:S(2)}, u32[]{:S(2)}) collective-permute-start(bf16[2,2,64,256]{3,2,1,0:T(8,128)(2,1)S(1)} %get-tuple-element.38.refs_0_), channel_id=1, source_target_pairs={{0,4},{4,0},{8,12},{12,8},{16,20},{20,16},{24,28},{28,24},{1,5},{5... | collective-permute-start | bytes 393224 | tf_op jit(solution)/shard_map/ppermute | solution.py:30
  16.3 2.5 %collective-permute-start.4 = (bf16[2,2,64,256]{3,2,1,0:T(8,128)(2,1)S(1)}, bf16[2,2,64,256]{3,2,1,0:T(8,128)(2,1)S(1)}, u32[]{:S(2)}, u32[]{:S(2)}) collective-permute-start(bf16[2,2,64,256]{3,2,1,0:T(8,128)(2,1)S(1)} %collective-permute-done.3.refs_2_), channel_id=1, source_target_pairs={{0,4},{4,0},{8,12},{12,8},{16,20},{20,16},{24,28},{28,24},{1,5},{5... | collective-permute-start | bytes 393224 | tf_op jit(solution)/shard_map/ppermute | solution.py:30
  17.7 1.3 %collective-permute-start.6 = (bf16[2,2,64,256]{3,2,1,0:T(8,128)(2,1)S(1)}, bf16[2,2,64,256]{3,2,1,0:T(8,128)(2,1)S(1)}, u32[]{:S(2)}, u32[]{:S(2)}) collective-permute-start(bf16[2,2,64,256]{3,2,1,0:T(8,128)(2,1)S(1)} %collective-permute-done.5.refs_4_), channel_id=1, source_target_pairs={{0,4},{4,0},{8,12},{12,8},{16,20},{20,16},{24,28},{28,24},{1,5},{5... | collective-permute-start | bytes 393224 | tf_op jit(solution)/shard_map/ppermute | solution.py:30
  17.8 1.4 %collective-permute-start.8 = (bf16[2,2,64,256]{3,2,1,0:T(8,128)(2,1)S(1)}, bf16[2,2,64,256]{3,2,1,0:T(8,128)(2,1)S(1)}, u32[]{:S(2)}, u32[]{:S(2)}) collective-permute-start(bf16[2,2,64,256]{3,2,1,0:T(8,128)(2,1)S(1)} %collective-permute-done.7.refs_6_), channel_id=1, source_target_pairs={{0,4},{4,0},{8,12},{12,8},{16,20},{20,16},{24,28},{28,24},{1,5},{5... | collective-permute-start | bytes 393224 | tf_op jit(solution)/shard_map/ppermute | solution.py:30
  20.4 4.7 %collective-permute-start.10 = (f32[36,128]{1,0:T(8,128)S(1)}, f32[36,128]{1,0:T(8,128)S(1)}, u32[]{:S(2)}, u32[]{:S(2)}) collective-permute-start(f32[36,128]{1,0:T(8,128)S(1)} %get-tuple-element.44), channel_id=1, source_target_pairs={{0,24},{24,0},{4,28},{28,4},{8,16},{16,8},{12,20},{20,12},{1,25},{... | collective-permute-start | bytes 55304 | tf_op jit(solution)/shard_map/ppermute | solution.py:30
  22.7 3.8 %collective-permute-start.11 = (f32[36,128]{1,0:T(8,128)S(1)}, f32[36,128]{1,0:T(8,128)S(1)}, u32[]{:S(2)}, u32[]{:S(2)}) collective-permute-start(f32[36,128]{1,0:T(8,128)S(1)} %get-tuple-element.45), channel_id=1, source_target_pairs={{0,16},{16,0},{4,20},{20,4},{8,24},{24,8},{12,28},{28,12},{1,17},{... | collective-permute-start | bytes 55304 | tf_op jit(solution)/shard_map/ppermute | solution.py:30
  23.4 3.8 %collective-permute-start.9 = (f32[36,128]{1,0:T(8,128)S(1)}, f32[36,128]{1,0:T(8,128)S(1)}, u32[]{:S(2)}, u32[]{:S(2)}) collective-permute-start(f32[36,128]{1,0:T(8,128)S(1)} %get-tuple-element.43), channel_id=1, source_target_pairs={{0,8},{8,0},{4,12},{12,4},{16,24},{24,16},{20,28},{28,20},{1,9},{9... | collective-permute-start | bytes 55304 | tf_op jit(solution)/shard_map/ppermute | solution.py:30

commit v17 on v15

--- a/solution.py
+++ b/solution.py
@@ -521,7 +521,7 @@
             compiler_params=pltpu.CompilerParams(vmem_limit_bytes=GRANT),
         )(master_epoch_image, gap, near(pool), *[near(tile) for tile in held])
         back = {number: swapped(results[number], CORES * number) for number in order}
-        last = [1, 3, 2]
+        last = [2, 3, 1]
         pieces = [results[0]] + [back[number] for number in last]
         return pl.pallas_call(
             functools.partial(chip_place_kernel, [0] + last),

time: 28.3 us -> 28.5 us (level)
  no operation moved by 1% of the time
where the time goes in v17:
time: 28.5 us; the launch traced here: 28 us
  starting transfers between devices  12.7 us (45%)
  waiting for transfers between devices  8.73 us (31%)
  Pallas kernels  5.13 us (18%)
  between operations  1.36 us (5%)
    ppermute x12, starting transfers between devices, exchanged(): lax.ppermute(array, axis, [route for a, b in pairs for route in ((a, b),...  12.7 us
    ppermute x12, waiting for transfers between devices, exchanged(): lax.ppermute(array, axis, [route for a, b in pairs for route in ((a, b),...  8.73 us
    pallas_call x1, Pallas kernels, body(): pl.pallas_call(start_kernel, out_shape=(pltpu.VMEM(block.shape, block.dty...  1.55 us
    pallas_call x1, Pallas kernels, body(): pl.pallas_call(functools.partial(chip_looks_kernel, positions), out_shape...  1.17 us
    pallas_call x1, Pallas kernels, body(): pl.pallas_call(functools.partial(taps_kernel, chips, tile_lines), out_sha...  1.06 us
    pallas_call x1, Pallas kernels, body(): pl.pallas_call(functools.partial(chip_place_kernel, [0] + last), out_shap...  0.76 us
    pallas_call x1, Pallas kernels, body(): pl.pallas_call(functools.partial(resample_kernel, (line_groups, column_gr...  0.58 us
  transfers between devices with their start and end apart: 12, of which 8 were waited for; matrix products, arithmetic and copies ran while one was open for 0% of the time, Pallas kernels for 4%

profile of v17, /device:TPU:8, one launch (start us, length us, event | category | flops | bytes accessed | tf_op | source)
XLA Modules:
  0.0 28.0 jit_solution(14948650635215505797)
XLA Ops:
  0.6 1.6 %start.1 = (bf16[2,2,256,256]{3,2,1,0:T(8,128)(2,1)S(1)}, bf16[128,128]{1,0:T(8,128)(2,1)S(1)}, bf16[128,128]{1,0:T(8,128)(2,1)S(1)}, s32[16]{0:T(128)S(4)}, s32...) custom-call(bf16[2,2,256,256]{3,2,1,0:T(8,128)(2,1)} %x_ref.1, ...), custom_call_target="tpu_custom_call" | custom-call | tf_op jit(solution)/shard_map/start/pallas_call | solution.py:439
  2.2 0.1 collective-permute-start
  2.3 5.0 %collective-permute-start.1 = (bf16[128,128]{1,0:T(8,128)(2,1)S(1)}, bf16[128,128]{1,0:T(8,128)(2,1)S(1)}, u32[]{:S(2)}, u32[]{:S(2)}) collective-permute-start(bf16[128,128]{1,0:T(8,128)(2,1)S(1)} %get-tuple-element.34), channel_id=1, source_target_pairs={{1,2},{2,1},{5,6},{6,5},{9,10},{10,9},{13,14},{14,13},{17,18},{18,... | collective-permute-start | bytes 98312 | tf_op jit(solution)/shard_map/ppermute | solution.py:30
  7.3 1.1 %taps.1 = (f32[2,2,256,256]{3,2,1,0:T(8,128)S(1)}, bf16[64,512]{1,0:T(8,128)(2,1)S(1)}, bf16[64,512]{1,0:T(8,128)(2,1)S(1)}, bf16[2,256,256]{2,1,0:T(8,128)(2,1)S(1)}, bf16[512,128]{1,0:T(8,128)(2,1)S(1)}) custom-call(s32[16]{0:T(128)S(4)} %get-tuple-element.25.az_whole, s32[16]{0:T(128)S(4)} %get-tuple-element.26.az_part, ...), custom_call_target="tpu_custom_call" | custom-call | flops 4000000 | bytes 800000 | tf_op jit(solution)/shard_map/taps/pallas_call | solution.py:458
  8.4 0.0 collective-permute-done.even_ref
  8.4 0.8 %collective-permute-done.1.odd_ref = bf16[128,128]{1,0:T(8,128)(2,1)S(1)} collective-permute-done((bf16[128,128]{1,0:T(8,128)(2,1)S(1)}, bf16[128,128]{1,0:T(8,128)(2,1)S(1)}, u32[]{:S(2)}, u32[]{:S(2)}) %collective-permute-start.1) | collective-permute-done | bytes 32800 | tf_op jit(solution)/shard_map/ppermute | solution.py:30
  9.2 0.6 %resample.1 = (bf16[2,2,64,256]{3,2,1,0:T(8,128)(2,1)S(1)}, bf16[2,2,64,256]{3,2,1,0:T(8,128)(2,1)S(1)}, bf16[2,2,64,256]{3,2,1,0:T(8,128)(2,1)S(1)}, bf16[2,2,64,256]{3,2,1,0:T(8,128)(2,1)S(1)}) custom-call(f32[2,2,256,256]{3,2,1,0:T(8,128)S(1)} %get-tuple-element.32.inner_ref, bf16[128,128]{1,0:T(8,128)(2,1)S(1)} %collective-permute-done.even_ref, ...), custom_call_target="tpu_custom_call" | custom-call | tf_op jit(solution)/shard_map/resample/pallas_call | solution.py:478
  9.8 2.5 %collective-permute-start.3 = (bf16[2,2,64,256]{3,2,1,0:T(8,128)(2,1)S(1)}, bf16[2,2,64,256]{3,2,1,0:T(8,128)(2,1)S(1)}, u32[]{:S(2)}, u32[]{:S(2)}) collective-permute-start(bf16[2,2,64,256]{3,2,1,0:T(8,128)(2,1)S(1)} %get-tuple-element.39), channel_id=1, source_target_pairs={{0,24},{24,0},{4,28},{28,4},{8,16},{16,8},{12,20},{20,12},{1,25},{... | collective-permute-start | bytes 393224 | tf_op jit(solution)/shard_map/ppermute | solution.py:30
  12.3 0.5 %collective-permute-start.5 = (bf16[2,2,64,256]{3,2,1,0:T(8,128)(2,1)S(1)}, bf16[2,2,64,256]{3,2,1,0:T(8,128)(2,1)S(1)}, u32[]{:S(2)}, u32[]{:S(2)}) collective-permute-start(bf16[2,2,64,256]{3,2,1,0:T(8,128)(2,1)S(1)} %get-tuple-element.40), channel_id=1, source_target_pairs={{0,16},{16,0},{4,20},{20,4},{8,24},{24,8},{12,28},{28,12},{1,17},{... | collective-permute-start | bytes 393224 | tf_op jit(solution)/shard_map/ppermute | solution.py:30
  12.8 0.5 %collective-permute-start.7 = (bf16[2,2,64,256]{3,2,1,0:T(8,128)(2,1)S(1)}, bf16[2,2,64,256]{3,2,1,0:T(8,128)(2,1)S(1)}, u32[]{:S(2)}, u32[]{:S(2)}) collective-permute-start(bf16[2,2,64,256]{3,2,1,0:T(8,128)(2,1)S(1)} %get-tuple-element.41), channel_id=1, source_target_pairs={{0,8},{8,0},{4,12},{12,4},{16,24},{24,16},{20,28},{28,20},{1,9},{9... | collective-permute-start | bytes 393224 | tf_op jit(solution)/shard_map/ppermute | solution.py:30
  13.3 0.0 collective-permute-start.2
  13.3 3.6 %collective-permute-done.3.refs_2_ = bf16[2,2,64,256]{3,2,1,0:T(8,128)(2,1)S(1)} collective-permute-done((bf16[2,2,64,256]{3,2,1,0:T(8,128)(2,1)S(1)}, bf16[2,2,64,256]{3,2,1,0:T(8,128)(2,1)S(1)}, u32[]{:S(2)}, u32[]{:S(2)}) %collective-permute-start.3) | collective-permute-done | bytes 131104 | tf_op jit(solution)/shard_map/ppermute | solution.py:30
  17.0 0.9 %collective-permute-done.5.refs_4_ = bf16[2,2,64,256]{3,2,1,0:T(8,128)(2,1)S(1)} collective-permute-done((bf16[2,2,64,256]{3,2,1,0:T(8,128)(2,1)S(1)}, bf16[2,2,64,256]{3,2,1,0:T(8,128)(2,1)S(1)}, u32[]{:S(2)}, u32[]{:S(2)}) %collective-permute-start.5) | collective-permute-done | bytes 131104 | tf_op jit(solution)/shard_map/ppermute | solution.py:30
  17.8 0.5 %collective-permute-start.8 = (bf16[2,2,64,256]{3,2,1,0:T(8,128)(2,1)S(1)}, bf16[2,2,64,256]{3,2,1,0:T(8,128)(2,1)S(1)}, u32[]{:S(2)}, u32[]{:S(2)}) collective-permute-start(bf16[2,2,64,256]{3,2,1,0:T(8,128)(2,1)S(1)} %collective-permute-done.7.refs_6_), channel_id=1, source_target_pairs={{0,4},{4,0},{8,12},{12,8},{16,20},{20,16},{24,28},{28,24},{1,5},{5... | collective-permute-start | bytes 393224 | tf_op jit(solution)/shard_map/ppermute | solution.py:30
  19.0 0.2 collective-permute-done.6.refs_5_
  19.2 0.2 collective-permute-done.8.refs_7_
  19.3 1.2 %looks.1 = (f32[36,128]{1,0:T(8,128)S(1)}, f32[36,128]{1,0:T(8,128)S(1)}, f32[36,128]{1,0:T(8,128)S(1)}, f32[36,128]{1,0:T(8,128)S(1)}) custom-call(s32[1]{0:T(128)S(6)} %copy.10.root_ref, s32[2,16]{1,0:T(2,128)S(4)} %get-tuple-element.24.gap_ref, bf16[512,128]{1,0:T(8,128)(2,1)S(1)} %get-tuple-element.31.pool_ref, ...), custom_call_target="tpu_custom_call" | custom-call | tf_op jit(solution)/shard_map/looks/pallas_call | solution.py:510
  20.5 1.6 %collective-permute-start.10 = (f32[36,128]{1,0:T(8,128)S(1)}, f32[36,128]{1,0:T(8,128)S(1)}, u32[]{:S(2)}, u32[]{:S(2)}) collective-permute-start(f32[36,128]{1,0:T(8,128)S(1)} %get-tuple-element.44), channel_id=1, source_target_pairs={{0,24},{24,0},{4,28},{28,4},{8,16},{16,8},{12,20},{20,12},{1,25},{... | collective-permute-start | bytes 55304 | tf_op jit(solution)/shard_map/ppermute | solution.py:30
  22.2 1.2 %collective-permute-start.11 = (f32[36,128]{1,0:T(8,128)S(1)}, f32[36,128]{1,0:T(8,128)S(1)}, u32[]{:S(2)}, u32[]{:S(2)}) collective-permute-start(f32[36,128]{1,0:T(8,128)S(1)} %get-tuple-element.45), channel_id=1, source_target_pairs={{0,8},{8,0},{4,12},{12,4},{16,24},{24,16},{20,28},{28,20},{1,9},{9... | collective-permute-start | bytes 55304 | tf_op jit(solution)/shard_map/ppermute | solution.py:30
  23.4 0.7 %collective-permute-start.9 = (f32[36,128]{1,0:T(8,128)S(1)}, f32[36,128]{1,0:T(8,128)S(1)}, u32[]{:S(2)}, u32[]{:S(2)}) collective-permute-start(f32[36,128]{1,0:T(8,128)S(1)} %get-tuple-element.43), channel_id=1, source_target_pairs={{0,16},{16,0},{4,20},{20,4},{8,24},{24,8},{12,28},{28,12},{1,17},{... | collective-permute-start | bytes 55304 | tf_op jit(solution)/shard_map/ppermute | solution.py:30
  24.1 1.2 %collective-permute-done.10.refs_2_ = f32[36,128]{1,0:T(8,128)S(1)} collective-permute-done((f32[36,128]{1,0:T(8,128)S(1)}, f32[36,128]{1,0:T(8,128)S(1)}, u32[]{:S(2)}, u32[]{:S(2)}) %collective-permute-start.10) | collective-permute-done | bytes 18464 | tf_op jit(solution)/shard_map/ppermute | solution.py:30
  25.3 0.7 %collective-permute-done.11.refs_3_ = f32[36,128]{1,0:T(8,128)S(1)} collective-permute-done((f32[36,128]{1,0:T(8,128)S(1)}, f32[36,128]{1,0:T(8,128)S(1)}, u32[]{:S(2)}, u32[]{:S(2)}) %collective-permute-start.11) | collective-permute-done | bytes 18464 | tf_op jit(solution)/shard_map/ppermute | solution.py:30
  26.0 1.2 %collective-permute-done.9.refs_1_ = f32[36,128]{1,0:T(8,128)S(1)} collective-permute-done((f32[36,128]{1,0:T(8,128)S(1)}, f32[36,128]{1,0:T(8,128)S(1)}, u32[]{:S(2)}, u32[]{:S(2)}) %collective-permute-start.9) | collective-permute-done | bytes 18464 | tf_op jit(solution)/shard_map/ppermute | solution.py:30
  27.2 0.8 %place.1 = (f32[2,6,16,64]{3,2,1,0:T(8,128)}, f32[2,3,16,64]{3,2,1,0:T(8,128)}) custom-call(f32[36,128]{1,0:T(8,128)S(1)} %get-tuple-element.42.refs_0_, f32[36,128]{1,0:T(8,128)S(1)} %collective-permute-done.9.refs_1_, f32[36,128]{1,0:T(8,128)S(1)} %collective-permute-done.10.refs_2_, f32[36,128]{1,0:T(8,128)S(1)} %collective-permute-done.11.refs_3_), custom_call_target="tpu_custom_call" | custom-call | tf_op jit(solution)/shard_map/place/pallas_call | solution.py:526
  (5 shorter events, 0.0 us)
Async XLA Ops:
  2.2 6.2 %collective-permute-start = (bf16[128,128]{1,0:T(8,128)(2,1)S(1)}, bf16[128,128]{1,0:T(8,128)(2,1)S(1)}, u32[]{:S(2)}, u32[]{:S(2)}) collective-permute-start(bf16[128,128]{1,0:T(8,128)(2,1)S(1)} %get-tuple-element.33), channel_id=1, source_target_pairs={{0,1},{1,0},{2,3},{3,2},{4,5},{5,4},{6,7},{7,6},{8,9},{9,8},{10,11... | collective-permute-start | bytes 98312 | tf_op jit(solution)/shard_map/ppermute | solution.py:30
  2.3 6.9 %collective-permute-start.1 = (bf16[128,128]{1,0:T(8,128)(2,1)S(1)}, bf16[128,128]{1,0:T(8,128)(2,1)S(1)}, u32[]{:S(2)}, u32[]{:S(2)}) collective-permute-start(bf16[128,128]{1,0:T(8,128)(2,1)S(1)} %get-tuple-element.34), channel_id=1, source_target_pairs={{1,2},{2,1},{5,6},{6,5},{9,10},{10,9},{13,14},{14,13},{17,18},{18,... | collective-permute-start | bytes 98312 | tf_op jit(solution)/shard_map/ppermute | solution.py:30
  9.8 7.2 %collective-permute-start.3 = (bf16[2,2,64,256]{3,2,1,0:T(8,128)(2,1)S(1)}, bf16[2,2,64,256]{3,2,1,0:T(8,128)(2,1)S(1)}, u32[]{:S(2)}, u32[]{:S(2)}) collective-permute-start(bf16[2,2,64,256]{3,2,1,0:T(8,128)(2,1)S(1)} %get-tuple-element.39), channel_id=1, source_target_pairs={{0,24},{24,0},{4,28},{28,4},{8,16},{16,8},{12,20},{20,12},{1,25},{... | collective-permute-start | bytes 393224 | tf_op jit(solution)/shard_map/ppermute | solution.py:30
  12.3 5.5 %collective-permute-start.5 = (bf16[2,2,64,256]{3,2,1,0:T(8,128)(2,1)S(1)}, bf16[2,2,64,256]{3,2,1,0:T(8,128)(2,1)S(1)}, u32[]{:S(2)}, u32[]{:S(2)}) collective-permute-start(bf16[2,2,64,256]{3,2,1,0:T(8,128)(2,1)S(1)} %get-tuple-element.40), channel_id=1, source_target_pairs={{0,16},{16,0},{4,20},{20,4},{8,24},{24,8},{12,28},{28,12},{1,17},{... | collective-permute-start | bytes 393224 | tf_op jit(solution)/shard_map/ppermute | solution.py:30
  12.8 5.0 %collective-permute-start.7 = (bf16[2,2,64,256]{3,2,1,0:T(8,128)(2,1)S(1)}, bf16[2,2,64,256]{3,2,1,0:T(8,128)(2,1)S(1)}, u32[]{:S(2)}, u32[]{:S(2)}) collective-permute-start(bf16[2,2,64,256]{3,2,1,0:T(8,128)(2,1)S(1)} %get-tuple-element.41), channel_id=1, source_target_pairs={{0,8},{8,0},{4,12},{12,4},{16,24},{24,16},{20,28},{28,20},{1,9},{9... | collective-permute-start | bytes 393224 | tf_op jit(solution)/shard_map/ppermute | solution.py:30
  13.3 5.6 %collective-permute-start.2 = (bf16[2,2,64,256]{3,2,1,0:T(8,128)(2,1)S(1)}, bf16[2,2,64,256]{3,2,1,0:T(8,128)(2,1)S(1)}, u32[]{:S(2)}, u32[]{:S(2)}) collective-permute-start(bf16[2,2,64,256]{3,2,1,0:T(8,128)(2,1)S(1)} %get-tuple-element.38.refs_0_), channel_id=1, source_target_pairs={{0,4},{4,0},{8,12},{12,8},{16,20},{20,16},{24,28},{28,24},{1,5},{5... | collective-permute-start | bytes 393224 | tf_op jit(solution)/shard_map/ppermute | solution.py:30
  17.0 2.0 %collective-permute-start.4 = (bf16[2,2,64,256]{3,2,1,0:T(8,128)(2,1)S(1)}, bf16[2,2,64,256]{3,2,1,0:T(8,128)(2,1)S(1)}, u32[]{:S(2)}, u32[]{:S(2)}) collective-permute-start(bf16[2,2,64,256]{3,2,1,0:T(8,128)(2,1)S(1)} %collective-permute-done.3.refs_2_), channel_id=1, source_target_pairs={{0,4},{4,0},{8,12},{12,8},{16,20},{20,16},{24,28},{28,24},{1,5},{5... | collective-permute-start | bytes 393224 | tf_op jit(solution)/shard_map/ppermute | solution.py:30
  17.8 1.3 %collective-permute-start.6 = (bf16[2,2,64,256]{3,2,1,0:T(8,128)(2,1)S(1)}, bf16[2,2,64,256]{3,2,1,0:T(8,128)(2,1)S(1)}, u32[]{:S(2)}, u32[]{:S(2)}) collective-permute-start(bf16[2,2,64,256]{3,2,1,0:T(8,128)(2,1)S(1)} %collective-permute-done.5.refs_4_), channel_id=1, source_target_pairs={{0,4},{4,0},{8,12},{12,8},{16,20},{20,16},{24,28},{28,24},{1,5},{5... | collective-permute-start | bytes 393224 | tf_op jit(solution)/shard_map/ppermute | solution.py:30
  17.8 1.5 %collective-permute-start.8 = (bf16[2,2,64,256]{3,2,1,0:T(8,128)(2,1)S(1)}, bf16[2,2,64,256]{3,2,1,0:T(8,128)(2,1)S(1)}, u32[]{:S(2)}, u32[]{:S(2)}) collective-permute-start(bf16[2,2,64,256]{3,2,1,0:T(8,128)(2,1)S(1)} %collective-permute-done.7.refs_6_), channel_id=1, source_target_pairs={{0,4},{4,0},{8,12},{12,8},{16,20},{20,16},{24,28},{28,24},{1,5},{5... | collective-permute-start | bytes 393224 | tf_op jit(solution)/shard_map/ppermute | solution.py:30
  20.5 4.7 %collective-permute-start.10 = (f32[36,128]{1,0:T(8,128)S(1)}, f32[36,128]{1,0:T(8,128)S(1)}, u32[]{:S(2)}, u32[]{:S(2)}) collective-permute-start(f32[36,128]{1,0:T(8,128)S(1)} %get-tuple-element.44), channel_id=1, source_target_pairs={{0,24},{24,0},{4,28},{28,4},{8,16},{16,8},{12,20},{20,12},{1,25},{... | collective-permute-start | bytes 55304 | tf_op jit(solution)/shard_map/ppermute | solution.py:30
  22.2 3.8 %collective-permute-start.11 = (f32[36,128]{1,0:T(8,128)S(1)}, f32[36,128]{1,0:T(8,128)S(1)}, u32[]{:S(2)}, u32[]{:S(2)}) collective-permute-start(f32[36,128]{1,0:T(8,128)S(1)} %get-tuple-element.45), channel_id=1, source_target_pairs={{0,8},{8,0},{4,12},{12,4},{16,24},{24,16},{20,28},{28,20},{1,9},{9... | collective-permute-start | bytes 55304 | tf_op jit(solution)/shard_map/ppermute | solution.py:30
  23.4 3.8 %collective-permute-start.9 = (f32[36,128]{1,0:T(8,128)S(1)}, f32[36,128]{1,0:T(8,128)S(1)}, u32[]{:S(2)}, u32[]{:S(2)}) collective-permute-start(f32[36,128]{1,0:T(8,128)S(1)} %get-tuple-element.43), channel_id=1, source_target_pairs={{0,16},{16,0},{4,20},{20,4},{8,24},{24,8},{12,28},{28,12},{1,17},{... | collective-permute-start | bytes 55304 | tf_op jit(solution)/shard_map/ppermute | solution.py:30

commit v18 on v15

--- a/solution.py
+++ b/solution.py
@@ -183,18 +183,21 @@
     low = jnp.dot(edges[0], low_ref[...], preferred_element_type=jnp.float32)
     high = jnp.dot(edges[1], high_ref[...], preferred_element_type=jnp.float32)
     for slot in range(dates):
+        pieces = []
         for part in range(parts):
             spot = slice((slot * parts + part) * LANES, (slot * parts + part + 1) * LANES)
-            pieces = [
+            ranged = [
                 inner_ref[slot, part, :, start : start + LANES]
                 for start in range(0, columns, LANES)
             ]
-            pieces[0] += low[:, spot]
-            pieces[-1] += high[:, spot]
-            ranged = jnp.concatenate(pieces, axis=1)
-            moved = jnp.dot(
-                line_ref[slot], ranged.astype(jnp.bfloat16), preferred_element_type=jnp.float32
-            ).astype(jnp.bfloat16)
+            ranged[0] += low[:, spot]
+            ranged[-1] += high[:, spot]
+            pieces += [piece.astype(jnp.bfloat16) for piece in ranged]
+        both = jnp.dot(
+            line_ref[slot], jnp.concatenate(pieces, axis=1), preferred_element_type=jnp.float32
+        ).astype(jnp.bfloat16)
+        for part in range(parts):
+            moved = both[:, part * columns : (part + 1) * columns]
             for i in range(line_groups):
                 for j in range(column_groups):
                     tile = moved[

time: 28.3 us -> 28.3 us (level)
  no operation moved by 1% of the time
where the time goes in v18:
time: 28.3 us; the launch traced here: 27.9 us
  starting transfers between devices  12.7 us (45%)
  waiting for transfers between devices  8.7 us (31%)
  Pallas kernels  5.14 us (18%)
  between operations  1.36 us (5%)
    ppermute x12, starting transfers between devices, exchanged(): lax.ppermute(array, axis, [route for a, b in pairs for route in ((a, b),...  12.7 us
    ppermute x12, waiting for transfers between devices, exchanged(): lax.ppermute(array, axis, [route for a, b in pairs for route in ((a, b),...  8.7 us
    pallas_call x1, Pallas kernels, body(): pl.pallas_call(start_kernel, out_shape=(pltpu.VMEM(block.shape, block.dty...  1.55 us
    pallas_call x1, Pallas kernels, body(): pl.pallas_call(functools.partial(chip_looks_kernel, positions), out_shape...  1.18 us
    pallas_call x1, Pallas kernels, body(): pl.pallas_call(functools.partial(taps_kernel, chips, tile_lines), out_sha...  1.06 us
    pallas_call x1, Pallas kernels, body(): pl.pallas_call(functools.partial(chip_place_kernel, [0] + last), out_shap...  0.76 us
    pallas_call x1, Pallas kernels, body(): pl.pallas_call(functools.partial(resample_kernel, (line_groups, column_gr...  0.58 us
  transfers between devices with their start and end apart: 12, of which 8 were waited for; matrix products, arithmetic and copies ran while one was open for 0% of the time, Pallas kernels for 4%

profile of v18, /device:TPU:8, one launch (start us, length us, event | category | flops | bytes accessed | tf_op | source)
XLA Modules:
  0.0 27.9 jit_solution(3594998079697015968)
XLA Ops:
  0.6 1.6 %start.1 = (bf16[2,2,256,256]{3,2,1,0:T(8,128)(2,1)S(1)}, bf16[128,128]{1,0:T(8,128)(2,1)S(1)}, bf16[128,128]{1,0:T(8,128)(2,1)S(1)}, s32[16]{0:T(128)S(4)}, s32...) custom-call(bf16[2,2,256,256]{3,2,1,0:T(8,128)(2,1)} %x_ref.1, ...), custom_call_target="tpu_custom_call" | custom-call | tf_op jit(solution)/shard_map/start/pallas_call | solution.py:442
  2.2 0.1 collective-permute-start
  2.3 5.0 %collective-permute-start.1 = (bf16[128,128]{1,0:T(8,128)(2,1)S(1)}, bf16[128,128]{1,0:T(8,128)(2,1)S(1)}, u32[]{:S(2)}, u32[]{:S(2)}) collective-permute-start(bf16[128,128]{1,0:T(8,128)(2,1)S(1)} %get-tuple-element.34), channel_id=1, source_target_pairs={{1,2},{2,1},{5,6},{6,5},{9,10},{10,9},{13,14},{14,13},{17,18},{18,... | collective-permute-start | bytes 98312 | tf_op jit(solution)/shard_map/ppermute | solution.py:30
  7.3 1.1 %taps.1 = (f32[2,2,256,256]{3,2,1,0:T(8,128)S(1)}, bf16[64,512]{1,0:T(8,128)(2,1)S(1)}, bf16[64,512]{1,0:T(8,128)(2,1)S(1)}, bf16[2,256,256]{2,1,0:T(8,128)(2,1)S(1)}, bf16[512,128]{1,0:T(8,128)(2,1)S(1)}) custom-call(s32[16]{0:T(128)S(4)} %get-tuple-element.25.az_whole, s32[16]{0:T(128)S(4)} %get-tuple-element.26.az_part, ...), custom_call_target="tpu_custom_call" | custom-call | flops 4000000 | bytes 800000 | tf_op jit(solution)/shard_map/taps/pallas_call | solution.py:461
  8.4 0.0 collective-permute-done.even_ref
  8.4 0.8 %collective-permute-done.1.odd_ref = bf16[128,128]{1,0:T(8,128)(2,1)S(1)} collective-permute-done((bf16[128,128]{1,0:T(8,128)(2,1)S(1)}, bf16[128,128]{1,0:T(8,128)(2,1)S(1)}, u32[]{:S(2)}, u32[]{:S(2)}) %collective-permute-start.1) | collective-permute-done | bytes 32800 | tf_op jit(solution)/shard_map/ppermute | solution.py:30
  9.2 0.6 %resample.1 = (bf16[2,2,64,256]{3,2,1,0:T(8,128)(2,1)S(1)}, bf16[2,2,64,256]{3,2,1,0:T(8,128)(2,1)S(1)}, bf16[2,2,64,256]{3,2,1,0:T(8,128)(2,1)S(1)}, bf16[2,2,64,256]{3,2,1,0:T(8,128)(2,1)S(1)}) custom-call(f32[2,2,256,256]{3,2,1,0:T(8,128)S(1)} %get-tuple-element.32.inner_ref, bf16[128,128]{1,0:T(8,128)(2,1)S(1)} %collective-permute-done.even_ref, ...), custom_call_target="tpu_custom_call" | custom-call | tf_op jit(solution)/shard_map/resample/pallas_call | solution.py:481
  9.8 2.5 %collective-permute-start.3 = (bf16[2,2,64,256]{3,2,1,0:T(8,128)(2,1)S(1)}, bf16[2,2,64,256]{3,2,1,0:T(8,128)(2,1)S(1)}, u32[]{:S(2)}, u32[]{:S(2)}) collective-permute-start(bf16[2,2,64,256]{3,2,1,0:T(8,128)(2,1)S(1)} %get-tuple-element.39), channel_id=1, source_target_pairs={{0,24},{24,0},{4,28},{28,4},{8,16},{16,8},{12,20},{20,12},{1,25},{... | collective-permute-start | bytes 393224 | tf_op jit(solution)/shard_map/ppermute | solution.py:30
  12.3 0.5 %collective-permute-start.5 = (bf16[2,2,64,256]{3,2,1,0:T(8,128)(2,1)S(1)}, bf16[2,2,64,256]{3,2,1,0:T(8,128)(2,1)S(1)}, u32[]{:S(2)}, u32[]{:S(2)}) collective-permute-start(bf16[2,2,64,256]{3,2,1,0:T(8,128)(2,1)S(1)} %get-tuple-element.40), channel_id=1, source_target_pairs={{0,16},{16,0},{4,20},{20,4},{8,24},{24,8},{12,28},{28,12},{1,17},{... | collective-permute-start | bytes 393224 | tf_op jit(solution)/shard_map/ppermute | solution.py:30
  12.8 0.5 %collective-permute-start.7 = (bf16[2,2,64,256]{3,2,1,0:T(8,128)(2,1)S(1)}, bf16[2,2,64,256]{3,2,1,0:T(8,128)(2,1)S(1)}, u32[]{:S(2)}, u32[]{:S(2)}) collective-permute-start(bf16[2,2,64,256]{3,2,1,0:T(8,128)(2,1)S(1)} %get-tuple-element.41), channel_id=1, source_target_pairs={{0,8},{8,0},{4,12},{12,4},{16,24},{24,16},{20,28},{28,20},{1,9},{9... | collective-permute-start | bytes 393224 | tf_op jit(solution)/shard_map/ppermute | solution.py:30
  13.3 3.6 %collective-permute-done.3.refs_2_ = bf16[2,2,64,256]{3,2,1,0:T(8,128)(2,1)S(1)} collective-permute-done((bf16[2,2,64,256]{3,2,1,0:T(8,128)(2,1)S(1)}, bf16[2,2,64,256]{3,2,1,0:T(8,128)(2,1)S(1)}, u32[]{:S(2)}, u32[]{:S(2)}) %collective-permute-start.3) | collective-permute-done | bytes 131104 | tf_op jit(solution)/shard_map/ppermute | solution.py:30
  17.0 0.0 collective-permute-start.4
  17.0 0.9 %collective-permute-done.5.refs_4_ = bf16[2,2,64,256]{3,2,1,0:T(8,128)(2,1)S(1)} collective-permute-done((bf16[2,2,64,256]{3,2,1,0:T(8,128)(2,1)S(1)}, bf16[2,2,64,256]{3,2,1,0:T(8,128)(2,1)S(1)}, u32[]{:S(2)}, u32[]{:S(2)}) %collective-permute-start.5) | collective-permute-done | bytes 131104 | tf_op jit(solution)/shard_map/ppermute | solution.py:30
  17.8 0.5 %collective-permute-start.8 = (bf16[2,2,64,256]{3,2,1,0:T(8,128)(2,1)S(1)}, bf16[2,2,64,256]{3,2,1,0:T(8,128)(2,1)S(1)}, u32[]{:S(2)}, u32[]{:S(2)}) collective-permute-start(bf16[2,2,64,256]{3,2,1,0:T(8,128)(2,1)S(1)} %collective-permute-done.7.refs_6_), channel_id=1, source_target_pairs={{0,4},{4,0},{8,12},{12,8},{16,20},{20,16},{24,28},{28,24},{1,5},{5... | collective-permute-start | bytes 393224 | tf_op jit(solution)/shard_map/ppermute | solution.py:30
  19.0 0.2 collective-permute-done.6.refs_5_
  19.2 0.2 collective-permute-done.8.refs_7_
  19.3 1.2 %looks.1 = (f32[36,128]{1,0:T(8,128)S(1)}, f32[36,128]{1,0:T(8,128)S(1)}, f32[36,128]{1,0:T(8,128)S(1)}, f32[36,128]{1,0:T(8,128)S(1)}) custom-call(s32[1]{0:T(128)S(6)} %copy.10.root_ref, s32[2,16]{1,0:T(2,128)S(4)} %get-tuple-element.24.gap_ref, bf16[512,128]{1,0:T(8,128)(2,1)S(1)} %get-tuple-element.31.pool_ref, ...), custom_call_target="tpu_custom_call" | custom-call | tf_op jit(solution)/shard_map/looks/pallas_call | solution.py:513
  20.5 1.6 %collective-permute-start.10 = (f32[36,128]{1,0:T(8,128)S(1)}, f32[36,128]{1,0:T(8,128)S(1)}, u32[]{:S(2)}, u32[]{:S(2)}) collective-permute-start(f32[36,128]{1,0:T(8,128)S(1)} %get-tuple-element.44), channel_id=1, source_target_pairs={{0,24},{24,0},{4,28},{28,4},{8,16},{16,8},{12,20},{20,12},{1,25},{... | collective-permute-start | bytes 55304 | tf_op jit(solution)/shard_map/ppermute | solution.py:30
  22.2 1.2 %collective-permute-start.11 = (f32[36,128]{1,0:T(8,128)S(1)}, f32[36,128]{1,0:T(8,128)S(1)}, u32[]{:S(2)}, u32[]{:S(2)}) collective-permute-start(f32[36,128]{1,0:T(8,128)S(1)} %get-tuple-element.45), channel_id=1, source_target_pairs={{0,16},{16,0},{4,20},{20,4},{8,24},{24,8},{12,28},{28,12},{1,17},{... | collective-permute-start | bytes 55304 | tf_op jit(solution)/shard_map/ppermute | solution.py:30
  23.4 0.7 %collective-permute-start.9 = (f32[36,128]{1,0:T(8,128)S(1)}, f32[36,128]{1,0:T(8,128)S(1)}, u32[]{:S(2)}, u32[]{:S(2)}) collective-permute-start(f32[36,128]{1,0:T(8,128)S(1)} %get-tuple-element.43), channel_id=1, source_target_pairs={{0,8},{8,0},{4,12},{12,4},{16,24},{24,16},{20,28},{28,20},{1,9},{9... | collective-permute-start | bytes 55304 | tf_op jit(solution)/shard_map/ppermute | solution.py:30
  24.1 1.2 %collective-permute-done.10.refs_2_ = f32[36,128]{1,0:T(8,128)S(1)} collective-permute-done((f32[36,128]{1,0:T(8,128)S(1)}, f32[36,128]{1,0:T(8,128)S(1)}, u32[]{:S(2)}, u32[]{:S(2)}) %collective-permute-start.10) | collective-permute-done | bytes 18464 | tf_op jit(solution)/shard_map/ppermute | solution.py:30
  25.3 0.7 %collective-permute-done.11.refs_3_ = f32[36,128]{1,0:T(8,128)S(1)} collective-permute-done((f32[36,128]{1,0:T(8,128)S(1)}, f32[36,128]{1,0:T(8,128)S(1)}, u32[]{:S(2)}, u32[]{:S(2)}) %collective-permute-start.11) | collective-permute-done | bytes 18464 | tf_op jit(solution)/shard_map/ppermute | solution.py:30
  26.0 1.2 %collective-permute-done.9.refs_1_ = f32[36,128]{1,0:T(8,128)S(1)} collective-permute-done((f32[36,128]{1,0:T(8,128)S(1)}, f32[36,128]{1,0:T(8,128)S(1)}, u32[]{:S(2)}, u32[]{:S(2)}) %collective-permute-start.9) | collective-permute-done | bytes 18464 | tf_op jit(solution)/shard_map/ppermute | solution.py:30
  27.2 0.8 %place.1 = (f32[2,6,16,64]{3,2,1,0:T(8,128)}, f32[2,3,16,64]{3,2,1,0:T(8,128)}) custom-call(f32[36,128]{1,0:T(8,128)S(1)} %get-tuple-element.42.refs_0_, f32[36,128]{1,0:T(8,128)S(1)} %collective-permute-done.9.refs_1_, f32[36,128]{1,0:T(8,128)S(1)} %collective-permute-done.10.refs_2_, f32[36,128]{1,0:T(8,128)S(1)} %collective-permute-done.11.refs_3_), custom_call_target="tpu_custom_call" | custom-call | tf_op jit(solution)/shard_map/place/pallas_call | solution.py:529
  (5 shorter events, 0.0 us)
Async XLA Ops:
  2.2 6.2 %collective-permute-start = (bf16[128,128]{1,0:T(8,128)(2,1)S(1)}, bf16[128,128]{1,0:T(8,128)(2,1)S(1)}, u32[]{:S(2)}, u32[]{:S(2)}) collective-permute-start(bf16[128,128]{1,0:T(8,128)(2,1)S(1)} %get-tuple-element.33), channel_id=1, source_target_pairs={{0,1},{1,0},{2,3},{3,2},{4,5},{5,4},{6,7},{7,6},{8,9},{9,8},{10,11... | collective-permute-start | bytes 98312 | tf_op jit(solution)/shard_map/ppermute | solution.py:30
  2.3 6.9 %collective-permute-start.1 = (bf16[128,128]{1,0:T(8,128)(2,1)S(1)}, bf16[128,128]{1,0:T(8,128)(2,1)S(1)}, u32[]{:S(2)}, u32[]{:S(2)}) collective-permute-start(bf16[128,128]{1,0:T(8,128)(2,1)S(1)} %get-tuple-element.34), channel_id=1, source_target_pairs={{1,2},{2,1},{5,6},{6,5},{9,10},{10,9},{13,14},{14,13},{17,18},{18,... | collective-permute-start | bytes 98312 | tf_op jit(solution)/shard_map/ppermute | solution.py:30
  9.8 7.2 %collective-permute-start.3 = (bf16[2,2,64,256]{3,2,1,0:T(8,128)(2,1)S(1)}, bf16[2,2,64,256]{3,2,1,0:T(8,128)(2,1)S(1)}, u32[]{:S(2)}, u32[]{:S(2)}) collective-permute-start(bf16[2,2,64,256]{3,2,1,0:T(8,128)(2,1)S(1)} %get-tuple-element.39), channel_id=1, source_target_pairs={{0,24},{24,0},{4,28},{28,4},{8,16},{16,8},{12,20},{20,12},{1,25},{... | collective-permute-start | bytes 393224 | tf_op jit(solution)/shard_map/ppermute | solution.py:30
  12.3 5.5 %collective-permute-start.5 = (bf16[2,2,64,256]{3,2,1,0:T(8,128)(2,1)S(1)}, bf16[2,2,64,256]{3,2,1,0:T(8,128)(2,1)S(1)}, u32[]{:S(2)}, u32[]{:S(2)}) collective-permute-start(bf16[2,2,64,256]{3,2,1,0:T(8,128)(2,1)S(1)} %get-tuple-element.40), channel_id=1, source_target_pairs={{0,16},{16,0},{4,20},{20,4},{8,24},{24,8},{12,28},{28,12},{1,17},{... | collective-permute-start | bytes 393224 | tf_op jit(solution)/shard_map/ppermute | solution.py:30
  12.8 5.0 %collective-permute-start.7 = (bf16[2,2,64,256]{3,2,1,0:T(8,128)(2,1)S(1)}, bf16[2,2,64,256]{3,2,1,0:T(8,128)(2,1)S(1)}, u32[]{:S(2)}, u32[]{:S(2)}) collective-permute-start(bf16[2,2,64,256]{3,2,1,0:T(8,128)(2,1)S(1)} %get-tuple-element.41), channel_id=1, source_target_pairs={{0,8},{8,0},{4,12},{12,4},{16,24},{24,16},{20,28},{28,20},{1,9},{9... | collective-permute-start | bytes 393224 | tf_op jit(solution)/shard_map/ppermute | solution.py:30
  13.3 5.6 %collective-permute-start.2 = (bf16[2,2,64,256]{3,2,1,0:T(8,128)(2,1)S(1)}, bf16[2,2,64,256]{3,2,1,0:T(8,128)(2,1)S(1)}, u32[]{:S(2)}, u32[]{:S(2)}) collective-permute-start(bf16[2,2,64,256]{3,2,1,0:T(8,128)(2,1)S(1)} %get-tuple-element.38.refs_0_), channel_id=1, source_target_pairs={{0,4},{4,0},{8,12},{12,8},{16,20},{20,16},{24,28},{28,24},{1,5},{5... | collective-permute-start | bytes 393224 | tf_op jit(solution)/shard_map/ppermute | solution.py:30
  17.0 2.0 %collective-permute-start.4 = (bf16[2,2,64,256]{3,2,1,0:T(8,128)(2,1)S(1)}, bf16[2,2,64,256]{3,2,1,0:T(8,128)(2,1)S(1)}, u32[]{:S(2)}, u32[]{:S(2)}) collective-permute-start(bf16[2,2,64,256]{3,2,1,0:T(8,128)(2,1)S(1)} %collective-permute-done.3.refs_2_), channel_id=1, source_target_pairs={{0,4},{4,0},{8,12},{12,8},{16,20},{20,16},{24,28},{28,24},{1,5},{5... | collective-permute-start | bytes 393224 | tf_op jit(solution)/shard_map/ppermute | solution.py:30
  17.8 1.3 %collective-permute-start.6 = (bf16[2,2,64,256]{3,2,1,0:T(8,128)(2,1)S(1)}, bf16[2,2,64,256]{3,2,1,0:T(8,128)(2,1)S(1)}, u32[]{:S(2)}, u32[]{:S(2)}) collective-permute-start(bf16[2,2,64,256]{3,2,1,0:T(8,128)(2,1)S(1)} %collective-permute-done.5.refs_4_), channel_id=1, source_target_pairs={{0,4},{4,0},{8,12},{12,8},{16,20},{20,16},{24,28},{28,24},{1,5},{5... | collective-permute-start | bytes 393224 | tf_op jit(solution)/shard_map/ppermute | solution.py:30
  17.8 1.5 %collective-permute-start.8 = (bf16[2,2,64,256]{3,2,1,0:T(8,128)(2,1)S(1)}, bf16[2,2,64,256]{3,2,1,0:T(8,128)(2,1)S(1)}, u32[]{:S(2)}, u32[]{:S(2)}) collective-permute-start(bf16[2,2,64,256]{3,2,1,0:T(8,128)(2,1)S(1)} %collective-permute-done.7.refs_6_), channel_id=1, source_target_pairs={{0,4},{4,0},{8,12},{12,8},{16,20},{20,16},{24,28},{28,24},{1,5},{5... | collective-permute-start | bytes 393224 | tf_op jit(solution)/shard_map/ppermute | solution.py:30
  20.5 4.7 %collective-permute-start.10 = (f32[36,128]{1,0:T(8,128)S(1)}, f32[36,128]{1,0:T(8,128)S(1)}, u32[]{:S(2)}, u32[]{:S(2)}) collective-permute-start(f32[36,128]{1,0:T(8,128)S(1)} %get-tuple-element.44), channel_id=1, source_target_pairs={{0,24},{24,0},{4,28},{28,4},{8,16},{16,8},{12,20},{20,12},{1,25},{... | collective-permute-start | bytes 55304 | tf_op jit(solution)/shard_map/ppermute | solution.py:30
  22.2 3.8 %collective-permute-start.11 = (f32[36,128]{1,0:T(8,128)S(1)}, f32[36,128]{1,0:T(8,128)S(1)}, u32[]{:S(2)}, u32[]{:S(2)}) collective-permute-start(f32[36,128]{1,0:T(8,128)S(1)} %get-tuple-element.45), channel_id=1, source_target_pairs={{0,16},{16,0},{4,20},{20,4},{8,24},{24,8},{12,28},{28,12},{1,17},{... | collective-permute-start | bytes 55304 | tf_op jit(solution)/shard_map/ppermute | solution.py:30
  23.4 3.8 %collective-permute-start.9 = (f32[36,128]{1,0:T(8,128)S(1)}, f32[36,128]{1,0:T(8,128)S(1)}, u32[]{:S(2)}, u32[]{:S(2)}) collective-permute-start(f32[36,128]{1,0:T(8,128)S(1)} %get-tuple-element.43), channel_id=1, source_target_pairs={{0,8},{8,0},{4,12},{12,4},{16,24},{24,16},{20,28},{28,20},{1,9},{9... | collective-permute-start | bytes 55304 | tf_op jit(solution)/shard_map/ppermute | solution.py:30
